TPU v7x, 512 devices: a whole 4x8x8 slice. The times are simulated.
512 devices in a mesh: rep: 16 (over z, x_hi), exp: 32 (over y, x_lo, core).
Axes of the slice: x: 4 (x_hi: 2, x_lo: 2; x = x_hi * 2 + x_lo), y: 8, z: 8, core: 2. Of those that a mesh axis runs over, the one named last changes fastest.
Arguments:
- activations: bfloat16 [65536, 4096], P(('rep', 'exp')), may hold values from -6 to 6
- grad_hidden: bfloat16 [65536, 1024], P(('rep', 'exp')), may hold values from -6 to 6
- pre_gate: bfloat16 [65536, 1024], P(('rep', 'exp')), may hold values from -12 to 12
- pre_up: bfloat16 [65536, 1024], P(('rep', 'exp')), may hold values from -6 to 6
- modality: int32 [65536], P(('rep', 'exp')), may hold values from 0 to 1, as said below
- expert_index: int32 [65536], P(('rep', 'exp')), may hold values from 0 to 1
- master: float32 [16384, 2048], P(('exp', 'rep')), may hold values from -0.09375 to 0.09375
- first_moment: float32 [16384, 2048], P(('exp', 'rep')), may hold values from -18 to 18
- second_moment: float32 [16384, 2048], P(('exp', 'rep')), may hold values from 200 to 2000
Outputs:
- input_grad: bfloat16 [65536, 4096], P(('rep', 'exp'))
- new_master: float32 [16384, 2048], P(('exp', 'rep'))
- new_first: float32 [16384, 2048], P(('exp', 'rep'))
- new_second: float32 [16384, 2048], P(('exp', 'rep'))
Inputs may be any that keep to these rules, and one draw needn't show every extreme that they name: Among the 128 tokens of one device no expert 2 * modality + expert_index is named more than 48 times; in every replica group of 4096 tokens one expert is named exactly 48 times on every device.
All inputs are finite; a program needn't handle non-finite values.
Results may differ from a plain program's by a relative error of at most 0.019.
Values may be sent and summed in bfloat16 or wider, within the bound.
No kernel may reach another device: no remote copies, remote signals or barrier semaphores. Data moves between devices by JAX's collectives and lax.ppermute only.
A program may use at most 128 MiB of HBM per device.

v0:
```python
import jax
import jax.numpy as jnp
from jax import lax
from jax.sharding import PartitionSpec as P

EXPERTS = 4
CAP = 48


beta_one = 0.9
beta_two = 0.999
learn_rate = 0.02
adam_eps = 1e-08
adam_count = 1000


def from_partner(block, axis, stride):
    count = lax.axis_size(axis)
    route = []
    for low in range(count):
        high = low | 1 << stride
        if high != low and high < count:
            route += [(low, high), (high, low)]
    return lax.ppermute(block, axis, route)


def hidden_grads(saved_rows):
    grad_val = saved_rows[:, 0].astype(jnp.float32)
    gate_val = saved_rows[:, 1].astype(jnp.float32)
    up_val = saved_rows[:, 2].astype(jnp.float32)
    sig = 1.0 / (1.0 + jnp.exp(-gate_val))
    grad_gate = (grad_val * up_val * sig * (1.0 + gate_val * (1.0 - sig))).astype(jnp.bfloat16)
    grad_up = (grad_val * gate_val * sig).astype(jnp.bfloat16)
    return jnp.stack([grad_gate, grad_up], axis=1)


def body(
    activations,
    grad_hidden,
    pre_gate,
    pre_up,
    modality,
    expert_index,
    master,
    first_moment,
    second_moment,
):
    tok_count = activations.shape[0]
    width = activations.shape[1]
    hidden = grad_hidden.shape[1]
    exp_size = lax.axis_size("exp")
    group = exp_size // EXPERTS
    piece_width = width // group
    piece_hidden = hidden // group
    capacity = CAP
    rows_total = exp_size * capacity
    expert = 2 * modality + expert_index
    onehot = (expert[:, None] == jnp.arange(EXPERTS, dtype=jnp.int32)[None, :]).astype(jnp.int32)
    before = jnp.cumsum(onehot, axis=0) - onehot
    slot_pos = jnp.sum(before * onehot, axis=1)
    same_expert = expert[None, None, :] == jnp.arange(EXPERTS, dtype=jnp.int32)[:, None, None]
    same_slot = slot_pos[None, None, :] == jnp.arange(capacity, dtype=jnp.int32)[None, :, None]
    routing = (same_expert & same_slot).astype(jnp.bfloat16)
    x_split = activations.reshape(tok_count, group, piece_width)
    x_send = jnp.einsum("ect,tgd->egcd", routing, x_split, preferred_element_type=jnp.float32)
    x_send = x_send.astype(jnp.bfloat16).reshape(EXPERTS * group, capacity, piece_width)
    saved = jnp.stack([grad_hidden, pre_gate, pre_up], axis=1)
    split_saved = saved.reshape(tok_count, 3, group, piece_hidden)
    parts = jnp.einsum("ect,tsgh->egcsh", routing, split_saved, preferred_element_type=jnp.float32)
    parts = parts.astype(jnp.bfloat16).reshape(EXPERTS * group, capacity, 3 * piece_hidden)
    x_recv, h_recv = (
        lax.all_to_all(x_send, "exp", split_axis=0, concat_axis=0, tiled=True),
        lax.all_to_all(parts, "exp", split_axis=0, concat_axis=0, tiled=True),
    )
    local = hidden_grads(h_recv.reshape(rows_total, 3, piece_hidden))
    blocks = local[None]
    position = lax.axis_index("exp")
    for level in range(group.bit_length() - 1):
        partner = from_partner(blocks, "exp", level)
        upper = position // 2**level % 2 == 1
        blocks = jnp.where(
            upper,
            jnp.concatenate([partner, blocks], axis=0),
            jnp.concatenate([blocks, partner], axis=0),
        )
    grads_flat = jnp.transpose(blocks, (1, 2, 0, 3)).reshape(rows_total, 2 * hidden)
    x_rows = x_recv.reshape(rows_total, piece_width)
    shard_bf = master.astype(jnp.bfloat16)
    dx_rows = lax.dot_general(
        grads_flat,
        lax.all_gather(shard_bf, "rep", axis=0, tiled=True),
        (((1,), (1,)), ((), ())),
        preferred_element_type=jnp.float32,
    )
    dx_send = dx_rows.astype(jnp.bfloat16).reshape(exp_size, capacity, piece_width)
    back = lax.all_to_all(dx_send, "exp", split_axis=0, concat_axis=0, tiled=True)
    back = back.reshape(EXPERTS, group, capacity, piece_width)
    input_grad = jnp.einsum("ect,egcd->tgd", routing, back, preferred_element_type=jnp.float32)
    input_grad = input_grad.reshape(tok_count, width).astype(jnp.bfloat16)
    weight_grad = lax.psum_scatter(
        lax.dot_general(
            x_rows, grads_flat, (((0,), (0,)), ((), ())), preferred_element_type=jnp.float32
        ).astype(jnp.bfloat16),
        "rep",
        scatter_dimension=0,
        tiled=True,
    ).astype(jnp.float32)
    new_first = beta_one * first_moment + (1.0 - beta_one) * weight_grad
    new_second = beta_two * second_moment + (1.0 - beta_two) * weight_grad * weight_grad
    corr_one = 1.0 - beta_one**adam_count
    corr_two = 1.0 - beta_two**adam_count
    update = new_first / corr_one / (jnp.sqrt(new_second / corr_two) + adam_eps)
    new_master = master - learn_rate * update
    return (input_grad, new_master, new_first, new_second)


def solution(mesh):
    in_specs = (
        P(("rep", "exp"), None),
        P(("rep", "exp"), None),
        P(("rep", "exp"), None),
        P(("rep", "exp"), None),
        P(("rep", "exp")),
        P(("rep", "exp")),
        P(("exp", "rep"), None),
        P(("exp", "rep"), None),
        P(("exp", "rep"), None),
    )
    out_specs = (
        P(("rep", "exp"), None),
        P(("exp", "rep"), None),
        P(("exp", "rep"), None),
        P(("exp", "rep"), None),
    )
    return jax.shard_map(body, mesh=mesh, in_specs=in_specs, out_specs=out_specs, check_vma=False)
```

profile of v0, /device:TPU:6, one launch (start us, length us, event | category | flops | bytes accessed | tf_op | source)
XLA Modules:
  0.0 592.5 jit_solution(8257956728713181121)
XLA Ops:
  7.2 0.0 copy-start.5
  7.2 0.7 multiply_add_fusion
  7.9 0.1 fusion.20
  8.0 0.2 reduce_window_sum.11
  8.2 0.2 select_reduce_fusion
  8.4 1.1 copy.25
  9.5 0.2 copy.28
  9.7 1.1 copy.26
  10.8 0.2 copy.29
  11.0 0.0 copy-done.5
  11.0 0.2 copy.27
  11.2 0.2 copy.30
  11.4 0.5 fusion.2
  11.8 1.0 copy.31
  12.9 1.1 reshape.88
  13.9 40.4 %all_to_all.15 = bf16[32,48,384]{2,1,0:T(8,128)(2,1)} all-to-all(bf16[32,48,384]{2,1,0:T(8,128)(2,1)S(1)} %reshape.88), channel_id=1, replica_groups=mesh['rep'=16,'exp'=32] {'exp'}, dimensions={0} | all-to-all | bytes 2359296 | tf_op jit(solution)/shard_map/all_to_all | solution.py:73
  54.3 3.3 reshape.89
  57.6 1.7 fusion.30
  59.3 0.4 fusion.6
  59.8 0.1 maximum_bitcast_fusion.2
  59.9 1.9 collective-permute-start
  61.8 2.2 collective-permute-done
  64.0 0.3 maximum_select_fusion.2
  64.3 0.0 copy-start
  64.3 2.5 collective-permute-start.1
  66.8 0.0 copy-done
  66.9 0.0 copy-start.1
  66.9 35.9 %collective-permute-done.1 = bf16[2,1536,2,128]{3,1,2,0:T(8,128)(2,1)} collective-permute-done((bf16[2,1536,2,128]{3,1,2,0:T(8,128)(2,1)S(1)}, bf16[2,1536,2,128]{3,1,2,0:T(8,128)(2,1)}, u32[]{:S(2)}, u32[]{:S(2)}) %collective-permute-start.1) | collective-permute-done | bytes 1572896 | tf_op jit(solution)/shard_map/ppermute | solution.py:24
  102.8 3.1 maximum_select_fusion.1
  105.8 2.5 collective-permute-start.2
  108.3 0.0 copy-done.1
  108.3 1.7 convolution_convert_fusion.2
  110.0 5.3 all-to-all-start.2
  115.3 0.0 reduce-scatter.2.cloned.1.call-start
  115.4 72.9 %collective-permute-done.2 = bf16[4,1536,2,128]{3,1,2,0:T(8,128)(2,1)} collective-permute-done((bf16[4,1536,2,128]{3,1,2,0:T(8,128)(2,1)S(1)}, bf16[4,1536,2,128]{3,1,2,0:T(8,128)(2,1)}, u32[]{:S(2)}, u32[]{:S(2)}) %collective-permute-start.2) | collective-permute-done | bytes 3145760 | tf_op jit(solution)/shard_map/ppermute | solution.py:24
  188.3 6.6 %fusion = bf16[1536,2,8,128]{3,0,1,2:T(8,128)(2,1)} fusion(bf16[4,1536,2,128]{3,1,2,0:T(8,128)(2,1)S(1)} %maximum_select_fusion.1, bf16[4,1536,2,128]{3,1,2,0:T(8,128)(2,1)} %collective-permute-done.2, pred[]{:T(512)S(6)} %eq.71), kind=kLoop, calls=%fused_computation.1 | loop fusion | flops 9437184 | bytes 12582913 | tf_op jit(solution)/shard_map/transpose | solution.py:86
  195.0 8.6 %copy.35 = bf16[1536,2,8,128]{0,3,2,1:T(8,128)(2,1)} copy(bf16[1536,2,8,128]{3,0,1,2:T(8,128)(2,1)} %fusion) | data formatting | bytes 12582912 | tf_op jit(solution)/shard_map/transpose | solution.py:86
  203.6 6.6 %all-to-all-done.2 = bf16[32,48,512]{2,1,0:T(8,128)(2,1)} async-done(((bf16[32,48,512]{2,1,0:T(8,128)(2,1)}), bf16[32,48,512]{2,1,0:T(8,128)(2,1)}, u32[]{:S(2)}, u32[]{:S(2)}) %all-to-all-start.2) | async-done | bytes 1572896 | tf_op jit(solution)/shard_map/all_to_all | solution.py:72
  210.2 8.1 %convolution_convert_fusion = bf16[512,2048]{1,0:T(8,128)(2,1)} fusion(bf16[1536,512]{1,0:T(8,128)(2,1)} %bitcast.20, bf16[1536,2048]{0,1:T(8,128)(2,1)} %bitcast.54), kind=kOutput, calls=%fused_computation.5 | convolution fusion | flops 3222274048 | bytes 9961472 | tf_op jit(solution)/shard_map/dot_general | solution.py:101
  218.3 0.0 copy-start.2
  218.3 0.0 copy-start.3
  218.3 0.0 copy-start.4
  218.3 0.0 reduce-scatter.2.cloned.1.call-update
  218.3 0.2 all-gather.2.cloned.1.call-start
  218.6 216.3 %reduce-scatter.2.cloned.1.call-done = bf16[32,2048]{1,0:T(8,128)(2,1)} async-done(((bf16[512,2048]{1,0:T(8,128)(2,1)}), bf16[32,2048]{1,0:T(8,128)(2,1)}) %reduce-scatter.2.cloned.1.call-update) | async-done | bytes 131088 | tf_op jit(solution)/shard_map/reduce_scatter | solution.py:100
  434.9 0.0 copy-done.2
  434.9 0.0 copy-done.3
  434.9 0.0 copy-done.4
  434.9 1.9 multiply_subtract_fusion
  436.8 0.0 all-gather.2.cloned.1.call-update
  436.8 90.5 %all-gather.2.cloned.1.call-done = bf16[512,2048]{1,0:T(8,128)(2,1)} async-done(((bf16[32,2048]{1,0:T(8,128)(2,1)}), bf16[512,2048]{1,0:T(8,128)(2,1)}) %all-gather.2.cloned.1.call-update) | async-done | bytes 2097168 | tf_op jit(solution)/shard_map/all_gather | solution.py:91
  527.3 6.9 %convolution_convert_fusion.1 = bf16[1536,512]{1,0:T(8,128)(2,1)S(1)} fusion(bf16[1536,2048]{0,1:T(8,128)(2,1)} %bitcast.55, bf16[512,2048]{1,0:T(8,128)(2,1)} %all-gather.2.cloned.1.call-done), kind=kOutput, calls=%fused_computation.6 | convolution fusion | flops 3222011904 | bytes 9961472 | tf_op jit(solution)/shard_map/dot_general | solution.py:89
  534.2 48.3 %all_to_all.16 = bf16[32,48,512]{2,1,0:T(8,128)(2,1)S(1)} all-to-all(bf16[32,48,512]{2,1,0:T(8,128)(2,1)S(1)} %bitcast.59), channel_id=1, replica_groups=mesh['rep'=16,'exp'=32] {'exp'}, dimensions={0} | all-to-all | bytes 3145728 | tf_op jit(solution)/shard_map/all_to_all | solution.py:96
  582.6 0.9 copy.55
  583.5 0.8 dot_general.22
  584.2 1.5 fusion.1
  (2 shorter events, 0.0 us)
Async XLA Ops:
  7.2 3.8 copy-start.5
  59.9 4.2 collective-permute-start
  64.3 2.5 copy-start
  64.3 38.4 %collective-permute-start.1 = (bf16[2,1536,2,128]{3,1,2,0:T(8,128)(2,1)S(1)}, bf16[2,1536,2,128]{3,1,2,0:T(8,128)(2,1)}, u32[]{:S(2)}, u32[]{:S(2)}) collective-permute-start(bf16[2,1536,2,128]{3,1,2,0:T(8,128)(2,1)S(1)} %maximum_select_fusion.2), channel_id=1, source_target_pairs={{0,2},{2,0},{1,3},{3,1},{4,6},{6,4},{5,7},{7,5},{8,10},{10,8},{9,1... | collective-permute-start | bytes 4718600 | tf_op jit(solution)/shard_map/ppermute | solution.py:24
  66.9 41.5 %copy-start.1 = (bf16[128,4096]{1,0:T(8,128)(2,1)S(1)}, bf16[128,4096]{1,0:T(8,128)(2,1)}, u32[]{:S(2)}) copy-start(bf16[128,4096]{1,0:T(8,128)(2,1)} %param.9) | copy-start | bytes 3145732
  105.8 82.5 %collective-permute-start.2 = (bf16[4,1536,2,128]{3,1,2,0:T(8,128)(2,1)S(1)}, bf16[4,1536,2,128]{3,1,2,0:T(8,128)(2,1)}, u32[]{:S(2)}, u32[]{:S(2)}) collective-permute-start(bf16[4,1536,2,128]{3,1,2,0:T(8,128)(2,1)S(1)} %maximum_select_fusion.1), channel_id=1, source_target_pairs={{0,4},{4,0},{1,5},{5,1},{2,6},{6,2},{3,7},{7,3},{8,12},{12,8},{9,1... | collective-permute-start | bytes 9437192 | tf_op jit(solution)/shard_map/ppermute | solution.py:24
  110.0 100.2 %all-to-all-start.2 = ((bf16[32,48,512]{2,1,0:T(8,128)(2,1)}), bf16[32,48,512]{2,1,0:T(8,128)(2,1)}, u32[]{:S(2)}, u32[]{:S(2)}) async-start(bf16[32,48,512]{2,1,0:T(8,128)(2,1)} %bitcast.56), calls=%async_computation.2 | async-start | bytes 3145728 | tf_op jit(solution)/shard_map/all_to_all | solution.py:72
  115.3 319.5 %reduce-scatter.2.cloned.1.call-start = ((), (), s32[]{:S(2)}) async-start(), calls=%async_computation.5 | async-start | bytes 2228224 | tf_op jit(solution)/shard_map/reduce_scatter | solution.py:100
  218.3 216.5 %copy-start.2 = (f32[32,2048]{1,0:T(8,128)S(1)}, f32[32,2048]{1,0:T(8,128)}, u32[]{:S(2)}) copy-start(f32[32,2048]{1,0:T(8,128)} %param.15) | copy-start | bytes 786436
  218.3 216.5 %copy-start.3 = (f32[32,2048]{1,0:T(8,128)S(1)}, f32[32,2048]{1,0:T(8,128)}, u32[]{:S(2)}) copy-start(f32[32,2048]{1,0:T(8,128)} %param.17) | copy-start | bytes 786436
  218.3 216.5 %copy-start.4 = (f32[32,2048]{1,0:T(8,128)S(1)}, f32[32,2048]{1,0:T(8,128)}, u32[]{:S(2)}) copy-start(f32[32,2048]{1,0:T(8,128)} %param.16) | copy-start | bytes 786436
  218.3 309.0 %all-gather.2.cloned.1.call-start = ((), (), s32[]{:S(2)}) async-start(), calls=%async_computation.4 | async-start | bytes 2228224 | tf_op jit(solution)/shard_map/all_gather | solution.py:91
Sparse Core Ops, SparseCore 0:
  218.5 216.3 reduce-scatter.1
  438.6 88.7 all-gather.1
where the time goes:
time: 595 us; the launch traced here: 593 us
  waiting for transfers between devices  424 us (71%)
  blocking collectives  88.7 us (15%)
  local copies, waits for them, and re-layouts  20.4 us (3%)
  matrix products  18.6 us (3%)
  between operations  14.3 us (2%)
  other arithmetic  13.6 us (2%)
  starting transfers between devices  12.5 us (2%)
    reduce_scatter x1, waiting for transfers between devices, body(): lax.psum_scatter(lax.dot_general(x_rows, grads_flat, (((0,), (0,)), ((),...  216 us
    ppermute x3, waiting for transfers between devices, from_partner(): return lax.ppermute(block, axis, route)  111 us
    all_gather x1, waiting for transfers between devices, body(): lax.all_gather(shard_bf, 'rep', axis=0, tiled=True)  90.5 us
    all_to_all x1, blocking collectives, body(): lax.all_to_all(dx_send, 'exp', split_axis=0, concat_axis=0, tiled=True)  48.3 us
    all_to_all x1, blocking collectives, body(): lax.all_to_all(parts, 'exp', split_axis=0, concat_axis=0, tiled=True)  40.4 us
  transfers between devices with their start and end apart: 6, of which 6 were waited for; matrix products, arithmetic and copies ran while one was open for 3% of the time, Pallas kernels for 0%

commit v1 on v0

v1 whole, which is shorter than its diff:
```python
import jax
import jax.numpy as jnp
from jax import lax
from jax.experimental import pallas as pl
from jax.experimental.pallas import tpu as pltpu
from jax.sharding import Mesh, PartitionSpec as P

EXPERTS = 4
CAP = 48
GROUP = 8

beta_one = 0.9
beta_two = 0.999
learn_rate = 0.02
adam_eps = 1e-08
adam_count = 1000

REP = ("z", "xh")
EXP = ("y", "xl", "core")
ALL = REP + EXP
VMEM = pl.BlockSpec(memory_space=pltpu.VMEM)
BIG = 56 * 1024 * 1024


def params():
    return pltpu.CompilerParams(vmem_limit_bytes=BIG)


def routing_rows(mod_ref, idx_ref):
    expert = 2 * mod_ref[...] + idx_ref[...]
    count = expert.shape[1]
    onehot = (
        lax.broadcasted_iota(jnp.int32, (8, count), 0) == jnp.broadcast_to(expert, (8, count))
    ).astype(jnp.float32)
    earlier = (
        lax.broadcasted_iota(jnp.int32, (count, count), 0)
        < lax.broadcasted_iota(jnp.int32, (count, count), 1)
    ).astype(jnp.float32)
    before = jnp.dot(onehot, earlier, preferred_element_type=jnp.float32)
    pos = jnp.sum(before * onehot, axis=0, keepdims=True).astype(jnp.int32)
    slot = lax.broadcasted_iota(jnp.int32, (CAP, count), 0)
    rows = [
        jnp.where((slot == pos) & (expert == e), 1.0, 0.0).astype(jnp.bfloat16)
        for e in range(EXPERTS)
    ]
    return rows


def pack_grads_kernel(mod_ref, idx_ref, grad_ref, gate_ref, up_ref, out_ref):
    rows = routing_rows(mod_ref, idx_ref)
    routing = jnp.concatenate(rows, axis=0)
    hidden = grad_ref.shape[1]
    piece = out_ref.shape[3]
    for start in range(0, hidden, piece):
        cols = pl.ds(start, piece)
        grad_val = grad_ref[:, cols].astype(jnp.float32)
        gate_val = gate_ref[:, cols].astype(jnp.float32)
        up_val = up_ref[:, cols].astype(jnp.float32)
        sig = 1.0 / (1.0 + jnp.exp(-gate_val))
        grad_gate = (grad_val * up_val * sig * (1.0 + gate_val * (1.0 - sig))).astype(jnp.bfloat16)
        grad_up = (grad_val * gate_val * sig).astype(jnp.bfloat16)
        g = start // piece
        for at, block in ((g, grad_gate), (g + GROUP // 2, grad_up)):
            packed = jnp.dot(routing, block, preferred_element_type=jnp.float32)
            packed = packed.astype(jnp.bfloat16)
            for e in range(EXPERTS):
                out_ref[e, at] = packed[e * CAP : (e + 1) * CAP]


def pack_rows_kernel(mod_ref, idx_ref, x_ref, out_ref):
    rows = routing_rows(mod_ref, idx_ref)
    routing = jnp.concatenate(rows, axis=0)
    piece = out_ref.shape[3]
    for g in range(GROUP):
        block = x_ref[:, g * piece : (g + 1) * piece]
        packed = jnp.dot(routing, block, preferred_element_type=jnp.float32).astype(jnp.bfloat16)
        for e in range(EXPERTS):
            out_ref[e, g] = packed[e * CAP : (e + 1) * CAP]


def combine_kernel(mod_ref, idx_ref, back_ref, out_ref):
    rows = routing_rows(mod_ref, idx_ref)
    routing = jnp.concatenate(rows, axis=0)
    piece = back_ref.shape[3]
    for g in range(GROUP):
        block = jnp.concatenate([back_ref[e, g] for e in range(EXPERTS)], axis=0)
        total = lax.dot_general(
            routing, block, (((0,), (0,)), ((), ())), preferred_element_type=jnp.float32
        )
        out_ref[:, g * piece : (g + 1) * piece] = total.astype(jnp.bfloat16)


def weight_grad_kernel(x_ref, g_ref, out_ref, xt_ref):
    @pl.when(pl.program_id(0) == 0)
    def _():
        xt_ref[...] = x_ref[...].T

    out_ref[...] = jnp.dot(
        xt_ref[...], g_ref[0], preferred_element_type=jnp.float32
    ).astype(jnp.bfloat16)


def input_grad_kernel(g_ref, w_ref, out_ref):
    piece = g_ref.shape[2]
    total = None
    for g in range(GROUP):
        part = lax.dot_general(
            g_ref[g],
            w_ref[:, g * piece : (g + 1) * piece],
            (((1,), (1,)), ((), ())),
            preferred_element_type=jnp.float32,
        )
        total = part if total is None else total + part
    out_ref[...] = total.astype(jnp.bfloat16)


def swap_pairs(count):
    return [(i, i ^ 1) for i in range(count)]


def body(
    activations,
    grad_hidden,
    pre_gate,
    pre_up,
    modality,
    expert_index,
    master,
    first_moment,
    second_moment,
):
    tok_count, width = activations.shape
    hidden = grad_hidden.shape[1]
    piece = width // GROUP
    gpiece = 2 * hidden // GROUP
    members = EXPERTS * GROUP
    rows_total = members * CAP
    mod = modality.reshape(1, tok_count)
    idx = expert_index.reshape(1, tok_count)
    half = lax.axis_index("xh")

    shard_bf = master.astype(jnp.bfloat16)
    pair_bf = lax.all_gather(shard_bf, "xh", axis=0, tiled=True)

    g_send = pl.pallas_call(
        pack_grads_kernel,
        out_shape=jax.ShapeDtypeStruct((EXPERTS, GROUP, CAP, gpiece), jnp.bfloat16),
        in_specs=[VMEM] * 5,
        out_specs=VMEM,
        compiler_params=params(),
        name="pack_grads",
    )(mod, idx, grad_hidden, pre_gate, pre_up)
    weights = lax.all_gather(pair_bf, "z", axis=0, tiled=True)
    g_recv = lax.all_to_all(
        g_send.reshape(members, CAP, gpiece), EXP, split_axis=0, concat_axis=0, tiled=True
    )
    g_mine = g_recv.reshape(rows_total, gpiece)
    g_all = lax.all_gather(
        g_mine,
        EXP,
        axis=0,
        tiled=False,
        axis_index_groups=[list(range(GROUP * e, GROUP * (e + 1))) for e in range(EXPERTS)],
    )
    x_send = pl.pallas_call(
        pack_rows_kernel,
        out_shape=jax.ShapeDtypeStruct((EXPERTS, GROUP, CAP, piece), jnp.bfloat16),
        in_specs=[VMEM] * 3,
        out_specs=VMEM,
        compiler_params=params(),
        name="pack_rows",
    )(mod, idx, activations)
    x_recv = lax.all_to_all(
        x_send.reshape(members, CAP, piece), EXP, split_axis=0, concat_axis=0, tiled=True
    )
    x_rows = x_recv.reshape(rows_total, piece)
    g_all, weights, x_rows = lax.optimization_barrier((g_all, weights, x_rows))

    grad_part = pl.pallas_call(
        weight_grad_kernel,
        grid=(GROUP,),
        out_shape=jax.ShapeDtypeStruct((piece, 2 * hidden), jnp.bfloat16),
        in_specs=[
            pl.BlockSpec((rows_total, piece), lambda g: (0, 0)),
            pl.BlockSpec((1, rows_total, gpiece), lambda g: (g, 0, 0)),
        ],
        out_specs=pl.BlockSpec((piece, gpiece), lambda g: (0, g)),
        scratch_shapes=[pltpu.VMEM((piece, rows_total), jnp.bfloat16)],
        compiler_params=params(),
        name="weight_grad",
    )(x_rows, g_all)
    grad_z = lax.psum_scatter(grad_part, "z", scatter_dimension=0, tiled=True)

    block = 256
    dx_rows = pl.pallas_call(
        input_grad_kernel,
        grid=(rows_total // block,),
        out_shape=jax.ShapeDtypeStruct((rows_total, piece), jnp.bfloat16),
        in_specs=[
            pl.BlockSpec((GROUP, block, gpiece), lambda t: (0, t, 0)),
            pl.BlockSpec((piece, 2 * hidden), lambda t: (0, 0)),
        ],
        out_specs=pl.BlockSpec((block, piece), lambda t: (t, 0)),
        compiler_params=params(),
        name="input_grad",
    )(g_all, weights)
    back = lax.all_to_all(
        dx_rows.reshape(members, CAP, piece), EXP, split_axis=0, concat_axis=0, tiled=True
    )
    input_grad = pl.pallas_call(
        combine_kernel,
        out_shape=jax.ShapeDtypeStruct((tok_count, width), jnp.bfloat16),
        in_specs=[VMEM] * 3,
        out_specs=VMEM,
        compiler_params=params(),
        name="combine",
    )(mod, idx, back.reshape(EXPERTS, GROUP, CAP, piece))

    keep_rows = master.shape[0]
    halves = grad_z.reshape(2, keep_rows, 2 * hidden)
    own = lax.dynamic_index_in_dim(halves, half, 0, keepdims=False)
    other = lax.dynamic_index_in_dim(halves, 1 - half, 0, keepdims=False)
    came = lax.ppermute(other, "xh", swap_pairs(2))
    weight_grad = own.astype(jnp.float32) + came.astype(jnp.float32)
    new_first = beta_one * first_moment + (1.0 - beta_one) * weight_grad
    new_second = beta_two * second_moment + (1.0 - beta_two) * weight_grad * weight_grad
    corr_one = 1.0 - beta_one**adam_count
    corr_two = 1.0 - beta_two**adam_count
    update = new_first / corr_one / (jnp.sqrt(new_second / corr_two) + adam_eps)
    new_master = master - learn_rate * update
    return (input_grad, new_master, new_first, new_second)


def solution(mesh):
    fine = Mesh(mesh.devices.reshape(8, 2, 8, 2, 2), ALL)
    tok = P(ALL, None)
    par = P(EXP + REP, None)
    in_specs = (tok, tok, tok, tok, P(ALL), P(ALL), par, par, par)
    out_specs = (tok, par, par, par)
    return jax.shard_map(body, mesh=fine, in_specs=in_specs, out_specs=out_specs, check_vma=False)
```

time: 595 us -> 201 us (0.34)
  waiting for transfers between devices: 424 us -> 53 us
  Pallas kernels: 0 us -> 26.9 us
  matrix products: 18.6 us -> 0 us
  local copies, waits for them, and re-layouts: 20.4 us -> 2.17 us
  other arithmetic: 13.6 us -> 1.96 us
    reduce_scatter x1, waiting for transfers between devices: 216 us -> 33.1 us  [body(): grad_z = lax.psum_scatter(grad_part, 'z', scatter_dimension=0, tiled=True)]
    ppermute x3 -> x1, waiting for transfers between devices: 111 us -> 0.01 us  [body(): came = lax.ppermute(other, 'xh', swap_pairs(2))]
    all_gather x1 -> x2, waiting for transfers between devices: 90.5 us -> 18 us  [the longest x1 18 us: body(): lax.all_gather(g_mine, EXP, axis=0, tiled=False, axis_index_groups=[list(...]
    pallas_call x0 -> x5, Pallas kernels: none -> 26.9 us  [the longest x1 9.67 us: body(): pl.pallas_call(weight_grad_kernel, grid=(GROUP,), out_shape=jax.ShapeDtyp...]
    dot_general x5 -> x0, matrix products: 18.6 us -> none  [the longest x1 8.09 us: body(): lax.dot_general(x_rows, grads_flat, (((0,), (0,)), ((), ())), preferred_e...]
    transpose x1 -> x0, local copies, waits for them, and re-layouts: 8.65 us -> none  [body(): jnp.transpose(blocks, (1, 2, 0, 3)).reshape(rows_total, 2 * hidden)]
    all_gather x0 -> x1, blocking collectives: none -> 7.52 us  [body(): pair_bf = lax.all_gather(shard_bf, 'xh', axis=0, tiled=True)]
    all_to_all x2, blocking collectives: 88.7 us -> 82 us  [the longest x1 49.8 us: body(): lax.all_to_all(x_send.reshape(members, CAP, piece), EXP, split_axis=0, co...]
  transfers between devices with their start and end apart: 6 -> 5, of which waited for: 6 -> 3; matrix products, arithmetic and copies ran while one was open for 3% -> 0% of each run, Pallas kernels for 0% -> 9%
where the time goes in v1:
time: 201 us; the launch traced here: 198 us
  blocking collectives  89.5 us (45%)
  waiting for transfers between devices  53 us (26%)
  Pallas kernels  26.9 us (13%)
  between operations  13.8 us (7%)
  starting transfers between devices  10.9 us (5%)
  local copies, waits for them, and re-layouts  2.17 us (1%)
    all_to_all x1, blocking collectives, body(): lax.all_to_all(x_send.reshape(members, CAP, piece), EXP, split_axis=0, co...  49.8 us
    reduce_scatter x1, waiting for transfers between devices, body(): grad_z = lax.psum_scatter(grad_part, 'z', scatter_dimension=0, tiled=True)  33.1 us
    all_to_all x1, blocking collectives, body(): lax.all_to_all(g_send.reshape(members, CAP, gpiece), EXP, split_axis=0, c...  32.1 us
    all_gather x1, waiting for transfers between devices, body(): lax.all_gather(g_mine, EXP, axis=0, tiled=False, axis_index_groups=[list(...  18 us
    pallas_call x1, Pallas kernels, body(): pl.pallas_call(weight_grad_kernel, grid=(GROUP,), out_shape=jax.ShapeDtyp...  9.67 us
    pallas_call x1, Pallas kernels, body(): pl.pallas_call(input_grad_kernel, grid=(rows_total // block,), out_shape=...  8.46 us
    all_to_all x1, starting transfers between devices, body(): lax.all_to_all(dx_rows.reshape(members, CAP, piece), EXP, split_axis=0, c...  7.55 us
    all_gather x1, blocking collectives, body(): pair_bf = lax.all_gather(shard_bf, 'xh', axis=0, tiled=True)  7.52 us
  transfers between devices with their start and end apart: 5, of which 3 were waited for; matrix products, arithmetic and copies ran while one was open for 0% of the time, Pallas kernels for 9%

profile of v1, /device:TPU:6, one launch (start us, length us, event | category | flops | bytes accessed | tf_op | source)
XLA Modules:
  0.0 198.3 jit_solution(6430483947804813405)
XLA Ops:
  7.2 0.0 all-gather.5.cloned.1.call-start
  7.2 1.0 convert_element_type.12
  8.2 7.5 %all_gather.10 = bf16[64,2048]{1,0:T(8,128)(2,1)} all-gather(bf16[32,2048]{1,0:T(8,128)(2,1)S(1)} %convert_element_type.12), channel_id=1, replica_groups=mesh['z'=8,'xh'=2,'y'=8,'xl'=2,'core'=2] {'xh'}, dimensions={0}, use_global_device_ids=true | all-gather | bytes 393216 | tf_op jit(solution)/shard_map/all_gather | solution.py:143
  15.7 0.0 all-gather.5.cloned.1.call-update
  15.7 0.0 all-gather.3.cloned.1.call-start
  15.8 2.6 %pack_grads.1 = bf16[4,8,48,256]{3,2,1,0:T(8,128)(2,1)} custom-call(s32[1,128]{1,0:T(1,128)} %bitcast.25, s32[1,128]{1,0:T(1,128)} %bitcast.28, bf16[128,1024]{1,0:T(8,128)(2,1)} %grad_ref.1, bf16[128,1024]{1,0:T(8,128)(2,1)} %gate_ref.1, bf16[128,1024]{1,0:T(8,128)(2,1)} %up_ref.1), custom_call_target="tpu_custom_call" | custom-call | tf_op jit(solution)/shard_map/pack_grads/pallas_call | solution.py:145
  18.4 32.1 %all_to_all.15 = bf16[32,48,256]{2,1,0:T(8,128)(2,1)} all-to-all(bf16[32,48,256]{2,1,0:T(8,128)(2,1)} %bitcast.22), channel_id=1, replica_groups=mesh['z'=8,'xh'=2,'y'=8,'xl'=2,'core'=2] {'y','xl','core'}, dimensions={0} | all-to-all | bytes 1572864 | tf_op jit(solution)/shard_map/all_to_all | solution.py:154
  50.5 0.0 all-gather.3.cloned.1.call-update
  50.5 0.0 reduce-scatter.2.cloned.1.call-start
  50.6 3.2 %pack_rows.1 = bf16[4,8,48,512]{3,2,1,0:T(8,128)(2,1)} custom-call(s32[1,128]{1,0:T(1,128)} %bitcast.26, s32[1,128]{1,0:T(1,128)} %bitcast.29, bf16[128,4096]{1,0:T(8,128)(2,1)} %x_ref.1), custom_call_target="tpu_custom_call" | custom-call | tf_op jit(solution)/shard_map/pack_rows/pallas_call | solution.py:165
  53.7 49.8 %all_to_all.16 = bf16[32,48,512]{2,1,0:T(8,128)(2,1)} all-to-all(bf16[32,48,512]{2,1,0:T(8,128)(2,1)} %bitcast.20), channel_id=1, replica_groups=mesh['z'=8,'xh'=2,'y'=8,'xl'=2,'core'=2] {'y','xl','core'}, dimensions={0} | all-to-all | bytes 3145728 | tf_op jit(solution)/shard_map/all_to_all | solution.py:173
  103.6 0.0 all-gather.5.cloned.1.call-done.w_ref
  103.6 18.0 %all-gather.3.cloned.1.call-done.g_ref = bf16[8,1536,256]{2,1,0:T(8,128)(2,1)} async-done(((bf16[1,1536,256]{2,1,0:T(8,128)(2,1)}), bf16[8,1536,256]{2,1,0:T(8,128)(2,1)}) %all-gather.3.cloned.1.call-update) | async-done | bytes 6291472 | tf_op jit(solution)/shard_map/all_gather | solution.py:158
  121.6 9.7 %weight_grad.1 = bf16[512,2048]{1,0:T(8,128)(2,1)} custom-call(bf16[1536,512]{1,0:T(8,128)(2,1)} %bitcast.19, bf16[8,1536,256]{2,1,0:T(8,128)(2,1)} %all-gather.3.cloned.1.call-done.g_ref), custom_call_target="tpu_custom_call" | custom-call | tf_op jit(solution)/shard_map/weight_grad/pallas_call | solution.py:179
  131.3 0.0 reduce-scatter.2.cloned.1.call-update
  131.3 8.5 %input_grad.1 = bf16[1536,512]{1,0:T(8,128)(2,1)} custom-call(bf16[8,1536,256]{2,1,0:T(8,128)(2,1)} %all-gather.3.cloned.1.call-done.g_ref, bf16[512,2048]{1,0:T(8,128)(2,1)} %all-gather.5.cloned.1.call-done.w_ref), custom_call_target="tpu_custom_call" | custom-call | tf_op jit(solution)/shard_map/input_grad/pallas_call | solution.py:195
  139.7 7.5 %all-to-all-start.2 = ((bf16[32,48,512]{2,1,0:T(8,128)(2,1)}), bf16[32,48,512]{2,1,0:T(8,128)(2,1)S(1)}, u32[]{:S(2)}, u32[]{:S(2)}) async-start(bf16[32,48,512]{2,1,0:T(8,128)(2,1)} %bitcast.18), calls=%async_computation.2 | async-start | bytes 3145728 | tf_op jit(solution)/shard_map/all_to_all | solution.py:207
  147.3 0.0 copy-start.1
  147.3 0.0 copy-start.2
  147.3 0.0 copy-start.3
  147.3 33.1 %reduce-scatter.2.cloned.1.call-done = bf16[64,2048]{1,0:T(8,128)(2,1)} async-done(((bf16[512,2048]{1,0:T(8,128)(2,1)}), bf16[64,2048]{1,0:T(8,128)(2,1)}) %reduce-scatter.2.cloned.1.call-update) | async-done | bytes 262160 | tf_op jit(solution)/shard_map/reduce_scatter | solution.py:192
  180.5 0.0 copy-start.4
  180.5 1.0 dynamic-slice_bitcast_fusion
  181.4 3.2 %collective-permute-start = (bf16[32,2048]{1,0:T(8,128)(2,1)S(1)}, bf16[32,2048]{1,0:T(8,128)(2,1)S(1)}, u32[]{:S(2)}, u32[]{:S(2)}) collective-permute-start(bf16[32,2048]{1,0:T(8,128)(2,1)S(1)} %dynamic-slice_bitcast_fusion), channel_id=1, source_target_pairs={{0,32},{32,0},{1,33},{33,1},{2,34},{34,2},{3,35},{35,3},{4,36},{36... | collective-permute-start | bytes 393224 | tf_op jit(solution)/shard_map/ppermute | solution.py:223
  184.7 1.8 all-to-all-done.2
  186.5 0.0 copy-start
  186.5 1.2 copy-done
  187.7 3.0 %combine.1 = bf16[128,4096]{1,0:T(8,128)(2,1)} custom-call(s32[1,128]{1,0:T(1,128)} %bitcast.27, s32[1,128]{1,0:T(1,128)} %bitcast.30, bf16[4,8,48,512]{3,2,1,0:T(8,128)(2,1)} %bitcast.17), custom_call_target="tpu_custom_call" | custom-call | tf_op jit(solution)/shard_map/combine/pallas_call | solution.py:210
  190.7 0.0 collective-permute-done
  190.7 0.0 copy-done.1
  190.7 0.0 copy-done.2
  190.7 0.0 copy-done.3
  190.7 0.0 copy-done.4
  190.7 1.0 multiply_subtract_fusion
Async XLA Ops:
  7.2 96.4 %all-gather.5.cloned.1.call-start = ((), (), s32[]{:S(2)}) async-start(), calls=%async_computation.5 | async-start | bytes 2359296 | tf_op jit(solution)/shard_map/all_gather | solution.py:153
  15.7 105.9 %all-gather.3.cloned.1.call-start = ((), (), s32[]{:S(2)}) async-start(), calls=%async_computation.4 | async-start | bytes 7077888 | tf_op jit(solution)/shard_map/all_gather | solution.py:158
  50.5 129.9 %reduce-scatter.2.cloned.1.call-start = ((), (), s32[]{:S(2)}) async-start(), calls=%async_computation.6 | async-start | bytes 2359296 | tf_op jit(solution)/shard_map/reduce_scatter | solution.py:192
  139.7 46.8 %all-to-all-start.2 = ((bf16[32,48,512]{2,1,0:T(8,128)(2,1)}), bf16[32,48,512]{2,1,0:T(8,128)(2,1)S(1)}, u32[]{:S(2)}, u32[]{:S(2)}) async-start(bf16[32,48,512]{2,1,0:T(8,128)(2,1)} %bitcast.18), calls=%async_computation.2 | async-start | bytes 3145728 | tf_op jit(solution)/shard_map/all_to_all | solution.py:207
  147.3 43.4 %copy-start.1 = (f32[32,2048]{1,0:T(8,128)S(1)}, f32[32,2048]{1,0:T(8,128)}, u32[]{:S(2)}) copy-start(f32[32,2048]{1,0:T(8,128)} %param.15) | copy-start | bytes 786436
  147.3 43.4 %copy-start.2 = (f32[32,2048]{1,0:T(8,128)S(1)}, f32[32,2048]{1,0:T(8,128)}, u32[]{:S(2)}) copy-start(f32[32,2048]{1,0:T(8,128)} %param.17) | copy-start | bytes 786436
  147.3 43.4 %copy-start.3 = (f32[32,2048]{1,0:T(8,128)S(1)}, f32[32,2048]{1,0:T(8,128)}, u32[]{:S(2)}) copy-start(f32[32,2048]{1,0:T(8,128)} %param.16) | copy-start | bytes 786436
  180.5 10.3 %copy-start.4 = (bf16[64,2048]{1,0:T(8,128)(2,1)S(1)}, bf16[64,2048]{1,0:T(8,128)(2,1)}, u32[]{:S(2)}) copy-start(bf16[64,2048]{1,0:T(8,128)(2,1)} %reduce-scatter.2.cloned.1.call-done) | copy-start | bytes 786436
  181.4 9.3 %collective-permute-start = (bf16[32,2048]{1,0:T(8,128)(2,1)S(1)}, bf16[32,2048]{1,0:T(8,128)(2,1)S(1)}, u32[]{:S(2)}, u32[]{:S(2)}) collective-permute-start(bf16[32,2048]{1,0:T(8,128)(2,1)S(1)} %dynamic-slice_bitcast_fusion), channel_id=1, source_target_pairs={{0,32},{32,0},{1,33},{33,1},{2,34},{34,2},{3,35},{35,3},{4,36},{36... | collective-permute-start | bytes 393224 | tf_op jit(solution)/shard_map/ppermute | solution.py:223
  186.5 1.2 copy-start
Sparse Core Ops, SparseCore 0:
  15.9 48.7 all-gather.4
  66.8 54.7 all-gather.2
  131.4 49.0 reduce-scatter.1

commit v2 on v1

--- a/solution.py
+++ b/solution.py
@@ -8,6 +8,7 @@
 EXPERTS = 4
 CAP = 48
 GROUP = 8
+PIECES = 4
 
 beta_one = 0.9
 beta_two = 0.999
@@ -50,7 +51,7 @@
     rows = routing_rows(mod_ref, idx_ref)
     routing = jnp.concatenate(rows, axis=0)
     hidden = grad_ref.shape[1]
-    piece = out_ref.shape[3]
+    piece = out_ref.shape[4]
     for start in range(0, hidden, piece):
         cols = pl.ds(start, piece)
         grad_val = grad_ref[:, cols].astype(jnp.float32)
@@ -59,12 +60,13 @@
         sig = 1.0 / (1.0 + jnp.exp(-gate_val))
         grad_gate = (grad_val * up_val * sig * (1.0 + gate_val * (1.0 - sig))).astype(jnp.bfloat16)
         grad_up = (grad_val * gate_val * sig).astype(jnp.bfloat16)
-        g = start // piece
-        for at, block in ((g, grad_gate), (g + GROUP // 2, grad_up)):
+        q = start // piece
+        for at, block in ((q, grad_gate), (q + PIECES // 2, grad_up)):
             packed = jnp.dot(routing, block, preferred_element_type=jnp.float32)
             packed = packed.astype(jnp.bfloat16)
             for e in range(EXPERTS):
-                out_ref[e, at] = packed[e * CAP : (e + 1) * CAP]
+                for copy in range(GROUP // PIECES):
+                    out_ref[e, copy, at] = packed[e * CAP : (e + 1) * CAP]
 
 
 def pack_rows_kernel(mod_ref, idx_ref, x_ref, out_ref):
@@ -90,23 +92,35 @@
         out_ref[:, g * piece : (g + 1) * piece] = total.astype(jnp.bfloat16)
 
 
-def weight_grad_kernel(x_ref, g_ref, out_ref, xt_ref):
-    @pl.when(pl.program_id(0) == 0)
-    def _():
-        xt_ref[...] = x_ref[...].T
-
-    out_ref[...] = jnp.dot(
-        xt_ref[...], g_ref[0], preferred_element_type=jnp.float32
-    ).astype(jnp.bfloat16)
-
-
-def input_grad_kernel(g_ref, w_ref, out_ref):
-    piece = g_ref.shape[2]
+def weight_grad_kernel(q_ref, x_ref, *rest):
+    parts = rest[:PIECES]
+    out_ref, x_buf, g_buf, xt_buf, sems = rest[PIECES:]
+    x_copy = pltpu.make_async_copy(x_ref, x_buf, sems.at[PIECES])
+    copies = [pltpu.make_async_copy(parts[j], g_buf.at[j], sems.at[j]) for j in range(PIECES)]
+    x_copy.start()
+    for copy in copies:
+        copy.start()
+    x_copy.wait()
+    xt_buf[...] = x_buf[...].T
+    piece = g_buf.shape[2]
+    for j in range(PIECES):
+        copies[j].wait()
+        at = pl.multiple_of((q_ref[0] ^ j) * piece, piece)
+        out_ref[:, pl.ds(at, piece)] = jnp.dot(
+            xt_buf[...], g_buf[j], preferred_element_type=jnp.float32
+        ).astype(jnp.bfloat16)
+
+
+def input_grad_kernel(q_ref, *rest):
+    parts = rest[:PIECES]
+    w_ref, out_ref = rest[PIECES:]
+    piece = parts[0].shape[1]
     total = None
-    for g in range(GROUP):
+    for j in range(PIECES):
+        at = pl.multiple_of((q_ref[0] ^ j) * piece, piece)
         part = lax.dot_general(
-            g_ref[g],
-            w_ref[:, g * piece : (g + 1) * piece],
+            parts[j][...],
+            w_ref[:, pl.ds(at, piece)],
             (((1,), (1,)), ((), ())),
             preferred_element_type=jnp.float32,
         )
@@ -132,36 +146,37 @@
     tok_count, width = activations.shape
     hidden = grad_hidden.shape[1]
     piece = width // GROUP
-    gpiece = 2 * hidden // GROUP
+    gpiece = 2 * hidden // PIECES
     members = EXPERTS * GROUP
     rows_total = members * CAP
     mod = modality.reshape(1, tok_count)
     idx = expert_index.reshape(1, tok_count)
     half = lax.axis_index("xh")
-
-    shard_bf = master.astype(jnp.bfloat16)
-    pair_bf = lax.all_gather(shard_bf, "xh", axis=0, tiled=True)
+    spot = (2 * lax.axis_index("xl") + lax.axis_index("core")).astype(jnp.int32).reshape(1)
 
     g_send = pl.pallas_call(
         pack_grads_kernel,
-        out_shape=jax.ShapeDtypeStruct((EXPERTS, GROUP, CAP, gpiece), jnp.bfloat16),
+        out_shape=jax.ShapeDtypeStruct(
+            (EXPERTS, GROUP // PIECES, PIECES, CAP, gpiece), jnp.bfloat16
+        ),
         in_specs=[VMEM] * 5,
         out_specs=VMEM,
         compiler_params=params(),
         name="pack_grads",
     )(mod, idx, grad_hidden, pre_gate, pre_up)
-    weights = lax.all_gather(pair_bf, "z", axis=0, tiled=True)
+    g_send, activations, shard = lax.optimization_barrier((g_send, activations, master))
     g_recv = lax.all_to_all(
         g_send.reshape(members, CAP, gpiece), EXP, split_axis=0, concat_axis=0, tiled=True
     )
-    g_mine = g_recv.reshape(rows_total, gpiece)
-    g_all = lax.all_gather(
-        g_mine,
-        EXP,
-        axis=0,
-        tiled=False,
-        axis_index_groups=[list(range(GROUP * e, GROUP * (e + 1))) for e in range(EXPERTS)],
-    )
+
+    own_bf = shard.astype(jnp.bfloat16)
+    came_bf = lax.ppermute(own_bf, "xh", swap_pairs(2))
+    pair_bf = jnp.where(
+        half == 0,
+        jnp.concatenate([own_bf, came_bf], axis=0),
+        jnp.concatenate([came_bf, own_bf], axis=0),
+    )
+    weights = lax.all_gather(pair_bf, "z", axis=0, tiled=True)
     x_send = pl.pallas_call(
         pack_rows_kernel,
         out_shape=jax.ShapeDtypeStruct((EXPERTS, GROUP, CAP, piece), jnp.bfloat16),
@@ -170,40 +185,49 @@
         compiler_params=params(),
         name="pack_rows",
     )(mod, idx, activations)
+    g_recv, x_send = lax.optimization_barrier((g_recv, x_send))
+
+    g_own = g_recv.reshape(rows_total, gpiece)
+    g_side = lax.ppermute(g_own, "xl", swap_pairs(2))
+    g_core = lax.ppermute(g_own, "core", swap_pairs(2))
+    g_both = lax.ppermute(g_side, "core", swap_pairs(2))
+    pieces = (g_own, g_core, g_side, g_both)
+
     x_recv = lax.all_to_all(
         x_send.reshape(members, CAP, piece), EXP, split_axis=0, concat_axis=0, tiled=True
     )
     x_rows = x_recv.reshape(rows_total, piece)
-    g_all, weights, x_rows = lax.optimization_barrier((g_all, weights, x_rows))
-
-    grad_part = pl.pallas_call(
-        weight_grad_kernel,
-        grid=(GROUP,),
-        out_shape=jax.ShapeDtypeStruct((piece, 2 * hidden), jnp.bfloat16),
-        in_specs=[
-            pl.BlockSpec((rows_total, piece), lambda g: (0, 0)),
-            pl.BlockSpec((1, rows_total, gpiece), lambda g: (g, 0, 0)),
-        ],
-        out_specs=pl.BlockSpec((piece, gpiece), lambda g: (0, g)),
-        scratch_shapes=[pltpu.VMEM((piece, rows_total), jnp.bfloat16)],
-        compiler_params=params(),
-        name="weight_grad",
-    )(x_rows, g_all)
-    grad_z = lax.psum_scatter(grad_part, "z", scatter_dimension=0, tiled=True)
-
-    block = 256
+
+    block = 512
     dx_rows = pl.pallas_call(
         input_grad_kernel,
         grid=(rows_total // block,),
         out_shape=jax.ShapeDtypeStruct((rows_total, piece), jnp.bfloat16),
-        in_specs=[
-            pl.BlockSpec((GROUP, block, gpiece), lambda t: (0, t, 0)),
-            pl.BlockSpec((piece, 2 * hidden), lambda t: (0, 0)),
+        in_specs=[pl.BlockSpec(memory_space=pltpu.SMEM)]
+        + [pl.BlockSpec((block, gpiece), lambda t: (t, 0))] * PIECES
+        + [pl.BlockSpec((piece, 2 * hidden), lambda t: (0, 0))],
+        out_specs=pl.BlockSpec((block, piece), lambda t: (t, 0)),
+        compiler_params=params(),
+        name="input_grad",
+    )(spot, *pieces, weights)
+    dx_rows, x_rows = lax.optimization_barrier((dx_rows, x_rows))
+
+    grad_part = pl.pallas_call(
+        weight_grad_kernel,
+        out_shape=jax.ShapeDtypeStruct((piece, 2 * hidden), jnp.bfloat16),
+        in_specs=[pl.BlockSpec(memory_space=pltpu.SMEM)]
+        + [pl.BlockSpec(memory_space=pl.ANY)] * (PIECES + 1),
+        out_specs=VMEM,
+        scratch_shapes=[
+            pltpu.VMEM((rows_total, piece), jnp.bfloat16),
+            pltpu.VMEM((PIECES, rows_total, gpiece), jnp.bfloat16),
+            pltpu.VMEM((piece, rows_total), jnp.bfloat16),
+            pltpu.SemaphoreType.DMA((PIECES + 1,)),
         ],
-        out_specs=pl.BlockSpec((block, piece), lambda t: (t, 0)),
-        compiler_params=params(),
-        name="input_grad",
-    )(g_all, weights)
+        compiler_params=params(),
+        name="weight_grad",
+    )(spot, x_rows, *pieces)
+    grad_z = lax.psum_scatter(grad_part, "z", scatter_dimension=0, tiled=True)
     back = lax.all_to_all(
         dx_rows.reshape(members, CAP, piece), EXP, split_axis=0, concat_axis=0, tiled=True
     )

time: 201 us -> 197 us (0.980)
  blocking collectives: 89.5 us -> 0 us
  waiting for transfers between devices: 53 us -> 121 us
  starting transfers between devices: 10.9 us -> 33 us
  Pallas kernels: 26.9 us -> 23.9 us
    all_to_all x2 -> x0, blocking collectives: 82 us -> none  [the longest x1 49.8 us: body(): lax.all_to_all(x_send.reshape(members, CAP, piece), EXP, split_axis=0, co...]
    ppermute x0 -> x4, waiting for transfers between devices: none -> 54.4 us  [the longest x1 43.5 us: body(): g_side = lax.ppermute(g_own, 'xl', swap_pairs(2))]
    all_to_all x0 -> x2, waiting for transfers between devices: none -> 23.5 us  [the longest x1 23.5 us: body(): lax.all_to_all(g_send.reshape(members, CAP, gpiece), EXP, split_axis=0, c...]
    all_gather x1 -> x0, waiting for transfers between devices: 18 us -> none  [body(): lax.all_gather(g_mine, EXP, axis=0, tiled=False, axis_index_groups=[list(...]
    all_to_all x0 -> x2, starting transfers between devices: none -> 14.7 us  [the longest x1 8.85 us: body(): lax.all_to_all(g_send.reshape(members, CAP, gpiece), EXP, split_axis=0, c...]
    ppermute x0 -> x4, starting transfers between devices: none -> 10.5 us  [the longest x1 4.13 us: body(): came_bf = lax.ppermute(own_bf, 'xh', swap_pairs(2))]
    reduce_scatter x1, waiting for transfers between devices: 33.1 us -> 41.6 us  [body(): grad_z = lax.psum_scatter(grad_part, 'z', scatter_dimension=0, tiled=True)]
    all_gather x1 -> x0, blocking collectives: 7.52 us -> none  [body(): pair_bf = lax.all_gather(shard_bf, 'xh', axis=0, tiled=True)]
  transfers between devices with their start and end apart: 5 -> 10, of which waited for: 3 -> 6; matrix products, arithmetic and copies ran while one was open for 0% -> 1% of each run, Pallas kernels for 9% -> 7%
where the time goes in v2:
time: 197 us; the launch traced here: 196 us
  waiting for transfers between devices  121 us (61%)
  starting transfers between devices  33 us (17%)
  Pallas kernels  23.9 us (12%)
  between operations  14.2 us (7%)
  local copies, waits for them, and re-layouts  2.17 us (1%)
    ppermute x1, waiting for transfers between devices, body(): g_side = lax.ppermute(g_own, 'xl', swap_pairs(2))  43.5 us
    reduce_scatter x1, waiting for transfers between devices, body(): grad_z = lax.psum_scatter(grad_part, 'z', scatter_dimension=0, tiled=True)  41.6 us
    all_to_all x1, waiting for transfers between devices, body(): lax.all_to_all(g_send.reshape(members, CAP, gpiece), EXP, split_axis=0, c...  23.5 us
    all_to_all x1, starting transfers between devices, body(): lax.all_to_all(g_send.reshape(members, CAP, gpiece), EXP, split_axis=0, c...  8.85 us
    pallas_call x1, Pallas kernels, body(): pl.pallas_call(input_grad_kernel, grid=(rows_total // block,), out_shape=...  7.65 us
    ppermute x1, waiting for transfers between devices, body(): came_bf = lax.ppermute(own_bf, 'xh', swap_pairs(2))  7.47 us
    pallas_call x1, Pallas kernels, body(): pl.pallas_call(weight_grad_kernel, out_shape=jax.ShapeDtypeStruct((piece,...  7.16 us
    all_to_all x1, starting transfers between devices, body(): lax.all_to_all(x_send.reshape(members, CAP, piece), EXP, split_axis=0, co...  5.86 us
  transfers between devices with their start and end apart: 10, of which 6 were waited for; matrix products, arithmetic and copies ran while one was open for 1% of the time, Pallas kernels for 7%

profile of v2, /device:TPU:6, one launch (start us, length us, event | category | flops | bytes accessed | tf_op | source)
XLA Modules:
  0.0 195.6 jit_solution(9125932414275060782)
XLA Ops:
  7.2 2.8 %pack_grads.1 = bf16[4,2,4,48,512]{4,3,2,1,0:T(8,128)(2,1)} custom-call(s32[1,128]{1,0:T(1,128)} %bitcast.27, s32[1,128]{1,0:T(1,128)} %bitcast.30, bf16[128,1024]{1,0:T(8,128)(2,1)} %grad_ref.1, bf16[128,1024]{1,0:T(8,128)(2,1)} %gate_ref.1, bf16[128,1024]{1,0:T(8,128)(2,1)} %up_ref.1), custom_call_target="tpu_custom_call" | custom-call | tf_op jit(solution)/shard_map/pack_grads/pallas_call | solution.py:157
  10.0 0.0 copy-start.3
  10.0 8.9 %all-to-all-start = ((bf16[32,48,512]{2,1,0:T(8,128)(2,1)}), bf16[32,48,512]{2,1,0:T(8,128)(2,1)S(1)}, u32[]{:S(2)}, u32[]{:S(2)}) async-start(bf16[32,48,512]{2,1,0:T(8,128)(2,1)} %bitcast.24), calls=%async_computation | async-start | bytes 3145728 | tf_op jit(solution)/shard_map/all_to_all | solution.py:168
  18.9 0.0 all-gather.2.cloned.1.call-start
  18.9 0.0 copy-done.3
  19.0 4.1 %collective-permute-start.3 = (bf16[32,2048]{1,0:T(8,128)(2,1)S(1)}, bf16[32,2048]{1,0:T(8,128)(2,1)S(1)}, u32[]{:S(2)}, u32[]{:S(2)}) collective-permute-start(bf16[32,2048]{1,0:T(8,128)(2,1)S(1)} %convert_element_type.12), channel_id=1, source_target_pairs={{0,32},{32,0},{1,33},{33,1},{2,34},{34,2},{3,35},{35,3},{4,36},{36... | collective-permute-start | bytes 393224 | tf_op jit(solution)/shard_map/ppermute | solution.py:173
  23.1 7.5 %collective-permute-done.3 = bf16[32,2048]{1,0:T(8,128)(2,1)S(1)} collective-permute-done((bf16[32,2048]{1,0:T(8,128)(2,1)S(1)}, bf16[32,2048]{1,0:T(8,128)(2,1)S(1)}, u32[]{:S(2)}, u32[]{:S(2)}) %collective-permute-start.3) | collective-permute-done | bytes 131104 | tf_op jit(solution)/shard_map/ppermute | solution.py:173
  30.6 0.8 maximum_select_fusion
  31.3 0.0 all-gather.2.cloned.1.call-update
  31.4 3.2 %pack_rows.1 = bf16[4,8,48,512]{3,2,1,0:T(8,128)(2,1)} custom-call(s32[1,128]{1,0:T(1,128)} %bitcast.28, s32[1,128]{1,0:T(1,128)} %bitcast.31, bf16[128,4096]{1,0:T(8,128)(2,1)} %x_ref), custom_call_target="tpu_custom_call" | custom-call | tf_op jit(solution)/shard_map/pack_rows/pallas_call | solution.py:180
  34.5 23.5 %all-to-all-done = bf16[32,48,512]{2,1,0:T(8,128)(2,1)S(1)} async-done(((bf16[32,48,512]{2,1,0:T(8,128)(2,1)}), bf16[32,48,512]{2,1,0:T(8,128)(2,1)S(1)}, u32[]{:S(2)}, u32[]{:S(2)}) %all-to-all-start) | async-done | bytes 1572896 | tf_op jit(solution)/shard_map/all_to_all | solution.py:168
  58.1 0.0 copy-start
  58.1 2.4 %collective-permute-start.1 = (bf16[1536,512]{1,0:T(8,128)(2,1)S(1)}, bf16[1536,512]{1,0:T(8,128)(2,1)S(1)}, u32[]{:S(2)}, u32[]{:S(2)}) collective-permute-start(bf16[1536,512]{1,0:T(8,128)(2,1)S(1)} %bitcast.18), channel_id=1, source_target_pairs={{0,2},{2,0},{1,3},{3,1},{4,6},{6,4},{5,7},{7,5},{8,10},{10,8},{9,1... | collective-permute-start | bytes 4718600 | tf_op jit(solution)/shard_map/ppermute | solution.py:191
  60.5 5.9 %all-to-all-start.1 = ((bf16[32,48,512]{2,1,0:T(8,128)(2,1)}), bf16[32,48,512]{2,1,0:T(8,128)(2,1)}, u32[]{:S(2)}, u32[]{:S(2)}) async-start(bf16[32,48,512]{2,1,0:T(8,128)(2,1)} %bitcast.22), calls=%async_computation.1 | async-start | bytes 3145728 | tf_op jit(solution)/shard_map/all_to_all | solution.py:196
  66.3 0.0 reduce-scatter.2.cloned.1.call-start
  66.4 0.0 copy-done
  66.4 2.1 %collective-permute-start = (bf16[1536,512]{1,0:T(8,128)(2,1)S(1)}, bf16[1536,512]{1,0:T(8,128)(2,1)}, u32[]{:S(2)}, u32[]{:S(2)}) collective-permute-start(bf16[1536,512]{1,0:T(8,128)(2,1)S(1)} %bitcast.19), channel_id=1, source_target_pairs={{0,1},{1,0},{2,3},{3,2},{4,5},{5,4},{6,7},{7,6},{8,9},{9,8},{10,11... | collective-permute-start | bytes 4718600 | tf_op jit(solution)/shard_map/ppermute | solution.py:192
  68.4 43.5 %collective-permute-done.1.rest_2_ = bf16[1536,512]{1,0:T(8,128)(2,1)S(1)} collective-permute-done((bf16[1536,512]{1,0:T(8,128)(2,1)S(1)}, bf16[1536,512]{1,0:T(8,128)(2,1)S(1)}, u32[]{:S(2)}, u32[]{:S(2)}) %collective-permute-start.1) | collective-permute-done | bytes 1572896 | tf_op jit(solution)/shard_map/ppermute | solution.py:191
  112.0 0.0 copy-start.1
  112.0 1.9 collective-permute-start.2
  113.9 0.0 all-gather.2.cloned.1.call-done.rest_4_
  113.9 0.0 collective-permute-done.rest_1_
  113.9 3.5 %collective-permute-done.2.rest_3_ = bf16[1536,512]{1,0:T(8,128)(2,1)} collective-permute-done((bf16[1536,512]{1,0:T(8,128)(2,1)S(1)}, bf16[1536,512]{1,0:T(8,128)(2,1)}, u32[]{:S(2)}, u32[]{:S(2)}) %collective-permute-start.2) | collective-permute-done | bytes 1572896 | tf_op jit(solution)/shard_map/ppermute | solution.py:193
  117.4 0.0 copy-done.1
  117.4 7.7 %input_grad.1 = bf16[1536,512]{1,0:T(8,128)(2,1)} custom-call(s32[1]{0:T(128)} %bitcast.2.q_ref, bf16[1536,512]{1,0:T(8,128)(2,1)} %bitcast.20, bf16[1536,512]{1,0:T(8,128)(2,1)} %collective-permute-done.rest_1_, bf16[1536,512]{1,0:T(8,128)(2,1)} %copy-done.1, bf16[1536,512]{1,0:T(8,128)(2,1)} %collective-permute-done.2.rest_3_, ...), custom_call_target="tpu_custom_call" | custom-call | tf_op jit(solution)/shard_map/input_grad/pallas_call | solution.py:202
  125.0 0.0 all-to-all-done.1
  125.0 7.2 %weight_grad.1 = bf16[512,2048]{1,0:T(8,128)(2,1)} custom-call(s32[1]{0:T(128)} %bitcast.2.q_ref, bf16[1536,512]{1,0:T(8,128)(2,1)} %bitcast.6.x_ref, bf16[1536,512]{1,0:T(8,128)(2,1)} %bitcast.21, bf16[1536,512]{1,0:T(8,128)(2,1)} %collective-permute-done.rest_1_, bf16[1536,512]{1,0:T(8,128)(2,1)} %copy-done.1, bf16[1536,512]{1,0:T(8,128)(2,1)} %collective-permute-done.2.rest_3_), custom_call_target="tpu_custom_call" | custom-call | tf_op jit(solution)/shard_map/weight_grad/pallas_call | solution.py:215
  132.2 0.0 reduce-scatter.2.cloned.1.call-update
  132.2 4.5 %all-to-all-start.2 = ((bf16[32,48,512]{2,1,0:T(8,128)(2,1)}), bf16[32,48,512]{2,1,0:T(8,128)(2,1)S(1)}, u32[]{:S(2)}, u32[]{:S(2)}) async-start(bf16[32,48,512]{2,1,0:T(8,128)(2,1)} %bitcast.7), calls=%async_computation.2 | async-start | bytes 3145728 | tf_op jit(solution)/shard_map/all_to_all | solution.py:231
  136.7 0.0 copy-start.4
  136.7 0.0 copy-start.5
  136.8 41.6 %reduce-scatter.2.cloned.1.call-done = bf16[64,2048]{1,0:T(8,128)(2,1)} async-done(((bf16[512,2048]{1,0:T(8,128)(2,1)}), bf16[64,2048]{1,0:T(8,128)(2,1)}) %reduce-scatter.2.cloned.1.call-update) | async-done | bytes 262160 | tf_op jit(solution)/shard_map/reduce_scatter | solution.py:230
  178.4 0.0 copy-start.6
  178.4 1.0 dynamic-slice_bitcast_fusion
  179.4 3.3 %collective-permute-start.4 = (bf16[32,2048]{1,0:T(8,128)(2,1)S(1)}, bf16[32,2048]{1,0:T(8,128)(2,1)S(1)}, u32[]{:S(2)}, u32[]{:S(2)}) collective-permute-start(bf16[32,2048]{1,0:T(8,128)(2,1)S(1)} %dynamic-slice_bitcast_fusion), channel_id=1, source_target_pairs={{0,32},{32,0},{1,33},{33,1},{2,34},{34,2},{3,35},{35,3},{4,36},{36... | collective-permute-start | bytes 393224 | tf_op jit(solution)/shard_map/ppermute | solution.py:247
  182.6 0.0 all-to-all-done.2
  182.7 0.0 copy-start.2
  182.7 1.2 copy-done.2
  183.8 3.0 %combine.1 = bf16[128,4096]{1,0:T(8,128)(2,1)} custom-call(s32[1,128]{1,0:T(1,128)} %bitcast.29, s32[1,128]{1,0:T(1,128)} %bitcast.32, bf16[4,8,48,512]{3,2,1,0:T(8,128)(2,1)} %bitcast.23), custom_call_target="tpu_custom_call" | custom-call | tf_op jit(solution)/shard_map/combine/pallas_call | solution.py:234
  186.8 0.9 collective-permute-done.4
  187.7 0.0 copy-done.4
  187.7 0.0 copy-done.5
  187.7 0.0 copy-done.6
  187.8 1.0 multiply_subtract_fusion
  (1 shorter events, 0.0 us)
Async XLA Ops:
  10.0 8.9 %copy-start.3 = (f32[32,2048]{1,0:T(8,128)S(1)}, f32[32,2048]{1,0:T(8,128)}, u32[]{:S(2)}) copy-start(f32[32,2048]{1,0:T(8,128)} %param.15) | copy-start | bytes 786436
  10.0 48.1 %all-to-all-start = ((bf16[32,48,512]{2,1,0:T(8,128)(2,1)}), bf16[32,48,512]{2,1,0:T(8,128)(2,1)S(1)}, u32[]{:S(2)}, u32[]{:S(2)}) async-start(bf16[32,48,512]{2,1,0:T(8,128)(2,1)} %bitcast.24), calls=%async_computation | async-start | bytes 3145728 | tf_op jit(solution)/shard_map/all_to_all | solution.py:168
  18.9 95.0 %all-gather.2.cloned.1.call-start = ((), (), s32[]{:S(2)}) async-start(), calls=%async_computation.4 | async-start | bytes 2359296 | tf_op jit(solution)/shard_map/all_gather | solution.py:179
  19.0 11.6 %collective-permute-start.3 = (bf16[32,2048]{1,0:T(8,128)(2,1)S(1)}, bf16[32,2048]{1,0:T(8,128)(2,1)S(1)}, u32[]{:S(2)}, u32[]{:S(2)}) collective-permute-start(bf16[32,2048]{1,0:T(8,128)(2,1)S(1)} %convert_element_type.12), channel_id=1, source_target_pairs={{0,32},{32,0},{1,33},{33,1},{2,34},{34,2},{3,35},{35,3},{4,36},{36... | collective-permute-start | bytes 393224 | tf_op jit(solution)/shard_map/ppermute | solution.py:173
  58.1 8.3 %copy-start = (bf16[32,48,512]{2,1,0:T(8,128)(2,1)}, bf16[32,48,512]{2,1,0:T(8,128)(2,1)S(1)}, u32[]{:S(2)}) copy-start(bf16[32,48,512]{2,1,0:T(8,128)(2,1)S(1)} %all-to-all-done) | copy-start | bytes 4718596
  58.1 53.9 %collective-permute-start.1 = (bf16[1536,512]{1,0:T(8,128)(2,1)S(1)}, bf16[1536,512]{1,0:T(8,128)(2,1)S(1)}, u32[]{:S(2)}, u32[]{:S(2)}) collective-permute-start(bf16[1536,512]{1,0:T(8,128)(2,1)S(1)} %bitcast.18), channel_id=1, source_target_pairs={{0,2},{2,0},{1,3},{3,1},{4,6},{6,4},{5,7},{7,5},{8,10},{10,8},{9,1... | collective-permute-start | bytes 4718600 | tf_op jit(solution)/shard_map/ppermute | solution.py:191
  60.5 64.6 %all-to-all-start.1 = ((bf16[32,48,512]{2,1,0:T(8,128)(2,1)}), bf16[32,48,512]{2,1,0:T(8,128)(2,1)}, u32[]{:S(2)}, u32[]{:S(2)}) async-start(bf16[32,48,512]{2,1,0:T(8,128)(2,1)} %bitcast.22), calls=%async_computation.1 | async-start | bytes 3145728 | tf_op jit(solution)/shard_map/all_to_all | solution.py:196
  66.3 112.1 %reduce-scatter.2.cloned.1.call-start = ((), (), s32[]{:S(2)}) async-start(), calls=%async_computation.5 | async-start | bytes 2359296 | tf_op jit(solution)/shard_map/reduce_scatter | solution.py:230
  66.4 47.5 %collective-permute-start = (bf16[1536,512]{1,0:T(8,128)(2,1)S(1)}, bf16[1536,512]{1,0:T(8,128)(2,1)}, u32[]{:S(2)}, u32[]{:S(2)}) collective-permute-start(bf16[1536,512]{1,0:T(8,128)(2,1)S(1)} %bitcast.19), channel_id=1, source_target_pairs={{0,1},{1,0},{2,3},{3,2},{4,5},{5,4},{6,7},{7,6},{8,9},{9,8},{10,11... | collective-permute-start | bytes 4718600 | tf_op jit(solution)/shard_map/ppermute | solution.py:192
  112.0 5.4 %copy-start.1 = (bf16[1536,512]{1,0:T(8,128)(2,1)}, bf16[1536,512]{1,0:T(8,128)(2,1)S(1)}, u32[]{:S(2)}) copy-start(bf16[1536,512]{1,0:T(8,128)(2,1)S(1)} %collective-permute-done.1.rest_2_) | copy-start | bytes 4718596
  112.0 5.4 %collective-permute-start.2 = (bf16[1536,512]{1,0:T(8,128)(2,1)S(1)}, bf16[1536,512]{1,0:T(8,128)(2,1)}, u32[]{:S(2)}, u32[]{:S(2)}) collective-permute-start(bf16[1536,512]{1,0:T(8,128)(2,1)S(1)} %collective-permute-done.1.rest_2_), channel_id=1, source_target_pairs={{0,1},{1,0},{2,3},{3,2},{4,5},{5,4},{6,7},{7,6},{8,9},{9,8},{10,11... | collective-permute-start | bytes 4718600 | tf_op jit(solution)/shard_map/ppermute | solution.py:193
  132.2 50.4 %all-to-all-start.2 = ((bf16[32,48,512]{2,1,0:T(8,128)(2,1)}), bf16[32,48,512]{2,1,0:T(8,128)(2,1)S(1)}, u32[]{:S(2)}, u32[]{:S(2)}) async-start(bf16[32,48,512]{2,1,0:T(8,128)(2,1)} %bitcast.7), calls=%async_computation.2 | async-start | bytes 3145728 | tf_op jit(solution)/shard_map/all_to_all | solution.py:231
  136.7 51.0 %copy-start.4 = (f32[32,2048]{1,0:T(8,128)S(1)}, f32[32,2048]{1,0:T(8,128)}, u32[]{:S(2)}) copy-start(f32[32,2048]{1,0:T(8,128)} %param.17) | copy-start | bytes 786436
  136.7 51.0 %copy-start.5 = (f32[32,2048]{1,0:T(8,128)S(1)}, f32[32,2048]{1,0:T(8,128)}, u32[]{:S(2)}) copy-start(f32[32,2048]{1,0:T(8,128)} %param.16) | copy-start | bytes 786436
  178.4 9.4 %copy-start.6 = (bf16[64,2048]{1,0:T(8,128)(2,1)S(1)}, bf16[64,2048]{1,0:T(8,128)(2,1)}, u32[]{:S(2)}) copy-start(bf16[64,2048]{1,0:T(8,128)(2,1)} %reduce-scatter.2.cloned.1.call-done) | copy-start | bytes 786436
  179.4 8.4 %collective-permute-start.4 = (bf16[32,2048]{1,0:T(8,128)(2,1)S(1)}, bf16[32,2048]{1,0:T(8,128)(2,1)S(1)}, u32[]{:S(2)}, u32[]{:S(2)}) collective-permute-start(bf16[32,2048]{1,0:T(8,128)(2,1)S(1)} %dynamic-slice_bitcast_fusion), channel_id=1, source_target_pairs={{0,32},{32,0},{1,33},{33,1},{2,34},{34,2},{3,35},{35,3},{4,36},{36... | collective-permute-start | bytes 393224 | tf_op jit(solution)/shard_map/ppermute | solution.py:247
  182.7 1.2 copy-start.2
Sparse Core Ops, SparseCore 0:
  31.5 50.1 all-gather.1
  132.4 45.9 reduce-scatter.1

commit v3 on v2

--- a/solution.py
+++ b/solution.py
@@ -8,7 +8,7 @@
 EXPERTS = 4
 CAP = 48
 GROUP = 8
-PIECES = 4
+KEEP = 32
 
 beta_one = 0.9
 beta_two = 0.999
@@ -51,7 +51,7 @@
     rows = routing_rows(mod_ref, idx_ref)
     routing = jnp.concatenate(rows, axis=0)
     hidden = grad_ref.shape[1]
-    piece = out_ref.shape[4]
+    piece = out_ref.shape[3]
     for start in range(0, hidden, piece):
         cols = pl.ds(start, piece)
         grad_val = grad_ref[:, cols].astype(jnp.float32)
@@ -60,13 +60,12 @@
         sig = 1.0 / (1.0 + jnp.exp(-gate_val))
         grad_gate = (grad_val * up_val * sig * (1.0 + gate_val * (1.0 - sig))).astype(jnp.bfloat16)
         grad_up = (grad_val * gate_val * sig).astype(jnp.bfloat16)
-        q = start // piece
-        for at, block in ((q, grad_gate), (q + PIECES // 2, grad_up)):
+        g = start // piece
+        for at, block in ((g, grad_gate), (g + GROUP // 2, grad_up)):
             packed = jnp.dot(routing, block, preferred_element_type=jnp.float32)
             packed = packed.astype(jnp.bfloat16)
             for e in range(EXPERTS):
-                for copy in range(GROUP // PIECES):
-                    out_ref[e, copy, at] = packed[e * CAP : (e + 1) * CAP]
+                out_ref[e, at] = packed[e * CAP : (e + 1) * CAP]
 
 
 def pack_rows_kernel(mod_ref, idx_ref, x_ref, out_ref):
@@ -93,30 +92,33 @@
 
 
 def weight_grad_kernel(q_ref, x_ref, *rest):
-    parts = rest[:PIECES]
-    out_ref, x_buf, g_buf, xt_buf, sems = rest[PIECES:]
-    x_copy = pltpu.make_async_copy(x_ref, x_buf, sems.at[PIECES])
-    copies = [pltpu.make_async_copy(parts[j], g_buf.at[j], sems.at[j]) for j in range(PIECES)]
+    parts = rest[:GROUP]
+    out_ref, x_buf, g_buf, xt_buf, sems = rest[GROUP:]
+    x_copy = pltpu.make_async_copy(x_ref, x_buf, sems.at[GROUP])
+    copies = [pltpu.make_async_copy(parts[j], g_buf.at[j], sems.at[j]) for j in range(GROUP)]
     x_copy.start()
     for copy in copies:
         copy.start()
     x_copy.wait()
     xt_buf[...] = x_buf[...].T
     piece = g_buf.shape[2]
-    for j in range(PIECES):
+    for j in range(GROUP):
         copies[j].wait()
         at = pl.multiple_of((q_ref[0] ^ j) * piece, piece)
-        out_ref[:, pl.ds(at, piece)] = jnp.dot(
+        block = jnp.dot(
             xt_buf[...], g_buf[j], preferred_element_type=jnp.float32
         ).astype(jnp.bfloat16)
+        for r in range(block.shape[0] // KEEP):
+            to = pl.multiple_of((r // 2 * 2 + (r % 2 ^ q_ref[1])) * KEEP, KEEP)
+            out_ref[pl.ds(to, KEEP), pl.ds(at, piece)] = block[r * KEEP : (r + 1) * KEEP]
 
 
 def input_grad_kernel(q_ref, *rest):
-    parts = rest[:PIECES]
-    w_ref, out_ref = rest[PIECES:]
+    parts = rest[:GROUP]
+    w_ref, out_ref = rest[GROUP:]
     piece = parts[0].shape[1]
     total = None
-    for j in range(PIECES):
+    for j in range(GROUP):
         at = pl.multiple_of((q_ref[0] ^ j) * piece, piece)
         part = lax.dot_general(
             parts[j][...],
@@ -146,19 +148,18 @@
     tok_count, width = activations.shape
     hidden = grad_hidden.shape[1]
     piece = width // GROUP
-    gpiece = 2 * hidden // PIECES
+    gpiece = 2 * hidden // GROUP
     members = EXPERTS * GROUP
     rows_total = members * CAP
     mod = modality.reshape(1, tok_count)
     idx = expert_index.reshape(1, tok_count)
     half = lax.axis_index("xh")
-    spot = (2 * lax.axis_index("xl") + lax.axis_index("core")).astype(jnp.int32).reshape(1)
+    member = lax.axis_index(EXP) % GROUP
+    spot = jnp.stack([member, half]).astype(jnp.int32)
 
     g_send = pl.pallas_call(
         pack_grads_kernel,
-        out_shape=jax.ShapeDtypeStruct(
-            (EXPERTS, GROUP // PIECES, PIECES, CAP, gpiece), jnp.bfloat16
-        ),
+        out_shape=jax.ShapeDtypeStruct((EXPERTS, GROUP, CAP, gpiece), jnp.bfloat16),
         in_specs=[VMEM] * 5,
         out_specs=VMEM,
         compiler_params=params(),
@@ -188,46 +189,50 @@
     g_recv, x_send = lax.optimization_barrier((g_recv, x_send))
 
     g_own = g_recv.reshape(rows_total, gpiece)
-    g_side = lax.ppermute(g_own, "xl", swap_pairs(2))
+    g_y = lax.ppermute(g_own, "y", swap_pairs(8))
+    g_x = lax.ppermute(g_own, "xl", swap_pairs(2))
     g_core = lax.ppermute(g_own, "core", swap_pairs(2))
-    g_both = lax.ppermute(g_side, "core", swap_pairs(2))
-    pieces = (g_own, g_core, g_side, g_both)
+    g_yx = lax.ppermute(g_y, "xl", swap_pairs(2))
+    g_x_core = lax.ppermute(g_x, "core", swap_pairs(2))
+    g_y_core = lax.ppermute(g_y, "core", swap_pairs(2))
+    g_yx_core = lax.ppermute(g_yx, "core", swap_pairs(2))
+    pieces = (g_own, g_core, g_x, g_x_core, g_y, g_y_core, g_yx, g_yx_core)
 
     x_recv = lax.all_to_all(
         x_send.reshape(members, CAP, piece), EXP, split_axis=0, concat_axis=0, tiled=True
     )
     x_rows = x_recv.reshape(rows_total, piece)
 
+    grad_part = pl.pallas_call(
+        weight_grad_kernel,
+        out_shape=jax.ShapeDtypeStruct((piece, 2 * hidden), jnp.bfloat16),
+        in_specs=[pl.BlockSpec(memory_space=pltpu.SMEM)]
+        + [pl.BlockSpec(memory_space=pl.ANY)] * (GROUP + 1),
+        out_specs=VMEM,
+        scratch_shapes=[
+            pltpu.VMEM((rows_total, piece), jnp.bfloat16),
+            pltpu.VMEM((GROUP, rows_total, gpiece), jnp.bfloat16),
+            pltpu.VMEM((piece, rows_total), jnp.bfloat16),
+            pltpu.SemaphoreType.DMA((GROUP + 1,)),
+        ],
+        compiler_params=params(),
+        name="weight_grad",
+    )(spot, x_rows, *pieces)
+    grad_z = lax.psum_scatter(grad_part, "z", scatter_dimension=0, tiled=True)
+
+    grad_part, *pieces = lax.optimization_barrier((grad_part, *pieces))
     block = 512
     dx_rows = pl.pallas_call(
         input_grad_kernel,
         grid=(rows_total // block,),
         out_shape=jax.ShapeDtypeStruct((rows_total, piece), jnp.bfloat16),
         in_specs=[pl.BlockSpec(memory_space=pltpu.SMEM)]
-        + [pl.BlockSpec((block, gpiece), lambda t: (t, 0))] * PIECES
+        + [pl.BlockSpec((block, gpiece), lambda t: (t, 0))] * GROUP
         + [pl.BlockSpec((piece, 2 * hidden), lambda t: (0, 0))],
         out_specs=pl.BlockSpec((block, piece), lambda t: (t, 0)),
         compiler_params=params(),
         name="input_grad",
     )(spot, *pieces, weights)
-    dx_rows, x_rows = lax.optimization_barrier((dx_rows, x_rows))
-
-    grad_part = pl.pallas_call(
-        weight_grad_kernel,
-        out_shape=jax.ShapeDtypeStruct((piece, 2 * hidden), jnp.bfloat16),
-        in_specs=[pl.BlockSpec(memory_space=pltpu.SMEM)]
-        + [pl.BlockSpec(memory_space=pl.ANY)] * (PIECES + 1),
-        out_specs=VMEM,
-        scratch_shapes=[
-            pltpu.VMEM((rows_total, piece), jnp.bfloat16),
-            pltpu.VMEM((PIECES, rows_total, gpiece), jnp.bfloat16),
-            pltpu.VMEM((piece, rows_total), jnp.bfloat16),
-            pltpu.SemaphoreType.DMA((PIECES + 1,)),
-        ],
-        compiler_params=params(),
-        name="weight_grad",
-    )(spot, x_rows, *pieces)
-    grad_z = lax.psum_scatter(grad_part, "z", scatter_dimension=0, tiled=True)
     back = lax.all_to_all(
         dx_rows.reshape(members, CAP, piece), EXP, split_axis=0, concat_axis=0, tiled=True
     )
@@ -241,9 +246,8 @@
     )(mod, idx, back.reshape(EXPERTS, GROUP, CAP, piece))
 
     keep_rows = master.shape[0]
-    halves = grad_z.reshape(2, keep_rows, 2 * hidden)
-    own = lax.dynamic_index_in_dim(halves, half, 0, keepdims=False)
-    other = lax.dynamic_index_in_dim(halves, 1 - half, 0, keepdims=False)
+    own = grad_z[:keep_rows]
+    other = grad_z[keep_rows:]
     came = lax.ppermute(other, "xh", swap_pairs(2))
     weight_grad = own.astype(jnp.float32) + came.astype(jnp.float32)
     new_first = beta_one * first_moment + (1.0 - beta_one) * weight_grad

time: 197 us -> 207 us (1.051)
  starting transfers between devices: 33 us -> 44.6 us
  waiting for transfers between devices: 121 us -> 112 us
  Pallas kernels: 23.9 us -> 28 us
    all_to_all x1, waiting for transfers between devices: 23.5 us -> 7.16 us  [body(): lax.all_to_all(g_send.reshape(members, CAP, gpiece), EXP, split_axis=0, c...]
    ppermute x2 -> x6, waiting for transfers between devices: 47 us -> 61.6 us  [the longest x1 47.2 us: body(): g_y = lax.ppermute(g_own, 'y', swap_pairs(8))]
    ppermute x2 -> x6, starting transfers between devices: 4.28 us -> 14.5 us  [the longest x1 3.4 us: body(): g_y = lax.ppermute(g_own, 'y', swap_pairs(8))]
    reduce_scatter x1, waiting for transfers between devices: 41.6 us -> 33.6 us  [body(): grad_z = lax.psum_scatter(grad_part, 'z', scatter_dimension=0, tiled=True)]
    pallas_call x1, Pallas kernels: 7.16 us -> 11.6 us  [body(): pl.pallas_call(weight_grad_kernel, out_shape=jax.ShapeDtypeStruct((piece,...]
    all_to_all x1, starting transfers between devices: 4.47 us -> 7.86 us  [body(): lax.all_to_all(dx_rows.reshape(members, CAP, piece), EXP, split_axis=0, c...]
  transfers between devices with their start and end apart: 10 -> 14, of which waited for: 6 -> 7; matrix products, arithmetic and copies ran while one was open for 1% -> 1% of each run, Pallas kernels for 7% -> 12%
where the time goes in v3:
time: 207 us; the launch traced here: 204 us
  waiting for transfers between devices  112 us (54%)
  starting transfers between devices  44.6 us (22%)
  Pallas kernels  28 us (14%)
  between operations  14.3 us (7%)
  local copies, waits for them, and re-layouts  3.37 us (2%)
  other arithmetic  2.31 us (1%)
    ppermute x1, waiting for transfers between devices, body(): g_y = lax.ppermute(g_own, 'y', swap_pairs(8))  47.2 us
    reduce_scatter x1, waiting for transfers between devices, body(): grad_z = lax.psum_scatter(grad_part, 'z', scatter_dimension=0, tiled=True)  33.6 us
    ppermute x1, waiting for transfers between devices, body(): g_yx = lax.ppermute(g_y, 'xl', swap_pairs(2))  12.3 us
    pallas_call x1, Pallas kernels, body(): pl.pallas_call(weight_grad_kernel, out_shape=jax.ShapeDtypeStruct((piece,...  11.6 us
    all_to_all x1, starting transfers between devices, body(): lax.all_to_all(g_send.reshape(members, CAP, gpiece), EXP, split_axis=0, c...  8.71 us
    ppermute x1, waiting for transfers between devices, body(): came_bf = lax.ppermute(own_bf, 'xh', swap_pairs(2))  8.13 us
    all_to_all x1, starting transfers between devices, body(): lax.all_to_all(dx_rows.reshape(members, CAP, piece), EXP, split_axis=0, c...  7.86 us
    pallas_call x1, Pallas kernels, body(): pl.pallas_call(input_grad_kernel, grid=(rows_total // block,), out_shape=...  7.63 us
  transfers between devices with their start and end apart: 14, of which 7 were waited for; matrix products, arithmetic and copies ran while one was open for 1% of the time, Pallas kernels for 12%

profile of v3, /device:TPU:6, one launch (start us, length us, event | category | flops | bytes accessed | tf_op | source)
XLA Modules:
  0.0 204.2 jit_solution(14163019156245538874)
XLA Ops:
  7.2 0.0 copy-start.4
  7.2 2.6 %pack_grads.1 = bf16[4,8,48,256]{3,2,1,0:T(8,128)(2,1)} custom-call(s32[1,128]{1,0:T(1,128)} %bitcast.20, s32[1,128]{1,0:T(1,128)} %bitcast.23, bf16[128,1024]{1,0:T(8,128)(2,1)} %grad_ref.1, bf16[128,1024]{1,0:T(8,128)(2,1)} %gate_ref.1, bf16[128,1024]{1,0:T(8,128)(2,1)} %up_ref.1), custom_call_target="tpu_custom_call" | custom-call | tf_op jit(solution)/shard_map/pack_grads/pallas_call | solution.py:160
  9.8 8.7 %all-to-all-start = ((bf16[32,48,256]{2,1,0:T(8,128)(2,1)}), bf16[32,48,256]{2,1,0:T(8,128)(2,1)S(1)}, u32[]{:S(2)}, u32[]{:S(2)}) async-start(bf16[32,48,256]{2,1,0:T(8,128)(2,1)} %bitcast.19), calls=%async_computation | async-start | bytes 1572864 | tf_op jit(solution)/shard_map/all_to_all | solution.py:169
  18.5 0.0 all-gather.2.cloned.1.call-start
  18.6 0.0 copy-done.4
  18.6 4.1 %collective-permute-start.7 = (bf16[32,2048]{1,0:T(8,128)(2,1)S(1)}, bf16[32,2048]{1,0:T(8,128)(2,1)S(1)}, u32[]{:S(2)}, u32[]{:S(2)}) collective-permute-start(bf16[32,2048]{1,0:T(8,128)(2,1)S(1)} %convert_element_type.9), channel_id=1, source_target_pairs={{0,32},{32,0},{1,33},{33,1},{2,34},{34,2},{3,35},{35,3},{4,36},{36... | collective-permute-start | bytes 393224 | tf_op jit(solution)/shard_map/ppermute | solution.py:174
  22.7 8.1 %collective-permute-done.7 = bf16[32,2048]{1,0:T(8,128)(2,1)S(1)} collective-permute-done((bf16[32,2048]{1,0:T(8,128)(2,1)S(1)}, bf16[32,2048]{1,0:T(8,128)(2,1)S(1)}, u32[]{:S(2)}, u32[]{:S(2)}) %collective-permute-start.7) | collective-permute-done | bytes 131104 | tf_op jit(solution)/shard_map/ppermute | solution.py:174
  30.8 0.8 maximum_select_fusion
  31.6 0.0 all-gather.2.cloned.1.call-update
  31.6 3.1 %pack_rows.1 = bf16[4,8,48,512]{3,2,1,0:T(8,128)(2,1)} custom-call(s32[1,128]{1,0:T(1,128)} %bitcast.21, s32[1,128]{1,0:T(1,128)} %bitcast.24, bf16[128,4096]{1,0:T(8,128)(2,1)} %x_ref), custom_call_target="tpu_custom_call" | custom-call | tf_op jit(solution)/shard_map/pack_rows/pallas_call | solution.py:181
  34.7 7.2 %all-to-all-done = bf16[32,48,256]{2,1,0:T(8,128)(2,1)S(1)} async-done(((bf16[32,48,256]{2,1,0:T(8,128)(2,1)}), bf16[32,48,256]{2,1,0:T(8,128)(2,1)S(1)}, u32[]{:S(2)}, u32[]{:S(2)}) %all-to-all-start) | async-done | bytes 786464 | tf_op jit(solution)/shard_map/all_to_all | solution.py:169
  41.8 0.0 copy-start
  41.8 4.0 %all-to-all-start.1 = ((bf16[32,48,512]{2,1,0:T(8,128)(2,1)}), bf16[32,48,512]{2,1,0:T(8,128)(2,1)S(1)}, u32[]{:S(2)}, u32[]{:S(2)}) async-start(bf16[32,48,512]{2,1,0:T(8,128)(2,1)} %bitcast.15), calls=%async_computation.1 | async-start | bytes 3145728 | tf_op jit(solution)/shard_map/all_to_all | solution.py:201
  45.9 0.0 reduce-scatter.2.cloned.1.call-start
  45.9 3.4 %collective-permute-start.3 = (bf16[1536,256]{1,0:T(8,128)(2,1)S(1)}, bf16[1536,256]{1,0:T(8,128)(2,1)S(1)}, u32[]{:S(2)}, u32[]{:S(2)}) collective-permute-start(bf16[1536,256]{1,0:T(8,128)(2,1)S(1)} %bitcast.10), channel_id=1, source_target_pairs={{0,4},{4,0},{8,12},{12,8},{16,20},{20,16},{24,28},{28,24},{1,5},{5... | collective-permute-start | bytes 2359304 | tf_op jit(solution)/shard_map/ppermute | solution.py:192
  49.3 2.5 %collective-permute-start.1 = (bf16[1536,256]{1,0:T(8,128)(2,1)S(1)}, bf16[1536,256]{1,0:T(8,128)(2,1)}, u32[]{:S(2)}, u32[]{:S(2)}) collective-permute-start(bf16[1536,256]{1,0:T(8,128)(2,1)S(1)} %bitcast.11), channel_id=1, source_target_pairs={{0,2},{2,0},{1,3},{3,1},{4,6},{6,4},{5,7},{7,5},{8,10},{10,8},{9,1... | collective-permute-start | bytes 2359304 | tf_op jit(solution)/shard_map/ppermute | solution.py:193
  51.8 47.2 %collective-permute-done.3.rest_4_ = bf16[1536,256]{1,0:T(8,128)(2,1)S(1)} collective-permute-done((bf16[1536,256]{1,0:T(8,128)(2,1)S(1)}, bf16[1536,256]{1,0:T(8,128)(2,1)S(1)}, u32[]{:S(2)}, u32[]{:S(2)}) %collective-permute-start.3) | collective-permute-done | bytes 786464 | tf_op jit(solution)/shard_map/ppermute | solution.py:192
  99.0 0.0 copy-start.3
  99.0 2.4 %collective-permute-start.5 = (bf16[1536,256]{1,0:T(8,128)(2,1)S(1)}, bf16[1536,256]{1,0:T(8,128)(2,1)}, u32[]{:S(2)}, u32[]{:S(2)}) collective-permute-start(bf16[1536,256]{1,0:T(8,128)(2,1)S(1)} %collective-permute-done.3.rest_4_), channel_id=1, source_target_pairs={{0,2},{2,0},{1,3},{3,1},{4,6},{6,4},{5,7},{7,5},{8,10},{10,8},{9,1... | collective-permute-start | bytes 2359304 | tf_op jit(solution)/shard_map/ppermute | solution.py:195
  101.5 0.0 copy-done
  101.5 1.9 collective-permute-start
  103.4 2.4 %collective-permute-start.4 = (bf16[1536,256]{1,0:T(8,128)(2,1)S(1)}, bf16[1536,256]{1,0:T(8,128)(2,1)}, u32[]{:S(2)}, u32[]{:S(2)}) collective-permute-start(bf16[1536,256]{1,0:T(8,128)(2,1)S(1)} %collective-permute-done.3.rest_4_), channel_id=1, source_target_pairs={{0,1},{1,0},{2,3},{3,2},{4,5},{5,4},{6,7},{7,6},{8,9},{9,8},{10,11... | collective-permute-start | bytes 2359304 | tf_op jit(solution)/shard_map/ppermute | solution.py:197
  105.8 0.0 collective-permute-done.1.rest_2_
  105.9 1.9 collective-permute-start.2
  107.8 12.3 %collective-permute-done.5.rest_6_ = bf16[1536,256]{1,0:T(8,128)(2,1)} collective-permute-done((bf16[1536,256]{1,0:T(8,128)(2,1)S(1)}, bf16[1536,256]{1,0:T(8,128)(2,1)}, u32[]{:S(2)}, u32[]{:S(2)}) %collective-permute-start.5) | collective-permute-done | bytes 786464 | tf_op jit(solution)/shard_map/ppermute | solution.py:195
  120.1 1.9 collective-permute-start.6
  122.0 0.6 pad_add_fusion.q_ref
  122.6 0.0 collective-permute-done.rest_1_
  122.6 0.0 collective-permute-done.4.rest_5_
  122.6 0.0 collective-permute-done.2.rest_3_
  122.6 2.0 collective-permute-done.6.rest_7_
  124.6 0.0 all-to-all-done.1
  124.6 0.0 copy-start.1
  124.6 0.0 copy-done.3
  124.6 1.2 copy-done.1
  125.8 11.6 %weight_grad.1 = bf16[512,2048]{1,0:T(8,128)(2,1)} custom-call(s32[2]{0:T(128)} %pad_add_fusion.q_ref, bf16[1536,512]{1,0:T(8,128)(2,1)} %bitcast.16, bf16[1536,256]{1,0:T(8,128)(2,1)} %bitcast.13, bf16[1536,256]{1,0:T(8,128)(2,1)} %collective-permute-done.rest_1_, bf16[1536,256]{1,0:T(8,128)(2,1)} %collective-permute-done.1.rest_2_, ...), custom_call_target="tpu_custom_call" | custom-call | tf_op jit(solution)/shard_map/weight_grad/pallas_call | solution.py:206
  137.4 0.0 reduce-scatter.2.cloned.1.call-update
  137.4 0.0 all-gather.2.cloned.1.call-done.rest_8_
  137.5 7.6 %input_grad.1 = bf16[1536,512]{1,0:T(8,128)(2,1)} custom-call(s32[2]{0:T(128)} %pad_add_fusion.q_ref, bf16[1536,256]{1,0:T(8,128)(2,1)} %bitcast.14, bf16[1536,256]{1,0:T(8,128)(2,1)} %collective-permute-done.rest_1_, bf16[1536,256]{1,0:T(8,128)(2,1)} %collective-permute-done.1.rest_2_, bf16[1536,256]{1,0:T(8,128)(2,1)} %collective-permute-done.2.rest_3_, ...), custom_call_target="tpu_custom_call" | custom-call | tf_op jit(solution)/shard_map/input_grad/pallas_call | solution.py:225
  145.1 7.9 %all-to-all-start.2 = ((bf16[32,48,512]{2,1,0:T(8,128)(2,1)}), bf16[32,48,512]{2,1,0:T(8,128)(2,1)S(1)}, u32[]{:S(2)}, u32[]{:S(2)}) async-start(bf16[32,48,512]{2,1,0:T(8,128)(2,1)} %bitcast.17), calls=%async_computation.2 | async-start | bytes 3145728 | tf_op jit(solution)/shard_map/all_to_all | solution.py:236
  153.0 0.0 copy-start.6
  153.0 0.0 copy-start.7
  153.0 33.6 %reduce-scatter.2.cloned.1.call-done = bf16[64,2048]{1,0:T(8,128)(2,1)} async-done(((bf16[512,2048]{1,0:T(8,128)(2,1)}), bf16[64,2048]{1,0:T(8,128)(2,1)}) %reduce-scatter.2.cloned.1.call-update) | async-done | bytes 262160 | tf_op jit(solution)/shard_map/reduce_scatter | solution.py:221
  186.6 0.0 copy-start.5
  186.6 1.0 slice.9
  187.6 3.4 %collective-permute-start.8 = (bf16[32,2048]{1,0:T(8,128)(2,1)S(1)}, bf16[32,2048]{1,0:T(8,128)(2,1)S(1)}, u32[]{:S(2)}, u32[]{:S(2)}) collective-permute-start(bf16[32,2048]{1,0:T(8,128)(2,1)S(1)} %slice.9), channel_id=1, source_target_pairs={{0,32},{32,0},{1,33},{33,1},{2,34},{34,2},{3,35},{35,3},{4,36},{36... | collective-permute-start | bytes 393224 | tf_op jit(solution)/shard_map/ppermute | solution.py:251
  190.9 1.2 all-to-all-done.2
  192.2 0.0 copy-start.2
  192.2 1.2 copy-done.2
  193.3 3.0 %combine.1 = bf16[128,4096]{1,0:T(8,128)(2,1)} custom-call(s32[1,128]{1,0:T(1,128)} %bitcast.22, s32[1,128]{1,0:T(1,128)} %bitcast.25, bf16[4,8,48,512]{3,2,1,0:T(8,128)(2,1)} %bitcast.18), custom_call_target="tpu_custom_call" | custom-call | tf_op jit(solution)/shard_map/combine/pallas_call | solution.py:239
  196.4 0.0 collective-permute-done.8
  196.4 0.0 copy-done.6
  196.4 0.0 copy-done.7
  196.4 0.0 copy-done.5
  196.4 1.0 multiply_subtract_fusion
  (1 shorter events, 0.0 us)
Async XLA Ops:
  7.2 11.4 %copy-start.4 = (f32[32,2048]{1,0:T(8,128)S(1)}, f32[32,2048]{1,0:T(8,128)}, u32[]{:S(2)}) copy-start(f32[32,2048]{1,0:T(8,128)} %param.15) | copy-start | bytes 786436
  9.8 32.0 %all-to-all-start = ((bf16[32,48,256]{2,1,0:T(8,128)(2,1)}), bf16[32,48,256]{2,1,0:T(8,128)(2,1)S(1)}, u32[]{:S(2)}, u32[]{:S(2)}) async-start(bf16[32,48,256]{2,1,0:T(8,128)(2,1)} %bitcast.19), calls=%async_computation | async-start | bytes 1572864 | tf_op jit(solution)/shard_map/all_to_all | solution.py:169
  18.5 118.9 %all-gather.2.cloned.1.call-start = ((), (), s32[]{:S(2)}) async-start(), calls=%async_computation.4 | async-start | bytes 2359296 | tf_op jit(solution)/shard_map/all_gather | solution.py:180
  18.6 12.2 %collective-permute-start.7 = (bf16[32,2048]{1,0:T(8,128)(2,1)S(1)}, bf16[32,2048]{1,0:T(8,128)(2,1)S(1)}, u32[]{:S(2)}, u32[]{:S(2)}) collective-permute-start(bf16[32,2048]{1,0:T(8,128)(2,1)S(1)} %convert_element_type.9), channel_id=1, source_target_pairs={{0,32},{32,0},{1,33},{33,1},{2,34},{34,2},{3,35},{35,3},{4,36},{36... | collective-permute-start | bytes 393224 | tf_op jit(solution)/shard_map/ppermute | solution.py:174
  41.8 59.6 %copy-start = (bf16[32,48,256]{2,1,0:T(8,128)(2,1)}, bf16[32,48,256]{2,1,0:T(8,128)(2,1)S(1)}, u32[]{:S(2)}) copy-start(bf16[32,48,256]{2,1,0:T(8,128)(2,1)S(1)} %all-to-all-done) | copy-start | bytes 2359300
  41.8 82.8 %all-to-all-start.1 = ((bf16[32,48,512]{2,1,0:T(8,128)(2,1)}), bf16[32,48,512]{2,1,0:T(8,128)(2,1)S(1)}, u32[]{:S(2)}, u32[]{:S(2)}) async-start(bf16[32,48,512]{2,1,0:T(8,128)(2,1)} %bitcast.15), calls=%async_computation.1 | async-start | bytes 3145728 | tf_op jit(solution)/shard_map/all_to_all | solution.py:201
  45.9 140.7 %reduce-scatter.2.cloned.1.call-start = ((), (), s32[]{:S(2)}) async-start(), calls=%async_computation.5 | async-start | bytes 2359296 | tf_op jit(solution)/shard_map/reduce_scatter | solution.py:221
  45.9 53.1 %collective-permute-start.3 = (bf16[1536,256]{1,0:T(8,128)(2,1)S(1)}, bf16[1536,256]{1,0:T(8,128)(2,1)S(1)}, u32[]{:S(2)}, u32[]{:S(2)}) collective-permute-start(bf16[1536,256]{1,0:T(8,128)(2,1)S(1)} %bitcast.10), channel_id=1, source_target_pairs={{0,4},{4,0},{8,12},{12,8},{16,20},{20,16},{24,28},{28,24},{1,5},{5... | collective-permute-start | bytes 2359304 | tf_op jit(solution)/shard_map/ppermute | solution.py:192
  49.3 56.5 %collective-permute-start.1 = (bf16[1536,256]{1,0:T(8,128)(2,1)S(1)}, bf16[1536,256]{1,0:T(8,128)(2,1)}, u32[]{:S(2)}, u32[]{:S(2)}) collective-permute-start(bf16[1536,256]{1,0:T(8,128)(2,1)S(1)} %bitcast.11), channel_id=1, source_target_pairs={{0,2},{2,0},{1,3},{3,1},{4,6},{6,4},{5,7},{7,5},{8,10},{10,8},{9,1... | collective-permute-start | bytes 2359304 | tf_op jit(solution)/shard_map/ppermute | solution.py:193
  99.0 25.6 %copy-start.3 = (bf16[1536,256]{1,0:T(8,128)(2,1)}, bf16[1536,256]{1,0:T(8,128)(2,1)S(1)}, u32[]{:S(2)}) copy-start(bf16[1536,256]{1,0:T(8,128)(2,1)S(1)} %collective-permute-done.3.rest_4_) | copy-start | bytes 2359300
  99.0 21.1 %collective-permute-start.5 = (bf16[1536,256]{1,0:T(8,128)(2,1)S(1)}, bf16[1536,256]{1,0:T(8,128)(2,1)}, u32[]{:S(2)}, u32[]{:S(2)}) collective-permute-start(bf16[1536,256]{1,0:T(8,128)(2,1)S(1)} %collective-permute-done.3.rest_4_), channel_id=1, source_target_pairs={{0,2},{2,0},{1,3},{3,1},{4,6},{6,4},{5,7},{7,5},{8,10},{10,8},{9,1... | collective-permute-start | bytes 2359304 | tf_op jit(solution)/shard_map/ppermute | solution.py:195
  101.5 21.1 %collective-permute-start = (bf16[1536,256]{1,0:T(8,128)(2,1)S(1)}, bf16[1536,256]{1,0:T(8,128)(2,1)}, u32[]{:S(2)}, u32[]{:S(2)}) collective-permute-start(bf16[1536,256]{1,0:T(8,128)(2,1)S(1)} %bitcast.12), channel_id=1, source_target_pairs={{0,1},{1,0},{2,3},{3,2},{4,5},{5,4},{6,7},{7,6},{8,9},{9,8},{10,11... | collective-permute-start | bytes 2359304 | tf_op jit(solution)/shard_map/ppermute | solution.py:194
  103.4 19.2 %collective-permute-start.4 = (bf16[1536,256]{1,0:T(8,128)(2,1)S(1)}, bf16[1536,256]{1,0:T(8,128)(2,1)}, u32[]{:S(2)}, u32[]{:S(2)}) collective-permute-start(bf16[1536,256]{1,0:T(8,128)(2,1)S(1)} %collective-permute-done.3.rest_4_), channel_id=1, source_target_pairs={{0,1},{1,0},{2,3},{3,2},{4,5},{5,4},{6,7},{7,6},{8,9},{9,8},{10,11... | collective-permute-start | bytes 2359304 | tf_op jit(solution)/shard_map/ppermute | solution.py:197
  105.9 16.8 %collective-permute-start.2 = (bf16[1536,256]{1,0:T(8,128)(2,1)}, bf16[1536,256]{1,0:T(8,128)(2,1)}, u32[]{:S(2)}, u32[]{:S(2)}) collective-permute-start(bf16[1536,256]{1,0:T(8,128)(2,1)} %collective-permute-done.1.rest_2_), channel_id=1, source_target_pairs={{0,1},{1,0},{2,3},{3,2},{4,5},{5,4},{6,7},{7,6},{8,9},{9,8},{10,11... | collective-permute-start | bytes 2359304 | tf_op jit(solution)/shard_map/ppermute | solution.py:196
  120.1 4.5 %collective-permute-start.6 = (bf16[1536,256]{1,0:T(8,128)(2,1)}, bf16[1536,256]{1,0:T(8,128)(2,1)}, u32[]{:S(2)}, u32[]{:S(2)}) collective-permute-start(bf16[1536,256]{1,0:T(8,128)(2,1)} %collective-permute-done.5.rest_6_), channel_id=1, source_target_pairs={{0,1},{1,0},{2,3},{3,2},{4,5},{5,4},{6,7},{7,6},{8,9},{9,8},{10,11... | collective-permute-start | bytes 2359304 | tf_op jit(solution)/shard_map/ppermute | solution.py:198
  124.6 1.2 copy-start.1
  145.1 47.1 %all-to-all-start.2 = ((bf16[32,48,512]{2,1,0:T(8,128)(2,1)}), bf16[32,48,512]{2,1,0:T(8,128)(2,1)S(1)}, u32[]{:S(2)}, u32[]{:S(2)}) async-start(bf16[32,48,512]{2,1,0:T(8,128)(2,1)} %bitcast.17), calls=%async_computation.2 | async-start | bytes 3145728 | tf_op jit(solution)/shard_map/all_to_all | solution.py:236
  153.0 43.4 %copy-start.6 = (f32[32,2048]{1,0:T(8,128)S(1)}, f32[32,2048]{1,0:T(8,128)}, u32[]{:S(2)}) copy-start(f32[32,2048]{1,0:T(8,128)} %param.17) | copy-start | bytes 786436
  153.0 43.4 %copy-start.7 = (f32[32,2048]{1,0:T(8,128)S(1)}, f32[32,2048]{1,0:T(8,128)}, u32[]{:S(2)}) copy-start(f32[32,2048]{1,0:T(8,128)} %param.16) | copy-start | bytes 786436
  186.6 9.8 %copy-start.5 = (bf16[64,2048]{1,0:T(8,128)(2,1)S(1)}, bf16[64,2048]{1,0:T(8,128)(2,1)}, u32[]{:S(2)}) copy-start(bf16[64,2048]{1,0:T(8,128)(2,1)} %reduce-scatter.2.cloned.1.call-done) | copy-start | bytes 786436
  187.6 8.8 %collective-permute-start.8 = (bf16[32,2048]{1,0:T(8,128)(2,1)S(1)}, bf16[32,2048]{1,0:T(8,128)(2,1)S(1)}, u32[]{:S(2)}, u32[]{:S(2)}) collective-permute-start(bf16[32,2048]{1,0:T(8,128)(2,1)S(1)} %slice.9), channel_id=1, source_target_pairs={{0,32},{32,0},{1,33},{33,1},{2,34},{34,2},{3,35},{35,3},{4,36},{36... | collective-permute-start | bytes 393224 | tf_op jit(solution)/shard_map/ppermute | solution.py:251
  192.2 1.2 copy-start.2
Sparse Core Ops, SparseCore 0:
  31.7 46.8 all-gather.1
  137.5 48.9 reduce-scatter.1

commit v4 on v2

--- a/solution.py
+++ b/solution.py
@@ -1,3 +1,5 @@
+import functools
+
 import jax
 import jax.numpy as jnp
 from jax import lax
@@ -92,40 +94,103 @@
         out_ref[:, g * piece : (g + 1) * piece] = total.astype(jnp.bfloat16)
 
 
-def weight_grad_kernel(q_ref, x_ref, *rest):
-    parts = rest[:PIECES]
-    out_ref, x_buf, g_buf, xt_buf, sems = rest[PIECES:]
-    x_copy = pltpu.make_async_copy(x_ref, x_buf, sems.at[PIECES])
-    copies = [pltpu.make_async_copy(parts[j], g_buf.at[j], sems.at[j]) for j in range(PIECES)]
+def weight_grad_kernel(slots, first, q_ref, x_ref, *rest):
+    count = len(slots)
+    parts, rest = rest[:count], rest[count:]
+    if first:
+        out_ref, xt_ref, x_buf, g_buf, o_buf, sems = rest
+    else:
+        _, out_ref, xt_ref, g_buf, o_buf, sems = rest
+    x_copy = pltpu.make_async_copy(x_ref, x_buf if first else xt_ref, sems.at[2 * count])
     x_copy.start()
-    for copy in copies:
-        copy.start()
+    loads = [pltpu.make_async_copy(parts[i], g_buf.at[i], sems.at[i]) for i in range(count)]
+    for load in loads:
+        load.start()
     x_copy.wait()
-    xt_buf[...] = x_buf[...].T
+    if first:
+        xt_ref[...] = x_buf[...].T
     piece = g_buf.shape[2]
-    for j in range(PIECES):
-        copies[j].wait()
-        at = pl.multiple_of((q_ref[0] ^ j) * piece, piece)
-        out_ref[:, pl.ds(at, piece)] = jnp.dot(
-            xt_buf[...], g_buf[j], preferred_element_type=jnp.float32
+    stores = []
+    for i, slot in enumerate(slots):
+        loads[i].wait()
+        o_buf[i] = jnp.dot(
+            xt_ref[...], g_buf[i], preferred_element_type=jnp.float32
         ).astype(jnp.bfloat16)
-
-
-def input_grad_kernel(q_ref, *rest):
-    parts = rest[:PIECES]
-    w_ref, out_ref = rest[PIECES:]
+        at = pl.multiple_of((q_ref[0] ^ slot) * piece, piece)
+        store = pltpu.make_async_copy(
+            o_buf.at[i], out_ref.at[:, pl.ds(at, piece)], sems.at[count + i]
+        )
+        store.start()
+        stores.append(store)
+    for store in stores:
+        store.wait()
+
+
+def weight_grad_call(slots, spot, x, parts, done, width):
+    first = done is None
+    rows, gpiece = parts[0].shape
+    piece = x.shape[1] if first else x.shape[0]
+    count = len(slots)
+    out = jax.ShapeDtypeStruct((piece, width), jnp.bfloat16)
+    xt = jax.ShapeDtypeStruct((piece, rows), jnp.bfloat16)
+    anywhere = pl.BlockSpec(memory_space=pl.ANY)
+    scratch = [
+        pltpu.VMEM((rows, piece) if first else (piece, rows), jnp.bfloat16),
+        pltpu.VMEM((count, rows, gpiece), jnp.bfloat16),
+        pltpu.VMEM((count, piece, gpiece), jnp.bfloat16),
+        pltpu.SemaphoreType.DMA((2 * count + 1,)),
+    ]
+    operands = (spot, x, *parts) if first else (spot, x, *parts, done)
+    return pl.pallas_call(
+        functools.partial(weight_grad_kernel, slots, first),
+        out_shape=(out, xt) if first else out,
+        in_specs=[pl.BlockSpec(memory_space=pltpu.SMEM)] + [anywhere] * (len(operands) - 1),
+        out_specs=(anywhere, VMEM) if first else anywhere,
+        input_output_aliases={} if first else {len(operands) - 1: 0},
+        scratch_shapes=scratch,
+        compiler_params=params(),
+        name="weight_grad",
+    )(*operands)
+
+
+def input_grad_kernel(slots, q_ref, *rest):
+    count = len(slots)
+    parts, rest = rest[:count], rest[count:]
+    w_ref, out_ref = rest[0], rest[-1]
     piece = parts[0].shape[1]
-    total = None
-    for j in range(PIECES):
-        at = pl.multiple_of((q_ref[0] ^ j) * piece, piece)
+    total = rest[1][...] if len(rest) == 3 else None
+    for part_ref, slot in zip(parts, slots):
+        at = pl.multiple_of((q_ref[0] ^ slot) * piece, piece)
         part = lax.dot_general(
-            parts[j][...],
+            part_ref[...],
             w_ref[:, pl.ds(at, piece)],
             (((1,), (1,)), ((), ())),
             preferred_element_type=jnp.float32,
         )
         total = part if total is None else total + part
-    out_ref[...] = total.astype(jnp.bfloat16)
+    out_ref[...] = total.astype(out_ref.dtype)
+
+
+def input_grad_call(slots, spot, parts, weights, partial):
+    rows, gpiece = parts[0].shape
+    piece = weights.shape[0]
+    block = 512
+    by_rows = pl.BlockSpec((block, piece), lambda t: (t, 0))
+    extra = [] if partial is None else [partial]
+    return pl.pallas_call(
+        functools.partial(input_grad_kernel, slots),
+        grid=(rows // block,),
+        out_shape=jax.ShapeDtypeStruct(
+            (rows, piece), jnp.float32 if partial is None else jnp.bfloat16
+        ),
+        in_specs=[pl.BlockSpec(memory_space=pltpu.SMEM)]
+        + [pl.BlockSpec((block, gpiece), lambda t: (t, 0))] * len(parts)
+        + [pl.BlockSpec(weights.shape, lambda t: (0, 0))]
+        + [by_rows] * len(extra),
+        out_specs=by_rows,
+        compiler_params=params(),
+        name="input_grad",
+    )(spot, *parts, weights, *extra)
 
 
 def swap_pairs(count):
@@ -190,44 +255,23 @@
     g_own = g_recv.reshape(rows_total, gpiece)
     g_side = lax.ppermute(g_own, "xl", swap_pairs(2))
     g_core = lax.ppermute(g_own, "core", swap_pairs(2))
-    g_both = lax.ppermute(g_side, "core", swap_pairs(2))
-    pieces = (g_own, g_core, g_side, g_both)
 
     x_recv = lax.all_to_all(
         x_send.reshape(members, CAP, piece), EXP, split_axis=0, concat_axis=0, tiled=True
     )
     x_rows = x_recv.reshape(rows_total, piece)
 
-    block = 512
-    dx_rows = pl.pallas_call(
-        input_grad_kernel,
-        grid=(rows_total // block,),
-        out_shape=jax.ShapeDtypeStruct((rows_total, piece), jnp.bfloat16),
-        in_specs=[pl.BlockSpec(memory_space=pltpu.SMEM)]
-        + [pl.BlockSpec((block, gpiece), lambda t: (t, 0))] * PIECES
-        + [pl.BlockSpec((piece, 2 * hidden), lambda t: (0, 0))],
-        out_specs=pl.BlockSpec((block, piece), lambda t: (t, 0)),
-        compiler_params=params(),
-        name="input_grad",
-    )(spot, *pieces, weights)
-    dx_rows, x_rows = lax.optimization_barrier((dx_rows, x_rows))
-
-    grad_part = pl.pallas_call(
-        weight_grad_kernel,
-        out_shape=jax.ShapeDtypeStruct((piece, 2 * hidden), jnp.bfloat16),
-        in_specs=[pl.BlockSpec(memory_space=pltpu.SMEM)]
-        + [pl.BlockSpec(memory_space=pl.ANY)] * (PIECES + 1),
-        out_specs=VMEM,
-        scratch_shapes=[
-            pltpu.VMEM((rows_total, piece), jnp.bfloat16),
-            pltpu.VMEM((PIECES, rows_total, gpiece), jnp.bfloat16),
-            pltpu.VMEM((piece, rows_total), jnp.bfloat16),
-            pltpu.SemaphoreType.DMA((PIECES + 1,)),
-        ],
-        compiler_params=params(),
-        name="weight_grad",
-    )(spot, x_rows, *pieces)
+    dx_part = input_grad_call((0, 1), spot, (g_own, g_core), weights, None)
+    dx_part, g_side = lax.optimization_barrier((dx_part, g_side))
+    g_both = lax.ppermute(g_side, "core", swap_pairs(2))
+    grad_part, x_turned = weight_grad_call(
+        (0, 1), spot, x_rows, (g_own, g_core), None, 2 * hidden
+    )
+    grad_part = weight_grad_call((2,), spot, x_turned, (g_side,), grad_part, 2 * hidden)
+    grad_part = weight_grad_call((3,), spot, x_turned, (g_both,), grad_part, 2 * hidden)
     grad_z = lax.psum_scatter(grad_part, "z", scatter_dimension=0, tiled=True)
+    grad_part, dx_part = lax.optimization_barrier((grad_part, dx_part))
+    dx_rows = input_grad_call((2, 3), spot, (g_side, g_both), weights, dx_part)
     back = lax.all_to_all(
         dx_rows.reshape(members, CAP, piece), EXP, split_axis=0, concat_axis=0, tiled=True
     )

time: 197 us -> 196 us (level)
  waiting for transfers between devices: 121 us -> 106 us
  Pallas kernels: 23.9 us -> 35 us
  local copies, waits for them, and re-layouts: 2.17 us -> 4.44 us
    ppermute x1, waiting for transfers between devices: 43.5 us -> 25.2 us  [body(): g_side = lax.ppermute(g_own, 'xl', swap_pairs(2))]
    all_gather x1, waiting for transfers between devices: 0.02 us -> 13.3 us  [body(): weights = lax.all_gather(pair_bf, 'z', axis=0, tiled=True)]
    pallas_call x2 -> x5, Pallas kernels: 14.8 us -> 26 us  [the longest x3 13.3 us: weight_grad_call(): pl.pallas_call(functools.partial(weight_grad_kernel, slots, first), out_s...]
    reduce_scatter x1, waiting for transfers between devices: 41.6 us -> 35.3 us  [body(): grad_z = lax.psum_scatter(grad_part, 'z', scatter_dimension=0, tiled=True)]
    ppermute x1, waiting for transfers between devices: 3.46 us -> 0.01 us  [body(): g_both = lax.ppermute(g_side, 'core', swap_pairs(2))]
    unnamed x14 -> x16, local copies, waits for them, and re-layouts: 1.18 us -> 3.45 us
  transfers between devices with their start and end apart: 10 -> 10, of which waited for: 6 -> 6; matrix products, arithmetic and copies ran while one was open for 1% -> 1% of each run, Pallas kernels for 7% -> 15%
where the time goes in v4:
time: 196 us; the launch traced here: 194 us
  waiting for transfers between devices  106 us (54%)
  Pallas kernels  35 us (18%)
  starting transfers between devices  33.1 us (17%)
  between operations  14.2 us (7%)
  local copies, waits for them, and re-layouts  4.44 us (2%)
    reduce_scatter x1, waiting for transfers between devices, body(): grad_z = lax.psum_scatter(grad_part, 'z', scatter_dimension=0, tiled=True)  35.3 us
    ppermute x1, waiting for transfers between devices, body(): g_side = lax.ppermute(g_own, 'xl', swap_pairs(2))  25.2 us
    all_to_all x1, waiting for transfers between devices, body(): lax.all_to_all(g_send.reshape(members, CAP, gpiece), EXP, split_axis=0, c...  23.6 us
    pallas_call x3, Pallas kernels, weight_grad_call(): pl.pallas_call(functools.partial(weight_grad_kernel, slots, first), out_s...  13.3 us
    all_gather x1, waiting for transfers between devices, body(): weights = lax.all_gather(pair_bf, 'z', axis=0, tiled=True)  13.3 us
    pallas_call x2, Pallas kernels, input_grad_call(): pl.pallas_call(functools.partial(input_grad_kernel, slots), grid=(rows //...  12.7 us
    all_to_all x1, starting transfers between devices, body(): lax.all_to_all(g_send.reshape(members, CAP, gpiece), EXP, split_axis=0, c...  8.85 us
    ppermute x1, waiting for transfers between devices, body(): came_bf = lax.ppermute(own_bf, 'xh', swap_pairs(2))  7.47 us
  transfers between devices with their start and end apart: 10, of which 6 were waited for; matrix products, arithmetic and copies ran while one was open for 1% of the time, Pallas kernels for 15%

profile of v4, /device:TPU:6, one launch (start us, length us, event | category | flops | bytes accessed | tf_op | source)
XLA Modules:
  0.0 194.2 jit_solution(14999955495473294474)
XLA Ops:
  7.2 2.9 %pack_grads.1 = bf16[4,2,4,48,512]{4,3,2,1,0:T(8,128)(2,1)} custom-call(s32[1,128]{1,0:T(1,128)} %bitcast.28, s32[1,128]{1,0:T(1,128)} %bitcast.31, bf16[128,1024]{1,0:T(8,128)(2,1)} %grad_ref.1, bf16[128,1024]{1,0:T(8,128)(2,1)} %gate_ref.1, bf16[128,1024]{1,0:T(8,128)(2,1)} %up_ref.1), custom_call_target="tpu_custom_call" | custom-call | tf_op jit(solution)/shard_map/pack_grads/pallas_call | solution.py:222
  10.0 0.0 copy-start.4
  10.0 8.9 %all-to-all-start = ((bf16[32,48,512]{2,1,0:T(8,128)(2,1)}), bf16[32,48,512]{2,1,0:T(8,128)(2,1)S(1)}, u32[]{:S(2)}, u32[]{:S(2)}) async-start(bf16[32,48,512]{2,1,0:T(8,128)(2,1)} %bitcast.25), calls=%async_computation | async-start | bytes 3145728 | tf_op jit(solution)/shard_map/all_to_all | solution.py:233
  18.9 0.0 all-gather.2.cloned.1.call-start
  18.9 0.0 copy-done.4
  19.0 4.1 %collective-permute-start.1 = (bf16[32,2048]{1,0:T(8,128)(2,1)S(1)}, bf16[32,2048]{1,0:T(8,128)(2,1)S(1)}, u32[]{:S(2)}, u32[]{:S(2)}) collective-permute-start(bf16[32,2048]{1,0:T(8,128)(2,1)S(1)} %convert_element_type.12), channel_id=1, source_target_pairs={{0,32},{32,0},{1,33},{33,1},{2,34},{34,2},{3,35},{35,3},{4,36},{36... | collective-permute-start | bytes 393224 | tf_op jit(solution)/shard_map/ppermute | solution.py:238
  23.1 7.5 %collective-permute-done.1 = bf16[32,2048]{1,0:T(8,128)(2,1)S(1)} collective-permute-done((bf16[32,2048]{1,0:T(8,128)(2,1)S(1)}, bf16[32,2048]{1,0:T(8,128)(2,1)S(1)}, u32[]{:S(2)}, u32[]{:S(2)}) %collective-permute-start.1) | collective-permute-done | bytes 131104 | tf_op jit(solution)/shard_map/ppermute | solution.py:238
  30.6 0.8 maximum_select_fusion
  31.3 0.0 all-gather.2.cloned.1.call-update
  31.4 3.1 %pack_rows.1 = bf16[4,8,48,512]{3,2,1,0:T(8,128)(2,1)} custom-call(s32[1,128]{1,0:T(1,128)} %bitcast.29, s32[1,128]{1,0:T(1,128)} %bitcast.32, bf16[128,4096]{1,0:T(8,128)(2,1)} %x_ref), custom_call_target="tpu_custom_call" | custom-call | tf_op jit(solution)/shard_map/pack_rows/pallas_call | solution.py:245
  34.4 23.6 %all-to-all-done = bf16[32,48,512]{2,1,0:T(8,128)(2,1)S(1)} async-done(((bf16[32,48,512]{2,1,0:T(8,128)(2,1)}), bf16[32,48,512]{2,1,0:T(8,128)(2,1)S(1)}, u32[]{:S(2)}, u32[]{:S(2)}) %all-to-all-start) | async-done | bytes 1572896 | tf_op jit(solution)/shard_map/all_to_all | solution.py:233
  58.1 0.0 copy-start
  58.1 2.0 %collective-permute-start = (bf16[1536,512]{1,0:T(8,128)(2,1)S(1)}, bf16[1536,512]{1,0:T(8,128)(2,1)S(1)}, u32[]{:S(2)}, u32[]{:S(2)}) collective-permute-start(bf16[1536,512]{1,0:T(8,128)(2,1)S(1)} %bitcast.18), channel_id=1, source_target_pairs={{0,1},{1,0},{2,3},{3,2},{4,5},{5,4},{6,7},{7,6},{8,9},{9,8},{10,11... | collective-permute-start | bytes 4718600 | tf_op jit(solution)/shard_map/ppermute | solution.py:257
  60.0 2.3 %collective-permute-start.2 = (bf16[1536,512]{1,0:T(8,128)(2,1)S(1)}, bf16[1536,512]{1,0:T(8,128)(2,1)}, u32[]{:S(2)}, u32[]{:S(2)}) collective-permute-start(bf16[1536,512]{1,0:T(8,128)(2,1)S(1)} %bitcast.19), channel_id=1, source_target_pairs={{0,2},{2,0},{1,3},{3,1},{4,6},{6,4},{5,7},{7,5},{8,10},{10,8},{9,1... | collective-permute-start | bytes 4718600 | tf_op jit(solution)/shard_map/ppermute | solution.py:256
  62.4 0.0 copy-done
  62.4 5.9 %all-to-all-start.1 = ((bf16[32,48,512]{2,1,0:T(8,128)(2,1)}), bf16[32,48,512]{2,1,0:T(8,128)(2,1)}, u32[]{:S(2)}, u32[]{:S(2)}) async-start(bf16[32,48,512]{2,1,0:T(8,128)(2,1)} %bitcast.22), calls=%async_computation.1 | async-start | bytes 3145728 | tf_op jit(solution)/shard_map/all_to_all | solution.py:259
  68.3 0.0 reduce-scatter.2.cloned.1.call-start
  68.4 13.3 %all-gather.2.cloned.1.call-done.rest_2_ = bf16[512,2048]{1,0:T(8,128)(2,1)} async-done(((bf16[64,2048]{1,0:T(8,128)(2,1)}), bf16[512,2048]{1,0:T(8,128)(2,1)}) %all-gather.2.cloned.1.call-update) | async-done | bytes 2097168 | tf_op jit(solution)/shard_map/all_gather | solution.py:244
  81.7 0.0 collective-permute-done.rest_1_
  81.7 0.0 copy-start.1
  81.7 1.1 copy-done.1
  82.8 6.0 %input_grad.2.rest_3_ = f32[1536,512]{1,0:T(8,128)} custom-call(s32[1]{0:T(128)} %bitcast.2.q_ref, bf16[1536,512]{1,0:T(8,128)(2,1)} %bitcast.20, bf16[1536,512]{1,0:T(8,128)(2,1)} %copy-done.1, bf16[512,2048]{1,0:T(8,128)(2,1)} %all-gather.2.cloned.1.call-done.rest_2_), custom_call_target="tpu_custom_call" | custom-call | tf_op jit(solution)/shard_map/input_grad/pallas_call | solution.py:180
  88.8 25.2 %collective-permute-done.2.rest_0_ = bf16[1536,512]{1,0:T(8,128)(2,1)} collective-permute-done((bf16[1536,512]{1,0:T(8,128)(2,1)S(1)}, bf16[1536,512]{1,0:T(8,128)(2,1)}, u32[]{:S(2)}, u32[]{:S(2)}) %collective-permute-start.2) | collective-permute-done | bytes 1572896 | tf_op jit(solution)/shard_map/ppermute | solution.py:256
  114.0 1.9 collective-permute-start.3
  115.9 0.0 all-to-all-done.1
  115.9 5.9 %weight_grad.3 = (bf16[512,2048]{1,0:T(8,128)(2,1)}, bf16[512,1536]{1,0:T(8,128)(2,1)}) custom-call(s32[1]{0:T(128)} %bitcast.2.q_ref, bf16[1536,512]{1,0:T(8,128)(2,1)} %bitcast.6.x_ref, bf16[1536,512]{1,0:T(8,128)(2,1)} %bitcast.21, bf16[1536,512]{1,0:T(8,128)(2,1)} %copy-done.1), custom_call_target="tpu_custom_call" | custom-call | tf_op jit(solution)/shard_map/weight_grad/pallas_call | solution.py:144
  121.8 3.7 %weight_grad.4.rest_1_ = bf16[512,2048]{1,0:T(8,128)(2,1)} custom-call(s32[1]{0:T(128)} %bitcast.2.q_ref, bf16[512,1536]{1,0:T(8,128)(2,1)} %get-tuple-element.20.x_ref, bf16[1536,512]{1,0:T(8,128)(2,1)} %collective-permute-done.2.rest_0_, bf16[512,2048]{1,0:T(8,128)(2,1)} %get-tuple-element.21.rest_1_), custom_call_target="tpu_custom_call", output_to_operand_aliasing={{}: (3, {})} | custom-call | tf_op jit(solution)/shard_map/weight_grad/pallas_call | solution.py:144
  125.5 0.0 collective-permute-done.3.rest_0_.rest_1_
  125.5 0.0 copy-start.3
  125.5 1.1 copy-done.3
  126.7 3.8 %weight_grad.5 = bf16[512,2048]{1,0:T(8,128)(2,1)} custom-call(s32[1]{0:T(128)} %bitcast.2.q_ref, bf16[512,1536]{1,0:T(8,128)(2,1)} %get-tuple-element.20.x_ref, bf16[1536,512]{1,0:T(8,128)(2,1)} %copy-done.3, bf16[512,2048]{1,0:T(8,128)(2,1)} %weight_grad.4.rest_1_), custom_call_target="tpu_custom_call", output_to_operand_aliasing={{}: (3, {})} | custom-call | tf_op jit(solution)/shard_map/weight_grad/pallas_call | solution.py:144
  130.4 0.0 reduce-scatter.2.cloned.1.call-update
  130.5 6.7 %input_grad.3 = bf16[1536,512]{1,0:T(8,128)(2,1)} custom-call(s32[1]{0:T(128)} %bitcast.2.q_ref, bf16[1536,512]{1,0:T(8,128)(2,1)} %collective-permute-done.2.rest_0_, bf16[1536,512]{1,0:T(8,128)(2,1)} %copy-done.3, bf16[512,2048]{1,0:T(8,128)(2,1)} %all-gather.2.cloned.1.call-done.rest_2_, f32[1536,512]{1,0:T(8,128)} %input_grad.2.rest_3_), custom_call_target="tpu_custom_call" | custom-call | tf_op jit(solution)/shard_map/input_grad/pallas_call | solution.py:180
  137.2 4.6 %all-to-all-start.2 = ((bf16[32,48,512]{2,1,0:T(8,128)(2,1)}), bf16[32,48,512]{2,1,0:T(8,128)(2,1)S(1)}, u32[]{:S(2)}, u32[]{:S(2)}) async-start(bf16[32,48,512]{2,1,0:T(8,128)(2,1)} %bitcast.23), calls=%async_computation.2 | async-start | bytes 3145728 | tf_op jit(solution)/shard_map/all_to_all | solution.py:275
  141.7 0.0 copy-start.5
  141.7 0.0 copy-start.6
  141.7 35.3 %reduce-scatter.2.cloned.1.call-done = bf16[64,2048]{1,0:T(8,128)(2,1)} async-done(((bf16[512,2048]{1,0:T(8,128)(2,1)}), bf16[64,2048]{1,0:T(8,128)(2,1)}) %reduce-scatter.2.cloned.1.call-update) | async-done | bytes 262160 | tf_op jit(solution)/shard_map/reduce_scatter | solution.py:272
  177.0 0.0 copy-start.7
  177.0 1.0 dynamic-slice_bitcast_fusion
  178.0 3.4 %collective-permute-start.4 = (bf16[32,2048]{1,0:T(8,128)(2,1)S(1)}, bf16[32,2048]{1,0:T(8,128)(2,1)S(1)}, u32[]{:S(2)}, u32[]{:S(2)}) collective-permute-start(bf16[32,2048]{1,0:T(8,128)(2,1)S(1)} %dynamic-slice_bitcast_fusion), channel_id=1, source_target_pairs={{0,32},{32,0},{1,33},{33,1},{2,34},{34,2},{3,35},{35,3},{4,36},{36... | collective-permute-start | bytes 393224 | tf_op jit(solution)/shard_map/ppermute | solution.py:291
  181.4 0.0 all-to-all-done.2
  181.4 0.0 copy-start.2
  181.4 1.1 copy-done.2
  182.6 3.0 %combine.1 = bf16[128,4096]{1,0:T(8,128)(2,1)} custom-call(s32[1,128]{1,0:T(1,128)} %bitcast.30, s32[1,128]{1,0:T(1,128)} %bitcast.33, bf16[4,8,48,512]{3,2,1,0:T(8,128)(2,1)} %bitcast.24), custom_call_target="tpu_custom_call" | custom-call | tf_op jit(solution)/shard_map/combine/pallas_call | solution.py:278
  185.6 0.8 collective-permute-done.4
  186.4 0.0 copy-done.5
  186.4 0.0 copy-done.6
  186.4 0.0 copy-done.7
  186.4 1.0 multiply_subtract_fusion
  (1 shorter events, 0.0 us)
Async XLA Ops:
  10.0 8.9 %copy-start.4 = (f32[32,2048]{1,0:T(8,128)S(1)}, f32[32,2048]{1,0:T(8,128)}, u32[]{:S(2)}) copy-start(f32[32,2048]{1,0:T(8,128)} %param.15) | copy-start | bytes 786436
  10.0 48.1 %all-to-all-start = ((bf16[32,48,512]{2,1,0:T(8,128)(2,1)}), bf16[32,48,512]{2,1,0:T(8,128)(2,1)S(1)}, u32[]{:S(2)}, u32[]{:S(2)}) async-start(bf16[32,48,512]{2,1,0:T(8,128)(2,1)} %bitcast.25), calls=%async_computation | async-start | bytes 3145728 | tf_op jit(solution)/shard_map/all_to_all | solution.py:233
  18.9 62.8 %all-gather.2.cloned.1.call-start = ((), (), s32[]{:S(2)}) async-start(), calls=%async_computation.4 | async-start | bytes 2359296 | tf_op jit(solution)/shard_map/all_gather | solution.py:244
  19.0 11.6 %collective-permute-start.1 = (bf16[32,2048]{1,0:T(8,128)(2,1)S(1)}, bf16[32,2048]{1,0:T(8,128)(2,1)S(1)}, u32[]{:S(2)}, u32[]{:S(2)}) collective-permute-start(bf16[32,2048]{1,0:T(8,128)(2,1)S(1)} %convert_element_type.12), channel_id=1, source_target_pairs={{0,32},{32,0},{1,33},{33,1},{2,34},{34,2},{3,35},{35,3},{4,36},{36... | collective-permute-start | bytes 393224 | tf_op jit(solution)/shard_map/ppermute | solution.py:238
  58.1 4.3 %copy-start = (bf16[32,48,512]{2,1,0:T(8,128)(2,1)}, bf16[32,48,512]{2,1,0:T(8,128)(2,1)S(1)}, u32[]{:S(2)}) copy-start(bf16[32,48,512]{2,1,0:T(8,128)(2,1)S(1)} %all-to-all-done) | copy-start | bytes 4718596
  58.1 23.6 %collective-permute-start = (bf16[1536,512]{1,0:T(8,128)(2,1)S(1)}, bf16[1536,512]{1,0:T(8,128)(2,1)S(1)}, u32[]{:S(2)}, u32[]{:S(2)}) collective-permute-start(bf16[1536,512]{1,0:T(8,128)(2,1)S(1)} %bitcast.18), channel_id=1, source_target_pairs={{0,1},{1,0},{2,3},{3,2},{4,5},{5,4},{6,7},{7,6},{8,9},{9,8},{10,11... | collective-permute-start | bytes 4718600 | tf_op jit(solution)/shard_map/ppermute | solution.py:257
  60.0 53.9 %collective-permute-start.2 = (bf16[1536,512]{1,0:T(8,128)(2,1)S(1)}, bf16[1536,512]{1,0:T(8,128)(2,1)}, u32[]{:S(2)}, u32[]{:S(2)}) collective-permute-start(bf16[1536,512]{1,0:T(8,128)(2,1)S(1)} %bitcast.19), channel_id=1, source_target_pairs={{0,2},{2,0},{1,3},{3,1},{4,6},{6,4},{5,7},{7,5},{8,10},{10,8},{9,1... | collective-permute-start | bytes 4718600 | tf_op jit(solution)/shard_map/ppermute | solution.py:256
  62.4 53.5 %all-to-all-start.1 = ((bf16[32,48,512]{2,1,0:T(8,128)(2,1)}), bf16[32,48,512]{2,1,0:T(8,128)(2,1)}, u32[]{:S(2)}, u32[]{:S(2)}) async-start(bf16[32,48,512]{2,1,0:T(8,128)(2,1)} %bitcast.22), calls=%async_computation.1 | async-start | bytes 3145728 | tf_op jit(solution)/shard_map/all_to_all | solution.py:259
  68.3 108.7 %reduce-scatter.2.cloned.1.call-start = ((), (), s32[]{:S(2)}) async-start(), calls=%async_computation.5 | async-start | bytes 2359296 | tf_op jit(solution)/shard_map/reduce_scatter | solution.py:272
  81.7 1.1 copy-start.1
  114.0 11.5 %collective-permute-start.3 = (bf16[1536,512]{1,0:T(8,128)(2,1)}, bf16[1536,512]{1,0:T(8,128)(2,1)S(1)}, u32[]{:S(2)}, u32[]{:S(2)}) collective-permute-start(bf16[1536,512]{1,0:T(8,128)(2,1)} %collective-permute-done.2.rest_0_), channel_id=1, source_target_pairs={{0,1},{1,0},{2,3},{3,2},{4,5},{5,4},{6,7},{7,6},{8,9},{9,8},{10,11... | collective-permute-start | bytes 4718600 | tf_op jit(solution)/shard_map/ppermute | solution.py:266
  125.5 1.2 copy-start.3
  137.2 44.3 %all-to-all-start.2 = ((bf16[32,48,512]{2,1,0:T(8,128)(2,1)}), bf16[32,48,512]{2,1,0:T(8,128)(2,1)S(1)}, u32[]{:S(2)}, u32[]{:S(2)}) async-start(bf16[32,48,512]{2,1,0:T(8,128)(2,1)} %bitcast.23), calls=%async_computation.2 | async-start | bytes 3145728 | tf_op jit(solution)/shard_map/all_to_all | solution.py:275
  141.7 44.7 %copy-start.5 = (f32[32,2048]{1,0:T(8,128)S(1)}, f32[32,2048]{1,0:T(8,128)}, u32[]{:S(2)}) copy-start(f32[32,2048]{1,0:T(8,128)} %param.17) | copy-start | bytes 786436
  141.7 44.7 %copy-start.6 = (f32[32,2048]{1,0:T(8,128)S(1)}, f32[32,2048]{1,0:T(8,128)}, u32[]{:S(2)}) copy-start(f32[32,2048]{1,0:T(8,128)} %param.16) | copy-start | bytes 786436
  177.0 9.4 %copy-start.7 = (bf16[64,2048]{1,0:T(8,128)(2,1)S(1)}, bf16[64,2048]{1,0:T(8,128)(2,1)}, u32[]{:S(2)}) copy-start(bf16[64,2048]{1,0:T(8,128)(2,1)} %reduce-scatter.2.cloned.1.call-done) | copy-start | bytes 786436
  178.0 8.4 %collective-permute-start.4 = (bf16[32,2048]{1,0:T(8,128)(2,1)S(1)}, bf16[32,2048]{1,0:T(8,128)(2,1)S(1)}, u32[]{:S(2)}, u32[]{:S(2)}) collective-permute-start(bf16[32,2048]{1,0:T(8,128)(2,1)S(1)} %dynamic-slice_bitcast_fusion), channel_id=1, source_target_pairs={{0,32},{32,0},{1,33},{33,1},{2,34},{34,2},{3,35},{35,3},{4,36},{36... | collective-permute-start | bytes 393224 | tf_op jit(solution)/shard_map/ppermute | solution.py:291
  181.4 1.2 copy-start.2
Sparse Core Ops, SparseCore 0:
  31.5 50.1 all-gather.1
  130.6 46.4 reduce-scatter.1

commit v5 on v1

--- a/solution.py
+++ b/solution.py
@@ -8,6 +8,7 @@
 EXPERTS = 4
 CAP = 48
 GROUP = 8
+RING = 8
 
 beta_one = 0.9
 beta_two = 0.999
@@ -90,28 +91,48 @@
         out_ref[:, g * piece : (g + 1) * piece] = total.astype(jnp.bfloat16)
 
 
-def weight_grad_kernel(x_ref, g_ref, out_ref, xt_ref):
+def weight_grad_kernel(x_ref, g_ref, out_ref, x_buf, g_buf, xt_buf, sems):
+    pairs = GROUP // 2
+    x_copy = pltpu.make_async_copy(x_ref, x_buf, sems.at[pairs])
+    copies = [
+        pltpu.make_async_copy(g_ref.at[pl.ds(2 * j, 2)], g_buf.at[pl.ds(2 * j, 2)], sems.at[j])
+        for j in range(pairs)
+    ]
+    x_copy.start()
+    for copy in copies:
+        copy.start()
+    x_copy.wait()
+    xt_buf[...] = x_buf[...].T
+    piece = g_buf.shape[2]
+    for j in range(pairs):
+        copies[j].wait()
+        both = jnp.concatenate([g_buf[2 * j], g_buf[2 * j + 1]], axis=1)
+        out_ref[:, 2 * j * piece : (2 * j + 2) * piece] = jnp.dot(
+            xt_buf[...], both, preferred_element_type=jnp.float32
+        ).astype(jnp.bfloat16)
+
+
+def input_grad_kernel(z_ref, g_ref, *rest):
+    shards, (out_ref, w_buf, sems) = rest[:RING], rest[RING:]
+    rows = shards[0].shape[0]
+
     @pl.when(pl.program_id(0) == 0)
     def _():
-        xt_ref[...] = x_ref[...].T
-
-    out_ref[...] = jnp.dot(
-        xt_ref[...], g_ref[0], preferred_element_type=jnp.float32
+        copies = []
+        for k in range(RING):
+            at = pl.multiple_of(lax.rem(z_ref[0] + RING - k, RING) * rows, rows)
+            copies.append(
+                pltpu.make_async_copy(shards[k], w_buf.at[pl.ds(at, rows)], sems.at[k])
+            )
+        for copy in copies:
+            copy.start()
+        for copy in copies:
+            copy.wait()
+
+    grads = jnp.concatenate([g_ref[g] for g in range(GROUP)], axis=1)
+    out_ref[...] = lax.dot_general(
+        grads, w_buf[...], (((1,), (1,)), ((), ())), preferred_element_type=jnp.float32
     ).astype(jnp.bfloat16)
-
-
-def input_grad_kernel(g_ref, w_ref, out_ref):
-    piece = g_ref.shape[2]
-    total = None
-    for g in range(GROUP):
-        part = lax.dot_general(
-            g_ref[g],
-            w_ref[:, g * piece : (g + 1) * piece],
-            (((1,), (1,)), ((), ())),
-            preferred_element_type=jnp.float32,
-        )
-        total = part if total is None else total + part
-    out_ref[...] = total.astype(jnp.bfloat16)
 
 
 def swap_pairs(count):
@@ -138,9 +159,7 @@
     mod = modality.reshape(1, tok_count)
     idx = expert_index.reshape(1, tok_count)
     half = lax.axis_index("xh")
-
-    shard_bf = master.astype(jnp.bfloat16)
-    pair_bf = lax.all_gather(shard_bf, "xh", axis=0, tiled=True)
+    place = lax.axis_index("z").astype(jnp.int32).reshape(1)
 
     g_send = pl.pallas_call(
         pack_grads_kernel,
@@ -150,10 +169,26 @@
         compiler_params=params(),
         name="pack_grads",
     )(mod, idx, grad_hidden, pre_gate, pre_up)
-    weights = lax.all_gather(pair_bf, "z", axis=0, tiled=True)
+    g_send, activations, shard = lax.optimization_barrier((g_send, activations, master))
     g_recv = lax.all_to_all(
         g_send.reshape(members, CAP, gpiece), EXP, split_axis=0, concat_axis=0, tiled=True
     )
+    own_bf = shard.astype(jnp.bfloat16)
+    came_bf = lax.ppermute(own_bf, "xh", swap_pairs(2))
+    pair_bf = jnp.where(
+        half == 0,
+        jnp.concatenate([own_bf, came_bf], axis=0),
+        jnp.concatenate([came_bf, own_bf], axis=0),
+    )
+    x_send = pl.pallas_call(
+        pack_rows_kernel,
+        out_shape=jax.ShapeDtypeStruct((EXPERTS, GROUP, CAP, piece), jnp.bfloat16),
+        in_specs=[VMEM] * 3,
+        out_specs=VMEM,
+        compiler_params=params(),
+        name="pack_rows",
+    )(mod, idx, activations)
+    g_recv, x_send, pair_bf = lax.optimization_barrier((g_recv, x_send, pair_bf))
     g_mine = g_recv.reshape(rows_total, gpiece)
     g_all = lax.all_gather(
         g_mine,
@@ -162,48 +197,51 @@
         tiled=False,
         axis_index_groups=[list(range(GROUP * e, GROUP * (e + 1))) for e in range(EXPERTS)],
     )
-    x_send = pl.pallas_call(
-        pack_rows_kernel,
-        out_shape=jax.ShapeDtypeStruct((EXPERTS, GROUP, CAP, piece), jnp.bfloat16),
-        in_specs=[VMEM] * 3,
-        out_specs=VMEM,
-        compiler_params=params(),
-        name="pack_rows",
-    )(mod, idx, activations)
     x_recv = lax.all_to_all(
         x_send.reshape(members, CAP, piece), EXP, split_axis=0, concat_axis=0, tiled=True
     )
     x_rows = x_recv.reshape(rows_total, piece)
-    g_all, weights, x_rows = lax.optimization_barrier((g_all, weights, x_rows))
+    shards = [pair_bf] + [
+        lax.ppermute(pair_bf, "z", [(i, (i + k) % RING) for i in range(RING)])
+        for k in range(1, RING)
+    ]
+    g_all, x_rows, *shards = lax.optimization_barrier((g_all, x_rows, *shards))
 
     grad_part = pl.pallas_call(
         weight_grad_kernel,
-        grid=(GROUP,),
         out_shape=jax.ShapeDtypeStruct((piece, 2 * hidden), jnp.bfloat16),
-        in_specs=[
-            pl.BlockSpec((rows_total, piece), lambda g: (0, 0)),
-            pl.BlockSpec((1, rows_total, gpiece), lambda g: (g, 0, 0)),
+        in_specs=[pl.BlockSpec(memory_space=pl.ANY)] * 2,
+        out_specs=VMEM,
+        scratch_shapes=[
+            pltpu.VMEM((rows_total, piece), jnp.bfloat16),
+            pltpu.VMEM((GROUP, rows_total, gpiece), jnp.bfloat16),
+            pltpu.VMEM((piece, rows_total), jnp.bfloat16),
+            pltpu.SemaphoreType.DMA((GROUP // 2 + 1,)),
         ],
-        out_specs=pl.BlockSpec((piece, gpiece), lambda g: (0, g)),
-        scratch_shapes=[pltpu.VMEM((piece, rows_total), jnp.bfloat16)],
         compiler_params=params(),
         name="weight_grad",
     )(x_rows, g_all)
     grad_z = lax.psum_scatter(grad_part, "z", scatter_dimension=0, tiled=True)
 
-    block = 256
+    grad_part, g_all, *shards = lax.optimization_barrier((grad_part, g_all, *shards))
+    block = 512
     dx_rows = pl.pallas_call(
         input_grad_kernel,
         grid=(rows_total // block,),
         out_shape=jax.ShapeDtypeStruct((rows_total, piece), jnp.bfloat16),
         in_specs=[
+            pl.BlockSpec(memory_space=pltpu.SMEM),
             pl.BlockSpec((GROUP, block, gpiece), lambda t: (0, t, 0)),
-            pl.BlockSpec((piece, 2 * hidden), lambda t: (0, 0)),
+        ]
+        + [pl.BlockSpec(memory_space=pl.ANY)] * RING,
+        out_specs=pl.BlockSpec((block, piece), lambda t: (t, 0)),
+        scratch_shapes=[
+            pltpu.VMEM((piece, 2 * hidden), jnp.bfloat16),
+            pltpu.SemaphoreType.DMA((RING,)),
         ],
-        out_specs=pl.BlockSpec((block, piece), lambda t: (t, 0)),
         compiler_params=params(),
         name="input_grad",
-    )(g_all, weights)
+    )(place, g_all, *shards)
     back = lax.all_to_all(
         dx_rows.reshape(members, CAP, piece), EXP, split_axis=0, concat_axis=0, tiled=True
     )

time: 201 us -> 192 us (0.955)
  blocking collectives: 89.5 us -> 0 us
  starting transfers between devices: 10.9 us -> 70.8 us
  waiting for transfers between devices: 53 us -> 74.3 us
  local copies, waits for them, and re-layouts: 2.17 us -> 4.96 us
  Pallas kernels: 26.9 us -> 24.5 us
    all_to_all x2 -> x0, blocking collectives: 82 us -> none  [the longest x1 49.8 us: body(): lax.all_to_all(x_send.reshape(members, CAP, piece), EXP, split_axis=0, co...]
    ppermute x0 -> x8, starting transfers between devices: none -> 45.7 us  [the longest x7 41.6 us: body(): lax.ppermute(pair_bf, 'z', [(i, (i + k) % RING) for i in range(RING)])]
    ppermute x0 -> x8, waiting for transfers between devices: none -> 29.1 us  [the longest x7 24 us: body(): lax.ppermute(pair_bf, 'z', [(i, (i + k) % RING) for i in range(RING)])]
    all_gather x1, waiting for transfers between devices: 18 us -> 0.01 us  [body(): lax.all_gather(g_mine, EXP, axis=0, tiled=False, axis_index_groups=[list(...]
    all_to_all x0 -> x2, starting transfers between devices: none -> 12.8 us  [the longest x1 8.71 us: body(): lax.all_to_all(g_send.reshape(members, CAP, gpiece), EXP, split_axis=0, c...]
    all_to_all x0 -> x2, waiting for transfers between devices: none -> 11 us  [the longest x1 11 us: body(): lax.all_to_all(g_send.reshape(members, CAP, gpiece), EXP, split_axis=0, c...]
    all_gather x1 -> x0, blocking collectives: 7.52 us -> none  [body(): pair_bf = lax.all_gather(shard_bf, 'xh', axis=0, tiled=True)]
    reduce_scatter x1, waiting for transfers between devices: 33.1 us -> 29 us  [body(): grad_z = lax.psum_scatter(grad_part, 'z', scatter_dimension=0, tiled=True)]
  transfers between devices with their start and end apart: 5 -> 14, of which waited for: 3 -> 9; matrix products, arithmetic and copies ran while one was open for 0% -> 1% of each run, Pallas kernels for 9% -> 8%
where the time goes in v5:
time: 192 us; the launch traced here: 190 us
  waiting for transfers between devices  74.3 us (39%)
  starting transfers between devices  70.8 us (37%)
  Pallas kernels  24.5 us (13%)
  between operations  14.3 us (7%)
  local copies, waits for them, and re-layouts  4.96 us (3%)
    ppermute x7, starting transfers between devices, body(): lax.ppermute(pair_bf, 'z', [(i, (i + k) % RING) for i in range(RING)])  41.6 us
    reduce_scatter x1, waiting for transfers between devices, body(): grad_z = lax.psum_scatter(grad_part, 'z', scatter_dimension=0, tiled=True)  29 us
    ppermute x7, waiting for transfers between devices, body(): lax.ppermute(pair_bf, 'z', [(i, (i + k) % RING) for i in range(RING)])  24 us
    all_to_all x1, waiting for transfers between devices, body(): lax.all_to_all(g_send.reshape(members, CAP, gpiece), EXP, split_axis=0, c...  11 us
    all_to_all x1, starting transfers between devices, body(): lax.all_to_all(g_send.reshape(members, CAP, gpiece), EXP, split_axis=0, c...  8.71 us
    pallas_call x1, Pallas kernels, body(): pl.pallas_call(input_grad_kernel, grid=(rows_total // block,), out_shape=...  8.49 us
    all_to_all x1, starting transfers between devices, body(): lax.all_to_all(dx_rows.reshape(members, CAP, piece), EXP, split_axis=0, c...  8.4 us
    pallas_call x1, Pallas kernels, body(): pl.pallas_call(weight_grad_kernel, out_shape=jax.ShapeDtypeStruct((piece,...  7.24 us
  transfers between devices with their start and end apart: 14, of which 9 were waited for; matrix products, arithmetic and copies ran while one was open for 1% of the time, Pallas kernels for 8%

profile of v5, /device:TPU:6, one launch (start us, length us, event | category | flops | bytes accessed | tf_op | source)
XLA Modules:
  0.0 189.9 jit_solution(9121230103908046655)
XLA Ops:
  7.2 0.0 copy-start.4
  7.2 2.6 %pack_grads.1 = bf16[4,8,48,256]{3,2,1,0:T(8,128)(2,1)} custom-call(s32[1,128]{1,0:T(1,128)} %bitcast.26, s32[1,128]{1,0:T(1,128)} %bitcast.29, bf16[128,1024]{1,0:T(8,128)(2,1)} %grad_ref.1, bf16[128,1024]{1,0:T(8,128)(2,1)} %gate_ref.1, bf16[128,1024]{1,0:T(8,128)(2,1)} %up_ref.1), custom_call_target="tpu_custom_call" | custom-call | tf_op jit(solution)/shard_map/pack_grads/pallas_call | solution.py:164
  9.8 8.7 %all-to-all-start = ((bf16[32,48,256]{2,1,0:T(8,128)(2,1)}), bf16[32,48,256]{2,1,0:T(8,128)(2,1)S(1)}, u32[]{:S(2)}, u32[]{:S(2)}) async-start(bf16[32,48,256]{2,1,0:T(8,128)(2,1)} %bitcast.23), calls=%async_computation | async-start | bytes 1572864 | tf_op jit(solution)/shard_map/all_to_all | solution.py:173
  18.5 0.0 all-gather.2.cloned.1.call-start
  18.6 0.0 copy-done.4
  18.6 4.1 %collective-permute-start = (bf16[32,2048]{1,0:T(8,128)(2,1)S(1)}, bf16[32,2048]{1,0:T(8,128)(2,1)S(1)}, u32[]{:S(2)}, u32[]{:S(2)}) collective-permute-start(bf16[32,2048]{1,0:T(8,128)(2,1)S(1)} %convert_element_type.12), channel_id=1, source_target_pairs={{0,32},{32,0},{1,33},{33,1},{2,34},{34,2},{3,35},{35,3},{4,36},{36... | collective-permute-start | bytes 393224 | tf_op jit(solution)/shard_map/ppermute | solution.py:177
  22.7 3.1 %pack_rows.1 = bf16[4,8,48,512]{3,2,1,0:T(8,128)(2,1)} custom-call(s32[1,128]{1,0:T(1,128)} %bitcast.27, s32[1,128]{1,0:T(1,128)} %bitcast.30, bf16[128,4096]{1,0:T(8,128)(2,1)} %x_ref), custom_call_target="tpu_custom_call" | custom-call | tf_op jit(solution)/shard_map/pack_rows/pallas_call | solution.py:183
  25.8 5.0 %collective-permute-done = bf16[32,2048]{1,0:T(8,128)(2,1)S(1)} collective-permute-done((bf16[32,2048]{1,0:T(8,128)(2,1)S(1)}, bf16[32,2048]{1,0:T(8,128)(2,1)S(1)}, u32[]{:S(2)}, u32[]{:S(2)}) %collective-permute-start) | collective-permute-done | bytes 131104 | tf_op jit(solution)/shard_map/ppermute | solution.py:177
  30.9 0.0 copy-start.3
  30.9 11.0 %all-to-all-done = bf16[32,48,256]{2,1,0:T(8,128)(2,1)S(1)} async-done(((bf16[32,48,256]{2,1,0:T(8,128)(2,1)}), bf16[32,48,256]{2,1,0:T(8,128)(2,1)S(1)}, u32[]{:S(2)}, u32[]{:S(2)}) %all-to-all-start) | async-done | bytes 786464 | tf_op jit(solution)/shard_map/all_to_all | solution.py:173
  41.8 0.0 copy-start.2
  41.8 0.9 copy-done.2
  42.7 0.0 all-gather.2.cloned.1.call-update
  42.7 4.0 %all-to-all-start.1 = ((bf16[32,48,512]{2,1,0:T(8,128)(2,1)}), bf16[32,48,512]{2,1,0:T(8,128)(2,1)S(1)}, u32[]{:S(2)}, u32[]{:S(2)}) async-start(bf16[32,48,512]{2,1,0:T(8,128)(2,1)} %bitcast.18), calls=%async_computation.1 | async-start | bytes 3145728 | tf_op jit(solution)/shard_map/all_to_all | solution.py:200
  46.8 0.0 reduce-scatter.2.cloned.1.call-start
  46.8 4.3 %collective-permute-start.1 = (bf16[64,2048]{1,0:T(8,128)(2,1)S(1)}, bf16[64,2048]{1,0:T(8,128)(2,1)S(1)}, u32[]{:S(2)}, u32[]{:S(2)}) collective-permute-start(bf16[64,2048]{1,0:T(8,128)(2,1)S(1)} %maximum_select_fusion.rest_0_), channel_id=1, source_target_pairs={{0,64},{64,128},{128,192},{192,256},{256,320},{320,384},{384,448},... | collective-permute-start | bytes 786440 | tf_op jit(solution)/shard_map/ppermute | solution.py:205
  51.1 6.1 %collective-permute-start.2 = (bf16[64,2048]{1,0:T(8,128)(2,1)S(1)}, bf16[64,2048]{1,0:T(8,128)(2,1)S(1)}, u32[]{:S(2)}, u32[]{:S(2)}) collective-permute-start(bf16[64,2048]{1,0:T(8,128)(2,1)S(1)} %maximum_select_fusion.rest_0_), channel_id=1, source_target_pairs={{0,128},{64,192},{128,256},{192,320},{256,384},{320,448},{384,0},{... | collective-permute-start | bytes 786440 | tf_op jit(solution)/shard_map/ppermute | solution.py:205
  57.2 7.3 %collective-permute-start.3 = (bf16[64,2048]{1,0:T(8,128)(2,1)S(1)}, bf16[64,2048]{1,0:T(8,128)(2,1)S(1)}, u32[]{:S(2)}, u32[]{:S(2)}) collective-permute-start(bf16[64,2048]{1,0:T(8,128)(2,1)S(1)} %maximum_select_fusion.rest_0_), channel_id=1, source_target_pairs={{0,192},{64,256},{128,320},{192,384},{256,448},{320,0},{384,64},{4... | collective-permute-start | bytes 786440 | tf_op jit(solution)/shard_map/ppermute | solution.py:205
  64.6 2.8 %collective-permute-start.4 = (bf16[64,2048]{1,0:T(8,128)(2,1)S(1)}, bf16[64,2048]{1,0:T(8,128)(2,1)S(1)}, u32[]{:S(2)}, u32[]{:S(2)}) collective-permute-start(bf16[64,2048]{1,0:T(8,128)(2,1)S(1)} %maximum_select_fusion.rest_0_), channel_id=1, source_target_pairs={{0,256},{64,320},{128,384},{192,448},{256,0},{320,64},{384,128},{4... | collective-permute-start | bytes 786440 | tf_op jit(solution)/shard_map/ppermute | solution.py:205
  67.4 6.9 %collective-permute-start.5 = (bf16[64,2048]{1,0:T(8,128)(2,1)S(1)}, bf16[64,2048]{1,0:T(8,128)(2,1)S(1)}, u32[]{:S(2)}, u32[]{:S(2)}) collective-permute-start(bf16[64,2048]{1,0:T(8,128)(2,1)S(1)} %maximum_select_fusion.rest_0_), channel_id=1, source_target_pairs={{0,320},{64,384},{128,448},{192,0},{256,64},{320,128},{384,192},{4... | collective-permute-start | bytes 786440 | tf_op jit(solution)/shard_map/ppermute | solution.py:205
  74.3 0.0 collective-permute-done.1.rest_1_
  74.3 0.0 copy-start.5
  74.4 3.7 %collective-permute-start.6 = (bf16[64,2048]{1,0:T(8,128)(2,1)S(1)}, bf16[64,2048]{1,0:T(8,128)(2,1)S(1)}, u32[]{:S(2)}, u32[]{:S(2)}) collective-permute-start(bf16[64,2048]{1,0:T(8,128)(2,1)S(1)} %maximum_select_fusion.rest_0_), channel_id=1, source_target_pairs={{0,384},{64,448},{128,0},{192,64},{256,128},{320,192},{384,256},{4... | collective-permute-start | bytes 786440 | tf_op jit(solution)/shard_map/ppermute | solution.py:205
  78.0 0.1 collective-permute-done.2.rest_2_
  78.1 0.0 copy-start.6
  78.1 10.5 %collective-permute-start.7 = (bf16[64,2048]{1,0:T(8,128)(2,1)S(1)}, bf16[64,2048]{1,0:T(8,128)(2,1)}, u32[]{:S(2)}, u32[]{:S(2)}) collective-permute-start(bf16[64,2048]{1,0:T(8,128)(2,1)S(1)} %maximum_select_fusion.rest_0_), channel_id=1, source_target_pairs={{0,448},{64,0},{128,64},{192,128},{256,192},{320,256},{384,320},{4... | collective-permute-start | bytes 786440 | tf_op jit(solution)/shard_map/ppermute | solution.py:205
  88.6 9.0 %collective-permute-done.3.rest_3_ = bf16[64,2048]{1,0:T(8,128)(2,1)S(1)} collective-permute-done((bf16[64,2048]{1,0:T(8,128)(2,1)S(1)}, bf16[64,2048]{1,0:T(8,128)(2,1)S(1)}, u32[]{:S(2)}, u32[]{:S(2)}) %collective-permute-start.3) | collective-permute-done | bytes 262176 | tf_op jit(solution)/shard_map/ppermute | solution.py:205
  97.7 0.0 copy-start.7
  97.7 0.0 collective-permute-done.4.rest_4_
  97.7 0.0 copy-start.8
  97.7 1.7 collective-permute-done.5.rest_5_
  99.3 0.0 copy-start.9
  99.3 10.9 %collective-permute-done.6.rest_6_ = bf16[64,2048]{1,0:T(8,128)(2,1)S(1)} collective-permute-done((bf16[64,2048]{1,0:T(8,128)(2,1)S(1)}, bf16[64,2048]{1,0:T(8,128)(2,1)S(1)}, u32[]{:S(2)}, u32[]{:S(2)}) %collective-permute-start.6) | collective-permute-done | bytes 262176 | tf_op jit(solution)/shard_map/ppermute | solution.py:205
  110.3 0.0 copy-start.10
  110.3 0.7 copy-done.10
  111.0 2.3 %collective-permute-done.7.rest_7_ = bf16[64,2048]{1,0:T(8,128)(2,1)} collective-permute-done((bf16[64,2048]{1,0:T(8,128)(2,1)S(1)}, bf16[64,2048]{1,0:T(8,128)(2,1)}, u32[]{:S(2)}, u32[]{:S(2)}) %collective-permute-start.7) | collective-permute-done | bytes 262176 | tf_op jit(solution)/shard_map/ppermute | solution.py:205
  113.2 0.0 all-to-all-done.1
  113.2 0.0 copy-start
  113.2 0.0 all-gather.2.cloned.1.call-done.g_ref
  113.2 1.2 copy-done
  114.4 7.2 %weight_grad.1 = bf16[512,2048]{1,0:T(8,128)(2,1)} custom-call(bf16[1536,512]{1,0:T(8,128)(2,1)} %bitcast.19, bf16[8,1536,256]{2,1,0:T(8,128)(2,1)} %all-gather.2.cloned.1.call-done.g_ref), custom_call_target="tpu_custom_call" | custom-call | tf_op jit(solution)/shard_map/weight_grad/pallas_call | solution.py:210
  121.7 0.0 copy-done.3
  121.7 0.0 copy-done.5
  121.7 0.0 copy-done.6
  121.7 0.0 copy-done.7
  121.7 0.0 copy-done.8
  121.7 0.0 copy-done.9
  121.7 0.0 reduce-scatter.2.cloned.1.call-update
  121.7 8.5 %input_grad.1 = bf16[1536,512]{1,0:T(8,128)(2,1)} custom-call(s32[1]{0:T(128)} %bitcast.2.z_ref, bf16[8,1536,256]{2,1,0:T(8,128)(2,1)} %all-gather.2.cloned.1.call-done.g_ref, bf16[64,2048]{1,0:T(8,128)(2,1)} %copy-done.3, bf16[64,2048]{1,0:T(8,128)(2,1)} %copy-done.5, bf16[64,2048]{1,0:T(8,128)(2,1)} %copy-done.6, bf16[64,2048]{1,0:T(8,128)(2,1)} %copy-done.7, ...), custom_call_target="tpu_custom_call" | custom-call | tf_op jit(solution)/shard_map/input_grad/pallas_call | solution.py:228
  130.2 8.4 %all-to-all-start.2 = ((bf16[32,48,512]{2,1,0:T(8,128)(2,1)}), bf16[32,48,512]{2,1,0:T(8,128)(2,1)S(1)}, u32[]{:S(2)}, u32[]{:S(2)}) async-start(bf16[32,48,512]{2,1,0:T(8,128)(2,1)} %bitcast.20), calls=%async_computation.2 | async-start | bytes 3145728 | tf_op jit(solution)/shard_map/all_to_all | solution.py:245
  138.6 0.0 copy-start.11
  138.7 0.0 copy-start.12
  138.7 29.0 %reduce-scatter.2.cloned.1.call-done = bf16[64,2048]{1,0:T(8,128)(2,1)} async-done(((bf16[512,2048]{1,0:T(8,128)(2,1)}), bf16[64,2048]{1,0:T(8,128)(2,1)}) %reduce-scatter.2.cloned.1.call-update) | async-done | bytes 262160 | tf_op jit(solution)/shard_map/reduce_scatter | solution.py:224
  167.7 0.0 copy-start.13
  167.7 1.0 dynamic-slice_bitcast_fusion
  168.7 3.9 %collective-permute-start.8 = (bf16[32,2048]{1,0:T(8,128)(2,1)S(1)}, bf16[32,2048]{1,0:T(8,128)(2,1)S(1)}, u32[]{:S(2)}, u32[]{:S(2)}) collective-permute-start(bf16[32,2048]{1,0:T(8,128)(2,1)S(1)} %dynamic-slice_bitcast_fusion), channel_id=1, source_target_pairs={{0,32},{32,0},{1,33},{33,1},{2,34},{34,2},{3,35},{35,3},{4,36},{36... | collective-permute-start | bytes 393224 | tf_op jit(solution)/shard_map/ppermute | solution.py:261
  172.6 5.3 %all-to-all-done.2 = bf16[32,48,512]{2,1,0:T(8,128)(2,1)S(1)} async-done(((bf16[32,48,512]{2,1,0:T(8,128)(2,1)}), bf16[32,48,512]{2,1,0:T(8,128)(2,1)S(1)}, u32[]{:S(2)}, u32[]{:S(2)}) %all-to-all-start.2) | async-done | bytes 1572896 | tf_op jit(solution)/shard_map/all_to_all | solution.py:245
  177.9 1.2 copy-done.1
  179.0 3.1 %combine.1 = bf16[128,4096]{1,0:T(8,128)(2,1)} custom-call(s32[1,128]{1,0:T(1,128)} %bitcast.28, s32[1,128]{1,0:T(1,128)} %bitcast.31, bf16[4,8,48,512]{3,2,1,0:T(8,128)(2,1)} %bitcast.21), custom_call_target="tpu_custom_call" | custom-call | tf_op jit(solution)/shard_map/combine/pallas_call | solution.py:248
  182.1 0.0 collective-permute-done.8
  182.1 0.0 copy-done.11
  182.1 0.0 copy-done.12
  182.1 0.0 copy-done.13
  182.1 1.0 multiply_subtract_fusion
  (3 shorter events, 0.1 us)
Async XLA Ops:
  7.2 11.4 %copy-start.4 = (f32[32,2048]{1,0:T(8,128)S(1)}, f32[32,2048]{1,0:T(8,128)}, u32[]{:S(2)}) copy-start(f32[32,2048]{1,0:T(8,128)} %param.15) | copy-start | bytes 786436
  9.8 32.0 %all-to-all-start = ((bf16[32,48,256]{2,1,0:T(8,128)(2,1)}), bf16[32,48,256]{2,1,0:T(8,128)(2,1)S(1)}, u32[]{:S(2)}, u32[]{:S(2)}) async-start(bf16[32,48,256]{2,1,0:T(8,128)(2,1)} %bitcast.23), calls=%async_computation | async-start | bytes 1572864 | tf_op jit(solution)/shard_map/all_to_all | solution.py:173
  18.5 94.7 %all-gather.2.cloned.1.call-start = ((), (), s32[]{:S(2)}) async-start(), calls=%async_computation.4 | async-start | bytes 7077888 | tf_op jit(solution)/shard_map/all_gather | solution.py:193
  18.6 12.2 %collective-permute-start = (bf16[32,2048]{1,0:T(8,128)(2,1)S(1)}, bf16[32,2048]{1,0:T(8,128)(2,1)S(1)}, u32[]{:S(2)}, u32[]{:S(2)}) collective-permute-start(bf16[32,2048]{1,0:T(8,128)(2,1)S(1)} %convert_element_type.12), channel_id=1, source_target_pairs={{0,32},{32,0},{1,33},{33,1},{2,34},{34,2},{3,35},{35,3},{4,36},{36... | collective-permute-start | bytes 393224 | tf_op jit(solution)/shard_map/ppermute | solution.py:177
  30.9 90.8 %copy-start.3 = (bf16[64,2048]{1,0:T(8,128)(2,1)}, bf16[64,2048]{1,0:T(8,128)(2,1)S(1)}, u32[]{:S(2)}) copy-start(bf16[64,2048]{1,0:T(8,128)(2,1)S(1)} %maximum_select_fusion.rest_0_) | copy-start | bytes 786436
  41.8 0.9 copy-start.2
  42.7 70.5 %all-to-all-start.1 = ((bf16[32,48,512]{2,1,0:T(8,128)(2,1)}), bf16[32,48,512]{2,1,0:T(8,128)(2,1)S(1)}, u32[]{:S(2)}, u32[]{:S(2)}) async-start(bf16[32,48,512]{2,1,0:T(8,128)(2,1)} %bitcast.18), calls=%async_computation.1 | async-start | bytes 3145728 | tf_op jit(solution)/shard_map/all_to_all | solution.py:200
  46.8 120.9 %reduce-scatter.2.cloned.1.call-start = ((), (), s32[]{:S(2)}) async-start(), calls=%async_computation.5 | async-start | bytes 2359296 | tf_op jit(solution)/shard_map/reduce_scatter | solution.py:224
  46.8 27.5 %collective-permute-start.1 = (bf16[64,2048]{1,0:T(8,128)(2,1)S(1)}, bf16[64,2048]{1,0:T(8,128)(2,1)S(1)}, u32[]{:S(2)}, u32[]{:S(2)}) collective-permute-start(bf16[64,2048]{1,0:T(8,128)(2,1)S(1)} %maximum_select_fusion.rest_0_), channel_id=1, source_target_pairs={{0,64},{64,128},{128,192},{192,256},{256,320},{320,384},{384,448},... | collective-permute-start | bytes 786440 | tf_op jit(solution)/shard_map/ppermute | solution.py:205
  51.1 27.0 %collective-permute-start.2 = (bf16[64,2048]{1,0:T(8,128)(2,1)S(1)}, bf16[64,2048]{1,0:T(8,128)(2,1)S(1)}, u32[]{:S(2)}, u32[]{:S(2)}) collective-permute-start(bf16[64,2048]{1,0:T(8,128)(2,1)S(1)} %maximum_select_fusion.rest_0_), channel_id=1, source_target_pairs={{0,128},{64,192},{128,256},{192,320},{256,384},{320,448},{384,0},{... | collective-permute-start | bytes 786440 | tf_op jit(solution)/shard_map/ppermute | solution.py:205
  57.2 40.4 %collective-permute-start.3 = (bf16[64,2048]{1,0:T(8,128)(2,1)S(1)}, bf16[64,2048]{1,0:T(8,128)(2,1)S(1)}, u32[]{:S(2)}, u32[]{:S(2)}) collective-permute-start(bf16[64,2048]{1,0:T(8,128)(2,1)S(1)} %maximum_select_fusion.rest_0_), channel_id=1, source_target_pairs={{0,192},{64,256},{128,320},{192,384},{256,448},{320,0},{384,64},{4... | collective-permute-start | bytes 786440 | tf_op jit(solution)/shard_map/ppermute | solution.py:205
  64.6 33.1 %collective-permute-start.4 = (bf16[64,2048]{1,0:T(8,128)(2,1)S(1)}, bf16[64,2048]{1,0:T(8,128)(2,1)S(1)}, u32[]{:S(2)}, u32[]{:S(2)}) collective-permute-start(bf16[64,2048]{1,0:T(8,128)(2,1)S(1)} %maximum_select_fusion.rest_0_), channel_id=1, source_target_pairs={{0,256},{64,320},{128,384},{192,448},{256,0},{320,64},{384,128},{4... | collective-permute-start | bytes 786440 | tf_op jit(solution)/shard_map/ppermute | solution.py:205
  67.4 31.9 %collective-permute-start.5 = (bf16[64,2048]{1,0:T(8,128)(2,1)S(1)}, bf16[64,2048]{1,0:T(8,128)(2,1)S(1)}, u32[]{:S(2)}, u32[]{:S(2)}) collective-permute-start(bf16[64,2048]{1,0:T(8,128)(2,1)S(1)} %maximum_select_fusion.rest_0_), channel_id=1, source_target_pairs={{0,320},{64,384},{128,448},{192,0},{256,64},{320,128},{384,192},{4... | collective-permute-start | bytes 786440 | tf_op jit(solution)/shard_map/ppermute | solution.py:205
  74.3 47.3 %copy-start.5 = (bf16[64,2048]{1,0:T(8,128)(2,1)}, bf16[64,2048]{1,0:T(8,128)(2,1)S(1)}, u32[]{:S(2)}) copy-start(bf16[64,2048]{1,0:T(8,128)(2,1)S(1)} %collective-permute-done.1.rest_1_) | copy-start | bytes 786436
  74.4 35.9 %collective-permute-start.6 = (bf16[64,2048]{1,0:T(8,128)(2,1)S(1)}, bf16[64,2048]{1,0:T(8,128)(2,1)S(1)}, u32[]{:S(2)}, u32[]{:S(2)}) collective-permute-start(bf16[64,2048]{1,0:T(8,128)(2,1)S(1)} %maximum_select_fusion.rest_0_), channel_id=1, source_target_pairs={{0,384},{64,448},{128,0},{192,64},{256,128},{320,192},{384,256},{4... | collective-permute-start | bytes 786440 | tf_op jit(solution)/shard_map/ppermute | solution.py:205
  78.1 43.5 %copy-start.6 = (bf16[64,2048]{1,0:T(8,128)(2,1)}, bf16[64,2048]{1,0:T(8,128)(2,1)S(1)}, u32[]{:S(2)}) copy-start(bf16[64,2048]{1,0:T(8,128)(2,1)S(1)} %collective-permute-done.2.rest_2_) | copy-start | bytes 786436
  78.1 35.1 %collective-permute-start.7 = (bf16[64,2048]{1,0:T(8,128)(2,1)S(1)}, bf16[64,2048]{1,0:T(8,128)(2,1)}, u32[]{:S(2)}, u32[]{:S(2)}) collective-permute-start(bf16[64,2048]{1,0:T(8,128)(2,1)S(1)} %maximum_select_fusion.rest_0_), channel_id=1, source_target_pairs={{0,448},{64,0},{128,64},{192,128},{256,192},{320,256},{384,320},{4... | collective-permute-start | bytes 786440 | tf_op jit(solution)/shard_map/ppermute | solution.py:205
  97.7 24.0 %copy-start.7 = (bf16[64,2048]{1,0:T(8,128)(2,1)}, bf16[64,2048]{1,0:T(8,128)(2,1)S(1)}, u32[]{:S(2)}) copy-start(bf16[64,2048]{1,0:T(8,128)(2,1)S(1)} %collective-permute-done.3.rest_3_) | copy-start | bytes 786436
  97.7 24.0 %copy-start.8 = (bf16[64,2048]{1,0:T(8,128)(2,1)}, bf16[64,2048]{1,0:T(8,128)(2,1)S(1)}, u32[]{:S(2)}) copy-start(bf16[64,2048]{1,0:T(8,128)(2,1)S(1)} %collective-permute-done.4.rest_4_) | copy-start | bytes 786436
  99.3 22.4 %copy-start.9 = (bf16[64,2048]{1,0:T(8,128)(2,1)}, bf16[64,2048]{1,0:T(8,128)(2,1)S(1)}, u32[]{:S(2)}) copy-start(bf16[64,2048]{1,0:T(8,128)(2,1)S(1)} %collective-permute-done.5.rest_5_) | copy-start | bytes 786436
  110.3 0.7 copy-start.10
  113.2 1.2 copy-start
  130.2 47.6 %all-to-all-start.2 = ((bf16[32,48,512]{2,1,0:T(8,128)(2,1)}), bf16[32,48,512]{2,1,0:T(8,128)(2,1)S(1)}, u32[]{:S(2)}, u32[]{:S(2)}) async-start(bf16[32,48,512]{2,1,0:T(8,128)(2,1)} %bitcast.20), calls=%async_computation.2 | async-start | bytes 3145728 | tf_op jit(solution)/shard_map/all_to_all | solution.py:245
  138.6 43.4 %copy-start.11 = (f32[32,2048]{1,0:T(8,128)S(1)}, f32[32,2048]{1,0:T(8,128)}, u32[]{:S(2)}) copy-start(f32[32,2048]{1,0:T(8,128)} %param.17) | copy-start | bytes 786436
  138.7 43.4 %copy-start.12 = (f32[32,2048]{1,0:T(8,128)S(1)}, f32[32,2048]{1,0:T(8,128)}, u32[]{:S(2)}) copy-start(f32[32,2048]{1,0:T(8,128)} %param.16) | copy-start | bytes 786436
  167.7 14.4 %copy-start.13 = (bf16[64,2048]{1,0:T(8,128)(2,1)S(1)}, bf16[64,2048]{1,0:T(8,128)(2,1)}, u32[]{:S(2)}) copy-start(bf16[64,2048]{1,0:T(8,128)(2,1)} %reduce-scatter.2.cloned.1.call-done) | copy-start | bytes 786436
  168.7 13.4 %collective-permute-start.8 = (bf16[32,2048]{1,0:T(8,128)(2,1)S(1)}, bf16[32,2048]{1,0:T(8,128)(2,1)S(1)}, u32[]{:S(2)}, u32[]{:S(2)}) collective-permute-start(bf16[32,2048]{1,0:T(8,128)(2,1)S(1)} %dynamic-slice_bitcast_fusion), channel_id=1, source_target_pairs={{0,32},{32,0},{1,33},{33,1},{2,34},{34,2},{3,35},{35,3},{4,36},{36... | collective-permute-start | bytes 393224 | tf_op jit(solution)/shard_map/ppermute | solution.py:261
  177.8 1.2 copy-start.1
Sparse Core Ops, SparseCore 0:
  42.9 67.0 all-gather.1
  121.9 45.7 reduce-scatter.1

commit v6 on v5

--- a/solution.py
+++ b/solution.py
@@ -9,6 +9,8 @@
 CAP = 48
 GROUP = 8
 RING = 8
+DX_BLOCKS = 3
+EARLY = (3, 4)
 
 beta_one = 0.9
 beta_two = 0.999
@@ -91,48 +93,52 @@
         out_ref[:, g * piece : (g + 1) * piece] = total.astype(jnp.bfloat16)
 
 
-def weight_grad_kernel(x_ref, g_ref, out_ref, x_buf, g_buf, xt_buf, sems):
+def both_grads_kernel(z_ref, x_ref, g_ref, *rest):
+    shards, rest = rest[:RING], rest[RING:]
+    dw_ref, dx_ref, g_buf, w_buf, xt_buf, dw_buf, dx_buf, g_sems, w_sems, out_sems = rest
     pairs = GROUP // 2
-    x_copy = pltpu.make_async_copy(x_ref, x_buf, sems.at[pairs])
-    copies = [
-        pltpu.make_async_copy(g_ref.at[pl.ds(2 * j, 2)], g_buf.at[pl.ds(2 * j, 2)], sems.at[j])
+    loads = [
+        pltpu.make_async_copy(g_ref.at[pl.ds(2 * j, 2)], g_buf.at[pl.ds(2 * j, 2)], g_sems.at[j])
         for j in range(pairs)
     ]
-    x_copy.start()
-    for copy in copies:
-        copy.start()
-    x_copy.wait()
-    xt_buf[...] = x_buf[...].T
+    rows = shards[0].shape[0]
+    w_loads = []
+    for k in range(RING):
+        at = pl.multiple_of(lax.rem(z_ref[0] + RING - k, RING) * rows, rows)
+        w_loads.append(
+            pltpu.make_async_copy(shards[k], w_buf.at[pl.ds(at, rows)], w_sems.at[k])
+        )
+    for load in loads + w_loads:
+        load.start()
+    xt_buf[...] = x_ref[...].T
+    stores = []
     piece = g_buf.shape[2]
     for j in range(pairs):
-        copies[j].wait()
-        both = jnp.concatenate([g_buf[2 * j], g_buf[2 * j + 1]], axis=1)
-        out_ref[:, 2 * j * piece : (2 * j + 2) * piece] = jnp.dot(
-            xt_buf[...], both, preferred_element_type=jnp.float32
+        loads[j].wait()
+        pair = jnp.concatenate([g_buf[2 * j], g_buf[2 * j + 1]], axis=1)
+        cols = slice(2 * j * piece, (2 * j + 2) * piece)
+        dw_buf[:, cols] = jnp.dot(
+            xt_buf[...], pair, preferred_element_type=jnp.float32
         ).astype(jnp.bfloat16)
-
-
-def input_grad_kernel(z_ref, g_ref, *rest):
-    shards, (out_ref, w_buf, sems) = rest[:RING], rest[RING:]
-    rows = shards[0].shape[0]
-
-    @pl.when(pl.program_id(0) == 0)
-    def _():
-        copies = []
-        for k in range(RING):
-            at = pl.multiple_of(lax.rem(z_ref[0] + RING - k, RING) * rows, rows)
-            copies.append(
-                pltpu.make_async_copy(shards[k], w_buf.at[pl.ds(at, rows)], sems.at[k])
-            )
-        for copy in copies:
-            copy.start()
-        for copy in copies:
-            copy.wait()
-
-    grads = jnp.concatenate([g_ref[g] for g in range(GROUP)], axis=1)
-    out_ref[...] = lax.dot_general(
-        grads, w_buf[...], (((1,), (1,)), ((), ())), preferred_element_type=jnp.float32
-    ).astype(jnp.bfloat16)
+        stores.append(
+            pltpu.make_async_copy(dw_buf.at[:, cols], dw_ref.at[:, cols], out_sems.at[j])
+        )
+        stores[-1].start()
+    for load in w_loads:
+        load.wait()
+    block = dx_buf.shape[0] // DX_BLOCKS
+    for j in range(DX_BLOCKS):
+        part = slice(j * block, (j + 1) * block)
+        grads = jnp.concatenate([g_buf[g, part] for g in range(GROUP)], axis=1)
+        dx_buf[part] = lax.dot_general(
+            grads, w_buf[...], (((1,), (1,)), ((), ())), preferred_element_type=jnp.float32
+        ).astype(jnp.bfloat16)
+        stores.append(
+            pltpu.make_async_copy(dx_buf.at[part], dx_ref.at[part], out_sems.at[pairs + j])
+        )
+        stores[-1].start()
+    for store in stores:
+        store.wait()
 
 
 def swap_pairs(count):
@@ -188,7 +194,7 @@
         compiler_params=params(),
         name="pack_rows",
     )(mod, idx, activations)
-    g_recv, x_send, pair_bf = lax.optimization_barrier((g_recv, x_send, pair_bf))
+    g_recv, x_send, pair_late = lax.optimization_barrier((g_recv, x_send, pair_bf))
     g_mine = g_recv.reshape(rows_total, gpiece)
     g_all = lax.all_gather(
         g_mine,
@@ -201,47 +207,36 @@
         x_send.reshape(members, CAP, piece), EXP, split_axis=0, concat_axis=0, tiled=True
     )
     x_rows = x_recv.reshape(rows_total, piece)
-    shards = [pair_bf] + [
-        lax.ppermute(pair_bf, "z", [(i, (i + k) % RING) for i in range(RING)])
-        for k in range(1, RING)
-    ]
+    shards = [pair_bf]
+    for k in range(1, RING):
+        moved = pair_bf if k in EARLY else pair_late
+        shards.append(lax.ppermute(moved, "z", [(i, (i + k) % RING) for i in range(RING)]))
     g_all, x_rows, *shards = lax.optimization_barrier((g_all, x_rows, *shards))
 
-    grad_part = pl.pallas_call(
-        weight_grad_kernel,
-        out_shape=jax.ShapeDtypeStruct((piece, 2 * hidden), jnp.bfloat16),
-        in_specs=[pl.BlockSpec(memory_space=pl.ANY)] * 2,
-        out_specs=VMEM,
+    anywhere = pl.BlockSpec(memory_space=pl.ANY)
+    grad_part, dx_rows = pl.pallas_call(
+        both_grads_kernel,
+        out_shape=(
+            jax.ShapeDtypeStruct((piece, 2 * hidden), jnp.bfloat16),
+            jax.ShapeDtypeStruct((rows_total, piece), jnp.bfloat16),
+        ),
+        in_specs=[pl.BlockSpec(memory_space=pltpu.SMEM), VMEM] + [anywhere] * (RING + 1),
+        out_specs=(anywhere, anywhere),
         scratch_shapes=[
+            pltpu.VMEM((GROUP, rows_total, gpiece), jnp.bfloat16),
+            pltpu.VMEM((piece, 2 * hidden), jnp.bfloat16),
+            pltpu.VMEM((piece, rows_total), jnp.bfloat16),
+            pltpu.VMEM((piece, 2 * hidden), jnp.bfloat16),
             pltpu.VMEM((rows_total, piece), jnp.bfloat16),
-            pltpu.VMEM((GROUP, rows_total, gpiece), jnp.bfloat16),
-            pltpu.VMEM((piece, rows_total), jnp.bfloat16),
-            pltpu.SemaphoreType.DMA((GROUP // 2 + 1,)),
+            pltpu.SemaphoreType.DMA((GROUP // 2,)),
+            pltpu.SemaphoreType.DMA((RING,)),
+            pltpu.SemaphoreType.DMA((GROUP // 2 + DX_BLOCKS,)),
         ],
         compiler_params=params(),
-        name="weight_grad",
-    )(x_rows, g_all)
+        name="both_grads",
+    )(place, pltpu.with_memory_space_constraint(x_rows, pltpu.VMEM), g_all, *shards)
     grad_z = lax.psum_scatter(grad_part, "z", scatter_dimension=0, tiled=True)
 
-    grad_part, g_all, *shards = lax.optimization_barrier((grad_part, g_all, *shards))
-    block = 512
-    dx_rows = pl.pallas_call(
-        input_grad_kernel,
-        grid=(rows_total // block,),
-        out_shape=jax.ShapeDtypeStruct((rows_total, piece), jnp.bfloat16),
-        in_specs=[
-            pl.BlockSpec(memory_space=pltpu.SMEM),
-            pl.BlockSpec((GROUP, block, gpiece), lambda t: (0, t, 0)),
-        ]
-        + [pl.BlockSpec(memory_space=pl.ANY)] * RING,
-        out_specs=pl.BlockSpec((block, piece), lambda t: (t, 0)),
-        scratch_shapes=[
-            pltpu.VMEM((piece, 2 * hidden), jnp.bfloat16),
-            pltpu.SemaphoreType.DMA((RING,)),
-        ],
-        compiler_params=params(),
-        name="input_grad",
-    )(place, g_all, *shards)
     back = lax.all_to_all(
         dx_rows.reshape(members, CAP, piece), EXP, split_axis=0, concat_axis=0, tiled=True
     )
@@ -252,7 +247,13 @@
         out_specs=VMEM,
         compiler_params=params(),
         name="combine",
-    )(mod, idx, back.reshape(EXPERTS, GROUP, CAP, piece))
+    )(
+        mod,
+        idx,
+        pltpu.with_memory_space_constraint(
+            back.reshape(EXPERTS, GROUP, CAP, piece), pltpu.VMEM
+        ),
+    )
 
     keep_rows = master.shape[0]
     halves = grad_z.reshape(2, keep_rows, 2 * hidden)

time: 192 us -> 187 us (0.974)
  Pallas kernels: 24.5 us -> 18.1 us
  starting transfers between devices: 70.8 us -> 76.6 us
  local copies, waits for them, and re-layouts: 4.96 us -> 1.91 us
    reduce_scatter x1, waiting for transfers between devices: 29 us -> 41.5 us  [body(): grad_z = lax.psum_scatter(grad_part, 'z', scatter_dimension=0, tiled=True)]
    ppermute x7, waiting for transfers between devices: 24 us -> 13 us  [body(): lax.ppermute(moved, 'z', [(i, (i + k) % RING) for i in range(RING)])]
    ppermute x7, starting transfers between devices: 41.6 us -> 48.7 us  [body(): lax.ppermute(moved, 'z', [(i, (i + k) % RING) for i in range(RING)])]
    pallas_call x2 -> x1, Pallas kernels: 15.7 us -> 10.1 us  [body(): pl.pallas_call(both_grads_kernel, out_shape=(jax.ShapeDtypeStruct((piece,...]
    all_to_all x1, waiting for transfers between devices: 5.26 us -> 0.01 us  [body(): lax.all_to_all(dx_rows.reshape(members, CAP, piece), EXP, split_axis=0, c...]
    unnamed x28 -> x22, local copies, waits for them, and re-layouts: 3.98 us -> 0.93 us
    ppermute x1, waiting for transfers between devices: 0.01 us -> 2.62 us  [body(): came = lax.ppermute(other, 'xh', swap_pairs(2))]
  transfers between devices with their start and end apart: 14 -> 14, of which waited for: 9 -> 9; matrix products, arithmetic and copies ran while one was open for 1% -> 1% of each run, Pallas kernels for 8% -> 3%
where the time goes in v6:
time: 187 us; the launch traced here: 186 us
  starting transfers between devices  76.6 us (41%)
  waiting for transfers between devices  74.5 us (40%)
  Pallas kernels  18.1 us (10%)
  between operations  14.3 us (8%)
  local copies, waits for them, and re-layouts  1.91 us (1%)
    ppermute x7, starting transfers between devices, body(): lax.ppermute(moved, 'z', [(i, (i + k) % RING) for i in range(RING)])  48.7 us
    reduce_scatter x1, waiting for transfers between devices, body(): grad_z = lax.psum_scatter(grad_part, 'z', scatter_dimension=0, tiled=True)  41.5 us
    ppermute x7, waiting for transfers between devices, body(): lax.ppermute(moved, 'z', [(i, (i + k) % RING) for i in range(RING)])  13 us
    all_to_all x1, waiting for transfers between devices, body(): lax.all_to_all(g_send.reshape(members, CAP, gpiece), EXP, split_axis=0, c...  11 us
    pallas_call x1, Pallas kernels, body(): pl.pallas_call(both_grads_kernel, out_shape=(jax.ShapeDtypeStruct((piece,...  10.1 us
    all_to_all x1, starting transfers between devices, body(): lax.all_to_all(g_send.reshape(members, CAP, gpiece), EXP, split_axis=0, c...  8.71 us
    all_to_all x1, starting transfers between devices, body(): lax.all_to_all(dx_rows.reshape(members, CAP, piece), EXP, split_axis=0, c...  7.56 us
    ppermute x1, waiting for transfers between devices, body(): came_bf = lax.ppermute(own_bf, 'xh', swap_pairs(2))  5.04 us
  transfers between devices with their start and end apart: 14, of which 9 were waited for; matrix products, arithmetic and copies ran while one was open for 1% of the time, Pallas kernels for 3%

profile of v6, /device:TPU:6, one launch (start us, length us, event | category | flops | bytes accessed | tf_op | source)
XLA Modules:
  0.0 186.5 jit_solution(18375100621482159801)
XLA Ops:
  7.2 0.0 copy-start.2
  7.2 2.6 %pack_grads.1 = bf16[4,8,48,256]{3,2,1,0:T(8,128)(2,1)} custom-call(s32[1,128]{1,0:T(1,128)} %bitcast.25, s32[1,128]{1,0:T(1,128)} %bitcast.28, bf16[128,1024]{1,0:T(8,128)(2,1)} %grad_ref.1, bf16[128,1024]{1,0:T(8,128)(2,1)} %gate_ref.1, bf16[128,1024]{1,0:T(8,128)(2,1)} %up_ref.1), custom_call_target="tpu_custom_call" | custom-call | tf_op jit(solution)/shard_map/pack_grads/pallas_call | solution.py:170
  9.8 8.7 %all-to-all-start = ((bf16[32,48,256]{2,1,0:T(8,128)(2,1)}), bf16[32,48,256]{2,1,0:T(8,128)(2,1)S(1)}, u32[]{:S(2)}, u32[]{:S(2)}) async-start(bf16[32,48,256]{2,1,0:T(8,128)(2,1)} %bitcast.22), calls=%async_computation | async-start | bytes 1572864 | tf_op jit(solution)/shard_map/all_to_all | solution.py:179
  18.5 0.0 all-gather.2.cloned.1.call-start
  18.6 0.0 copy-done.2
  18.6 4.1 %collective-permute-start = (bf16[32,2048]{1,0:T(8,128)(2,1)S(1)}, bf16[32,2048]{1,0:T(8,128)(2,1)S(1)}, u32[]{:S(2)}, u32[]{:S(2)}) collective-permute-start(bf16[32,2048]{1,0:T(8,128)(2,1)S(1)} %convert_element_type.12), channel_id=1, source_target_pairs={{0,32},{32,0},{1,33},{33,1},{2,34},{34,2},{3,35},{35,3},{4,36},{36... | collective-permute-start | bytes 393224 | tf_op jit(solution)/shard_map/ppermute | solution.py:183
  22.7 3.1 %pack_rows.1 = bf16[4,8,48,512]{3,2,1,0:T(8,128)(2,1)} custom-call(s32[1,128]{1,0:T(1,128)} %bitcast.26, s32[1,128]{1,0:T(1,128)} %bitcast.29, bf16[128,4096]{1,0:T(8,128)(2,1)} %x_ref), custom_call_target="tpu_custom_call" | custom-call | tf_op jit(solution)/shard_map/pack_rows/pallas_call | solution.py:189
  25.8 5.0 %collective-permute-done = bf16[32,2048]{1,0:T(8,128)(2,1)S(1)} collective-permute-done((bf16[32,2048]{1,0:T(8,128)(2,1)S(1)}, bf16[32,2048]{1,0:T(8,128)(2,1)S(1)}, u32[]{:S(2)}, u32[]{:S(2)}) %collective-permute-start) | collective-permute-done | bytes 131104 | tf_op jit(solution)/shard_map/ppermute | solution.py:183
  30.9 0.0 copy-start.1
  30.9 11.0 %all-to-all-done = bf16[32,48,256]{2,1,0:T(8,128)(2,1)S(1)} async-done(((bf16[32,48,256]{2,1,0:T(8,128)(2,1)}), bf16[32,48,256]{2,1,0:T(8,128)(2,1)S(1)}, u32[]{:S(2)}, u32[]{:S(2)}) %all-to-all-start) | async-done | bytes 786464 | tf_op jit(solution)/shard_map/all_to_all | solution.py:179
  41.8 0.0 copy-start
  41.8 0.9 copy-done
  42.7 0.0 all-gather.2.cloned.1.call-update
  42.7 4.0 %all-to-all-start.1 = ((bf16[32,48,512]{2,1,0:T(8,128)(2,1)}), bf16[32,48,512]{2,1,0:T(8,128)(2,1)S(1)}, u32[]{:S(2)}, u32[]{:S(2)}) async-start(bf16[32,48,512]{2,1,0:T(8,128)(2,1)} %bitcast.20), calls=%async_computation.1 | async-start | bytes 3145728 | tf_op jit(solution)/shard_map/all_to_all | solution.py:206
  46.8 0.0 reduce-scatter.2.cloned.1.call-start
  46.9 7.9 %collective-permute-start.3 = (bf16[64,2048]{1,0:T(8,128)(2,1)S(1)}, bf16[64,2048]{1,0:T(8,128)(2,1)S(1)}, u32[]{:S(2)}, u32[]{:S(2)}) collective-permute-start(bf16[64,2048]{1,0:T(8,128)(2,1)S(1)} %maximum_select_fusion.rest_0_), channel_id=1, source_target_pairs={{0,192},{64,256},{128,320},{192,384},{256,448},{320,0},{384,64},{4... | collective-permute-start | bytes 786440 | tf_op jit(solution)/shard_map/ppermute | solution.py:213
  54.8 8.2 %collective-permute-start.4 = (bf16[64,2048]{1,0:T(8,128)(2,1)S(1)}, bf16[64,2048]{1,0:T(8,128)(2,1)S(1)}, u32[]{:S(2)}, u32[]{:S(2)}) collective-permute-start(bf16[64,2048]{1,0:T(8,128)(2,1)S(1)} %maximum_select_fusion.rest_0_), channel_id=1, source_target_pairs={{0,256},{64,320},{128,384},{192,448},{256,0},{320,64},{384,128},{4... | collective-permute-start | bytes 786440 | tf_op jit(solution)/shard_map/ppermute | solution.py:213
  63.0 1.9 %collective-permute-start.1 = (bf16[64,2048]{1,0:T(8,128)(2,1)S(1)}, bf16[64,2048]{1,0:T(8,128)(2,1)S(1)}, u32[]{:S(2)}, u32[]{:S(2)}) collective-permute-start(bf16[64,2048]{1,0:T(8,128)(2,1)S(1)} %maximum_select_fusion.rest_0_), channel_id=1, source_target_pairs={{0,64},{64,128},{128,192},{192,256},{256,320},{320,384},{384,448},... | collective-permute-start | bytes 786440 | tf_op jit(solution)/shard_map/ppermute | solution.py:213
  64.9 2.5 %collective-permute-start.2 = (bf16[64,2048]{1,0:T(8,128)(2,1)S(1)}, bf16[64,2048]{1,0:T(8,128)(2,1)S(1)}, u32[]{:S(2)}, u32[]{:S(2)}) collective-permute-start(bf16[64,2048]{1,0:T(8,128)(2,1)S(1)} %maximum_select_fusion.rest_0_), channel_id=1, source_target_pairs={{0,128},{64,192},{128,256},{192,320},{256,384},{320,448},{384,0},{... | collective-permute-start | bytes 786440 | tf_op jit(solution)/shard_map/ppermute | solution.py:213
  67.4 6.9 %collective-permute-start.5 = (bf16[64,2048]{1,0:T(8,128)(2,1)S(1)}, bf16[64,2048]{1,0:T(8,128)(2,1)S(1)}, u32[]{:S(2)}, u32[]{:S(2)}) collective-permute-start(bf16[64,2048]{1,0:T(8,128)(2,1)S(1)} %maximum_select_fusion.rest_0_), channel_id=1, source_target_pairs={{0,320},{64,384},{128,448},{192,0},{256,64},{320,128},{384,192},{4... | collective-permute-start | bytes 786440 | tf_op jit(solution)/shard_map/ppermute | solution.py:213
  74.3 0.5 collective-permute-done.3.rest_3_
  74.8 0.0 copy-start.3
  74.8 19.3 %collective-permute-start.6 = (bf16[64,2048]{1,0:T(8,128)(2,1)S(1)}, bf16[64,2048]{1,0:T(8,128)(2,1)}, u32[]{:S(2)}, u32[]{:S(2)}) collective-permute-start(bf16[64,2048]{1,0:T(8,128)(2,1)S(1)} %maximum_select_fusion.rest_0_), channel_id=1, source_target_pairs={{0,384},{64,448},{128,0},{192,64},{256,128},{320,192},{384,256},{4... | collective-permute-start | bytes 786440 | tf_op jit(solution)/shard_map/ppermute | solution.py:213
  94.2 0.0 collective-permute-done.4.rest_4_
  94.2 0.0 copy-start.4
  94.2 1.9 %collective-permute-start.7 = (bf16[64,2048]{1,0:T(8,128)(2,1)S(1)}, bf16[64,2048]{1,0:T(8,128)(2,1)}, u32[]{:S(2)}, u32[]{:S(2)}) collective-permute-start(bf16[64,2048]{1,0:T(8,128)(2,1)S(1)} %maximum_select_fusion.rest_0_), channel_id=1, source_target_pairs={{0,448},{64,0},{128,64},{192,128},{256,192},{320,256},{384,320},{4... | collective-permute-start | bytes 786440 | tf_op jit(solution)/shard_map/ppermute | solution.py:213
  96.1 0.0 collective-permute-done.1.rest_1_
  96.1 0.0 copy-start.5
  96.1 6.3 %collective-permute-done.2.rest_2_ = bf16[64,2048]{1,0:T(8,128)(2,1)S(1)} collective-permute-done((bf16[64,2048]{1,0:T(8,128)(2,1)S(1)}, bf16[64,2048]{1,0:T(8,128)(2,1)S(1)}, u32[]{:S(2)}, u32[]{:S(2)}) %collective-permute-start.2) | collective-permute-done | bytes 262176 | tf_op jit(solution)/shard_map/ppermute | solution.py:213
  102.5 0.0 copy-start.6
  102.5 0.0 collective-permute-done.5.rest_5_
  102.5 0.0 copy-start.7
  102.5 0.8 collective-permute-done.6.rest_6_
  103.3 5.3 %collective-permute-done.7.rest_7_ = bf16[64,2048]{1,0:T(8,128)(2,1)} collective-permute-done((bf16[64,2048]{1,0:T(8,128)(2,1)S(1)}, bf16[64,2048]{1,0:T(8,128)(2,1)}, u32[]{:S(2)}, u32[]{:S(2)}) %collective-permute-start.7) | collective-permute-done | bytes 262176 | tf_op jit(solution)/shard_map/ppermute | solution.py:213
  108.6 0.0 all-to-all-done.1
  108.6 1.4 all-gather.2.cloned.1.call-done.g_ref
  110.0 0.0 copy-done.1
  110.0 0.0 copy-done.3
  110.0 0.0 copy-done.4
  110.0 0.0 copy-done.5
  110.0 0.0 copy-done.6
  110.0 0.0 copy-done.7
  110.0 10.1 %both_grads.1 = (bf16[512,2048]{1,0:T(8,128)(2,1)}, bf16[1536,512]{1,0:T(8,128)(2,1)}) custom-call(s32[1]{0:T(128)} %bitcast.2.z_ref, bf16[1536,512]{1,0:T(8,128)(2,1)S(1)} %bitcast.18, bf16[8,1536,256]{2,1,0:T(8,128)(2,1)} %all-gather.2.cloned.1.call-done.g_ref, bf16[64,2048]{1,0:T(8,128)(2,1)} %copy-done.1, bf16[64,2048]{1,0:T(8,128)(2,1)} %copy-done.5, ...), custom_call_target="tpu_custom_call" | custom-call | tf_op jit(solution)/shard_map/both_grads/pallas_call | solution.py:217
  120.1 0.0 reduce-scatter.2.cloned.1.call-update
  120.2 7.6 %all-to-all-start.2 = ((bf16[32,48,512]{2,1,0:T(8,128)(2,1)}), bf16[32,48,512]{2,1,0:T(8,128)(2,1)S(1)}, u32[]{:S(2)}, u32[]{:S(2)}) async-start(bf16[32,48,512]{2,1,0:T(8,128)(2,1)} %bitcast.7), calls=%async_computation.2 | async-start | bytes 3145728 | tf_op jit(solution)/shard_map/all_to_all | solution.py:240
  127.7 0.0 copy-start.8
  127.7 0.0 copy-start.9
  127.8 41.5 %reduce-scatter.2.cloned.1.call-done = bf16[64,2048]{1,0:T(8,128)(2,1)} async-done(((bf16[512,2048]{1,0:T(8,128)(2,1)}), bf16[64,2048]{1,0:T(8,128)(2,1)}) %reduce-scatter.2.cloned.1.call-update) | async-done | bytes 262160 | tf_op jit(solution)/shard_map/reduce_scatter | solution.py:238
  169.3 0.0 copy-start.10
  169.3 1.0 dynamic-slice_bitcast_fusion
  170.2 3.5 %collective-permute-start.8 = (bf16[32,2048]{1,0:T(8,128)(2,1)S(1)}, bf16[32,2048]{1,0:T(8,128)(2,1)S(1)}, u32[]{:S(2)}, u32[]{:S(2)}) collective-permute-start(bf16[32,2048]{1,0:T(8,128)(2,1)S(1)} %dynamic-slice_bitcast_fusion), channel_id=1, source_target_pairs={{0,32},{32,0},{1,33},{33,1},{2,34},{34,2},{3,35},{35,3},{4,36},{36... | collective-permute-start | bytes 393224 | tf_op jit(solution)/shard_map/ppermute | solution.py:262
  173.7 0.0 all-to-all-done.2
  173.7 2.3 %combine.1 = bf16[128,4096]{1,0:T(8,128)(2,1)} custom-call(s32[1,128]{1,0:T(1,128)} %bitcast.27, s32[1,128]{1,0:T(1,128)} %bitcast.30, bf16[4,8,48,512]{3,2,1,0:T(8,128)(2,1)S(1)} %bitcast.19), custom_call_target="tpu_custom_call" | custom-call | tf_op jit(solution)/shard_map/combine/pallas_call | solution.py:243
  176.0 2.6 %collective-permute-done.8 = bf16[32,2048]{1,0:T(8,128)(2,1)S(1)} collective-permute-done((bf16[32,2048]{1,0:T(8,128)(2,1)S(1)}, bf16[32,2048]{1,0:T(8,128)(2,1)S(1)}, u32[]{:S(2)}, u32[]{:S(2)}) %collective-permute-start.8) | collective-permute-done | bytes 131104 | tf_op jit(solution)/shard_map/ppermute | solution.py:262
  178.6 0.0 copy-done.8
  178.6 0.0 copy-done.9
  178.6 0.0 copy-done.10
  178.6 1.0 multiply_subtract_fusion
  (2 shorter events, 0.1 us)
Async XLA Ops:
  7.2 11.4 %copy-start.2 = (f32[32,2048]{1,0:T(8,128)S(1)}, f32[32,2048]{1,0:T(8,128)}, u32[]{:S(2)}) copy-start(f32[32,2048]{1,0:T(8,128)} %param.15) | copy-start | bytes 786436
  9.8 32.0 %all-to-all-start = ((bf16[32,48,256]{2,1,0:T(8,128)(2,1)}), bf16[32,48,256]{2,1,0:T(8,128)(2,1)S(1)}, u32[]{:S(2)}, u32[]{:S(2)}) async-start(bf16[32,48,256]{2,1,0:T(8,128)(2,1)} %bitcast.22), calls=%async_computation | async-start | bytes 1572864 | tf_op jit(solution)/shard_map/all_to_all | solution.py:179
  18.5 91.5 %all-gather.2.cloned.1.call-start = ((), (), s32[]{:S(2)}) async-start(), calls=%async_computation.4 | async-start | bytes 7077888 | tf_op jit(solution)/shard_map/all_gather | solution.py:199
  18.6 12.2 %collective-permute-start = (bf16[32,2048]{1,0:T(8,128)(2,1)S(1)}, bf16[32,2048]{1,0:T(8,128)(2,1)S(1)}, u32[]{:S(2)}, u32[]{:S(2)}) collective-permute-start(bf16[32,2048]{1,0:T(8,128)(2,1)S(1)} %convert_element_type.12), channel_id=1, source_target_pairs={{0,32},{32,0},{1,33},{33,1},{2,34},{34,2},{3,35},{35,3},{4,36},{36... | collective-permute-start | bytes 393224 | tf_op jit(solution)/shard_map/ppermute | solution.py:183
  30.9 79.1 %copy-start.1 = (bf16[64,2048]{1,0:T(8,128)(2,1)}, bf16[64,2048]{1,0:T(8,128)(2,1)S(1)}, u32[]{:S(2)}) copy-start(bf16[64,2048]{1,0:T(8,128)(2,1)S(1)} %maximum_select_fusion.rest_0_) | copy-start | bytes 786436
  41.8 0.9 copy-start
  42.7 65.9 %all-to-all-start.1 = ((bf16[32,48,512]{2,1,0:T(8,128)(2,1)}), bf16[32,48,512]{2,1,0:T(8,128)(2,1)S(1)}, u32[]{:S(2)}, u32[]{:S(2)}) async-start(bf16[32,48,512]{2,1,0:T(8,128)(2,1)} %bitcast.20), calls=%async_computation.1 | async-start | bytes 3145728 | tf_op jit(solution)/shard_map/all_to_all | solution.py:206
  46.8 122.4 %reduce-scatter.2.cloned.1.call-start = ((), (), s32[]{:S(2)}) async-start(), calls=%async_computation.5 | async-start | bytes 2359296 | tf_op jit(solution)/shard_map/reduce_scatter | solution.py:238
  46.9 28.0 %collective-permute-start.3 = (bf16[64,2048]{1,0:T(8,128)(2,1)S(1)}, bf16[64,2048]{1,0:T(8,128)(2,1)S(1)}, u32[]{:S(2)}, u32[]{:S(2)}) collective-permute-start(bf16[64,2048]{1,0:T(8,128)(2,1)S(1)} %maximum_select_fusion.rest_0_), channel_id=1, source_target_pairs={{0,192},{64,256},{128,320},{192,384},{256,448},{320,0},{384,64},{4... | collective-permute-start | bytes 786440 | tf_op jit(solution)/shard_map/ppermute | solution.py:213
  54.8 39.4 %collective-permute-start.4 = (bf16[64,2048]{1,0:T(8,128)(2,1)S(1)}, bf16[64,2048]{1,0:T(8,128)(2,1)S(1)}, u32[]{:S(2)}, u32[]{:S(2)}) collective-permute-start(bf16[64,2048]{1,0:T(8,128)(2,1)S(1)} %maximum_select_fusion.rest_0_), channel_id=1, source_target_pairs={{0,256},{64,320},{128,384},{192,448},{256,0},{320,64},{384,128},{4... | collective-permute-start | bytes 786440 | tf_op jit(solution)/shard_map/ppermute | solution.py:213
  63.0 33.1 %collective-permute-start.1 = (bf16[64,2048]{1,0:T(8,128)(2,1)S(1)}, bf16[64,2048]{1,0:T(8,128)(2,1)S(1)}, u32[]{:S(2)}, u32[]{:S(2)}) collective-permute-start(bf16[64,2048]{1,0:T(8,128)(2,1)S(1)} %maximum_select_fusion.rest_0_), channel_id=1, source_target_pairs={{0,64},{64,128},{128,192},{192,256},{256,320},{320,384},{384,448},... | collective-permute-start | bytes 786440 | tf_op jit(solution)/shard_map/ppermute | solution.py:213
  64.9 37.6 %collective-permute-start.2 = (bf16[64,2048]{1,0:T(8,128)(2,1)S(1)}, bf16[64,2048]{1,0:T(8,128)(2,1)S(1)}, u32[]{:S(2)}, u32[]{:S(2)}) collective-permute-start(bf16[64,2048]{1,0:T(8,128)(2,1)S(1)} %maximum_select_fusion.rest_0_), channel_id=1, source_target_pairs={{0,128},{64,192},{128,256},{192,320},{256,384},{320,448},{384,0},{... | collective-permute-start | bytes 786440 | tf_op jit(solution)/shard_map/ppermute | solution.py:213
  67.4 35.1 %collective-permute-start.5 = (bf16[64,2048]{1,0:T(8,128)(2,1)S(1)}, bf16[64,2048]{1,0:T(8,128)(2,1)S(1)}, u32[]{:S(2)}, u32[]{:S(2)}) collective-permute-start(bf16[64,2048]{1,0:T(8,128)(2,1)S(1)} %maximum_select_fusion.rest_0_), channel_id=1, source_target_pairs={{0,320},{64,384},{128,448},{192,0},{256,64},{320,128},{384,192},{4... | collective-permute-start | bytes 786440 | tf_op jit(solution)/shard_map/ppermute | solution.py:213
  74.8 35.2 %copy-start.3 = (bf16[64,2048]{1,0:T(8,128)(2,1)}, bf16[64,2048]{1,0:T(8,128)(2,1)S(1)}, u32[]{:S(2)}) copy-start(bf16[64,2048]{1,0:T(8,128)(2,1)S(1)} %collective-permute-done.3.rest_3_) | copy-start | bytes 786436
  74.8 28.5 %collective-permute-start.6 = (bf16[64,2048]{1,0:T(8,128)(2,1)S(1)}, bf16[64,2048]{1,0:T(8,128)(2,1)}, u32[]{:S(2)}, u32[]{:S(2)}) collective-permute-start(bf16[64,2048]{1,0:T(8,128)(2,1)S(1)} %maximum_select_fusion.rest_0_), channel_id=1, source_target_pairs={{0,384},{64,448},{128,0},{192,64},{256,128},{320,192},{384,256},{4... | collective-permute-start | bytes 786440 | tf_op jit(solution)/shard_map/ppermute | solution.py:213
  94.2 15.8 %copy-start.4 = (bf16[64,2048]{1,0:T(8,128)(2,1)}, bf16[64,2048]{1,0:T(8,128)(2,1)S(1)}, u32[]{:S(2)}) copy-start(bf16[64,2048]{1,0:T(8,128)(2,1)S(1)} %collective-permute-done.4.rest_4_) | copy-start | bytes 786436
  94.2 14.4 %collective-permute-start.7 = (bf16[64,2048]{1,0:T(8,128)(2,1)S(1)}, bf16[64,2048]{1,0:T(8,128)(2,1)}, u32[]{:S(2)}, u32[]{:S(2)}) collective-permute-start(bf16[64,2048]{1,0:T(8,128)(2,1)S(1)} %maximum_select_fusion.rest_0_), channel_id=1, source_target_pairs={{0,448},{64,0},{128,64},{192,128},{256,192},{320,256},{384,320},{4... | collective-permute-start | bytes 786440 | tf_op jit(solution)/shard_map/ppermute | solution.py:213
  96.1 13.9 %copy-start.5 = (bf16[64,2048]{1,0:T(8,128)(2,1)}, bf16[64,2048]{1,0:T(8,128)(2,1)S(1)}, u32[]{:S(2)}) copy-start(bf16[64,2048]{1,0:T(8,128)(2,1)S(1)} %collective-permute-done.1.rest_1_) | copy-start | bytes 786436
  102.5 7.5 %copy-start.6 = (bf16[64,2048]{1,0:T(8,128)(2,1)}, bf16[64,2048]{1,0:T(8,128)(2,1)S(1)}, u32[]{:S(2)}) copy-start(bf16[64,2048]{1,0:T(8,128)(2,1)S(1)} %collective-permute-done.2.rest_2_) | copy-start | bytes 786436
  102.5 7.5 %copy-start.7 = (bf16[64,2048]{1,0:T(8,128)(2,1)}, bf16[64,2048]{1,0:T(8,128)(2,1)S(1)}, u32[]{:S(2)}) copy-start(bf16[64,2048]{1,0:T(8,128)(2,1)S(1)} %collective-permute-done.5.rest_5_) | copy-start | bytes 786436
  120.2 53.5 %all-to-all-start.2 = ((bf16[32,48,512]{2,1,0:T(8,128)(2,1)}), bf16[32,48,512]{2,1,0:T(8,128)(2,1)S(1)}, u32[]{:S(2)}, u32[]{:S(2)}) async-start(bf16[32,48,512]{2,1,0:T(8,128)(2,1)} %bitcast.7), calls=%async_computation.2 | async-start | bytes 3145728 | tf_op jit(solution)/shard_map/all_to_all | solution.py:240
  127.7 50.9 %copy-start.8 = (f32[32,2048]{1,0:T(8,128)S(1)}, f32[32,2048]{1,0:T(8,128)}, u32[]{:S(2)}) copy-start(f32[32,2048]{1,0:T(8,128)} %param.17) | copy-start | bytes 786436
  127.7 50.9 %copy-start.9 = (f32[32,2048]{1,0:T(8,128)S(1)}, f32[32,2048]{1,0:T(8,128)}, u32[]{:S(2)}) copy-start(f32[32,2048]{1,0:T(8,128)} %param.16) | copy-start | bytes 786436
  169.3 9.4 %copy-start.10 = (bf16[64,2048]{1,0:T(8,128)(2,1)S(1)}, bf16[64,2048]{1,0:T(8,128)(2,1)}, u32[]{:S(2)}) copy-start(bf16[64,2048]{1,0:T(8,128)(2,1)} %reduce-scatter.2.cloned.1.call-done) | copy-start | bytes 786436
  170.2 8.4 %collective-permute-start.8 = (bf16[32,2048]{1,0:T(8,128)(2,1)S(1)}, bf16[32,2048]{1,0:T(8,128)(2,1)S(1)}, u32[]{:S(2)}, u32[]{:S(2)}) collective-permute-start(bf16[32,2048]{1,0:T(8,128)(2,1)S(1)} %dynamic-slice_bitcast_fusion), channel_id=1, source_target_pairs={{0,32},{32,0},{1,33},{33,1},{2,34},{34,2},{3,35},{35,3},{4,36},{36... | collective-permute-start | bytes 393224 | tf_op jit(solution)/shard_map/ppermute | solution.py:262
Sparse Core Ops, SparseCore 0:
  42.9 67.0 all-gather.1
  120.3 48.9 reduce-scatter.1

commit v7 on v6

--- a/solution.py
+++ b/solution.py
@@ -93,22 +93,13 @@
         out_ref[:, g * piece : (g + 1) * piece] = total.astype(jnp.bfloat16)
 
 
-def both_grads_kernel(z_ref, x_ref, g_ref, *rest):
-    shards, rest = rest[:RING], rest[RING:]
-    dw_ref, dx_ref, g_buf, w_buf, xt_buf, dw_buf, dx_buf, g_sems, w_sems, out_sems = rest
+def weight_grad_kernel(x_ref, g_ref, dw_ref, g_buf, xt_buf, dw_buf, g_sems, out_sems):
     pairs = GROUP // 2
     loads = [
         pltpu.make_async_copy(g_ref.at[pl.ds(2 * j, 2)], g_buf.at[pl.ds(2 * j, 2)], g_sems.at[j])
         for j in range(pairs)
     ]
-    rows = shards[0].shape[0]
-    w_loads = []
-    for k in range(RING):
-        at = pl.multiple_of(lax.rem(z_ref[0] + RING - k, RING) * rows, rows)
-        w_loads.append(
-            pltpu.make_async_copy(shards[k], w_buf.at[pl.ds(at, rows)], w_sems.at[k])
-        )
-    for load in loads + w_loads:
+    for load in loads:
         load.start()
     xt_buf[...] = x_ref[...].T
     stores = []
@@ -124,18 +115,38 @@
             pltpu.make_async_copy(dw_buf.at[:, cols], dw_ref.at[:, cols], out_sems.at[j])
         )
         stores[-1].start()
+    for store in stores:
+        store.wait()
+
+
+def input_grad_kernel(z_ref, g_ref, *rest):
+    shards, rest = rest[:RING], rest[RING:]
+    dx_ref, g_buf, w_buf, dx_buf, g_sems, w_sems, out_sems = rest
+    rows = shards[0].shape[0]
+    w_loads = []
+    for k in range(RING):
+        at = pl.multiple_of(lax.rem(z_ref[0] + RING - k, RING) * rows, rows)
+        w_loads.append(
+            pltpu.make_async_copy(shards[k], w_buf.at[pl.ds(at, rows)], w_sems.at[k])
+        )
+    block = dx_buf.shape[0] // DX_BLOCKS
+    parts = [slice(j * block, (j + 1) * block) for j in range(DX_BLOCKS)]
+    loads = [
+        pltpu.make_async_copy(g_ref.at[:, part], g_buf.at[:, part], g_sems.at[j])
+        for j, part in enumerate(parts)
+    ]
+    for load in w_loads + loads:
+        load.start()
     for load in w_loads:
         load.wait()
-    block = dx_buf.shape[0] // DX_BLOCKS
-    for j in range(DX_BLOCKS):
-        part = slice(j * block, (j + 1) * block)
+    stores = []
+    for j, part in enumerate(parts):
+        loads[j].wait()
         grads = jnp.concatenate([g_buf[g, part] for g in range(GROUP)], axis=1)
         dx_buf[part] = lax.dot_general(
             grads, w_buf[...], (((1,), (1,)), ((), ())), preferred_element_type=jnp.float32
         ).astype(jnp.bfloat16)
-        stores.append(
-            pltpu.make_async_copy(dx_buf.at[part], dx_ref.at[part], out_sems.at[pairs + j])
-        )
+        stores.append(pltpu.make_async_copy(dx_buf.at[part], dx_ref.at[part], out_sems.at[j]))
         stores[-1].start()
     for store in stores:
         store.wait()
@@ -214,29 +225,40 @@
     g_all, x_rows, *shards = lax.optimization_barrier((g_all, x_rows, *shards))
 
     anywhere = pl.BlockSpec(memory_space=pl.ANY)
-    grad_part, dx_rows = pl.pallas_call(
-        both_grads_kernel,
-        out_shape=(
-            jax.ShapeDtypeStruct((piece, 2 * hidden), jnp.bfloat16),
-            jax.ShapeDtypeStruct((rows_total, piece), jnp.bfloat16),
-        ),
-        in_specs=[pl.BlockSpec(memory_space=pltpu.SMEM), VMEM] + [anywhere] * (RING + 1),
-        out_specs=(anywhere, anywhere),
+    grad_part = pl.pallas_call(
+        weight_grad_kernel,
+        out_shape=jax.ShapeDtypeStruct((piece, 2 * hidden), jnp.bfloat16),
+        in_specs=[VMEM, anywhere],
+        out_specs=anywhere,
+        scratch_shapes=[
+            pltpu.VMEM((GROUP, rows_total, gpiece), jnp.bfloat16),
+            pltpu.VMEM((piece, rows_total), jnp.bfloat16),
+            pltpu.VMEM((piece, 2 * hidden), jnp.bfloat16),
+            pltpu.SemaphoreType.DMA((GROUP // 2,)),
+            pltpu.SemaphoreType.DMA((GROUP // 2,)),
+        ],
+        compiler_params=params(),
+        name="weight_grad",
+    )(pltpu.with_memory_space_constraint(x_rows, pltpu.VMEM), g_all)
+    grad_z = lax.psum_scatter(grad_part, "z", scatter_dimension=0, tiled=True)
+
+    grad_part, g_all, *shards = lax.optimization_barrier((grad_part, g_all, *shards))
+    dx_rows = pl.pallas_call(
+        input_grad_kernel,
+        out_shape=jax.ShapeDtypeStruct((rows_total, piece), jnp.bfloat16),
+        in_specs=[pl.BlockSpec(memory_space=pltpu.SMEM)] + [anywhere] * (RING + 1),
+        out_specs=anywhere,
         scratch_shapes=[
             pltpu.VMEM((GROUP, rows_total, gpiece), jnp.bfloat16),
             pltpu.VMEM((piece, 2 * hidden), jnp.bfloat16),
-            pltpu.VMEM((piece, rows_total), jnp.bfloat16),
-            pltpu.VMEM((piece, 2 * hidden), jnp.bfloat16),
             pltpu.VMEM((rows_total, piece), jnp.bfloat16),
-            pltpu.SemaphoreType.DMA((GROUP // 2,)),
+            pltpu.SemaphoreType.DMA((DX_BLOCKS,)),
             pltpu.SemaphoreType.DMA((RING,)),
-            pltpu.SemaphoreType.DMA((GROUP // 2 + DX_BLOCKS,)),
+            pltpu.SemaphoreType.DMA((DX_BLOCKS,)),
         ],
         compiler_params=params(),
-        name="both_grads",
-    )(place, pltpu.with_memory_space_constraint(x_rows, pltpu.VMEM), g_all, *shards)
-    grad_z = lax.psum_scatter(grad_part, "z", scatter_dimension=0, tiled=True)
-
+        name="input_grad",
+    )(place, g_all, *shards)
     back = lax.all_to_all(
         dx_rows.reshape(members, CAP, piece), EXP, split_axis=0, concat_axis=0, tiled=True
     )

time: 187 us -> 184 us (0.984)
  waiting for transfers between devices: 74.5 us -> 66.9 us
  Pallas kernels: 18.1 us -> 21.7 us
    reduce_scatter x1, waiting for transfers between devices: 41.5 us -> 34.1 us  [body(): grad_z = lax.psum_scatter(grad_part, 'z', scatter_dimension=0, tiled=True)]
    pallas_call x1 -> x2, Pallas kernels: 10.1 us -> 13.8 us  [the longest x1 7.53 us: body(): pl.pallas_call(input_grad_kernel, out_shape=jax.ShapeDtypeStruct((rows_to...]
  transfers between devices with their start and end apart: 14 -> 14, of which waited for: 9 -> 10; matrix products, arithmetic and copies ran while one was open for 1% -> 1% of each run, Pallas kernels for 3% -> 7%
where the time goes in v7:
time: 184 us; the launch traced here: 183 us
  starting transfers between devices  76.1 us (41%)
  waiting for transfers between devices  66.9 us (36%)
  Pallas kernels  21.7 us (12%)
  between operations  14.3 us (8%)
  local copies, waits for them, and re-layouts  2.61 us (1%)
    ppermute x7, starting transfers between devices, body(): lax.ppermute(moved, 'z', [(i, (i + k) % RING) for i in range(RING)])  48.7 us
    reduce_scatter x1, waiting for transfers between devices, body(): grad_z = lax.psum_scatter(grad_part, 'z', scatter_dimension=0, tiled=True)  34.1 us
    ppermute x7, waiting for transfers between devices, body(): lax.ppermute(moved, 'z', [(i, (i + k) % RING) for i in range(RING)])  12.3 us
    all_to_all x1, waiting for transfers between devices, body(): lax.all_to_all(g_send.reshape(members, CAP, gpiece), EXP, split_axis=0, c...  11 us
    all_to_all x1, starting transfers between devices, body(): lax.all_to_all(g_send.reshape(members, CAP, gpiece), EXP, split_axis=0, c...  8.71 us
    all_to_all x1, starting transfers between devices, body(): lax.all_to_all(dx_rows.reshape(members, CAP, piece), EXP, split_axis=0, c...  7.56 us
    pallas_call x1, Pallas kernels, body(): pl.pallas_call(input_grad_kernel, out_shape=jax.ShapeDtypeStruct((rows_to...  7.53 us
    pallas_call x1, Pallas kernels, body(): pl.pallas_call(weight_grad_kernel, out_shape=jax.ShapeDtypeStruct((piece,...  6.23 us
  transfers between devices with their start and end apart: 14, of which 10 were waited for; matrix products, arithmetic and copies ran while one was open for 1% of the time, Pallas kernels for 7%

profile of v7, /device:TPU:6, one launch (start us, length us, event | category | flops | bytes accessed | tf_op | source)
XLA Modules:
  0.0 182.7 jit_solution(8216320735586533809)
XLA Ops:
  7.2 0.0 copy-start.2
  7.2 2.6 %pack_grads.1 = bf16[4,8,48,256]{3,2,1,0:T(8,128)(2,1)} custom-call(s32[1,128]{1,0:T(1,128)} %bitcast.26, s32[1,128]{1,0:T(1,128)} %bitcast.29, bf16[128,1024]{1,0:T(8,128)(2,1)} %grad_ref.1, bf16[128,1024]{1,0:T(8,128)(2,1)} %gate_ref.1, bf16[128,1024]{1,0:T(8,128)(2,1)} %up_ref.1), custom_call_target="tpu_custom_call" | custom-call | tf_op jit(solution)/shard_map/pack_grads/pallas_call | solution.py:181
  9.8 8.7 %all-to-all-start = ((bf16[32,48,256]{2,1,0:T(8,128)(2,1)}), bf16[32,48,256]{2,1,0:T(8,128)(2,1)S(1)}, u32[]{:S(2)}, u32[]{:S(2)}) async-start(bf16[32,48,256]{2,1,0:T(8,128)(2,1)} %bitcast.23), calls=%async_computation | async-start | bytes 1572864 | tf_op jit(solution)/shard_map/all_to_all | solution.py:190
  18.5 0.0 all-gather.2.cloned.1.call-start
  18.6 0.0 copy-done.2
  18.6 4.1 %collective-permute-start = (bf16[32,2048]{1,0:T(8,128)(2,1)S(1)}, bf16[32,2048]{1,0:T(8,128)(2,1)S(1)}, u32[]{:S(2)}, u32[]{:S(2)}) collective-permute-start(bf16[32,2048]{1,0:T(8,128)(2,1)S(1)} %convert_element_type.12), channel_id=1, source_target_pairs={{0,32},{32,0},{1,33},{33,1},{2,34},{34,2},{3,35},{35,3},{4,36},{36... | collective-permute-start | bytes 393224 | tf_op jit(solution)/shard_map/ppermute | solution.py:194
  22.7 3.1 %pack_rows.1 = bf16[4,8,48,512]{3,2,1,0:T(8,128)(2,1)} custom-call(s32[1,128]{1,0:T(1,128)} %bitcast.27, s32[1,128]{1,0:T(1,128)} %bitcast.30, bf16[128,4096]{1,0:T(8,128)(2,1)} %x_ref), custom_call_target="tpu_custom_call" | custom-call | tf_op jit(solution)/shard_map/pack_rows/pallas_call | solution.py:200
  25.8 5.0 %collective-permute-done = bf16[32,2048]{1,0:T(8,128)(2,1)S(1)} collective-permute-done((bf16[32,2048]{1,0:T(8,128)(2,1)S(1)}, bf16[32,2048]{1,0:T(8,128)(2,1)S(1)}, u32[]{:S(2)}, u32[]{:S(2)}) %collective-permute-start) | collective-permute-done | bytes 131104 | tf_op jit(solution)/shard_map/ppermute | solution.py:194
  30.9 0.0 copy-start.1
  30.9 11.0 %all-to-all-done = bf16[32,48,256]{2,1,0:T(8,128)(2,1)S(1)} async-done(((bf16[32,48,256]{2,1,0:T(8,128)(2,1)}), bf16[32,48,256]{2,1,0:T(8,128)(2,1)S(1)}, u32[]{:S(2)}, u32[]{:S(2)}) %all-to-all-start) | async-done | bytes 786464 | tf_op jit(solution)/shard_map/all_to_all | solution.py:190
  41.8 0.0 copy-start
  41.8 0.9 copy-done
  42.7 0.0 all-gather.2.cloned.1.call-update
  42.7 4.0 %all-to-all-start.1 = ((bf16[32,48,512]{2,1,0:T(8,128)(2,1)}), bf16[32,48,512]{2,1,0:T(8,128)(2,1)S(1)}, u32[]{:S(2)}, u32[]{:S(2)}) async-start(bf16[32,48,512]{2,1,0:T(8,128)(2,1)} %bitcast.20), calls=%async_computation.1 | async-start | bytes 3145728 | tf_op jit(solution)/shard_map/all_to_all | solution.py:217
  46.8 0.0 reduce-scatter.2.cloned.1.call-start
  46.8 7.9 %collective-permute-start.3 = (bf16[64,2048]{1,0:T(8,128)(2,1)S(1)}, bf16[64,2048]{1,0:T(8,128)(2,1)S(1)}, u32[]{:S(2)}, u32[]{:S(2)}) collective-permute-start(bf16[64,2048]{1,0:T(8,128)(2,1)S(1)} %maximum_select_fusion.rest_0_), channel_id=1, source_target_pairs={{0,192},{64,256},{128,320},{192,384},{256,448},{320,0},{384,64},{4... | collective-permute-start | bytes 786440 | tf_op jit(solution)/shard_map/ppermute | solution.py:224
  54.8 8.2 %collective-permute-start.4 = (bf16[64,2048]{1,0:T(8,128)(2,1)S(1)}, bf16[64,2048]{1,0:T(8,128)(2,1)S(1)}, u32[]{:S(2)}, u32[]{:S(2)}) collective-permute-start(bf16[64,2048]{1,0:T(8,128)(2,1)S(1)} %maximum_select_fusion.rest_0_), channel_id=1, source_target_pairs={{0,256},{64,320},{128,384},{192,448},{256,0},{320,64},{384,128},{4... | collective-permute-start | bytes 786440 | tf_op jit(solution)/shard_map/ppermute | solution.py:224
  63.0 1.9 %collective-permute-start.1 = (bf16[64,2048]{1,0:T(8,128)(2,1)S(1)}, bf16[64,2048]{1,0:T(8,128)(2,1)S(1)}, u32[]{:S(2)}, u32[]{:S(2)}) collective-permute-start(bf16[64,2048]{1,0:T(8,128)(2,1)S(1)} %maximum_select_fusion.rest_0_), channel_id=1, source_target_pairs={{0,64},{64,128},{128,192},{192,256},{256,320},{320,384},{384,448},... | collective-permute-start | bytes 786440 | tf_op jit(solution)/shard_map/ppermute | solution.py:224
  64.9 2.5 %collective-permute-start.2 = (bf16[64,2048]{1,0:T(8,128)(2,1)S(1)}, bf16[64,2048]{1,0:T(8,128)(2,1)S(1)}, u32[]{:S(2)}, u32[]{:S(2)}) collective-permute-start(bf16[64,2048]{1,0:T(8,128)(2,1)S(1)} %maximum_select_fusion.rest_0_), channel_id=1, source_target_pairs={{0,128},{64,192},{128,256},{192,320},{256,384},{320,448},{384,0},{... | collective-permute-start | bytes 786440 | tf_op jit(solution)/shard_map/ppermute | solution.py:224
  67.4 6.9 %collective-permute-start.5 = (bf16[64,2048]{1,0:T(8,128)(2,1)S(1)}, bf16[64,2048]{1,0:T(8,128)(2,1)S(1)}, u32[]{:S(2)}, u32[]{:S(2)}) collective-permute-start(bf16[64,2048]{1,0:T(8,128)(2,1)S(1)} %maximum_select_fusion.rest_0_), channel_id=1, source_target_pairs={{0,320},{64,384},{128,448},{192,0},{256,64},{320,128},{384,192},{4... | collective-permute-start | bytes 786440 | tf_op jit(solution)/shard_map/ppermute | solution.py:224
  74.3 0.5 collective-permute-done.3.rest_3_
  74.8 0.0 copy-start.3
  74.8 19.3 %collective-permute-start.6 = (bf16[64,2048]{1,0:T(8,128)(2,1)S(1)}, bf16[64,2048]{1,0:T(8,128)(2,1)S(1)}, u32[]{:S(2)}, u32[]{:S(2)}) collective-permute-start(bf16[64,2048]{1,0:T(8,128)(2,1)S(1)} %maximum_select_fusion.rest_0_), channel_id=1, source_target_pairs={{0,384},{64,448},{128,0},{192,64},{256,128},{320,192},{384,256},{4... | collective-permute-start | bytes 786440 | tf_op jit(solution)/shard_map/ppermute | solution.py:224
  94.2 0.0 collective-permute-done.4.rest_4_
  94.2 0.0 copy-start.4
  94.2 1.9 %collective-permute-start.7 = (bf16[64,2048]{1,0:T(8,128)(2,1)S(1)}, bf16[64,2048]{1,0:T(8,128)(2,1)}, u32[]{:S(2)}, u32[]{:S(2)}) collective-permute-start(bf16[64,2048]{1,0:T(8,128)(2,1)S(1)} %maximum_select_fusion.rest_0_), channel_id=1, source_target_pairs={{0,448},{64,0},{128,64},{192,128},{256,192},{320,256},{384,320},{4... | collective-permute-start | bytes 786440 | tf_op jit(solution)/shard_map/ppermute | solution.py:224
  96.1 0.0 collective-permute-done.1.rest_1_
  96.1 0.0 copy-start.5
  96.1 6.3 %collective-permute-done.2.rest_2_ = bf16[64,2048]{1,0:T(8,128)(2,1)S(1)} collective-permute-done((bf16[64,2048]{1,0:T(8,128)(2,1)S(1)}, bf16[64,2048]{1,0:T(8,128)(2,1)S(1)}, u32[]{:S(2)}, u32[]{:S(2)}) %collective-permute-start.2) | collective-permute-done | bytes 262176 | tf_op jit(solution)/shard_map/ppermute | solution.py:224
  102.5 0.0 copy-start.6
  102.5 0.0 collective-permute-done.5.rest_5_
  102.5 0.0 copy-start.7
  102.5 0.7 collective-permute-done.6.rest_6_
  103.2 0.0 copy-start.8
  103.2 0.7 copy-done.8
  103.9 4.7 %collective-permute-done.7.rest_7_ = bf16[64,2048]{1,0:T(8,128)(2,1)} collective-permute-done((bf16[64,2048]{1,0:T(8,128)(2,1)S(1)}, bf16[64,2048]{1,0:T(8,128)(2,1)}, u32[]{:S(2)}, u32[]{:S(2)}) %collective-permute-start.7) | collective-permute-done | bytes 262176 | tf_op jit(solution)/shard_map/ppermute | solution.py:224
  108.6 0.0 all-to-all-done.1
  108.6 1.4 all-gather.2.cloned.1.call-done.g_ref
  110.0 6.2 %weight_grad.1 = bf16[512,2048]{1,0:T(8,128)(2,1)} custom-call(bf16[1536,512]{1,0:T(8,128)(2,1)S(1)} %bitcast.18, bf16[8,1536,256]{2,1,0:T(8,128)(2,1)} %all-gather.2.cloned.1.call-done.g_ref), custom_call_target="tpu_custom_call" | custom-call | tf_op jit(solution)/shard_map/weight_grad/pallas_call | solution.py:228
  116.2 0.0 copy-done.1
  116.2 0.0 copy-done.3
  116.3 0.0 copy-done.4
  116.3 0.0 copy-done.5
  116.3 0.0 copy-done.6
  116.3 0.0 copy-done.7
  116.3 0.0 reduce-scatter.2.cloned.1.call-update
  116.3 7.5 %input_grad.1 = bf16[1536,512]{1,0:T(8,128)(2,1)} custom-call(s32[1]{0:T(128)} %bitcast.2.z_ref, bf16[8,1536,256]{2,1,0:T(8,128)(2,1)} %all-gather.2.cloned.1.call-done.g_ref, bf16[64,2048]{1,0:T(8,128)(2,1)} %copy-done.1, bf16[64,2048]{1,0:T(8,128)(2,1)} %copy-done.5, bf16[64,2048]{1,0:T(8,128)(2,1)} %copy-done.6, bf16[64,2048]{1,0:T(8,128)(2,1)} %copy-done.3, ...), custom_call_target="tpu_custom_call" | custom-call | tf_op jit(solution)/shard_map/input_grad/pallas_call | solution.py:246
  123.9 7.6 %all-to-all-start.2 = ((bf16[32,48,512]{2,1,0:T(8,128)(2,1)}), bf16[32,48,512]{2,1,0:T(8,128)(2,1)S(1)}, u32[]{:S(2)}, u32[]{:S(2)}) async-start(bf16[32,48,512]{2,1,0:T(8,128)(2,1)} %bitcast.21), calls=%async_computation.2 | async-start | bytes 3145728 | tf_op jit(solution)/shard_map/all_to_all | solution.py:262
  131.4 0.0 copy-start.9
  131.4 0.0 copy-start.10
  131.5 34.1 %reduce-scatter.2.cloned.1.call-done = bf16[64,2048]{1,0:T(8,128)(2,1)} async-done(((bf16[512,2048]{1,0:T(8,128)(2,1)}), bf16[64,2048]{1,0:T(8,128)(2,1)}) %reduce-scatter.2.cloned.1.call-update) | async-done | bytes 262160 | tf_op jit(solution)/shard_map/reduce_scatter | solution.py:243
  165.5 0.0 copy-start.11
  165.5 1.0 dynamic-slice_bitcast_fusion
  166.5 3.0 %collective-permute-start.8 = (bf16[32,2048]{1,0:T(8,128)(2,1)S(1)}, bf16[32,2048]{1,0:T(8,128)(2,1)S(1)}, u32[]{:S(2)}, u32[]{:S(2)}) collective-permute-start(bf16[32,2048]{1,0:T(8,128)(2,1)S(1)} %dynamic-slice_bitcast_fusion), channel_id=1, source_target_pairs={{0,32},{32,0},{1,33},{33,1},{2,34},{34,2},{3,35},{35,3},{4,36},{36... | collective-permute-start | bytes 393224 | tf_op jit(solution)/shard_map/ppermute | solution.py:284
  169.5 1.2 all-to-all-done.2
  170.6 2.3 %combine.1 = bf16[128,4096]{1,0:T(8,128)(2,1)} custom-call(s32[1,128]{1,0:T(1,128)} %bitcast.28, s32[1,128]{1,0:T(1,128)} %bitcast.31, bf16[4,8,48,512]{3,2,1,0:T(8,128)(2,1)S(1)} %bitcast.19), custom_call_target="tpu_custom_call" | custom-call | tf_op jit(solution)/shard_map/combine/pallas_call | solution.py:265
  172.9 2.0 %collective-permute-done.8 = bf16[32,2048]{1,0:T(8,128)(2,1)S(1)} collective-permute-done((bf16[32,2048]{1,0:T(8,128)(2,1)S(1)}, bf16[32,2048]{1,0:T(8,128)(2,1)S(1)}, u32[]{:S(2)}, u32[]{:S(2)}) %collective-permute-start.8) | collective-permute-done | bytes 131104 | tf_op jit(solution)/shard_map/ppermute | solution.py:284
  174.9 0.0 copy-done.9
  174.9 0.0 copy-done.10
  174.9 0.0 copy-done.11
  174.9 1.0 multiply_subtract_fusion
  (2 shorter events, 0.1 us)
Async XLA Ops:
  7.2 11.4 %copy-start.2 = (f32[32,2048]{1,0:T(8,128)S(1)}, f32[32,2048]{1,0:T(8,128)}, u32[]{:S(2)}) copy-start(f32[32,2048]{1,0:T(8,128)} %param.15) | copy-start | bytes 786436
  9.8 32.0 %all-to-all-start = ((bf16[32,48,256]{2,1,0:T(8,128)(2,1)}), bf16[32,48,256]{2,1,0:T(8,128)(2,1)S(1)}, u32[]{:S(2)}, u32[]{:S(2)}) async-start(bf16[32,48,256]{2,1,0:T(8,128)(2,1)} %bitcast.23), calls=%async_computation | async-start | bytes 1572864 | tf_op jit(solution)/shard_map/all_to_all | solution.py:190
  18.5 91.5 %all-gather.2.cloned.1.call-start = ((), (), s32[]{:S(2)}) async-start(), calls=%async_computation.4 | async-start | bytes 7077888 | tf_op jit(solution)/shard_map/all_gather | solution.py:210
  18.6 12.2 %collective-permute-start = (bf16[32,2048]{1,0:T(8,128)(2,1)S(1)}, bf16[32,2048]{1,0:T(8,128)(2,1)S(1)}, u32[]{:S(2)}, u32[]{:S(2)}) collective-permute-start(bf16[32,2048]{1,0:T(8,128)(2,1)S(1)} %convert_element_type.12), channel_id=1, source_target_pairs={{0,32},{32,0},{1,33},{33,1},{2,34},{34,2},{3,35},{35,3},{4,36},{36... | collective-permute-start | bytes 393224 | tf_op jit(solution)/shard_map/ppermute | solution.py:194
  30.9 85.4 %copy-start.1 = (bf16[64,2048]{1,0:T(8,128)(2,1)}, bf16[64,2048]{1,0:T(8,128)(2,1)S(1)}, u32[]{:S(2)}) copy-start(bf16[64,2048]{1,0:T(8,128)(2,1)S(1)} %maximum_select_fusion.rest_0_) | copy-start | bytes 786436
  41.8 0.9 copy-start
  42.7 65.9 %all-to-all-start.1 = ((bf16[32,48,512]{2,1,0:T(8,128)(2,1)}), bf16[32,48,512]{2,1,0:T(8,128)(2,1)S(1)}, u32[]{:S(2)}, u32[]{:S(2)}) async-start(bf16[32,48,512]{2,1,0:T(8,128)(2,1)} %bitcast.20), calls=%async_computation.1 | async-start | bytes 3145728 | tf_op jit(solution)/shard_map/all_to_all | solution.py:217
  46.8 118.7 %reduce-scatter.2.cloned.1.call-start = ((), (), s32[]{:S(2)}) async-start(), calls=%async_computation.5 | async-start | bytes 2359296 | tf_op jit(solution)/shard_map/reduce_scatter | solution.py:243
  46.8 28.0 %collective-permute-start.3 = (bf16[64,2048]{1,0:T(8,128)(2,1)S(1)}, bf16[64,2048]{1,0:T(8,128)(2,1)S(1)}, u32[]{:S(2)}, u32[]{:S(2)}) collective-permute-start(bf16[64,2048]{1,0:T(8,128)(2,1)S(1)} %maximum_select_fusion.rest_0_), channel_id=1, source_target_pairs={{0,192},{64,256},{128,320},{192,384},{256,448},{320,0},{384,64},{4... | collective-permute-start | bytes 786440 | tf_op jit(solution)/shard_map/ppermute | solution.py:224
  54.8 39.4 %collective-permute-start.4 = (bf16[64,2048]{1,0:T(8,128)(2,1)S(1)}, bf16[64,2048]{1,0:T(8,128)(2,1)S(1)}, u32[]{:S(2)}, u32[]{:S(2)}) collective-permute-start(bf16[64,2048]{1,0:T(8,128)(2,1)S(1)} %maximum_select_fusion.rest_0_), channel_id=1, source_target_pairs={{0,256},{64,320},{128,384},{192,448},{256,0},{320,64},{384,128},{4... | collective-permute-start | bytes 786440 | tf_op jit(solution)/shard_map/ppermute | solution.py:224
  63.0 33.1 %collective-permute-start.1 = (bf16[64,2048]{1,0:T(8,128)(2,1)S(1)}, bf16[64,2048]{1,0:T(8,128)(2,1)S(1)}, u32[]{:S(2)}, u32[]{:S(2)}) collective-permute-start(bf16[64,2048]{1,0:T(8,128)(2,1)S(1)} %maximum_select_fusion.rest_0_), channel_id=1, source_target_pairs={{0,64},{64,128},{128,192},{192,256},{256,320},{320,384},{384,448},... | collective-permute-start | bytes 786440 | tf_op jit(solution)/shard_map/ppermute | solution.py:224
  64.9 37.6 %collective-permute-start.2 = (bf16[64,2048]{1,0:T(8,128)(2,1)S(1)}, bf16[64,2048]{1,0:T(8,128)(2,1)S(1)}, u32[]{:S(2)}, u32[]{:S(2)}) collective-permute-start(bf16[64,2048]{1,0:T(8,128)(2,1)S(1)} %maximum_select_fusion.rest_0_), channel_id=1, source_target_pairs={{0,128},{64,192},{128,256},{192,320},{256,384},{320,448},{384,0},{... | collective-permute-start | bytes 786440 | tf_op jit(solution)/shard_map/ppermute | solution.py:224
  67.4 35.1 %collective-permute-start.5 = (bf16[64,2048]{1,0:T(8,128)(2,1)S(1)}, bf16[64,2048]{1,0:T(8,128)(2,1)S(1)}, u32[]{:S(2)}, u32[]{:S(2)}) collective-permute-start(bf16[64,2048]{1,0:T(8,128)(2,1)S(1)} %maximum_select_fusion.rest_0_), channel_id=1, source_target_pairs={{0,320},{64,384},{128,448},{192,0},{256,64},{320,128},{384,192},{4... | collective-permute-start | bytes 786440 | tf_op jit(solution)/shard_map/ppermute | solution.py:224
  74.8 41.4 %copy-start.3 = (bf16[64,2048]{1,0:T(8,128)(2,1)}, bf16[64,2048]{1,0:T(8,128)(2,1)S(1)}, u32[]{:S(2)}) copy-start(bf16[64,2048]{1,0:T(8,128)(2,1)S(1)} %collective-permute-done.3.rest_3_) | copy-start | bytes 786436
  74.8 28.4 %collective-permute-start.6 = (bf16[64,2048]{1,0:T(8,128)(2,1)S(1)}, bf16[64,2048]{1,0:T(8,128)(2,1)S(1)}, u32[]{:S(2)}, u32[]{:S(2)}) collective-permute-start(bf16[64,2048]{1,0:T(8,128)(2,1)S(1)} %maximum_select_fusion.rest_0_), channel_id=1, source_target_pairs={{0,384},{64,448},{128,0},{192,64},{256,128},{320,192},{384,256},{4... | collective-permute-start | bytes 786440 | tf_op jit(solution)/shard_map/ppermute | solution.py:224
  94.2 22.1 %copy-start.4 = (bf16[64,2048]{1,0:T(8,128)(2,1)}, bf16[64,2048]{1,0:T(8,128)(2,1)S(1)}, u32[]{:S(2)}) copy-start(bf16[64,2048]{1,0:T(8,128)(2,1)S(1)} %collective-permute-done.4.rest_4_) | copy-start | bytes 786436
  94.2 14.4 %collective-permute-start.7 = (bf16[64,2048]{1,0:T(8,128)(2,1)S(1)}, bf16[64,2048]{1,0:T(8,128)(2,1)}, u32[]{:S(2)}, u32[]{:S(2)}) collective-permute-start(bf16[64,2048]{1,0:T(8,128)(2,1)S(1)} %maximum_select_fusion.rest_0_), channel_id=1, source_target_pairs={{0,448},{64,0},{128,64},{192,128},{256,192},{320,256},{384,320},{4... | collective-permute-start | bytes 786440 | tf_op jit(solution)/shard_map/ppermute | solution.py:224
  96.1 20.1 %copy-start.5 = (bf16[64,2048]{1,0:T(8,128)(2,1)}, bf16[64,2048]{1,0:T(8,128)(2,1)S(1)}, u32[]{:S(2)}) copy-start(bf16[64,2048]{1,0:T(8,128)(2,1)S(1)} %collective-permute-done.1.rest_1_) | copy-start | bytes 786436
  102.5 13.8 %copy-start.6 = (bf16[64,2048]{1,0:T(8,128)(2,1)}, bf16[64,2048]{1,0:T(8,128)(2,1)S(1)}, u32[]{:S(2)}) copy-start(bf16[64,2048]{1,0:T(8,128)(2,1)S(1)} %collective-permute-done.2.rest_2_) | copy-start | bytes 786436
  102.5 13.8 %copy-start.7 = (bf16[64,2048]{1,0:T(8,128)(2,1)}, bf16[64,2048]{1,0:T(8,128)(2,1)S(1)}, u32[]{:S(2)}) copy-start(bf16[64,2048]{1,0:T(8,128)(2,1)S(1)} %collective-permute-done.5.rest_5_) | copy-start | bytes 786436
  103.2 0.7 copy-start.8
  123.9 46.8 %all-to-all-start.2 = ((bf16[32,48,512]{2,1,0:T(8,128)(2,1)}), bf16[32,48,512]{2,1,0:T(8,128)(2,1)S(1)}, u32[]{:S(2)}, u32[]{:S(2)}) async-start(bf16[32,48,512]{2,1,0:T(8,128)(2,1)} %bitcast.21), calls=%async_computation.2 | async-start | bytes 3145728 | tf_op jit(solution)/shard_map/all_to_all | solution.py:262
  131.4 43.4 %copy-start.9 = (f32[32,2048]{1,0:T(8,128)S(1)}, f32[32,2048]{1,0:T(8,128)}, u32[]{:S(2)}) copy-start(f32[32,2048]{1,0:T(8,128)} %param.17) | copy-start | bytes 786436
  131.4 43.4 %copy-start.10 = (f32[32,2048]{1,0:T(8,128)S(1)}, f32[32,2048]{1,0:T(8,128)}, u32[]{:S(2)}) copy-start(f32[32,2048]{1,0:T(8,128)} %param.16) | copy-start | bytes 786436
  165.5 9.4 %copy-start.11 = (bf16[64,2048]{1,0:T(8,128)(2,1)S(1)}, bf16[64,2048]{1,0:T(8,128)(2,1)}, u32[]{:S(2)}) copy-start(bf16[64,2048]{1,0:T(8,128)(2,1)} %reduce-scatter.2.cloned.1.call-done) | copy-start | bytes 786436
  166.5 8.4 %collective-permute-start.8 = (bf16[32,2048]{1,0:T(8,128)(2,1)S(1)}, bf16[32,2048]{1,0:T(8,128)(2,1)S(1)}, u32[]{:S(2)}, u32[]{:S(2)}) collective-permute-start(bf16[32,2048]{1,0:T(8,128)(2,1)S(1)} %dynamic-slice_bitcast_fusion), channel_id=1, source_target_pairs={{0,32},{32,0},{1,33},{33,1},{2,34},{34,2},{3,35},{35,3},{4,36},{36... | collective-permute-start | bytes 393224 | tf_op jit(solution)/shard_map/ppermute | solution.py:284
Sparse Core Ops, SparseCore 0:
  42.9 67.0 all-gather.1
  116.4 49.0 reduce-scatter.1

commit v8 on v7

--- a/solution.py
+++ b/solution.py
@@ -23,10 +23,11 @@
 ALL = REP + EXP
 VMEM = pl.BlockSpec(memory_space=pltpu.VMEM)
 BIG = 56 * 1024 * 1024
-
-
-def params():
-    return pltpu.CompilerParams(vmem_limit_bytes=BIG)
+FULL = 63 * 1024 * 1024 + 512 * 1024
+
+
+def params(limit=BIG):
+    return pltpu.CompilerParams(vmem_limit_bytes=limit)
 
 
 def routing_rows(mod_ref, idx_ref):
@@ -49,30 +50,54 @@
     return rows
 
 
-def pack_grads_kernel(mod_ref, idx_ref, grad_ref, gate_ref, up_ref, out_ref):
-    rows = routing_rows(mod_ref, idx_ref)
-    routing = jnp.concatenate(rows, axis=0)
-    hidden = grad_ref.shape[1]
-    piece = out_ref.shape[3]
-    for start in range(0, hidden, piece):
-        cols = pl.ds(start, piece)
-        grad_val = grad_ref[:, cols].astype(jnp.float32)
-        gate_val = gate_ref[:, cols].astype(jnp.float32)
-        up_val = up_ref[:, cols].astype(jnp.float32)
+def pack_grads_kernel(mod_ref, idx_ref, *rest):
+    sources, rest = rest[:3], rest[3:]
+    out_ref, in_buf, out_buf, in_sems, out_sems = rest
+    hidden = in_buf.shape[2]
+    piece = out_buf.shape[3]
+    steps = hidden // piece
+    loads = []
+    for j in range(steps):
+        cols = pl.ds(j * piece, piece)
+        loads.append(
+            [
+                pltpu.make_async_copy(
+                    sources[i].at[:, cols], in_buf.at[i, :, cols], in_sems.at[3 * j + i]
+                )
+                for i in range(3)
+            ]
+        )
+    for group in loads:
+        for load in group:
+            load.start()
+    routing = jnp.concatenate(routing_rows(mod_ref, idx_ref), axis=0)
+    stores = []
+    for j in range(steps):
+        for load in loads[j]:
+            load.wait()
+        cols = pl.ds(j * piece, piece)
+        grad_val = in_buf[0, :, cols].astype(jnp.float32)
+        gate_val = in_buf[1, :, cols].astype(jnp.float32)
+        up_val = in_buf[2, :, cols].astype(jnp.float32)
         sig = 1.0 / (1.0 + jnp.exp(-gate_val))
         grad_gate = (grad_val * up_val * sig * (1.0 + gate_val * (1.0 - sig))).astype(jnp.bfloat16)
         grad_up = (grad_val * gate_val * sig).astype(jnp.bfloat16)
-        g = start // piece
-        for at, block in ((g, grad_gate), (g + GROUP // 2, grad_up)):
+        for at, block in ((j, grad_gate), (j + steps, grad_up)):
             packed = jnp.dot(routing, block, preferred_element_type=jnp.float32)
             packed = packed.astype(jnp.bfloat16)
             for e in range(EXPERTS):
-                out_ref[e, at] = packed[e * CAP : (e + 1) * CAP]
-
-
-def pack_rows_kernel(mod_ref, idx_ref, x_ref, out_ref):
-    rows = routing_rows(mod_ref, idx_ref)
-    routing = jnp.concatenate(rows, axis=0)
+                out_buf[at, e] = packed[e * CAP : (e + 1) * CAP]
+            stores.append(
+                pltpu.make_async_copy(out_buf.at[at], out_ref.at[:, at], out_sems.at[at])
+            )
+            stores[-1].start()
+    for store in stores:
+        store.wait()
+
+
+def pack_rows_kernel(mod_ref, idx_ref, x_ref, out_ref, routing_ref):
+    routing = jnp.concatenate(routing_rows(mod_ref, idx_ref), axis=0)
+    routing_ref[...] = routing
     piece = out_ref.shape[3]
     for g in range(GROUP):
         block = x_ref[:, g * piece : (g + 1) * piece]
@@ -81,16 +106,23 @@
             out_ref[e, g] = packed[e * CAP : (e + 1) * CAP]
 
 
-def combine_kernel(mod_ref, idx_ref, back_ref, out_ref):
-    rows = routing_rows(mod_ref, idx_ref)
-    routing = jnp.concatenate(rows, axis=0)
+def combine_kernel(routing_ref, back_ref, out_ref, out_buf, sems):
+    routing = routing_ref[...]
     piece = back_ref.shape[3]
+    stores = []
     for g in range(GROUP):
         block = jnp.concatenate([back_ref[e, g] for e in range(EXPERTS)], axis=0)
         total = lax.dot_general(
             routing, block, (((0,), (0,)), ((), ())), preferred_element_type=jnp.float32
         )
-        out_ref[:, g * piece : (g + 1) * piece] = total.astype(jnp.bfloat16)
+        cols = pl.ds(g * piece, piece)
+        out_buf[:, cols] = total.astype(jnp.bfloat16)
+        stores.append(
+            pltpu.make_async_copy(out_buf.at[:, cols], out_ref.at[:, cols], sems.at[g])
+        )
+        stores[-1].start()
+    for store in stores:
+        store.wait()
 
 
 def weight_grad_kernel(x_ref, g_ref, dw_ref, g_buf, xt_buf, dw_buf, g_sems, out_sems):
@@ -178,11 +210,18 @@
     half = lax.axis_index("xh")
     place = lax.axis_index("z").astype(jnp.int32).reshape(1)
 
+    anywhere = pl.BlockSpec(memory_space=pl.ANY)
     g_send = pl.pallas_call(
         pack_grads_kernel,
         out_shape=jax.ShapeDtypeStruct((EXPERTS, GROUP, CAP, gpiece), jnp.bfloat16),
-        in_specs=[VMEM] * 5,
-        out_specs=VMEM,
+        in_specs=[VMEM] * 2 + [anywhere] * 3,
+        out_specs=anywhere,
+        scratch_shapes=[
+            pltpu.VMEM((3, tok_count, hidden), jnp.bfloat16),
+            pltpu.VMEM((GROUP, EXPERTS, CAP, gpiece), jnp.bfloat16),
+            pltpu.SemaphoreType.DMA((3 * GROUP // 2,)),
+            pltpu.SemaphoreType.DMA((GROUP,)),
+        ],
         compiler_params=params(),
         name="pack_grads",
     )(mod, idx, grad_hidden, pre_gate, pre_up)
@@ -197,12 +236,15 @@
         jnp.concatenate([own_bf, came_bf], axis=0),
         jnp.concatenate([came_bf, own_bf], axis=0),
     )
-    x_send = pl.pallas_call(
+    x_send, routing = pl.pallas_call(
         pack_rows_kernel,
-        out_shape=jax.ShapeDtypeStruct((EXPERTS, GROUP, CAP, piece), jnp.bfloat16),
+        out_shape=(
+            jax.ShapeDtypeStruct((EXPERTS, GROUP, CAP, piece), jnp.bfloat16),
+            jax.ShapeDtypeStruct((EXPERTS * CAP, tok_count), jnp.bfloat16),
+        ),
         in_specs=[VMEM] * 3,
-        out_specs=VMEM,
-        compiler_params=params(),
+        out_specs=(VMEM, VMEM),
+        compiler_params=params(FULL),
         name="pack_rows",
     )(mod, idx, activations)
     g_recv, x_send, pair_late = lax.optimization_barrier((g_recv, x_send, pair_bf))
@@ -224,7 +266,6 @@
         shards.append(lax.ppermute(moved, "z", [(i, (i + k) % RING) for i in range(RING)]))
     g_all, x_rows, *shards = lax.optimization_barrier((g_all, x_rows, *shards))
 
-    anywhere = pl.BlockSpec(memory_space=pl.ANY)
     grad_part = pl.pallas_call(
         weight_grad_kernel,
         out_shape=jax.ShapeDtypeStruct((piece, 2 * hidden), jnp.bfloat16),
@@ -265,13 +306,16 @@
     input_grad = pl.pallas_call(
         combine_kernel,
         out_shape=jax.ShapeDtypeStruct((tok_count, width), jnp.bfloat16),
-        in_specs=[VMEM] * 3,
-        out_specs=VMEM,
+        in_specs=[VMEM] * 2,
+        out_specs=anywhere,
+        scratch_shapes=[
+            pltpu.VMEM((tok_count, width), jnp.bfloat16),
+            pltpu.SemaphoreType.DMA((GROUP,)),
+        ],
         compiler_params=params(),
         name="combine",
     )(
-        mod,
-        idx,
+        routing,
         pltpu.with_memory_space_constraint(
             back.reshape(EXPERTS, GROUP, CAP, piece), pltpu.VMEM
         ),

time: 184 us -> 184 us (level)
  waiting for transfers between devices: 66.9 us -> 64.6 us
where the time goes in v8:
time: 184 us; the launch traced here: 183 us
  starting transfers between devices  77.3 us (42%)
  waiting for transfers between devices  64.6 us (35%)
  Pallas kernels  22.4 us (12%)
  between operations  14.3 us (8%)
  other arithmetic  2.04 us (1%)
    ppermute x7, starting transfers between devices, body(): lax.ppermute(moved, 'z', [(i, (i + k) % RING) for i in range(RING)])  48.7 us
    reduce_scatter x1, waiting for transfers between devices, body(): grad_z = lax.psum_scatter(grad_part, 'z', scatter_dimension=0, tiled=True)  33.7 us
    ppermute x7, waiting for transfers between devices, body(): lax.ppermute(moved, 'z', [(i, (i + k) % RING) for i in range(RING)])  12.2 us
    all_to_all x1, waiting for transfers between devices, body(): lax.all_to_all(g_send.reshape(members, CAP, gpiece), EXP, split_axis=0, c...  9.88 us
    all_to_all x1, starting transfers between devices, body(): lax.all_to_all(g_send.reshape(members, CAP, gpiece), EXP, split_axis=0, c...  8.78 us
    all_to_all x1, starting transfers between devices, body(): lax.all_to_all(dx_rows.reshape(members, CAP, piece), EXP, split_axis=0, c...  7.56 us
    pallas_call x1, Pallas kernels, body(): pl.pallas_call(input_grad_kernel, out_shape=jax.ShapeDtypeStruct((rows_to...  7.53 us
    pallas_call x1, Pallas kernels, body(): pl.pallas_call(weight_grad_kernel, out_shape=jax.ShapeDtypeStruct((piece,...  6.23 us
  transfers between devices with their start and end apart: 14, of which 10 were waited for; matrix products, arithmetic and copies ran while one was open for 1% of the time, Pallas kernels for 7%

profile of v8, /device:TPU:6, one launch (start us, length us, event | category | flops | bytes accessed | tf_op | source)
XLA Modules:
  0.0 182.5 jit_solution(5957752888350262700)
XLA Ops:
  7.2 0.0 copy-start.1
  7.2 3.5 %pack_grads.1 = bf16[4,8,48,256]{3,2,1,0:T(8,128)(2,1)} custom-call(s32[1,128]{1,0:T(1,128)} %bitcast.25, s32[1,128]{1,0:T(1,128)} %bitcast.27, bf16[128,1024]{1,0:T(8,128)(2,1)} %rest_0_.1, bf16[128,1024]{1,0:T(8,128)(2,1)} %rest_1_.1, bf16[128,1024]{1,0:T(8,128)(2,1)} %rest_2_.1), custom_call_target="tpu_custom_call" | custom-call | tf_op jit(solution)/shard_map/pack_grads/pallas_call | solution.py:214
  10.7 8.8 %all-to-all-start = ((bf16[32,48,256]{2,1,0:T(8,128)(2,1)}), bf16[32,48,256]{2,1,0:T(8,128)(2,1)}, u32[]{:S(2)}, u32[]{:S(2)}) async-start(bf16[32,48,256]{2,1,0:T(8,128)(2,1)} %bitcast.21), calls=%async_computation | async-start | bytes 1572864 | tf_op jit(solution)/shard_map/all_to_all | solution.py:229
  19.5 0.0 all-gather.2.cloned.1.call-start
  19.6 0.0 copy-done.1
  19.6 4.7 %collective-permute-start = (bf16[32,2048]{1,0:T(8,128)(2,1)S(1)}, bf16[32,2048]{1,0:T(8,128)(2,1)}, u32[]{:S(2)}, u32[]{:S(2)}) collective-permute-start(bf16[32,2048]{1,0:T(8,128)(2,1)S(1)} %convert_element_type.12), channel_id=1, source_target_pairs={{0,32},{32,0},{1,33},{33,1},{2,34},{34,2},{3,35},{35,3},{4,36},{36... | collective-permute-start | bytes 393224 | tf_op jit(solution)/shard_map/ppermute | solution.py:233
  24.3 3.1 %pack_rows.1 = (bf16[4,8,48,512]{3,2,1,0:T(8,128)(2,1)}, bf16[192,128]{1,0:T(8,128)(2,1)}) custom-call(s32[1,128]{1,0:T(1,128)} %bitcast.26, s32[1,128]{1,0:T(1,128)} %bitcast.28, bf16[128,4096]{1,0:T(8,128)(2,1)} %x_ref), custom_call_target="tpu_custom_call" | custom-call | tf_op jit(solution)/shard_map/pack_rows/pallas_call | solution.py:239
  27.4 4.6 %collective-permute-done = bf16[32,2048]{1,0:T(8,128)(2,1)} collective-permute-done((bf16[32,2048]{1,0:T(8,128)(2,1)S(1)}, bf16[32,2048]{1,0:T(8,128)(2,1)}, u32[]{:S(2)}, u32[]{:S(2)}) %collective-permute-start) | collective-permute-done | bytes 131104 | tf_op jit(solution)/shard_map/ppermute | solution.py:233
  32.0 1.0 maximum_select_fusion.rest_0_
  33.0 0.0 copy-start
  33.0 9.9 %all-to-all-done = bf16[32,48,256]{2,1,0:T(8,128)(2,1)} async-done(((bf16[32,48,256]{2,1,0:T(8,128)(2,1)}), bf16[32,48,256]{2,1,0:T(8,128)(2,1)}, u32[]{:S(2)}, u32[]{:S(2)}) %all-to-all-start) | async-done | bytes 786464 | tf_op jit(solution)/shard_map/all_to_all | solution.py:229
  42.9 0.0 all-gather.2.cloned.1.call-update
  42.9 4.0 %all-to-all-start.1 = ((bf16[32,48,512]{2,1,0:T(8,128)(2,1)}), bf16[32,48,512]{2,1,0:T(8,128)(2,1)S(1)}, u32[]{:S(2)}, u32[]{:S(2)}) async-start(bf16[32,48,512]{2,1,0:T(8,128)(2,1)} %bitcast.22), calls=%async_computation.1 | async-start | bytes 3145728 | tf_op jit(solution)/shard_map/all_to_all | solution.py:259
  47.0 0.0 reduce-scatter.2.cloned.1.call-start
  47.0 7.9 %collective-permute-start.3 = (bf16[64,2048]{1,0:T(8,128)(2,1)S(1)}, bf16[64,2048]{1,0:T(8,128)(2,1)S(1)}, u32[]{:S(2)}, u32[]{:S(2)}) collective-permute-start(bf16[64,2048]{1,0:T(8,128)(2,1)S(1)} %maximum_select_fusion.rest_0_), channel_id=1, source_target_pairs={{0,192},{64,256},{128,320},{192,384},{256,448},{320,0},{384,64},{4... | collective-permute-start | bytes 786440 | tf_op jit(solution)/shard_map/ppermute | solution.py:266
  54.9 8.2 %collective-permute-start.4 = (bf16[64,2048]{1,0:T(8,128)(2,1)S(1)}, bf16[64,2048]{1,0:T(8,128)(2,1)S(1)}, u32[]{:S(2)}, u32[]{:S(2)}) collective-permute-start(bf16[64,2048]{1,0:T(8,128)(2,1)S(1)} %maximum_select_fusion.rest_0_), channel_id=1, source_target_pairs={{0,256},{64,320},{128,384},{192,448},{256,0},{320,64},{384,128},{4... | collective-permute-start | bytes 786440 | tf_op jit(solution)/shard_map/ppermute | solution.py:266
  63.2 1.9 %collective-permute-start.1 = (bf16[64,2048]{1,0:T(8,128)(2,1)S(1)}, bf16[64,2048]{1,0:T(8,128)(2,1)S(1)}, u32[]{:S(2)}, u32[]{:S(2)}) collective-permute-start(bf16[64,2048]{1,0:T(8,128)(2,1)S(1)} %maximum_select_fusion.rest_0_), channel_id=1, source_target_pairs={{0,64},{64,128},{128,192},{192,256},{256,320},{320,384},{384,448},... | collective-permute-start | bytes 786440 | tf_op jit(solution)/shard_map/ppermute | solution.py:266
  65.1 2.5 %collective-permute-start.2 = (bf16[64,2048]{1,0:T(8,128)(2,1)S(1)}, bf16[64,2048]{1,0:T(8,128)(2,1)S(1)}, u32[]{:S(2)}, u32[]{:S(2)}) collective-permute-start(bf16[64,2048]{1,0:T(8,128)(2,1)S(1)} %maximum_select_fusion.rest_0_), channel_id=1, source_target_pairs={{0,128},{64,192},{128,256},{192,320},{256,384},{320,448},{384,0},{... | collective-permute-start | bytes 786440 | tf_op jit(solution)/shard_map/ppermute | solution.py:266
  67.6 6.9 %collective-permute-start.5 = (bf16[64,2048]{1,0:T(8,128)(2,1)S(1)}, bf16[64,2048]{1,0:T(8,128)(2,1)S(1)}, u32[]{:S(2)}, u32[]{:S(2)}) collective-permute-start(bf16[64,2048]{1,0:T(8,128)(2,1)S(1)} %maximum_select_fusion.rest_0_), channel_id=1, source_target_pairs={{0,320},{64,384},{128,448},{192,0},{256,64},{320,128},{384,192},{4... | collective-permute-start | bytes 786440 | tf_op jit(solution)/shard_map/ppermute | solution.py:266
  74.5 0.5 collective-permute-done.3.rest_3_
  75.0 0.0 copy-start.2
  75.0 19.3 %collective-permute-start.6 = (bf16[64,2048]{1,0:T(8,128)(2,1)S(1)}, bf16[64,2048]{1,0:T(8,128)(2,1)S(1)}, u32[]{:S(2)}, u32[]{:S(2)}) collective-permute-start(bf16[64,2048]{1,0:T(8,128)(2,1)S(1)} %maximum_select_fusion.rest_0_), channel_id=1, source_target_pairs={{0,384},{64,448},{128,0},{192,64},{256,128},{320,192},{384,256},{4... | collective-permute-start | bytes 786440 | tf_op jit(solution)/shard_map/ppermute | solution.py:266
  94.3 0.0 collective-permute-done.4.rest_4_
  94.3 0.0 copy-done
  94.3 0.0 copy-start.3
  94.4 1.9 %collective-permute-start.7 = (bf16[64,2048]{1,0:T(8,128)(2,1)S(1)}, bf16[64,2048]{1,0:T(8,128)(2,1)}, u32[]{:S(2)}, u32[]{:S(2)}) collective-permute-start(bf16[64,2048]{1,0:T(8,128)(2,1)S(1)} %maximum_select_fusion.rest_0_), channel_id=1, source_target_pairs={{0,448},{64,0},{128,64},{192,128},{256,192},{320,256},{384,320},{4... | collective-permute-start | bytes 786440 | tf_op jit(solution)/shard_map/ppermute | solution.py:266
  96.3 0.0 collective-permute-done.1.rest_1_
  96.3 0.0 copy-start.4
  96.3 6.3 %collective-permute-done.2.rest_2_ = bf16[64,2048]{1,0:T(8,128)(2,1)S(1)} collective-permute-done((bf16[64,2048]{1,0:T(8,128)(2,1)S(1)}, bf16[64,2048]{1,0:T(8,128)(2,1)S(1)}, u32[]{:S(2)}, u32[]{:S(2)}) %collective-permute-start.2) | collective-permute-done | bytes 262176 | tf_op jit(solution)/shard_map/ppermute | solution.py:266
  102.6 0.0 copy-start.5
  102.6 0.0 collective-permute-done.5.rest_5_
  102.6 0.0 copy-start.6
  102.6 0.7 collective-permute-done.6.rest_6_
  103.4 0.0 copy-done.6
  103.4 0.0 copy-start.7
  103.4 0.7 copy-done.7
  104.1 4.7 %collective-permute-done.7.rest_7_ = bf16[64,2048]{1,0:T(8,128)(2,1)} collective-permute-done((bf16[64,2048]{1,0:T(8,128)(2,1)S(1)}, bf16[64,2048]{1,0:T(8,128)(2,1)}, u32[]{:S(2)}, u32[]{:S(2)}) %collective-permute-start.7) | collective-permute-done | bytes 262176 | tf_op jit(solution)/shard_map/ppermute | solution.py:266
  108.8 0.0 all-to-all-done.1
  108.8 1.4 all-gather.2.cloned.1.call-done.g_ref
  110.2 6.2 %weight_grad.1 = bf16[512,2048]{1,0:T(8,128)(2,1)} custom-call(bf16[1536,512]{1,0:T(8,128)(2,1)S(1)} %bitcast.18, bf16[8,1536,256]{2,1,0:T(8,128)(2,1)} %all-gather.2.cloned.1.call-done.g_ref), custom_call_target="tpu_custom_call" | custom-call | tf_op jit(solution)/shard_map/weight_grad/pallas_call | solution.py:269
  116.4 0.0 copy-done.2
  116.4 0.0 copy-done.3
  116.4 0.0 copy-done.4
  116.4 0.0 copy-done.5
  116.4 0.0 reduce-scatter.2.cloned.1.call-update
  116.5 7.5 %input_grad.1 = bf16[1536,512]{1,0:T(8,128)(2,1)} custom-call(s32[1]{0:T(128)} %bitcast.2.z_ref, bf16[8,1536,256]{2,1,0:T(8,128)(2,1)} %all-gather.2.cloned.1.call-done.g_ref, bf16[64,2048]{1,0:T(8,128)(2,1)} %copy-done, bf16[64,2048]{1,0:T(8,128)(2,1)} %copy-done.4, bf16[64,2048]{1,0:T(8,128)(2,1)} %copy-done.5, bf16[64,2048]{1,0:T(8,128)(2,1)} %copy-done.2, ...), custom_call_target="tpu_custom_call" | custom-call | tf_op jit(solution)/shard_map/input_grad/pallas_call | solution.py:287
  124.0 7.6 %all-to-all-start.2 = ((bf16[32,48,512]{2,1,0:T(8,128)(2,1)}), bf16[32,48,512]{2,1,0:T(8,128)(2,1)S(1)}, u32[]{:S(2)}, u32[]{:S(2)}) async-start(bf16[32,48,512]{2,1,0:T(8,128)(2,1)} %bitcast.20), calls=%async_computation.2 | async-start | bytes 3145728 | tf_op jit(solution)/shard_map/all_to_all | solution.py:303
  131.6 0.0 copy-start.8
  131.6 0.0 copy-start.9
  131.6 33.7 %reduce-scatter.2.cloned.1.call-done = bf16[64,2048]{1,0:T(8,128)(2,1)} async-done(((bf16[512,2048]{1,0:T(8,128)(2,1)}), bf16[64,2048]{1,0:T(8,128)(2,1)}) %reduce-scatter.2.cloned.1.call-update) | async-done | bytes 262160 | tf_op jit(solution)/shard_map/reduce_scatter | solution.py:284
  165.3 0.0 copy-start.10
  165.3 1.0 dynamic-slice_bitcast_fusion
  166.3 3.5 %collective-permute-start.8 = (bf16[32,2048]{1,0:T(8,128)(2,1)S(1)}, bf16[32,2048]{1,0:T(8,128)(2,1)S(1)}, u32[]{:S(2)}, u32[]{:S(2)}) collective-permute-start(bf16[32,2048]{1,0:T(8,128)(2,1)S(1)} %dynamic-slice_bitcast_fusion), channel_id=1, source_target_pairs={{0,32},{32,0},{1,33},{33,1},{2,34},{34,2},{3,35},{35,3},{4,36},{36... | collective-permute-start | bytes 393224 | tf_op jit(solution)/shard_map/ppermute | solution.py:328
  169.8 1.0 all-to-all-done.2
  170.8 2.0 %combine.1 = bf16[128,4096]{1,0:T(8,128)(2,1)} custom-call(bf16[192,128]{1,0:T(8,128)(2,1)} %get-tuple-element.32.routing_ref, bf16[4,8,48,512]{3,2,1,0:T(8,128)(2,1)S(1)} %bitcast.19), custom_call_target="tpu_custom_call" | custom-call | tf_op jit(solution)/shard_map/combine/pallas_call | solution.py:306
  172.8 1.8 %collective-permute-done.8 = bf16[32,2048]{1,0:T(8,128)(2,1)S(1)} collective-permute-done((bf16[32,2048]{1,0:T(8,128)(2,1)S(1)}, bf16[32,2048]{1,0:T(8,128)(2,1)S(1)}, u32[]{:S(2)}, u32[]{:S(2)}) %collective-permute-start.8) | collective-permute-done | bytes 131104 | tf_op jit(solution)/shard_map/ppermute | solution.py:328
  174.7 0.0 copy-done.8
  174.7 0.0 copy-done.9
  174.7 0.0 copy-done.10
  174.7 1.0 multiply_subtract_fusion
  (1 shorter events, 0.0 us)
Async XLA Ops:
  7.2 12.4 %copy-start.1 = (f32[32,2048]{1,0:T(8,128)S(1)}, f32[32,2048]{1,0:T(8,128)}, u32[]{:S(2)}) copy-start(f32[32,2048]{1,0:T(8,128)} %param.15) | copy-start | bytes 786436
  10.7 32.2 %all-to-all-start = ((bf16[32,48,256]{2,1,0:T(8,128)(2,1)}), bf16[32,48,256]{2,1,0:T(8,128)(2,1)}, u32[]{:S(2)}, u32[]{:S(2)}) async-start(bf16[32,48,256]{2,1,0:T(8,128)(2,1)} %bitcast.21), calls=%async_computation | async-start | bytes 1572864 | tf_op jit(solution)/shard_map/all_to_all | solution.py:229
  19.5 90.7 %all-gather.2.cloned.1.call-start = ((), (), s32[]{:S(2)}) async-start(), calls=%async_computation.4 | async-start | bytes 7077888 | tf_op jit(solution)/shard_map/all_gather | solution.py:252
  19.6 12.4 %collective-permute-start = (bf16[32,2048]{1,0:T(8,128)(2,1)S(1)}, bf16[32,2048]{1,0:T(8,128)(2,1)}, u32[]{:S(2)}, u32[]{:S(2)}) collective-permute-start(bf16[32,2048]{1,0:T(8,128)(2,1)S(1)} %convert_element_type.12), channel_id=1, source_target_pairs={{0,32},{32,0},{1,33},{33,1},{2,34},{34,2},{3,35},{35,3},{4,36},{36... | collective-permute-start | bytes 393224 | tf_op jit(solution)/shard_map/ppermute | solution.py:233
  33.0 61.3 %copy-start = (bf16[64,2048]{1,0:T(8,128)(2,1)}, bf16[64,2048]{1,0:T(8,128)(2,1)S(1)}, u32[]{:S(2)}) copy-start(bf16[64,2048]{1,0:T(8,128)(2,1)S(1)} %maximum_select_fusion.rest_0_) | copy-start | bytes 786436
  42.9 65.9 %all-to-all-start.1 = ((bf16[32,48,512]{2,1,0:T(8,128)(2,1)}), bf16[32,48,512]{2,1,0:T(8,128)(2,1)S(1)}, u32[]{:S(2)}, u32[]{:S(2)}) async-start(bf16[32,48,512]{2,1,0:T(8,128)(2,1)} %bitcast.22), calls=%async_computation.1 | async-start | bytes 3145728 | tf_op jit(solution)/shard_map/all_to_all | solution.py:259
  47.0 118.3 %reduce-scatter.2.cloned.1.call-start = ((), (), s32[]{:S(2)}) async-start(), calls=%async_computation.5 | async-start | bytes 2359296 | tf_op jit(solution)/shard_map/reduce_scatter | solution.py:284
  47.0 28.0 %collective-permute-start.3 = (bf16[64,2048]{1,0:T(8,128)(2,1)S(1)}, bf16[64,2048]{1,0:T(8,128)(2,1)S(1)}, u32[]{:S(2)}, u32[]{:S(2)}) collective-permute-start(bf16[64,2048]{1,0:T(8,128)(2,1)S(1)} %maximum_select_fusion.rest_0_), channel_id=1, source_target_pairs={{0,192},{64,256},{128,320},{192,384},{256,448},{320,0},{384,64},{4... | collective-permute-start | bytes 786440 | tf_op jit(solution)/shard_map/ppermute | solution.py:266
  54.9 39.4 %collective-permute-start.4 = (bf16[64,2048]{1,0:T(8,128)(2,1)S(1)}, bf16[64,2048]{1,0:T(8,128)(2,1)S(1)}, u32[]{:S(2)}, u32[]{:S(2)}) collective-permute-start(bf16[64,2048]{1,0:T(8,128)(2,1)S(1)} %maximum_select_fusion.rest_0_), channel_id=1, source_target_pairs={{0,256},{64,320},{128,384},{192,448},{256,0},{320,64},{384,128},{4... | collective-permute-start | bytes 786440 | tf_op jit(solution)/shard_map/ppermute | solution.py:266
  63.2 33.1 %collective-permute-start.1 = (bf16[64,2048]{1,0:T(8,128)(2,1)S(1)}, bf16[64,2048]{1,0:T(8,128)(2,1)S(1)}, u32[]{:S(2)}, u32[]{:S(2)}) collective-permute-start(bf16[64,2048]{1,0:T(8,128)(2,1)S(1)} %maximum_select_fusion.rest_0_), channel_id=1, source_target_pairs={{0,64},{64,128},{128,192},{192,256},{256,320},{320,384},{384,448},... | collective-permute-start | bytes 786440 | tf_op jit(solution)/shard_map/ppermute | solution.py:266
  65.1 37.5 %collective-permute-start.2 = (bf16[64,2048]{1,0:T(8,128)(2,1)S(1)}, bf16[64,2048]{1,0:T(8,128)(2,1)S(1)}, u32[]{:S(2)}, u32[]{:S(2)}) collective-permute-start(bf16[64,2048]{1,0:T(8,128)(2,1)S(1)} %maximum_select_fusion.rest_0_), channel_id=1, source_target_pairs={{0,128},{64,192},{128,256},{192,320},{256,384},{320,448},{384,0},{... | collective-permute-start | bytes 786440 | tf_op jit(solution)/shard_map/ppermute | solution.py:266
  67.6 35.1 %collective-permute-start.5 = (bf16[64,2048]{1,0:T(8,128)(2,1)S(1)}, bf16[64,2048]{1,0:T(8,128)(2,1)S(1)}, u32[]{:S(2)}, u32[]{:S(2)}) collective-permute-start(bf16[64,2048]{1,0:T(8,128)(2,1)S(1)} %maximum_select_fusion.rest_0_), channel_id=1, source_target_pairs={{0,320},{64,384},{128,448},{192,0},{256,64},{320,128},{384,192},{4... | collective-permute-start | bytes 786440 | tf_op jit(solution)/shard_map/ppermute | solution.py:266
  75.0 41.4 %copy-start.2 = (bf16[64,2048]{1,0:T(8,128)(2,1)}, bf16[64,2048]{1,0:T(8,128)(2,1)S(1)}, u32[]{:S(2)}) copy-start(bf16[64,2048]{1,0:T(8,128)(2,1)S(1)} %collective-permute-done.3.rest_3_) | copy-start | bytes 786436
  75.0 28.4 %collective-permute-start.6 = (bf16[64,2048]{1,0:T(8,128)(2,1)S(1)}, bf16[64,2048]{1,0:T(8,128)(2,1)S(1)}, u32[]{:S(2)}, u32[]{:S(2)}) collective-permute-start(bf16[64,2048]{1,0:T(8,128)(2,1)S(1)} %maximum_select_fusion.rest_0_), channel_id=1, source_target_pairs={{0,384},{64,448},{128,0},{192,64},{256,128},{320,192},{384,256},{4... | collective-permute-start | bytes 786440 | tf_op jit(solution)/shard_map/ppermute | solution.py:266
  94.3 22.1 %copy-start.3 = (bf16[64,2048]{1,0:T(8,128)(2,1)}, bf16[64,2048]{1,0:T(8,128)(2,1)S(1)}, u32[]{:S(2)}) copy-start(bf16[64,2048]{1,0:T(8,128)(2,1)S(1)} %collective-permute-done.4.rest_4_) | copy-start | bytes 786436
  94.4 14.4 %collective-permute-start.7 = (bf16[64,2048]{1,0:T(8,128)(2,1)S(1)}, bf16[64,2048]{1,0:T(8,128)(2,1)}, u32[]{:S(2)}, u32[]{:S(2)}) collective-permute-start(bf16[64,2048]{1,0:T(8,128)(2,1)S(1)} %maximum_select_fusion.rest_0_), channel_id=1, source_target_pairs={{0,448},{64,0},{128,64},{192,128},{256,192},{320,256},{384,320},{4... | collective-permute-start | bytes 786440 | tf_op jit(solution)/shard_map/ppermute | solution.py:266
  96.3 20.1 %copy-start.4 = (bf16[64,2048]{1,0:T(8,128)(2,1)}, bf16[64,2048]{1,0:T(8,128)(2,1)S(1)}, u32[]{:S(2)}) copy-start(bf16[64,2048]{1,0:T(8,128)(2,1)S(1)} %collective-permute-done.1.rest_1_) | copy-start | bytes 786436
  102.6 13.8 %copy-start.5 = (bf16[64,2048]{1,0:T(8,128)(2,1)}, bf16[64,2048]{1,0:T(8,128)(2,1)S(1)}, u32[]{:S(2)}) copy-start(bf16[64,2048]{1,0:T(8,128)(2,1)S(1)} %collective-permute-done.2.rest_2_) | copy-start | bytes 786436
  102.6 0.7 copy-start.6
  103.4 0.7 copy-start.7
  124.0 46.8 %all-to-all-start.2 = ((bf16[32,48,512]{2,1,0:T(8,128)(2,1)}), bf16[32,48,512]{2,1,0:T(8,128)(2,1)S(1)}, u32[]{:S(2)}, u32[]{:S(2)}) async-start(bf16[32,48,512]{2,1,0:T(8,128)(2,1)} %bitcast.20), calls=%async_computation.2 | async-start | bytes 3145728 | tf_op jit(solution)/shard_map/all_to_all | solution.py:303
  131.6 43.1 %copy-start.8 = (f32[32,2048]{1,0:T(8,128)S(1)}, f32[32,2048]{1,0:T(8,128)}, u32[]{:S(2)}) copy-start(f32[32,2048]{1,0:T(8,128)} %param.17) | copy-start | bytes 786436
  131.6 43.1 %copy-start.9 = (f32[32,2048]{1,0:T(8,128)S(1)}, f32[32,2048]{1,0:T(8,128)}, u32[]{:S(2)}) copy-start(f32[32,2048]{1,0:T(8,128)} %param.16) | copy-start | bytes 786436
  165.3 9.4 %copy-start.10 = (bf16[64,2048]{1,0:T(8,128)(2,1)S(1)}, bf16[64,2048]{1,0:T(8,128)(2,1)}, u32[]{:S(2)}) copy-start(bf16[64,2048]{1,0:T(8,128)(2,1)} %reduce-scatter.2.cloned.1.call-done) | copy-start | bytes 786436
  166.3 8.4 %collective-permute-start.8 = (bf16[32,2048]{1,0:T(8,128)(2,1)S(1)}, bf16[32,2048]{1,0:T(8,128)(2,1)S(1)}, u32[]{:S(2)}, u32[]{:S(2)}) collective-permute-start(bf16[32,2048]{1,0:T(8,128)(2,1)S(1)} %dynamic-slice_bitcast_fusion), channel_id=1, source_target_pairs={{0,32},{32,0},{1,33},{33,1},{2,34},{34,2},{3,35},{35,3},{4,36},{36... | collective-permute-start | bytes 393224 | tf_op jit(solution)/shard_map/ppermute | solution.py:328
Sparse Core Ops, SparseCore 0:
  43.0 67.0 all-gather.1
  116.6 48.6 reduce-scatter.1

commit v9 on v7

--- a/solution.py
+++ b/solution.py
@@ -23,10 +23,11 @@
 ALL = REP + EXP
 VMEM = pl.BlockSpec(memory_space=pltpu.VMEM)
 BIG = 56 * 1024 * 1024
-
-
-def params():
-    return pltpu.CompilerParams(vmem_limit_bytes=BIG)
+FULL = 63 * 1024 * 1024 + 512 * 1024
+
+
+def params(limit=BIG):
+    return pltpu.CompilerParams(vmem_limit_bytes=limit)
 
 
 def routing_rows(mod_ref, idx_ref):
@@ -70,9 +71,9 @@
                 out_ref[e, at] = packed[e * CAP : (e + 1) * CAP]
 
 
-def pack_rows_kernel(mod_ref, idx_ref, x_ref, out_ref):
-    rows = routing_rows(mod_ref, idx_ref)
-    routing = jnp.concatenate(rows, axis=0)
+def pack_rows_kernel(mod_ref, idx_ref, x_ref, out_ref, routing_ref):
+    routing = jnp.concatenate(routing_rows(mod_ref, idx_ref), axis=0)
+    routing_ref[...] = routing
     piece = out_ref.shape[3]
     for g in range(GROUP):
         block = x_ref[:, g * piece : (g + 1) * piece]
@@ -81,19 +82,30 @@
             out_ref[e, g] = packed[e * CAP : (e + 1) * CAP]
 
 
-def combine_kernel(mod_ref, idx_ref, back_ref, out_ref):
-    rows = routing_rows(mod_ref, idx_ref)
-    routing = jnp.concatenate(rows, axis=0)
+def combine_kernel(routing_ref, back_ref, out_ref, out_buf, sems):
+    routing = routing_ref[...]
     piece = back_ref.shape[3]
+    stores = []
     for g in range(GROUP):
         block = jnp.concatenate([back_ref[e, g] for e in range(EXPERTS)], axis=0)
         total = lax.dot_general(
             routing, block, (((0,), (0,)), ((), ())), preferred_element_type=jnp.float32
         )
-        out_ref[:, g * piece : (g + 1) * piece] = total.astype(jnp.bfloat16)
-
-
-def weight_grad_kernel(x_ref, g_ref, dw_ref, g_buf, xt_buf, dw_buf, g_sems, out_sems):
+        cols = pl.ds(g * piece, piece)
+        out_buf[:, cols] = total.astype(jnp.bfloat16)
+        stores.append(
+            pltpu.make_async_copy(out_buf.at[:, cols], out_ref.at[:, cols], sems.at[g])
+        )
+        stores[-1].start()
+    for store in stores:
+        store.wait()
+
+
+def turn_kernel(x_ref, xt_ref):
+    xt_ref[...] = x_ref[...].T
+
+
+def weight_grad_kernel(xt_ref, g_ref, dw_ref, g_buf, dw_buf, g_sems, out_sems):
     pairs = GROUP // 2
     loads = [
         pltpu.make_async_copy(g_ref.at[pl.ds(2 * j, 2)], g_buf.at[pl.ds(2 * j, 2)], g_sems.at[j])
@@ -101,7 +113,6 @@
     ]
     for load in loads:
         load.start()
-    xt_buf[...] = x_ref[...].T
     stores = []
     piece = g_buf.shape[2]
     for j in range(pairs):
@@ -109,7 +120,7 @@
         pair = jnp.concatenate([g_buf[2 * j], g_buf[2 * j + 1]], axis=1)
         cols = slice(2 * j * piece, (2 * j + 2) * piece)
         dw_buf[:, cols] = jnp.dot(
-            xt_buf[...], pair, preferred_element_type=jnp.float32
+            xt_ref[...], pair, preferred_element_type=jnp.float32
         ).astype(jnp.bfloat16)
         stores.append(
             pltpu.make_async_copy(dw_buf.at[:, cols], dw_ref.at[:, cols], out_sems.at[j])
@@ -178,6 +189,8 @@
     half = lax.axis_index("xh")
     place = lax.axis_index("z").astype(jnp.int32).reshape(1)
 
+    anywhere = pl.BlockSpec(memory_space=pl.ANY)
+    anywhere = pl.BlockSpec(memory_space=pl.ANY)
     g_send = pl.pallas_call(
         pack_grads_kernel,
         out_shape=jax.ShapeDtypeStruct((EXPERTS, GROUP, CAP, gpiece), jnp.bfloat16),
@@ -197,12 +210,15 @@
         jnp.concatenate([own_bf, came_bf], axis=0),
         jnp.concatenate([came_bf, own_bf], axis=0),
     )
-    x_send = pl.pallas_call(
+    x_send, routing = pl.pallas_call(
         pack_rows_kernel,
-        out_shape=jax.ShapeDtypeStruct((EXPERTS, GROUP, CAP, piece), jnp.bfloat16),
+        out_shape=(
+            jax.ShapeDtypeStruct((EXPERTS, GROUP, CAP, piece), jnp.bfloat16),
+            jax.ShapeDtypeStruct((EXPERTS * CAP, tok_count), jnp.bfloat16),
+        ),
         in_specs=[VMEM] * 3,
-        out_specs=VMEM,
-        compiler_params=params(),
+        out_specs=(VMEM, VMEM),
+        compiler_params=params(FULL),
         name="pack_rows",
     )(mod, idx, activations)
     g_recv, x_send, pair_late = lax.optimization_barrier((g_recv, x_send, pair_bf))
@@ -222,9 +238,16 @@
     for k in range(1, RING):
         moved = pair_bf if k in EARLY else pair_late
         shards.append(lax.ppermute(moved, "z", [(i, (i + k) % RING) for i in range(RING)]))
-    g_all, x_rows, *shards = lax.optimization_barrier((g_all, x_rows, *shards))
-
-    anywhere = pl.BlockSpec(memory_space=pl.ANY)
+    x_turned = pl.pallas_call(
+        turn_kernel,
+        out_shape=pltpu.VMEM((piece, rows_total), jnp.bfloat16),
+        in_specs=[VMEM],
+        out_specs=VMEM,
+        compiler_params=params(),
+        name="turn",
+    )(pltpu.with_memory_space_constraint(x_rows, pltpu.VMEM))
+    g_all, *shards = lax.optimization_barrier((g_all, *shards))
+
     grad_part = pl.pallas_call(
         weight_grad_kernel,
         out_shape=jax.ShapeDtypeStruct((piece, 2 * hidden), jnp.bfloat16),
@@ -232,14 +255,13 @@
         out_specs=anywhere,
         scratch_shapes=[
             pltpu.VMEM((GROUP, rows_total, gpiece), jnp.bfloat16),
-            pltpu.VMEM((piece, rows_total), jnp.bfloat16),
             pltpu.VMEM((piece, 2 * hidden), jnp.bfloat16),
             pltpu.SemaphoreType.DMA((GROUP // 2,)),
             pltpu.SemaphoreType.DMA((GROUP // 2,)),
         ],
         compiler_params=params(),
         name="weight_grad",
-    )(pltpu.with_memory_space_constraint(x_rows, pltpu.VMEM), g_all)
+    )(pltpu.with_memory_space_constraint(x_turned, pltpu.VMEM), g_all)
     grad_z = lax.psum_scatter(grad_part, "z", scatter_dimension=0, tiled=True)
 
     grad_part, g_all, *shards = lax.optimization_barrier((grad_part, g_all, *shards))
@@ -265,13 +287,16 @@
     input_grad = pl.pallas_call(
         combine_kernel,
         out_shape=jax.ShapeDtypeStruct((tok_count, width), jnp.bfloat16),
-        in_specs=[VMEM] * 3,
-        out_specs=VMEM,
+        in_specs=[VMEM] * 2,
+        out_specs=anywhere,
+        scratch_shapes=[
+            pltpu.VMEM((tok_count, width), jnp.bfloat16),
+            pltpu.SemaphoreType.DMA((GROUP,)),
+        ],
         compiler_params=params(),
         name="combine",
     )(
-        mod,
-        idx,
+        routing,
         pltpu.with_memory_space_constraint(
             back.reshape(EXPERTS, GROUP, CAP, piece), pltpu.VMEM
         ),

time: 184 us -> 183 us (level)
  transfers between devices with their start and end apart: 14 -> 14, of which waited for: 10 -> 11; matrix products, arithmetic and copies ran while one was open for 1% -> 1% of each run, Pallas kernels for 7% -> 7%
where the time goes in v9:
time: 183 us; the launch traced here: 182 us
  starting transfers between devices  77.1 us (42%)
  waiting for transfers between devices  65.3 us (36%)
  Pallas kernels  22.1 us (12%)
  between operations  14.3 us (8%)
  other arithmetic  2.04 us (1%)
    ppermute x7, starting transfers between devices, body(): lax.ppermute(moved, 'z', [(i, (i + k) % RING) for i in range(RING)])  48.7 us
    reduce_scatter x1, waiting for transfers between devices, body(): grad_z = lax.psum_scatter(grad_part, 'z', scatter_dimension=0, tiled=True)  33.9 us
    ppermute x7, waiting for transfers between devices, body(): lax.ppermute(moved, 'z', [(i, (i + k) % RING) for i in range(RING)])  10.8 us
    all_to_all x1, waiting for transfers between devices, body(): lax.all_to_all(g_send.reshape(members, CAP, gpiece), EXP, split_axis=0, c...  9.88 us
    all_to_all x1, starting transfers between devices, body(): lax.all_to_all(g_send.reshape(members, CAP, gpiece), EXP, split_axis=0, c...  8.77 us
    all_to_all x1, starting transfers between devices, body(): lax.all_to_all(dx_rows.reshape(members, CAP, piece), EXP, split_axis=0, c...  7.56 us
    pallas_call x1, Pallas kernels, body(): pl.pallas_call(input_grad_kernel, out_shape=jax.ShapeDtypeStruct((rows_to...  7.54 us
    pallas_call x1, Pallas kernels, body(): pl.pallas_call(weight_grad_kernel, out_shape=jax.ShapeDtypeStruct((piece,...  6.31 us
  transfers between devices with their start and end apart: 14, of which 11 were waited for; matrix products, arithmetic and copies ran while one was open for 1% of the time, Pallas kernels for 7%

profile of v9, /device:TPU:6, one launch (start us, length us, event | category | flops | bytes accessed | tf_op | source)
XLA Modules:
  0.0 181.8 jit_solution(9302425372556371183)
XLA Ops:
  7.2 0.0 copy-start.1
  7.2 2.6 %pack_grads.1 = bf16[4,8,48,256]{3,2,1,0:T(8,128)(2,1)} custom-call(s32[1,128]{1,0:T(1,128)} %bitcast.25, s32[1,128]{1,0:T(1,128)} %bitcast.27, bf16[128,1024]{1,0:T(8,128)(2,1)} %grad_ref.1, bf16[128,1024]{1,0:T(8,128)(2,1)} %gate_ref.1, bf16[128,1024]{1,0:T(8,128)(2,1)} %up_ref.1), custom_call_target="tpu_custom_call" | custom-call | tf_op jit(solution)/shard_map/pack_grads/pallas_call | solution.py:194
  9.8 8.8 %all-to-all-start = ((bf16[32,48,256]{2,1,0:T(8,128)(2,1)}), bf16[32,48,256]{2,1,0:T(8,128)(2,1)}, u32[]{:S(2)}, u32[]{:S(2)}) async-start(bf16[32,48,256]{2,1,0:T(8,128)(2,1)} %bitcast.21), calls=%async_computation | async-start | bytes 1572864 | tf_op jit(solution)/shard_map/all_to_all | solution.py:203
  18.6 0.0 all-gather.2.cloned.1.call-start
  18.6 0.0 copy-done.1
  18.7 4.7 %collective-permute-start = (bf16[32,2048]{1,0:T(8,128)(2,1)S(1)}, bf16[32,2048]{1,0:T(8,128)(2,1)}, u32[]{:S(2)}, u32[]{:S(2)}) collective-permute-start(bf16[32,2048]{1,0:T(8,128)(2,1)S(1)} %convert_element_type.12), channel_id=1, source_target_pairs={{0,32},{32,0},{1,33},{33,1},{2,34},{34,2},{3,35},{35,3},{4,36},{36... | collective-permute-start | bytes 393224 | tf_op jit(solution)/shard_map/ppermute | solution.py:207
  23.4 3.1 %pack_rows.1 = (bf16[4,8,48,512]{3,2,1,0:T(8,128)(2,1)}, bf16[192,128]{1,0:T(8,128)(2,1)}) custom-call(s32[1,128]{1,0:T(1,128)} %bitcast.26, s32[1,128]{1,0:T(1,128)} %bitcast.28, bf16[128,4096]{1,0:T(8,128)(2,1)} %x_ref), custom_call_target="tpu_custom_call" | custom-call | tf_op jit(solution)/shard_map/pack_rows/pallas_call | solution.py:213
  26.5 4.6 %collective-permute-done = bf16[32,2048]{1,0:T(8,128)(2,1)} collective-permute-done((bf16[32,2048]{1,0:T(8,128)(2,1)S(1)}, bf16[32,2048]{1,0:T(8,128)(2,1)}, u32[]{:S(2)}, u32[]{:S(2)}) %collective-permute-start) | collective-permute-done | bytes 131104 | tf_op jit(solution)/shard_map/ppermute | solution.py:207
  31.0 1.0 maximum_select_fusion.rest_0_
  32.1 0.0 copy-start
  32.1 9.9 %all-to-all-done = bf16[32,48,256]{2,1,0:T(8,128)(2,1)} async-done(((bf16[32,48,256]{2,1,0:T(8,128)(2,1)}), bf16[32,48,256]{2,1,0:T(8,128)(2,1)}, u32[]{:S(2)}, u32[]{:S(2)}) %all-to-all-start) | async-done | bytes 786464 | tf_op jit(solution)/shard_map/all_to_all | solution.py:203
  42.0 0.0 all-gather.2.cloned.1.call-update
  42.0 4.0 %all-to-all-start.1 = ((bf16[32,48,512]{2,1,0:T(8,128)(2,1)}), bf16[32,48,512]{2,1,0:T(8,128)(2,1)S(1)}, u32[]{:S(2)}, u32[]{:S(2)}) async-start(bf16[32,48,512]{2,1,0:T(8,128)(2,1)} %bitcast.22), calls=%async_computation.1 | async-start | bytes 3145728 | tf_op jit(solution)/shard_map/all_to_all | solution.py:233
  46.0 0.0 reduce-scatter.2.cloned.1.call-start
  46.1 7.9 %collective-permute-start.3 = (bf16[64,2048]{1,0:T(8,128)(2,1)S(1)}, bf16[64,2048]{1,0:T(8,128)(2,1)S(1)}, u32[]{:S(2)}, u32[]{:S(2)}) collective-permute-start(bf16[64,2048]{1,0:T(8,128)(2,1)S(1)} %maximum_select_fusion.rest_0_), channel_id=1, source_target_pairs={{0,192},{64,256},{128,320},{192,384},{256,448},{320,0},{384,64},{4... | collective-permute-start | bytes 786440 | tf_op jit(solution)/shard_map/ppermute | solution.py:240
  54.0 8.2 %collective-permute-start.4 = (bf16[64,2048]{1,0:T(8,128)(2,1)S(1)}, bf16[64,2048]{1,0:T(8,128)(2,1)S(1)}, u32[]{:S(2)}, u32[]{:S(2)}) collective-permute-start(bf16[64,2048]{1,0:T(8,128)(2,1)S(1)} %maximum_select_fusion.rest_0_), channel_id=1, source_target_pairs={{0,256},{64,320},{128,384},{192,448},{256,0},{320,64},{384,128},{4... | collective-permute-start | bytes 786440 | tf_op jit(solution)/shard_map/ppermute | solution.py:240
  62.2 1.9 %collective-permute-start.1 = (bf16[64,2048]{1,0:T(8,128)(2,1)S(1)}, bf16[64,2048]{1,0:T(8,128)(2,1)}, u32[]{:S(2)}, u32[]{:S(2)}) collective-permute-start(bf16[64,2048]{1,0:T(8,128)(2,1)S(1)} %maximum_select_fusion.rest_0_), channel_id=1, source_target_pairs={{0,64},{64,128},{128,192},{192,256},{256,320},{320,384},{384,448},... | collective-permute-start | bytes 786440 | tf_op jit(solution)/shard_map/ppermute | solution.py:240
  64.1 2.5 %collective-permute-start.2 = (bf16[64,2048]{1,0:T(8,128)(2,1)S(1)}, bf16[64,2048]{1,0:T(8,128)(2,1)}, u32[]{:S(2)}, u32[]{:S(2)}) collective-permute-start(bf16[64,2048]{1,0:T(8,128)(2,1)S(1)} %maximum_select_fusion.rest_0_), channel_id=1, source_target_pairs={{0,128},{64,192},{128,256},{192,320},{256,384},{320,448},{384,0},{... | collective-permute-start | bytes 786440 | tf_op jit(solution)/shard_map/ppermute | solution.py:240
  66.6 6.9 %collective-permute-start.5 = (bf16[64,2048]{1,0:T(8,128)(2,1)S(1)}, bf16[64,2048]{1,0:T(8,128)(2,1)}, u32[]{:S(2)}, u32[]{:S(2)}) collective-permute-start(bf16[64,2048]{1,0:T(8,128)(2,1)S(1)} %maximum_select_fusion.rest_0_), channel_id=1, source_target_pairs={{0,320},{64,384},{128,448},{192,0},{256,64},{320,128},{384,192},{4... | collective-permute-start | bytes 786440 | tf_op jit(solution)/shard_map/ppermute | solution.py:240
  73.6 0.5 collective-permute-done.3.rest_3_
  74.0 0.0 copy-start.3
  74.0 19.3 %collective-permute-start.6 = (bf16[64,2048]{1,0:T(8,128)(2,1)S(1)}, bf16[64,2048]{1,0:T(8,128)(2,1)}, u32[]{:S(2)}, u32[]{:S(2)}) collective-permute-start(bf16[64,2048]{1,0:T(8,128)(2,1)S(1)} %maximum_select_fusion.rest_0_), channel_id=1, source_target_pairs={{0,384},{64,448},{128,0},{192,64},{256,128},{320,192},{384,256},{4... | collective-permute-start | bytes 786440 | tf_op jit(solution)/shard_map/ppermute | solution.py:240
  93.4 0.0 collective-permute-done.4.rest_4_
  93.4 0.0 copy-done
  93.4 0.0 copy-start.4
  93.4 1.9 %collective-permute-start.7 = (bf16[64,2048]{1,0:T(8,128)(2,1)S(1)}, bf16[64,2048]{1,0:T(8,128)(2,1)}, u32[]{:S(2)}, u32[]{:S(2)}) collective-permute-start(bf16[64,2048]{1,0:T(8,128)(2,1)S(1)} %maximum_select_fusion.rest_0_), channel_id=1, source_target_pairs={{0,448},{64,0},{128,64},{192,128},{256,192},{320,256},{384,320},{4... | collective-permute-start | bytes 786440 | tf_op jit(solution)/shard_map/ppermute | solution.py:240
  95.4 1.7 all-to-all-done.1
  97.0 0.0 copy-done.3
  97.0 0.0 copy-done.4
  97.0 0.5 turn.1.xt_ref
  97.5 0.0 collective-permute-done.1.rest_1_
  97.5 4.3 %collective-permute-done.2.rest_2_ = bf16[64,2048]{1,0:T(8,128)(2,1)} collective-permute-done((bf16[64,2048]{1,0:T(8,128)(2,1)S(1)}, bf16[64,2048]{1,0:T(8,128)(2,1)}, u32[]{:S(2)}, u32[]{:S(2)}) %collective-permute-start.2) | collective-permute-done | bytes 262176 | tf_op jit(solution)/shard_map/ppermute | solution.py:240
  101.8 0.0 collective-permute-done.5.rest_5_
  101.8 0.7 collective-permute-done.6.rest_6_
  102.5 5.3 %collective-permute-done.7.rest_7_ = bf16[64,2048]{1,0:T(8,128)(2,1)} collective-permute-done((bf16[64,2048]{1,0:T(8,128)(2,1)S(1)}, bf16[64,2048]{1,0:T(8,128)(2,1)}, u32[]{:S(2)}, u32[]{:S(2)}) %collective-permute-start.7) | collective-permute-done | bytes 262176 | tf_op jit(solution)/shard_map/ppermute | solution.py:240
  107.8 1.4 all-gather.2.cloned.1.call-done.g_ref
  109.2 6.3 %weight_grad.1 = bf16[512,2048]{1,0:T(8,128)(2,1)} custom-call(bf16[512,1536]{1,0:T(8,128)(2,1)S(1)} %turn.1.xt_ref, bf16[8,1536,256]{2,1,0:T(8,128)(2,1)} %all-gather.2.cloned.1.call-done.g_ref), custom_call_target="tpu_custom_call" | custom-call | tf_op jit(solution)/shard_map/weight_grad/pallas_call | solution.py:251
  115.6 0.0 reduce-scatter.2.cloned.1.call-update
  115.6 7.5 %input_grad.1 = bf16[1536,512]{1,0:T(8,128)(2,1)} custom-call(s32[1]{0:T(128)} %bitcast.2.z_ref, bf16[8,1536,256]{2,1,0:T(8,128)(2,1)} %all-gather.2.cloned.1.call-done.g_ref, bf16[64,2048]{1,0:T(8,128)(2,1)} %copy-done, bf16[64,2048]{1,0:T(8,128)(2,1)} %collective-permute-done.1.rest_1_, bf16[64,2048]{1,0:T(8,128)(2,1)} %collective-permute-done.2.rest_2_, ...), custom_call_target="tpu_custom_call" | custom-call | tf_op jit(solution)/shard_map/input_grad/pallas_call | solution.py:268
  123.1 7.6 %all-to-all-start.2 = ((bf16[32,48,512]{2,1,0:T(8,128)(2,1)}), bf16[32,48,512]{2,1,0:T(8,128)(2,1)S(1)}, u32[]{:S(2)}, u32[]{:S(2)}) async-start(bf16[32,48,512]{2,1,0:T(8,128)(2,1)} %bitcast.20), calls=%async_computation.2 | async-start | bytes 3145728 | tf_op jit(solution)/shard_map/all_to_all | solution.py:284
  130.7 0.0 copy-start.2
  130.7 0.0 copy-start.5
  130.7 0.0 copy-start.6
  130.7 33.9 %reduce-scatter.2.cloned.1.call-done = bf16[64,2048]{1,0:T(8,128)(2,1)} async-done(((bf16[512,2048]{1,0:T(8,128)(2,1)}), bf16[64,2048]{1,0:T(8,128)(2,1)}) %reduce-scatter.2.cloned.1.call-update) | async-done | bytes 262160 | tf_op jit(solution)/shard_map/reduce_scatter | solution.py:265
  164.6 0.0 copy-start.7
  164.6 1.0 dynamic-slice_bitcast_fusion
  165.6 3.2 %collective-permute-start.8 = (bf16[32,2048]{1,0:T(8,128)(2,1)S(1)}, bf16[32,2048]{1,0:T(8,128)(2,1)S(1)}, u32[]{:S(2)}, u32[]{:S(2)}) collective-permute-start(bf16[32,2048]{1,0:T(8,128)(2,1)S(1)} %dynamic-slice_bitcast_fusion), channel_id=1, source_target_pairs={{0,32},{32,0},{1,33},{33,1},{2,34},{34,2},{3,35},{35,3},{4,36},{36... | collective-permute-start | bytes 393224 | tf_op jit(solution)/shard_map/ppermute | solution.py:309
  168.9 1.0 all-to-all-done.2
  169.9 2.0 %combine.1 = bf16[128,4096]{1,0:T(8,128)(2,1)} custom-call(bf16[192,128]{1,0:T(8,128)(2,1)} %get-tuple-element.31.routing_ref, bf16[4,8,48,512]{3,2,1,0:T(8,128)(2,1)S(1)} %bitcast.19), custom_call_target="tpu_custom_call" | custom-call | tf_op jit(solution)/shard_map/combine/pallas_call | solution.py:287
  172.0 2.0 %collective-permute-done.8 = bf16[32,2048]{1,0:T(8,128)(2,1)S(1)} collective-permute-done((bf16[32,2048]{1,0:T(8,128)(2,1)S(1)}, bf16[32,2048]{1,0:T(8,128)(2,1)S(1)}, u32[]{:S(2)}, u32[]{:S(2)}) %collective-permute-start.8) | collective-permute-done | bytes 131104 | tf_op jit(solution)/shard_map/ppermute | solution.py:309
  174.0 0.0 copy-done.2
  174.0 0.0 copy-done.5
  174.0 0.0 copy-done.6
  174.0 0.0 copy-done.7
  174.0 1.0 multiply_subtract_fusion
  (1 shorter events, 0.0 us)
Async XLA Ops:
  7.2 11.5 %copy-start.1 = (f32[32,2048]{1,0:T(8,128)S(1)}, f32[32,2048]{1,0:T(8,128)}, u32[]{:S(2)}) copy-start(f32[32,2048]{1,0:T(8,128)} %param.15) | copy-start | bytes 786436
  9.8 32.2 %all-to-all-start = ((bf16[32,48,256]{2,1,0:T(8,128)(2,1)}), bf16[32,48,256]{2,1,0:T(8,128)(2,1)}, u32[]{:S(2)}, u32[]{:S(2)}) async-start(bf16[32,48,256]{2,1,0:T(8,128)(2,1)} %bitcast.21), calls=%async_computation | async-start | bytes 1572864 | tf_op jit(solution)/shard_map/all_to_all | solution.py:203
  18.6 90.7 %all-gather.2.cloned.1.call-start = ((), (), s32[]{:S(2)}) async-start(), calls=%async_computation.4 | async-start | bytes 7077888 | tf_op jit(solution)/shard_map/all_gather | solution.py:226
  18.7 12.4 %collective-permute-start = (bf16[32,2048]{1,0:T(8,128)(2,1)S(1)}, bf16[32,2048]{1,0:T(8,128)(2,1)}, u32[]{:S(2)}, u32[]{:S(2)}) collective-permute-start(bf16[32,2048]{1,0:T(8,128)(2,1)S(1)} %convert_element_type.12), channel_id=1, source_target_pairs={{0,32},{32,0},{1,33},{33,1},{2,34},{34,2},{3,35},{35,3},{4,36},{36... | collective-permute-start | bytes 393224 | tf_op jit(solution)/shard_map/ppermute | solution.py:207
  32.1 61.3 %copy-start = (bf16[64,2048]{1,0:T(8,128)(2,1)}, bf16[64,2048]{1,0:T(8,128)(2,1)S(1)}, u32[]{:S(2)}) copy-start(bf16[64,2048]{1,0:T(8,128)(2,1)S(1)} %maximum_select_fusion.rest_0_) | copy-start | bytes 786436
  42.0 55.0 %all-to-all-start.1 = ((bf16[32,48,512]{2,1,0:T(8,128)(2,1)}), bf16[32,48,512]{2,1,0:T(8,128)(2,1)S(1)}, u32[]{:S(2)}, u32[]{:S(2)}) async-start(bf16[32,48,512]{2,1,0:T(8,128)(2,1)} %bitcast.22), calls=%async_computation.1 | async-start | bytes 3145728 | tf_op jit(solution)/shard_map/all_to_all | solution.py:233
  46.0 118.6 %reduce-scatter.2.cloned.1.call-start = ((), (), s32[]{:S(2)}) async-start(), calls=%async_computation.5 | async-start | bytes 2359296 | tf_op jit(solution)/shard_map/reduce_scatter | solution.py:265
  46.1 27.9 %collective-permute-start.3 = (bf16[64,2048]{1,0:T(8,128)(2,1)S(1)}, bf16[64,2048]{1,0:T(8,128)(2,1)S(1)}, u32[]{:S(2)}, u32[]{:S(2)}) collective-permute-start(bf16[64,2048]{1,0:T(8,128)(2,1)S(1)} %maximum_select_fusion.rest_0_), channel_id=1, source_target_pairs={{0,192},{64,256},{128,320},{192,384},{256,448},{320,0},{384,64},{4... | collective-permute-start | bytes 786440 | tf_op jit(solution)/shard_map/ppermute | solution.py:240
  54.0 39.4 %collective-permute-start.4 = (bf16[64,2048]{1,0:T(8,128)(2,1)S(1)}, bf16[64,2048]{1,0:T(8,128)(2,1)S(1)}, u32[]{:S(2)}, u32[]{:S(2)}) collective-permute-start(bf16[64,2048]{1,0:T(8,128)(2,1)S(1)} %maximum_select_fusion.rest_0_), channel_id=1, source_target_pairs={{0,256},{64,320},{128,384},{192,448},{256,0},{320,64},{384,128},{4... | collective-permute-start | bytes 786440 | tf_op jit(solution)/shard_map/ppermute | solution.py:240
  62.2 35.3 %collective-permute-start.1 = (bf16[64,2048]{1,0:T(8,128)(2,1)S(1)}, bf16[64,2048]{1,0:T(8,128)(2,1)}, u32[]{:S(2)}, u32[]{:S(2)}) collective-permute-start(bf16[64,2048]{1,0:T(8,128)(2,1)S(1)} %maximum_select_fusion.rest_0_), channel_id=1, source_target_pairs={{0,64},{64,128},{128,192},{192,256},{256,320},{320,384},{384,448},... | collective-permute-start | bytes 786440 | tf_op jit(solution)/shard_map/ppermute | solution.py:240
  64.1 37.6 %collective-permute-start.2 = (bf16[64,2048]{1,0:T(8,128)(2,1)S(1)}, bf16[64,2048]{1,0:T(8,128)(2,1)}, u32[]{:S(2)}, u32[]{:S(2)}) collective-permute-start(bf16[64,2048]{1,0:T(8,128)(2,1)S(1)} %maximum_select_fusion.rest_0_), channel_id=1, source_target_pairs={{0,128},{64,192},{128,256},{192,320},{256,384},{320,448},{384,0},{... | collective-permute-start | bytes 786440 | tf_op jit(solution)/shard_map/ppermute | solution.py:240
  66.6 35.2 %collective-permute-start.5 = (bf16[64,2048]{1,0:T(8,128)(2,1)S(1)}, bf16[64,2048]{1,0:T(8,128)(2,1)}, u32[]{:S(2)}, u32[]{:S(2)}) collective-permute-start(bf16[64,2048]{1,0:T(8,128)(2,1)S(1)} %maximum_select_fusion.rest_0_), channel_id=1, source_target_pairs={{0,320},{64,384},{128,448},{192,0},{256,64},{320,128},{384,192},{4... | collective-permute-start | bytes 786440 | tf_op jit(solution)/shard_map/ppermute | solution.py:240
  74.0 23.0 %copy-start.3 = (bf16[64,2048]{1,0:T(8,128)(2,1)}, bf16[64,2048]{1,0:T(8,128)(2,1)S(1)}, u32[]{:S(2)}) copy-start(bf16[64,2048]{1,0:T(8,128)(2,1)S(1)} %collective-permute-done.3.rest_3_) | copy-start | bytes 786436
  74.0 28.5 %collective-permute-start.6 = (bf16[64,2048]{1,0:T(8,128)(2,1)S(1)}, bf16[64,2048]{1,0:T(8,128)(2,1)}, u32[]{:S(2)}, u32[]{:S(2)}) collective-permute-start(bf16[64,2048]{1,0:T(8,128)(2,1)S(1)} %maximum_select_fusion.rest_0_), channel_id=1, source_target_pairs={{0,384},{64,448},{128,0},{192,64},{256,128},{320,192},{384,256},{4... | collective-permute-start | bytes 786440 | tf_op jit(solution)/shard_map/ppermute | solution.py:240
  93.4 3.6 %copy-start.4 = (bf16[64,2048]{1,0:T(8,128)(2,1)}, bf16[64,2048]{1,0:T(8,128)(2,1)S(1)}, u32[]{:S(2)}) copy-start(bf16[64,2048]{1,0:T(8,128)(2,1)S(1)} %collective-permute-done.4.rest_4_) | copy-start | bytes 786436
  93.4 14.4 %collective-permute-start.7 = (bf16[64,2048]{1,0:T(8,128)(2,1)S(1)}, bf16[64,2048]{1,0:T(8,128)(2,1)}, u32[]{:S(2)}, u32[]{:S(2)}) collective-permute-start(bf16[64,2048]{1,0:T(8,128)(2,1)S(1)} %maximum_select_fusion.rest_0_), channel_id=1, source_target_pairs={{0,448},{64,0},{128,64},{192,128},{256,192},{320,256},{384,320},{4... | collective-permute-start | bytes 786440 | tf_op jit(solution)/shard_map/ppermute | solution.py:240
  123.1 46.8 %all-to-all-start.2 = ((bf16[32,48,512]{2,1,0:T(8,128)(2,1)}), bf16[32,48,512]{2,1,0:T(8,128)(2,1)S(1)}, u32[]{:S(2)}, u32[]{:S(2)}) async-start(bf16[32,48,512]{2,1,0:T(8,128)(2,1)} %bitcast.20), calls=%async_computation.2 | async-start | bytes 3145728 | tf_op jit(solution)/shard_map/all_to_all | solution.py:284
  130.7 43.3 %copy-start.2 = (f32[32,2048]{1,0:T(8,128)S(1)}, f32[32,2048]{1,0:T(8,128)}, u32[]{:S(2)}) copy-start(f32[32,2048]{1,0:T(8,128)} %param.15) | copy-start | bytes 786436
  130.7 43.3 %copy-start.5 = (f32[32,2048]{1,0:T(8,128)S(1)}, f32[32,2048]{1,0:T(8,128)}, u32[]{:S(2)}) copy-start(f32[32,2048]{1,0:T(8,128)} %param.17) | copy-start | bytes 786436
  130.7 43.3 %copy-start.6 = (f32[32,2048]{1,0:T(8,128)S(1)}, f32[32,2048]{1,0:T(8,128)}, u32[]{:S(2)}) copy-start(f32[32,2048]{1,0:T(8,128)} %param.16) | copy-start | bytes 786436
  164.6 9.4 %copy-start.7 = (bf16[64,2048]{1,0:T(8,128)(2,1)S(1)}, bf16[64,2048]{1,0:T(8,128)(2,1)}, u32[]{:S(2)}) copy-start(bf16[64,2048]{1,0:T(8,128)(2,1)} %reduce-scatter.2.cloned.1.call-done) | copy-start | bytes 786436
  165.6 8.4 %collective-permute-start.8 = (bf16[32,2048]{1,0:T(8,128)(2,1)S(1)}, bf16[32,2048]{1,0:T(8,128)(2,1)S(1)}, u32[]{:S(2)}, u32[]{:S(2)}) collective-permute-start(bf16[32,2048]{1,0:T(8,128)(2,1)S(1)} %dynamic-slice_bitcast_fusion), channel_id=1, source_target_pairs={{0,32},{32,0},{1,33},{33,1},{2,34},{34,2},{3,35},{35,3},{4,36},{36... | collective-permute-start | bytes 393224 | tf_op jit(solution)/shard_map/ppermute | solution.py:309
Sparse Core Ops, SparseCore 0:
  42.1 67.0 all-gather.1
  115.7 48.8 reduce-scatter.1

commit v10 on v9

--- a/solution.py
+++ b/solution.py
@@ -35,13 +35,13 @@
     count = expert.shape[1]
     onehot = (
         lax.broadcasted_iota(jnp.int32, (8, count), 0) == jnp.broadcast_to(expert, (8, count))
-    ).astype(jnp.float32)
+    ).astype(jnp.bfloat16)
     earlier = (
         lax.broadcasted_iota(jnp.int32, (count, count), 0)
         < lax.broadcasted_iota(jnp.int32, (count, count), 1)
-    ).astype(jnp.float32)
+    ).astype(jnp.bfloat16)
     before = jnp.dot(onehot, earlier, preferred_element_type=jnp.float32)
-    pos = jnp.sum(before * onehot, axis=0, keepdims=True).astype(jnp.int32)
+    pos = jnp.sum(before * onehot.astype(jnp.float32), axis=0, keepdims=True).astype(jnp.int32)
     slot = lax.broadcasted_iota(jnp.int32, (CAP, count), 0)
     rows = [
         jnp.where((slot == pos) & (expert == e), 1.0, 0.0).astype(jnp.bfloat16)
@@ -111,12 +111,14 @@
         pltpu.make_async_copy(g_ref.at[pl.ds(2 * j, 2)], g_buf.at[pl.ds(2 * j, 2)], g_sems.at[j])
         for j in range(pairs)
     ]
-    for load in loads:
+    for load in loads[:-1]:
         load.start()
     stores = []
     piece = g_buf.shape[2]
     for j in range(pairs):
         loads[j].wait()
+        if j == 0:
+            loads[-1].start()
         pair = jnp.concatenate([g_buf[2 * j], g_buf[2 * j + 1]], axis=1)
         cols = slice(2 * j * piece, (2 * j + 2) * piece)
         dw_buf[:, cols] = jnp.dot(
@@ -140,19 +142,22 @@
         w_loads.append(
             pltpu.make_async_copy(shards[k], w_buf.at[pl.ds(at, rows)], w_sems.at[k])
         )
-    block = dx_buf.shape[0] // DX_BLOCKS
-    parts = [slice(j * block, (j + 1) * block) for j in range(DX_BLOCKS)]
+    total = dx_buf.shape[0]
+    edges = [0, total // 6, total * 7 // 12, total]
+    parts = [slice(edges[j], edges[j + 1]) for j in range(DX_BLOCKS)]
     loads = [
         pltpu.make_async_copy(g_ref.at[:, part], g_buf.at[:, part], g_sems.at[j])
         for j, part in enumerate(parts)
     ]
-    for load in w_loads + loads:
+    for load in w_loads + loads[:-1]:
         load.start()
     for load in w_loads:
         load.wait()
     stores = []
     for j, part in enumerate(parts):
         loads[j].wait()
+        if j == 0:
+            loads[-1].start()
         grads = jnp.concatenate([g_buf[g, part] for g in range(GROUP)], axis=1)
         dx_buf[part] = lax.dot_general(
             grads, w_buf[...], (((1,), (1,)), ((), ())), preferred_element_type=jnp.float32

time: 183 us -> 183 us (level)
  no operation moved by 1% of the time
where the time goes in v10:
time: 183 us; the launch traced here: 182 us
  starting transfers between devices  77.3 us (42%)
  waiting for transfers between devices  65.7 us (36%)
  Pallas kernels  21.3 us (12%)
  between operations  14.3 us (8%)
  other arithmetic  2.04 us (1%)
    ppermute x7, starting transfers between devices, body(): lax.ppermute(moved, 'z', [(i, (i + k) % RING) for i in range(RING)])  48.7 us
    reduce_scatter x1, waiting for transfers between devices, body(): grad_z = lax.psum_scatter(grad_part, 'z', scatter_dimension=0, tiled=True)  34.5 us
    ppermute x7, waiting for transfers between devices, body(): lax.ppermute(moved, 'z', [(i, (i + k) % RING) for i in range(RING)])  10.8 us
    all_to_all x1, waiting for transfers between devices, body(): lax.all_to_all(g_send.reshape(members, CAP, gpiece), EXP, split_axis=0, c...  9.88 us
    all_to_all x1, starting transfers between devices, body(): lax.all_to_all(g_send.reshape(members, CAP, gpiece), EXP, split_axis=0, c...  8.77 us
    all_to_all x1, starting transfers between devices, body(): lax.all_to_all(dx_rows.reshape(members, CAP, piece), EXP, split_axis=0, c...  7.56 us
    pallas_call x1, Pallas kernels, body(): pl.pallas_call(input_grad_kernel, out_shape=jax.ShapeDtypeStruct((rows_to...  6.78 us
    pallas_call x1, Pallas kernels, body(): pl.pallas_call(weight_grad_kernel, out_shape=jax.ShapeDtypeStruct((piece,...  6.31 us
  transfers between devices with their start and end apart: 14, of which 11 were waited for; matrix products, arithmetic and copies ran while one was open for 1% of the time, Pallas kernels for 7%

profile of v10, /device:TPU:6, one launch (start us, length us, event | category | flops | bytes accessed | tf_op | source)
XLA Modules:
  0.0 181.7 jit_solution(12319088458489020109)
XLA Ops:
  7.2 0.0 copy-start.1
  7.2 2.6 %pack_grads.1 = bf16[4,8,48,256]{3,2,1,0:T(8,128)(2,1)} custom-call(s32[1,128]{1,0:T(1,128)} %bitcast.25, s32[1,128]{1,0:T(1,128)} %bitcast.27, bf16[128,1024]{1,0:T(8,128)(2,1)} %grad_ref.1, bf16[128,1024]{1,0:T(8,128)(2,1)} %gate_ref.1, bf16[128,1024]{1,0:T(8,128)(2,1)} %up_ref.1), custom_call_target="tpu_custom_call" | custom-call | tf_op jit(solution)/shard_map/pack_grads/pallas_call | solution.py:199
  9.8 8.8 %all-to-all-start = ((bf16[32,48,256]{2,1,0:T(8,128)(2,1)}), bf16[32,48,256]{2,1,0:T(8,128)(2,1)}, u32[]{:S(2)}, u32[]{:S(2)}) async-start(bf16[32,48,256]{2,1,0:T(8,128)(2,1)} %bitcast.21), calls=%async_computation | async-start | bytes 1572864 | tf_op jit(solution)/shard_map/all_to_all | solution.py:208
  18.6 0.0 all-gather.2.cloned.1.call-start
  18.6 0.0 copy-done.1
  18.7 4.7 %collective-permute-start = (bf16[32,2048]{1,0:T(8,128)(2,1)S(1)}, bf16[32,2048]{1,0:T(8,128)(2,1)}, u32[]{:S(2)}, u32[]{:S(2)}) collective-permute-start(bf16[32,2048]{1,0:T(8,128)(2,1)S(1)} %convert_element_type.12), channel_id=1, source_target_pairs={{0,32},{32,0},{1,33},{33,1},{2,34},{34,2},{3,35},{35,3},{4,36},{36... | collective-permute-start | bytes 393224 | tf_op jit(solution)/shard_map/ppermute | solution.py:212
  23.4 3.1 %pack_rows.1 = (bf16[4,8,48,512]{3,2,1,0:T(8,128)(2,1)}, bf16[192,128]{1,0:T(8,128)(2,1)}) custom-call(s32[1,128]{1,0:T(1,128)} %bitcast.26, s32[1,128]{1,0:T(1,128)} %bitcast.28, bf16[128,4096]{1,0:T(8,128)(2,1)} %x_ref), custom_call_target="tpu_custom_call" | custom-call | tf_op jit(solution)/shard_map/pack_rows/pallas_call | solution.py:218
  26.5 4.5 %collective-permute-done = bf16[32,2048]{1,0:T(8,128)(2,1)} collective-permute-done((bf16[32,2048]{1,0:T(8,128)(2,1)S(1)}, bf16[32,2048]{1,0:T(8,128)(2,1)}, u32[]{:S(2)}, u32[]{:S(2)}) %collective-permute-start) | collective-permute-done | bytes 131104 | tf_op jit(solution)/shard_map/ppermute | solution.py:212
  31.0 1.0 maximum_select_fusion.rest_0_
  32.1 0.0 copy-start
  32.1 9.9 %all-to-all-done = bf16[32,48,256]{2,1,0:T(8,128)(2,1)} async-done(((bf16[32,48,256]{2,1,0:T(8,128)(2,1)}), bf16[32,48,256]{2,1,0:T(8,128)(2,1)}, u32[]{:S(2)}, u32[]{:S(2)}) %all-to-all-start) | async-done | bytes 786464 | tf_op jit(solution)/shard_map/all_to_all | solution.py:208
  42.0 0.0 all-gather.2.cloned.1.call-update
  42.0 4.0 %all-to-all-start.1 = ((bf16[32,48,512]{2,1,0:T(8,128)(2,1)}), bf16[32,48,512]{2,1,0:T(8,128)(2,1)S(1)}, u32[]{:S(2)}, u32[]{:S(2)}) async-start(bf16[32,48,512]{2,1,0:T(8,128)(2,1)} %bitcast.22), calls=%async_computation.1 | async-start | bytes 3145728 | tf_op jit(solution)/shard_map/all_to_all | solution.py:238
  46.0 0.0 reduce-scatter.2.cloned.1.call-start
  46.1 7.9 %collective-permute-start.3 = (bf16[64,2048]{1,0:T(8,128)(2,1)S(1)}, bf16[64,2048]{1,0:T(8,128)(2,1)S(1)}, u32[]{:S(2)}, u32[]{:S(2)}) collective-permute-start(bf16[64,2048]{1,0:T(8,128)(2,1)S(1)} %maximum_select_fusion.rest_0_), channel_id=1, source_target_pairs={{0,192},{64,256},{128,320},{192,384},{256,448},{320,0},{384,64},{4... | collective-permute-start | bytes 786440 | tf_op jit(solution)/shard_map/ppermute | solution.py:245
  54.0 8.2 %collective-permute-start.4 = (bf16[64,2048]{1,0:T(8,128)(2,1)S(1)}, bf16[64,2048]{1,0:T(8,128)(2,1)S(1)}, u32[]{:S(2)}, u32[]{:S(2)}) collective-permute-start(bf16[64,2048]{1,0:T(8,128)(2,1)S(1)} %maximum_select_fusion.rest_0_), channel_id=1, source_target_pairs={{0,256},{64,320},{128,384},{192,448},{256,0},{320,64},{384,128},{4... | collective-permute-start | bytes 786440 | tf_op jit(solution)/shard_map/ppermute | solution.py:245
  62.2 1.9 %collective-permute-start.1 = (bf16[64,2048]{1,0:T(8,128)(2,1)S(1)}, bf16[64,2048]{1,0:T(8,128)(2,1)}, u32[]{:S(2)}, u32[]{:S(2)}) collective-permute-start(bf16[64,2048]{1,0:T(8,128)(2,1)S(1)} %maximum_select_fusion.rest_0_), channel_id=1, source_target_pairs={{0,64},{64,128},{128,192},{192,256},{256,320},{320,384},{384,448},... | collective-permute-start | bytes 786440 | tf_op jit(solution)/shard_map/ppermute | solution.py:245
  64.1 2.5 %collective-permute-start.2 = (bf16[64,2048]{1,0:T(8,128)(2,1)S(1)}, bf16[64,2048]{1,0:T(8,128)(2,1)}, u32[]{:S(2)}, u32[]{:S(2)}) collective-permute-start(bf16[64,2048]{1,0:T(8,128)(2,1)S(1)} %maximum_select_fusion.rest_0_), channel_id=1, source_target_pairs={{0,128},{64,192},{128,256},{192,320},{256,384},{320,448},{384,0},{... | collective-permute-start | bytes 786440 | tf_op jit(solution)/shard_map/ppermute | solution.py:245
  66.6 6.9 %collective-permute-start.5 = (bf16[64,2048]{1,0:T(8,128)(2,1)S(1)}, bf16[64,2048]{1,0:T(8,128)(2,1)}, u32[]{:S(2)}, u32[]{:S(2)}) collective-permute-start(bf16[64,2048]{1,0:T(8,128)(2,1)S(1)} %maximum_select_fusion.rest_0_), channel_id=1, source_target_pairs={{0,320},{64,384},{128,448},{192,0},{256,64},{320,128},{384,192},{4... | collective-permute-start | bytes 786440 | tf_op jit(solution)/shard_map/ppermute | solution.py:245
  73.6 0.5 collective-permute-done.3.rest_3_
  74.0 0.0 copy-start.3
  74.0 19.3 %collective-permute-start.6 = (bf16[64,2048]{1,0:T(8,128)(2,1)S(1)}, bf16[64,2048]{1,0:T(8,128)(2,1)}, u32[]{:S(2)}, u32[]{:S(2)}) collective-permute-start(bf16[64,2048]{1,0:T(8,128)(2,1)S(1)} %maximum_select_fusion.rest_0_), channel_id=1, source_target_pairs={{0,384},{64,448},{128,0},{192,64},{256,128},{320,192},{384,256},{4... | collective-permute-start | bytes 786440 | tf_op jit(solution)/shard_map/ppermute | solution.py:245
  93.4 0.0 collective-permute-done.4.rest_4_
  93.4 0.0 copy-done
  93.4 0.0 copy-start.4
  93.4 1.9 %collective-permute-start.7 = (bf16[64,2048]{1,0:T(8,128)(2,1)S(1)}, bf16[64,2048]{1,0:T(8,128)(2,1)}, u32[]{:S(2)}, u32[]{:S(2)}) collective-permute-start(bf16[64,2048]{1,0:T(8,128)(2,1)S(1)} %maximum_select_fusion.rest_0_), channel_id=1, source_target_pairs={{0,448},{64,0},{128,64},{192,128},{256,192},{320,256},{384,320},{4... | collective-permute-start | bytes 786440 | tf_op jit(solution)/shard_map/ppermute | solution.py:245
  95.4 1.7 all-to-all-done.1
  97.0 0.0 copy-done.3
  97.0 0.0 copy-done.4
  97.0 0.5 turn.1.xt_ref
  97.5 0.0 collective-permute-done.1.rest_1_
  97.5 4.3 %collective-permute-done.2.rest_2_ = bf16[64,2048]{1,0:T(8,128)(2,1)} collective-permute-done((bf16[64,2048]{1,0:T(8,128)(2,1)S(1)}, bf16[64,2048]{1,0:T(8,128)(2,1)}, u32[]{:S(2)}, u32[]{:S(2)}) %collective-permute-start.2) | collective-permute-done | bytes 262176 | tf_op jit(solution)/shard_map/ppermute | solution.py:245
  101.8 0.0 collective-permute-done.5.rest_5_
  101.8 0.7 collective-permute-done.6.rest_6_
  102.5 5.3 %collective-permute-done.7.rest_7_ = bf16[64,2048]{1,0:T(8,128)(2,1)} collective-permute-done((bf16[64,2048]{1,0:T(8,128)(2,1)S(1)}, bf16[64,2048]{1,0:T(8,128)(2,1)}, u32[]{:S(2)}, u32[]{:S(2)}) %collective-permute-start.7) | collective-permute-done | bytes 262176 | tf_op jit(solution)/shard_map/ppermute | solution.py:245
  107.8 1.4 all-gather.2.cloned.1.call-done.g_ref
  109.2 6.3 %weight_grad.1 = bf16[512,2048]{1,0:T(8,128)(2,1)} custom-call(bf16[512,1536]{1,0:T(8,128)(2,1)S(1)} %turn.1.xt_ref, bf16[8,1536,256]{2,1,0:T(8,128)(2,1)} %all-gather.2.cloned.1.call-done.g_ref), custom_call_target="tpu_custom_call" | custom-call | tf_op jit(solution)/shard_map/weight_grad/pallas_call | solution.py:256
  115.5 0.0 reduce-scatter.2.cloned.1.call-update
  115.6 6.8 %input_grad.1 = bf16[1536,512]{1,0:T(8,128)(2,1)} custom-call(s32[1]{0:T(128)} %bitcast.2.z_ref, bf16[8,1536,256]{2,1,0:T(8,128)(2,1)} %all-gather.2.cloned.1.call-done.g_ref, bf16[64,2048]{1,0:T(8,128)(2,1)} %copy-done, bf16[64,2048]{1,0:T(8,128)(2,1)} %collective-permute-done.1.rest_1_, bf16[64,2048]{1,0:T(8,128)(2,1)} %collective-permute-done.2.rest_2_, ...), custom_call_target="tpu_custom_call" | custom-call | tf_op jit(solution)/shard_map/input_grad/pallas_call | solution.py:273
  122.4 7.6 %all-to-all-start.2 = ((bf16[32,48,512]{2,1,0:T(8,128)(2,1)}), bf16[32,48,512]{2,1,0:T(8,128)(2,1)S(1)}, u32[]{:S(2)}, u32[]{:S(2)}) async-start(bf16[32,48,512]{2,1,0:T(8,128)(2,1)} %bitcast.20), calls=%async_computation.2 | async-start | bytes 3145728 | tf_op jit(solution)/shard_map/all_to_all | solution.py:289
  129.9 0.0 copy-start.2
  129.9 0.0 copy-start.5
  130.0 0.0 copy-start.6
  130.0 34.5 %reduce-scatter.2.cloned.1.call-done = bf16[64,2048]{1,0:T(8,128)(2,1)} async-done(((bf16[512,2048]{1,0:T(8,128)(2,1)}), bf16[64,2048]{1,0:T(8,128)(2,1)}) %reduce-scatter.2.cloned.1.call-update) | async-done | bytes 262160 | tf_op jit(solution)/shard_map/reduce_scatter | solution.py:270
  164.5 0.0 copy-start.7
  164.5 1.0 dynamic-slice_bitcast_fusion
  165.5 3.4 %collective-permute-start.8 = (bf16[32,2048]{1,0:T(8,128)(2,1)S(1)}, bf16[32,2048]{1,0:T(8,128)(2,1)S(1)}, u32[]{:S(2)}, u32[]{:S(2)}) collective-permute-start(bf16[32,2048]{1,0:T(8,128)(2,1)S(1)} %dynamic-slice_bitcast_fusion), channel_id=1, source_target_pairs={{0,32},{32,0},{1,33},{33,1},{2,34},{34,2},{3,35},{35,3},{4,36},{36... | collective-permute-start | bytes 393224 | tf_op jit(solution)/shard_map/ppermute | solution.py:314
  169.0 0.2 all-to-all-done.2
  169.1 2.0 %combine.1 = bf16[128,4096]{1,0:T(8,128)(2,1)} custom-call(bf16[192,128]{1,0:T(8,128)(2,1)} %get-tuple-element.31.routing_ref, bf16[4,8,48,512]{3,2,1,0:T(8,128)(2,1)S(1)} %bitcast.19), custom_call_target="tpu_custom_call" | custom-call | tf_op jit(solution)/shard_map/combine/pallas_call | solution.py:292
  171.2 2.7 %collective-permute-done.8 = bf16[32,2048]{1,0:T(8,128)(2,1)S(1)} collective-permute-done((bf16[32,2048]{1,0:T(8,128)(2,1)S(1)}, bf16[32,2048]{1,0:T(8,128)(2,1)S(1)}, u32[]{:S(2)}, u32[]{:S(2)}) %collective-permute-start.8) | collective-permute-done | bytes 131104 | tf_op jit(solution)/shard_map/ppermute | solution.py:314
  173.9 0.0 copy-done.2
  173.9 0.0 copy-done.5
  173.9 0.0 copy-done.6
  173.9 0.0 copy-done.7
  173.9 1.0 multiply_subtract_fusion
  (1 shorter events, 0.0 us)
Async XLA Ops:
  7.2 11.5 %copy-start.1 = (f32[32,2048]{1,0:T(8,128)S(1)}, f32[32,2048]{1,0:T(8,128)}, u32[]{:S(2)}) copy-start(f32[32,2048]{1,0:T(8,128)} %param.15) | copy-start | bytes 786436
  9.8 32.2 %all-to-all-start = ((bf16[32,48,256]{2,1,0:T(8,128)(2,1)}), bf16[32,48,256]{2,1,0:T(8,128)(2,1)}, u32[]{:S(2)}, u32[]{:S(2)}) async-start(bf16[32,48,256]{2,1,0:T(8,128)(2,1)} %bitcast.21), calls=%async_computation | async-start | bytes 1572864 | tf_op jit(solution)/shard_map/all_to_all | solution.py:208
  18.6 90.7 %all-gather.2.cloned.1.call-start = ((), (), s32[]{:S(2)}) async-start(), calls=%async_computation.4 | async-start | bytes 7077888 | tf_op jit(solution)/shard_map/all_gather | solution.py:231
  18.7 12.4 %collective-permute-start = (bf16[32,2048]{1,0:T(8,128)(2,1)S(1)}, bf16[32,2048]{1,0:T(8,128)(2,1)}, u32[]{:S(2)}, u32[]{:S(2)}) collective-permute-start(bf16[32,2048]{1,0:T(8,128)(2,1)S(1)} %convert_element_type.12), channel_id=1, source_target_pairs={{0,32},{32,0},{1,33},{33,1},{2,34},{34,2},{3,35},{35,3},{4,36},{36... | collective-permute-start | bytes 393224 | tf_op jit(solution)/shard_map/ppermute | solution.py:212
  32.1 61.3 %copy-start = (bf16[64,2048]{1,0:T(8,128)(2,1)}, bf16[64,2048]{1,0:T(8,128)(2,1)S(1)}, u32[]{:S(2)}) copy-start(bf16[64,2048]{1,0:T(8,128)(2,1)S(1)} %maximum_select_fusion.rest_0_) | copy-start | bytes 786436
  42.0 55.0 %all-to-all-start.1 = ((bf16[32,48,512]{2,1,0:T(8,128)(2,1)}), bf16[32,48,512]{2,1,0:T(8,128)(2,1)S(1)}, u32[]{:S(2)}, u32[]{:S(2)}) async-start(bf16[32,48,512]{2,1,0:T(8,128)(2,1)} %bitcast.22), calls=%async_computation.1 | async-start | bytes 3145728 | tf_op jit(solution)/shard_map/all_to_all | solution.py:238
  46.0 118.5 %reduce-scatter.2.cloned.1.call-start = ((), (), s32[]{:S(2)}) async-start(), calls=%async_computation.5 | async-start | bytes 2359296 | tf_op jit(solution)/shard_map/reduce_scatter | solution.py:270
  46.1 28.0 %collective-permute-start.3 = (bf16[64,2048]{1,0:T(8,128)(2,1)S(1)}, bf16[64,2048]{1,0:T(8,128)(2,1)S(1)}, u32[]{:S(2)}, u32[]{:S(2)}) collective-permute-start(bf16[64,2048]{1,0:T(8,128)(2,1)S(1)} %maximum_select_fusion.rest_0_), channel_id=1, source_target_pairs={{0,192},{64,256},{128,320},{192,384},{256,448},{320,0},{384,64},{4... | collective-permute-start | bytes 786440 | tf_op jit(solution)/shard_map/ppermute | solution.py:245
  54.0 39.4 %collective-permute-start.4 = (bf16[64,2048]{1,0:T(8,128)(2,1)S(1)}, bf16[64,2048]{1,0:T(8,128)(2,1)S(1)}, u32[]{:S(2)}, u32[]{:S(2)}) collective-permute-start(bf16[64,2048]{1,0:T(8,128)(2,1)S(1)} %maximum_select_fusion.rest_0_), channel_id=1, source_target_pairs={{0,256},{64,320},{128,384},{192,448},{256,0},{320,64},{384,128},{4... | collective-permute-start | bytes 786440 | tf_op jit(solution)/shard_map/ppermute | solution.py:245
  62.2 35.3 %collective-permute-start.1 = (bf16[64,2048]{1,0:T(8,128)(2,1)S(1)}, bf16[64,2048]{1,0:T(8,128)(2,1)}, u32[]{:S(2)}, u32[]{:S(2)}) collective-permute-start(bf16[64,2048]{1,0:T(8,128)(2,1)S(1)} %maximum_select_fusion.rest_0_), channel_id=1, source_target_pairs={{0,64},{64,128},{128,192},{192,256},{256,320},{320,384},{384,448},... | collective-permute-start | bytes 786440 | tf_op jit(solution)/shard_map/ppermute | solution.py:245
  64.1 37.6 %collective-permute-start.2 = (bf16[64,2048]{1,0:T(8,128)(2,1)S(1)}, bf16[64,2048]{1,0:T(8,128)(2,1)}, u32[]{:S(2)}, u32[]{:S(2)}) collective-permute-start(bf16[64,2048]{1,0:T(8,128)(2,1)S(1)} %maximum_select_fusion.rest_0_), channel_id=1, source_target_pairs={{0,128},{64,192},{128,256},{192,320},{256,384},{320,448},{384,0},{... | collective-permute-start | bytes 786440 | tf_op jit(solution)/shard_map/ppermute | solution.py:245
  66.6 35.2 %collective-permute-start.5 = (bf16[64,2048]{1,0:T(8,128)(2,1)S(1)}, bf16[64,2048]{1,0:T(8,128)(2,1)}, u32[]{:S(2)}, u32[]{:S(2)}) collective-permute-start(bf16[64,2048]{1,0:T(8,128)(2,1)S(1)} %maximum_select_fusion.rest_0_), channel_id=1, source_target_pairs={{0,320},{64,384},{128,448},{192,0},{256,64},{320,128},{384,192},{4... | collective-permute-start | bytes 786440 | tf_op jit(solution)/shard_map/ppermute | solution.py:245
  74.0 23.0 %copy-start.3 = (bf16[64,2048]{1,0:T(8,128)(2,1)}, bf16[64,2048]{1,0:T(8,128)(2,1)S(1)}, u32[]{:S(2)}) copy-start(bf16[64,2048]{1,0:T(8,128)(2,1)S(1)} %collective-permute-done.3.rest_3_) | copy-start | bytes 786436
  74.0 28.5 %collective-permute-start.6 = (bf16[64,2048]{1,0:T(8,128)(2,1)S(1)}, bf16[64,2048]{1,0:T(8,128)(2,1)}, u32[]{:S(2)}, u32[]{:S(2)}) collective-permute-start(bf16[64,2048]{1,0:T(8,128)(2,1)S(1)} %maximum_select_fusion.rest_0_), channel_id=1, source_target_pairs={{0,384},{64,448},{128,0},{192,64},{256,128},{320,192},{384,256},{4... | collective-permute-start | bytes 786440 | tf_op jit(solution)/shard_map/ppermute | solution.py:245
  93.4 3.6 %copy-start.4 = (bf16[64,2048]{1,0:T(8,128)(2,1)}, bf16[64,2048]{1,0:T(8,128)(2,1)S(1)}, u32[]{:S(2)}) copy-start(bf16[64,2048]{1,0:T(8,128)(2,1)S(1)} %collective-permute-done.4.rest_4_) | copy-start | bytes 786436
  93.4 14.4 %collective-permute-start.7 = (bf16[64,2048]{1,0:T(8,128)(2,1)S(1)}, bf16[64,2048]{1,0:T(8,128)(2,1)}, u32[]{:S(2)}, u32[]{:S(2)}) collective-permute-start(bf16[64,2048]{1,0:T(8,128)(2,1)S(1)} %maximum_select_fusion.rest_0_), channel_id=1, source_target_pairs={{0,448},{64,0},{128,64},{192,128},{256,192},{320,256},{384,320},{4... | collective-permute-start | bytes 786440 | tf_op jit(solution)/shard_map/ppermute | solution.py:245
  122.4 46.8 %all-to-all-start.2 = ((bf16[32,48,512]{2,1,0:T(8,128)(2,1)}), bf16[32,48,512]{2,1,0:T(8,128)(2,1)S(1)}, u32[]{:S(2)}, u32[]{:S(2)}) async-start(bf16[32,48,512]{2,1,0:T(8,128)(2,1)} %bitcast.20), calls=%async_computation.2 | async-start | bytes 3145728 | tf_op jit(solution)/shard_map/all_to_all | solution.py:289
  129.9 43.9 %copy-start.2 = (f32[32,2048]{1,0:T(8,128)S(1)}, f32[32,2048]{1,0:T(8,128)}, u32[]{:S(2)}) copy-start(f32[32,2048]{1,0:T(8,128)} %param.15) | copy-start | bytes 786436
  129.9 43.9 %copy-start.5 = (f32[32,2048]{1,0:T(8,128)S(1)}, f32[32,2048]{1,0:T(8,128)}, u32[]{:S(2)}) copy-start(f32[32,2048]{1,0:T(8,128)} %param.17) | copy-start | bytes 786436
  130.0 43.9 %copy-start.6 = (f32[32,2048]{1,0:T(8,128)S(1)}, f32[32,2048]{1,0:T(8,128)}, u32[]{:S(2)}) copy-start(f32[32,2048]{1,0:T(8,128)} %param.16) | copy-start | bytes 786436
  164.5 9.4 %copy-start.7 = (bf16[64,2048]{1,0:T(8,128)(2,1)S(1)}, bf16[64,2048]{1,0:T(8,128)(2,1)}, u32[]{:S(2)}) copy-start(bf16[64,2048]{1,0:T(8,128)(2,1)} %reduce-scatter.2.cloned.1.call-done) | copy-start | bytes 786436
  165.5 8.4 %collective-permute-start.8 = (bf16[32,2048]{1,0:T(8,128)(2,1)S(1)}, bf16[32,2048]{1,0:T(8,128)(2,1)S(1)}, u32[]{:S(2)}, u32[]{:S(2)}) collective-permute-start(bf16[32,2048]{1,0:T(8,128)(2,1)S(1)} %dynamic-slice_bitcast_fusion), channel_id=1, source_target_pairs={{0,32},{32,0},{1,33},{33,1},{2,34},{34,2},{3,35},{35,3},{4,36},{36... | collective-permute-start | bytes 393224 | tf_op jit(solution)/shard_map/ppermute | solution.py:314
Sparse Core Ops, SparseCore 0:
  42.1 67.0 all-gather.1
  115.7 48.7 reduce-scatter.1

commit v11 on v10

--- a/solution.py
+++ b/solution.py
@@ -270,10 +270,15 @@
     grad_z = lax.psum_scatter(grad_part, "z", scatter_dimension=0, tiled=True)
 
     grad_part, g_all, *shards = lax.optimization_barrier((grad_part, g_all, *shards))
+    near = [
+        shard if k in EARLY else pltpu.with_memory_space_constraint(shard, pltpu.VMEM)
+        for k, shard in enumerate(shards)
+    ]
     dx_rows = pl.pallas_call(
         input_grad_kernel,
         out_shape=jax.ShapeDtypeStruct((rows_total, piece), jnp.bfloat16),
-        in_specs=[pl.BlockSpec(memory_space=pltpu.SMEM)] + [anywhere] * (RING + 1),
+        in_specs=[pl.BlockSpec(memory_space=pltpu.SMEM), anywhere]
+        + [anywhere if k in EARLY else VMEM for k in range(RING)],
         out_specs=anywhere,
         scratch_shapes=[
             pltpu.VMEM((GROUP, rows_total, gpiece), jnp.bfloat16),
@@ -285,7 +290,7 @@
         ],
         compiler_params=params(),
         name="input_grad",
-    )(place, g_all, *shards)
+    )(place, g_all, *near)
     back = lax.all_to_all(
         dx_rows.reshape(members, CAP, piece), EXP, split_axis=0, concat_axis=0, tiled=True
     )

time: 183 us -> 183 us (level)
  no operation moved by 1% of the time
where the time goes in v11:
time: 183 us; the launch traced here: 182 us
  starting transfers between devices  77.3 us (42%)
  waiting for transfers between devices  65.3 us (36%)
  Pallas kernels  22.1 us (12%)
  between operations  14.3 us (8%)
    ppermute x7, starting transfers between devices, body(): lax.ppermute(moved, 'z', [(i, (i + k) % RING) for i in range(RING)])  48.7 us
    reduce_scatter x1, waiting for transfers between devices, body(): grad_z = lax.psum_scatter(grad_part, 'z', scatter_dimension=0, tiled=True)  33.8 us
    all_to_all x1, waiting for transfers between devices, body(): lax.all_to_all(g_send.reshape(members, CAP, gpiece), EXP, split_axis=0, c...  11 us
    ppermute x7, waiting for transfers between devices, body(): lax.ppermute(moved, 'z', [(i, (i + k) % RING) for i in range(RING)])  10.8 us
    all_to_all x1, starting transfers between devices, body(): lax.all_to_all(g_send.reshape(members, CAP, gpiece), EXP, split_axis=0, c...  8.77 us
    pallas_call x1, Pallas kernels, body(): pl.pallas_call(input_grad_kernel, out_shape=jax.ShapeDtypeStruct((rows_to...  7.65 us
    all_to_all x1, starting transfers between devices, body(): lax.all_to_all(dx_rows.reshape(members, CAP, piece), EXP, split_axis=0, c...  7.56 us
    pallas_call x1, Pallas kernels, body(): pl.pallas_call(weight_grad_kernel, out_shape=jax.ShapeDtypeStruct((piece,...  6.23 us
  transfers between devices with their start and end apart: 14, of which 11 were waited for; matrix products, arithmetic and copies ran while one was open for 1% of the time, Pallas kernels for 7%

profile of v11, /device:TPU:6, one launch (start us, length us, event | category | flops | bytes accessed | tf_op | source)
XLA Modules:
  0.0 181.8 jit_solution(16636188021337697907)
XLA Ops:
  7.2 0.0 copy-start
  7.2 2.6 %pack_grads.1 = bf16[4,8,48,256]{3,2,1,0:T(8,128)(2,1)} custom-call(s32[1,128]{1,0:T(1,128)} %bitcast.25, s32[1,128]{1,0:T(1,128)} %bitcast.27, bf16[128,1024]{1,0:T(8,128)(2,1)} %grad_ref.1, bf16[128,1024]{1,0:T(8,128)(2,1)} %gate_ref.1, bf16[128,1024]{1,0:T(8,128)(2,1)} %up_ref.1), custom_call_target="tpu_custom_call" | custom-call | tf_op jit(solution)/shard_map/pack_grads/pallas_call | solution.py:199
  9.8 8.8 %all-to-all-start = ((bf16[32,48,256]{2,1,0:T(8,128)(2,1)}), bf16[32,48,256]{2,1,0:T(8,128)(2,1)}, u32[]{:S(2)}, u32[]{:S(2)}) async-start(bf16[32,48,256]{2,1,0:T(8,128)(2,1)} %bitcast.21), calls=%async_computation | async-start | bytes 1572864 | tf_op jit(solution)/shard_map/all_to_all | solution.py:208
  18.6 0.0 all-gather.2.cloned.1.call-start
  18.6 0.0 copy-done
  18.7 4.7 %collective-permute-start = (bf16[32,2048]{1,0:T(8,128)(2,1)S(1)}, bf16[32,2048]{1,0:T(8,128)(2,1)S(1)}, u32[]{:S(2)}, u32[]{:S(2)}) collective-permute-start(bf16[32,2048]{1,0:T(8,128)(2,1)S(1)} %convert_element_type.12), channel_id=1, source_target_pairs={{0,32},{32,0},{1,33},{33,1},{2,34},{34,2},{3,35},{35,3},{4,36},{36... | collective-permute-start | bytes 393224 | tf_op jit(solution)/shard_map/ppermute | solution.py:212
  23.4 3.1 %pack_rows.1 = (bf16[4,8,48,512]{3,2,1,0:T(8,128)(2,1)}, bf16[192,128]{1,0:T(8,128)(2,1)}) custom-call(s32[1,128]{1,0:T(1,128)} %bitcast.26, s32[1,128]{1,0:T(1,128)} %bitcast.28, bf16[128,4096]{1,0:T(8,128)(2,1)} %x_ref), custom_call_target="tpu_custom_call" | custom-call | tf_op jit(solution)/shard_map/pack_rows/pallas_call | solution.py:218
  26.5 4.4 %collective-permute-done = bf16[32,2048]{1,0:T(8,128)(2,1)S(1)} collective-permute-done((bf16[32,2048]{1,0:T(8,128)(2,1)S(1)}, bf16[32,2048]{1,0:T(8,128)(2,1)S(1)}, u32[]{:S(2)}, u32[]{:S(2)}) %collective-permute-start) | collective-permute-done | bytes 131104 | tf_op jit(solution)/shard_map/ppermute | solution.py:212
  31.0 11.0 %all-to-all-done = bf16[32,48,256]{2,1,0:T(8,128)(2,1)} async-done(((bf16[32,48,256]{2,1,0:T(8,128)(2,1)}), bf16[32,48,256]{2,1,0:T(8,128)(2,1)}, u32[]{:S(2)}, u32[]{:S(2)}) %all-to-all-start) | async-done | bytes 786464 | tf_op jit(solution)/shard_map/all_to_all | solution.py:208
  42.0 0.0 all-gather.2.cloned.1.call-update
  42.0 4.0 %all-to-all-start.1 = ((bf16[32,48,512]{2,1,0:T(8,128)(2,1)}), bf16[32,48,512]{2,1,0:T(8,128)(2,1)S(1)}, u32[]{:S(2)}, u32[]{:S(2)}) async-start(bf16[32,48,512]{2,1,0:T(8,128)(2,1)} %bitcast.22), calls=%async_computation.1 | async-start | bytes 3145728 | tf_op jit(solution)/shard_map/all_to_all | solution.py:238
  46.0 0.0 reduce-scatter.2.cloned.1.call-start
  46.1 7.9 %collective-permute-start.3 = (bf16[64,2048]{1,0:T(8,128)(2,1)S(1)}, bf16[64,2048]{1,0:T(8,128)(2,1)S(1)}, u32[]{:S(2)}, u32[]{:S(2)}) collective-permute-start(bf16[64,2048]{1,0:T(8,128)(2,1)S(1)} %maximum_select_fusion.rest_0_), channel_id=1, source_target_pairs={{0,192},{64,256},{128,320},{192,384},{256,448},{320,0},{384,64},{4... | collective-permute-start | bytes 786440 | tf_op jit(solution)/shard_map/ppermute | solution.py:245
  54.0 8.2 %collective-permute-start.4 = (bf16[64,2048]{1,0:T(8,128)(2,1)S(1)}, bf16[64,2048]{1,0:T(8,128)(2,1)S(1)}, u32[]{:S(2)}, u32[]{:S(2)}) collective-permute-start(bf16[64,2048]{1,0:T(8,128)(2,1)S(1)} %maximum_select_fusion.rest_0_), channel_id=1, source_target_pairs={{0,256},{64,320},{128,384},{192,448},{256,0},{320,64},{384,128},{4... | collective-permute-start | bytes 786440 | tf_op jit(solution)/shard_map/ppermute | solution.py:245
  62.2 1.9 %collective-permute-start.1 = (bf16[64,2048]{1,0:T(8,128)(2,1)S(1)}, bf16[64,2048]{1,0:T(8,128)(2,1)}, u32[]{:S(2)}, u32[]{:S(2)}) collective-permute-start(bf16[64,2048]{1,0:T(8,128)(2,1)S(1)} %maximum_select_fusion.rest_0_), channel_id=1, source_target_pairs={{0,64},{64,128},{128,192},{192,256},{256,320},{320,384},{384,448},... | collective-permute-start | bytes 786440 | tf_op jit(solution)/shard_map/ppermute | solution.py:245
  64.1 2.5 %collective-permute-start.2 = (bf16[64,2048]{1,0:T(8,128)(2,1)S(1)}, bf16[64,2048]{1,0:T(8,128)(2,1)}, u32[]{:S(2)}, u32[]{:S(2)}) collective-permute-start(bf16[64,2048]{1,0:T(8,128)(2,1)S(1)} %maximum_select_fusion.rest_0_), channel_id=1, source_target_pairs={{0,128},{64,192},{128,256},{192,320},{256,384},{320,448},{384,0},{... | collective-permute-start | bytes 786440 | tf_op jit(solution)/shard_map/ppermute | solution.py:245
  66.6 6.9 %collective-permute-start.5 = (bf16[64,2048]{1,0:T(8,128)(2,1)S(1)}, bf16[64,2048]{1,0:T(8,128)(2,1)}, u32[]{:S(2)}, u32[]{:S(2)}) collective-permute-start(bf16[64,2048]{1,0:T(8,128)(2,1)S(1)} %maximum_select_fusion.rest_0_), channel_id=1, source_target_pairs={{0,320},{64,384},{128,448},{192,0},{256,64},{320,128},{384,192},{4... | collective-permute-start | bytes 786440 | tf_op jit(solution)/shard_map/ppermute | solution.py:245
  73.6 0.5 collective-permute-done.3.rest_3_
  74.0 0.0 copy-start.2
  74.0 19.3 %collective-permute-start.6 = (bf16[64,2048]{1,0:T(8,128)(2,1)S(1)}, bf16[64,2048]{1,0:T(8,128)(2,1)}, u32[]{:S(2)}, u32[]{:S(2)}) collective-permute-start(bf16[64,2048]{1,0:T(8,128)(2,1)S(1)} %maximum_select_fusion.rest_0_), channel_id=1, source_target_pairs={{0,384},{64,448},{128,0},{192,64},{256,128},{320,192},{384,256},{4... | collective-permute-start | bytes 786440 | tf_op jit(solution)/shard_map/ppermute | solution.py:245
  93.4 0.0 collective-permute-done.4.rest_4_
  93.4 0.0 copy-done.2
  93.4 0.0 copy-start.3
  93.4 0.7 copy-done.3
  94.1 1.9 %collective-permute-start.7 = (bf16[64,2048]{1,0:T(8,128)(2,1)S(1)}, bf16[64,2048]{1,0:T(8,128)(2,1)}, u32[]{:S(2)}, u32[]{:S(2)}) collective-permute-start(bf16[64,2048]{1,0:T(8,128)(2,1)S(1)} %maximum_select_fusion.rest_0_), channel_id=1, source_target_pairs={{0,448},{64,0},{128,64},{192,128},{256,192},{320,256},{384,320},{4... | collective-permute-start | bytes 786440 | tf_op jit(solution)/shard_map/ppermute | solution.py:245
  96.0 1.0 all-to-all-done.1
  97.0 0.5 turn.1.xt_ref
  97.5 0.0 collective-permute-done.1.rest_1_
  97.5 4.3 %collective-permute-done.2.rest_2_ = bf16[64,2048]{1,0:T(8,128)(2,1)} collective-permute-done((bf16[64,2048]{1,0:T(8,128)(2,1)S(1)}, bf16[64,2048]{1,0:T(8,128)(2,1)}, u32[]{:S(2)}, u32[]{:S(2)}) %collective-permute-start.2) | collective-permute-done | bytes 262176 | tf_op jit(solution)/shard_map/ppermute | solution.py:245
  101.8 0.0 collective-permute-done.5.rest_5_
  101.8 0.7 collective-permute-done.6.rest_6_
  102.5 5.3 %collective-permute-done.7.rest_7_ = bf16[64,2048]{1,0:T(8,128)(2,1)} collective-permute-done((bf16[64,2048]{1,0:T(8,128)(2,1)S(1)}, bf16[64,2048]{1,0:T(8,128)(2,1)}, u32[]{:S(2)}, u32[]{:S(2)}) %collective-permute-start.7) | collective-permute-done | bytes 262176 | tf_op jit(solution)/shard_map/ppermute | solution.py:245
  107.8 1.4 all-gather.2.cloned.1.call-done.g_ref
  109.2 6.2 %weight_grad.1 = bf16[512,2048]{1,0:T(8,128)(2,1)} custom-call(bf16[512,1536]{1,0:T(8,128)(2,1)S(1)} %turn.1.xt_ref, bf16[8,1536,256]{2,1,0:T(8,128)(2,1)} %all-gather.2.cloned.1.call-done.g_ref), custom_call_target="tpu_custom_call" | custom-call | tf_op jit(solution)/shard_map/weight_grad/pallas_call | solution.py:256
  115.5 0.0 reduce-scatter.2.cloned.1.call-update
  115.5 7.6 %input_grad.1 = bf16[1536,512]{1,0:T(8,128)(2,1)} custom-call(s32[1]{0:T(128)} %bitcast.2.z_ref, bf16[8,1536,256]{2,1,0:T(8,128)(2,1)} %all-gather.2.cloned.1.call-done.g_ref, bf16[64,2048]{1,0:T(8,128)(2,1)S(1)} %maximum_select_fusion.rest_0_, bf16[64,2048]{1,0:T(8,128)(2,1)} %collective-permute-done.1.rest_1_, ...), custom_call_target="tpu_custom_call" | custom-call | tf_op jit(solution)/shard_map/input_grad/pallas_call | solution.py:277
  123.2 7.6 %all-to-all-start.2 = ((bf16[32,48,512]{2,1,0:T(8,128)(2,1)}), bf16[32,48,512]{2,1,0:T(8,128)(2,1)S(1)}, u32[]{:S(2)}, u32[]{:S(2)}) async-start(bf16[32,48,512]{2,1,0:T(8,128)(2,1)} %bitcast.20), calls=%async_computation.2 | async-start | bytes 3145728 | tf_op jit(solution)/shard_map/all_to_all | solution.py:294
  130.7 0.0 copy-start.1
  130.7 0.0 copy-start.4
  130.7 0.0 copy-start.5
  130.8 33.8 %reduce-scatter.2.cloned.1.call-done = bf16[64,2048]{1,0:T(8,128)(2,1)} async-done(((bf16[512,2048]{1,0:T(8,128)(2,1)}), bf16[64,2048]{1,0:T(8,128)(2,1)}) %reduce-scatter.2.cloned.1.call-update) | async-done | bytes 262160 | tf_op jit(solution)/shard_map/reduce_scatter | solution.py:270
  164.6 0.0 copy-start.6
  164.6 1.0 dynamic-slice_bitcast_fusion
  165.5 3.5 %collective-permute-start.8 = (bf16[32,2048]{1,0:T(8,128)(2,1)S(1)}, bf16[32,2048]{1,0:T(8,128)(2,1)S(1)}, u32[]{:S(2)}, u32[]{:S(2)}) collective-permute-start(bf16[32,2048]{1,0:T(8,128)(2,1)S(1)} %dynamic-slice_bitcast_fusion), channel_id=1, source_target_pairs={{0,32},{32,0},{1,33},{33,1},{2,34},{34,2},{3,35},{35,3},{4,36},{36... | collective-permute-start | bytes 393224 | tf_op jit(solution)/shard_map/ppermute | solution.py:319
  169.0 0.9 all-to-all-done.2
  169.9 2.0 %combine.1 = bf16[128,4096]{1,0:T(8,128)(2,1)} custom-call(bf16[192,128]{1,0:T(8,128)(2,1)} %get-tuple-element.31.routing_ref, bf16[4,8,48,512]{3,2,1,0:T(8,128)(2,1)S(1)} %bitcast.19), custom_call_target="tpu_custom_call" | custom-call | tf_op jit(solution)/shard_map/combine/pallas_call | solution.py:297
  172.0 1.9 %collective-permute-done.8 = bf16[32,2048]{1,0:T(8,128)(2,1)S(1)} collective-permute-done((bf16[32,2048]{1,0:T(8,128)(2,1)S(1)}, bf16[32,2048]{1,0:T(8,128)(2,1)S(1)}, u32[]{:S(2)}, u32[]{:S(2)}) %collective-permute-start.8) | collective-permute-done | bytes 131104 | tf_op jit(solution)/shard_map/ppermute | solution.py:319
  173.9 0.0 copy-done.1
  173.9 0.0 copy-done.4
  173.9 0.0 copy-done.5
  173.9 0.0 copy-done.6
  173.9 1.0 multiply_subtract_fusion
  (2 shorter events, 0.1 us)
Async XLA Ops:
  7.2 11.5 %copy-start = (f32[32,2048]{1,0:T(8,128)S(1)}, f32[32,2048]{1,0:T(8,128)}, u32[]{:S(2)}) copy-start(f32[32,2048]{1,0:T(8,128)} %param.15) | copy-start | bytes 786436
  9.8 32.2 %all-to-all-start = ((bf16[32,48,256]{2,1,0:T(8,128)(2,1)}), bf16[32,48,256]{2,1,0:T(8,128)(2,1)}, u32[]{:S(2)}, u32[]{:S(2)}) async-start(bf16[32,48,256]{2,1,0:T(8,128)(2,1)} %bitcast.21), calls=%async_computation | async-start | bytes 1572864 | tf_op jit(solution)/shard_map/all_to_all | solution.py:208
  18.6 90.7 %all-gather.2.cloned.1.call-start = ((), (), s32[]{:S(2)}) async-start(), calls=%async_computation.4 | async-start | bytes 7077888 | tf_op jit(solution)/shard_map/all_gather | solution.py:231
  18.7 12.3 %collective-permute-start = (bf16[32,2048]{1,0:T(8,128)(2,1)S(1)}, bf16[32,2048]{1,0:T(8,128)(2,1)S(1)}, u32[]{:S(2)}, u32[]{:S(2)}) collective-permute-start(bf16[32,2048]{1,0:T(8,128)(2,1)S(1)} %convert_element_type.12), channel_id=1, source_target_pairs={{0,32},{32,0},{1,33},{33,1},{2,34},{34,2},{3,35},{35,3},{4,36},{36... | collective-permute-start | bytes 393224 | tf_op jit(solution)/shard_map/ppermute | solution.py:212
  42.0 55.0 %all-to-all-start.1 = ((bf16[32,48,512]{2,1,0:T(8,128)(2,1)}), bf16[32,48,512]{2,1,0:T(8,128)(2,1)S(1)}, u32[]{:S(2)}, u32[]{:S(2)}) async-start(bf16[32,48,512]{2,1,0:T(8,128)(2,1)} %bitcast.22), calls=%async_computation.1 | async-start | bytes 3145728 | tf_op jit(solution)/shard_map/all_to_all | solution.py:238
  46.0 118.5 %reduce-scatter.2.cloned.1.call-start = ((), (), s32[]{:S(2)}) async-start(), calls=%async_computation.5 | async-start | bytes 2359296 | tf_op jit(solution)/shard_map/reduce_scatter | solution.py:270
  46.1 28.0 %collective-permute-start.3 = (bf16[64,2048]{1,0:T(8,128)(2,1)S(1)}, bf16[64,2048]{1,0:T(8,128)(2,1)S(1)}, u32[]{:S(2)}, u32[]{:S(2)}) collective-permute-start(bf16[64,2048]{1,0:T(8,128)(2,1)S(1)} %maximum_select_fusion.rest_0_), channel_id=1, source_target_pairs={{0,192},{64,256},{128,320},{192,384},{256,448},{320,0},{384,64},{4... | collective-permute-start | bytes 786440 | tf_op jit(solution)/shard_map/ppermute | solution.py:245
  54.0 39.4 %collective-permute-start.4 = (bf16[64,2048]{1,0:T(8,128)(2,1)S(1)}, bf16[64,2048]{1,0:T(8,128)(2,1)S(1)}, u32[]{:S(2)}, u32[]{:S(2)}) collective-permute-start(bf16[64,2048]{1,0:T(8,128)(2,1)S(1)} %maximum_select_fusion.rest_0_), channel_id=1, source_target_pairs={{0,256},{64,320},{128,384},{192,448},{256,0},{320,64},{384,128},{4... | collective-permute-start | bytes 786440 | tf_op jit(solution)/shard_map/ppermute | solution.py:245
  62.2 35.3 %collective-permute-start.1 = (bf16[64,2048]{1,0:T(8,128)(2,1)S(1)}, bf16[64,2048]{1,0:T(8,128)(2,1)}, u32[]{:S(2)}, u32[]{:S(2)}) collective-permute-start(bf16[64,2048]{1,0:T(8,128)(2,1)S(1)} %maximum_select_fusion.rest_0_), channel_id=1, source_target_pairs={{0,64},{64,128},{128,192},{192,256},{256,320},{320,384},{384,448},... | collective-permute-start | bytes 786440 | tf_op jit(solution)/shard_map/ppermute | solution.py:245
  64.1 37.6 %collective-permute-start.2 = (bf16[64,2048]{1,0:T(8,128)(2,1)S(1)}, bf16[64,2048]{1,0:T(8,128)(2,1)}, u32[]{:S(2)}, u32[]{:S(2)}) collective-permute-start(bf16[64,2048]{1,0:T(8,128)(2,1)S(1)} %maximum_select_fusion.rest_0_), channel_id=1, source_target_pairs={{0,128},{64,192},{128,256},{192,320},{256,384},{320,448},{384,0},{... | collective-permute-start | bytes 786440 | tf_op jit(solution)/shard_map/ppermute | solution.py:245
  66.6 35.2 %collective-permute-start.5 = (bf16[64,2048]{1,0:T(8,128)(2,1)S(1)}, bf16[64,2048]{1,0:T(8,128)(2,1)}, u32[]{:S(2)}, u32[]{:S(2)}) collective-permute-start(bf16[64,2048]{1,0:T(8,128)(2,1)S(1)} %maximum_select_fusion.rest_0_), channel_id=1, source_target_pairs={{0,320},{64,384},{128,448},{192,0},{256,64},{320,128},{384,192},{4... | collective-permute-start | bytes 786440 | tf_op jit(solution)/shard_map/ppermute | solution.py:245
  74.0 19.4 %copy-start.2 = (bf16[64,2048]{1,0:T(8,128)(2,1)}, bf16[64,2048]{1,0:T(8,128)(2,1)S(1)}, u32[]{:S(2)}) copy-start(bf16[64,2048]{1,0:T(8,128)(2,1)S(1)} %collective-permute-done.3.rest_3_) | copy-start | bytes 786436
  74.0 28.5 %collective-permute-start.6 = (bf16[64,2048]{1,0:T(8,128)(2,1)S(1)}, bf16[64,2048]{1,0:T(8,128)(2,1)}, u32[]{:S(2)}, u32[]{:S(2)}) collective-permute-start(bf16[64,2048]{1,0:T(8,128)(2,1)S(1)} %maximum_select_fusion.rest_0_), channel_id=1, source_target_pairs={{0,384},{64,448},{128,0},{192,64},{256,128},{320,192},{384,256},{4... | collective-permute-start | bytes 786440 | tf_op jit(solution)/shard_map/ppermute | solution.py:245
  93.4 0.7 copy-start.3
  94.1 13.7 %collective-permute-start.7 = (bf16[64,2048]{1,0:T(8,128)(2,1)S(1)}, bf16[64,2048]{1,0:T(8,128)(2,1)}, u32[]{:S(2)}, u32[]{:S(2)}) collective-permute-start(bf16[64,2048]{1,0:T(8,128)(2,1)S(1)} %maximum_select_fusion.rest_0_), channel_id=1, source_target_pairs={{0,448},{64,0},{128,64},{192,128},{256,192},{320,256},{384,320},{4... | collective-permute-start | bytes 786440 | tf_op jit(solution)/shard_map/ppermute | solution.py:245
  123.2 46.8 %all-to-all-start.2 = ((bf16[32,48,512]{2,1,0:T(8,128)(2,1)}), bf16[32,48,512]{2,1,0:T(8,128)(2,1)S(1)}, u32[]{:S(2)}, u32[]{:S(2)}) async-start(bf16[32,48,512]{2,1,0:T(8,128)(2,1)} %bitcast.20), calls=%async_computation.2 | async-start | bytes 3145728 | tf_op jit(solution)/shard_map/all_to_all | solution.py:294
  130.7 43.2 %copy-start.1 = (f32[32,2048]{1,0:T(8,128)S(1)}, f32[32,2048]{1,0:T(8,128)}, u32[]{:S(2)}) copy-start(f32[32,2048]{1,0:T(8,128)} %param.15) | copy-start | bytes 786436
  130.7 43.2 %copy-start.4 = (f32[32,2048]{1,0:T(8,128)S(1)}, f32[32,2048]{1,0:T(8,128)}, u32[]{:S(2)}) copy-start(f32[32,2048]{1,0:T(8,128)} %param.17) | copy-start | bytes 786436
  130.7 43.2 %copy-start.5 = (f32[32,2048]{1,0:T(8,128)S(1)}, f32[32,2048]{1,0:T(8,128)}, u32[]{:S(2)}) copy-start(f32[32,2048]{1,0:T(8,128)} %param.16) | copy-start | bytes 786436
  164.6 9.4 %copy-start.6 = (bf16[64,2048]{1,0:T(8,128)(2,1)S(1)}, bf16[64,2048]{1,0:T(8,128)(2,1)}, u32[]{:S(2)}) copy-start(bf16[64,2048]{1,0:T(8,128)(2,1)} %reduce-scatter.2.cloned.1.call-done) | copy-start | bytes 786436
  165.5 8.4 %collective-permute-start.8 = (bf16[32,2048]{1,0:T(8,128)(2,1)S(1)}, bf16[32,2048]{1,0:T(8,128)(2,1)S(1)}, u32[]{:S(2)}, u32[]{:S(2)}) collective-permute-start(bf16[32,2048]{1,0:T(8,128)(2,1)S(1)} %dynamic-slice_bitcast_fusion), channel_id=1, source_target_pairs={{0,32},{32,0},{1,33},{33,1},{2,34},{34,2},{3,35},{35,3},{4,36},{36... | collective-permute-start | bytes 393224 | tf_op jit(solution)/shard_map/ppermute | solution.py:319
Sparse Core Ops, SparseCore 0:
  42.1 67.0 all-gather.1
  115.6 48.8 reduce-scatter.1

commit v12 on v10

--- a/solution.py
+++ b/solution.py
@@ -115,14 +115,15 @@
         load.start()
     stores = []
     piece = g_buf.shape[2]
-    for j in range(pairs):
-        loads[j].wait()
+    for j, (first, last) in enumerate(((0, 1), (1, 2), (2, pairs))):
+        for load in loads[first:last]:
+            load.wait()
         if j == 0:
             loads[-1].start()
-        pair = jnp.concatenate([g_buf[2 * j], g_buf[2 * j + 1]], axis=1)
-        cols = slice(2 * j * piece, (2 * j + 2) * piece)
+        wide = jnp.concatenate([g_buf[i] for i in range(2 * first, 2 * last)], axis=1)
+        cols = slice(2 * first * piece, 2 * last * piece)
         dw_buf[:, cols] = jnp.dot(
-            xt_ref[...], pair, preferred_element_type=jnp.float32
+            xt_ref[...], wide, preferred_element_type=jnp.float32
         ).astype(jnp.bfloat16)
         stores.append(
             pltpu.make_async_copy(dw_buf.at[:, cols], dw_ref.at[:, cols], out_sems.at[j])

time: 183 us -> 183 us (level)
  no operation moved by 1% of the time
where the time goes in v12:
time: 183 us; the launch traced here: 182 us
  starting transfers between devices  77.1 us (42%)
  waiting for transfers between devices  66.2 us (36%)
  Pallas kernels  21.3 us (12%)
  between operations  14.3 us (8%)
  other arithmetic  2.04 us (1%)
    ppermute x7, starting transfers between devices, body(): lax.ppermute(moved, 'z', [(i, (i + k) % RING) for i in range(RING)])  48.7 us
    reduce_scatter x1, waiting for transfers between devices, body(): grad_z = lax.psum_scatter(grad_part, 'z', scatter_dimension=0, tiled=True)  34.8 us
    ppermute x7, waiting for transfers between devices, body(): lax.ppermute(moved, 'z', [(i, (i + k) % RING) for i in range(RING)])  10.8 us
    all_to_all x1, waiting for transfers between devices, body(): lax.all_to_all(g_send.reshape(members, CAP, gpiece), EXP, split_axis=0, c...  9.88 us
    all_to_all x1, starting transfers between devices, body(): lax.all_to_all(g_send.reshape(members, CAP, gpiece), EXP, split_axis=0, c...  8.77 us
    all_to_all x1, starting transfers between devices, body(): lax.all_to_all(dx_rows.reshape(members, CAP, piece), EXP, split_axis=0, c...  7.56 us
    pallas_call x1, Pallas kernels, body(): pl.pallas_call(input_grad_kernel, out_shape=jax.ShapeDtypeStruct((rows_to...  6.79 us
    pallas_call x1, Pallas kernels, body(): pl.pallas_call(weight_grad_kernel, out_shape=jax.ShapeDtypeStruct((piece,...  6.31 us
  transfers between devices with their start and end apart: 14, of which 11 were waited for; matrix products, arithmetic and copies ran while one was open for 1% of the time, Pallas kernels for 7%

profile of v12, /device:TPU:6, one launch (start us, length us, event | category | flops | bytes accessed | tf_op | source)
XLA Modules:
  0.0 182.0 jit_solution(12966137064241900608)
XLA Ops:
  7.2 0.0 copy-start.1
  7.2 2.6 %pack_grads.1 = bf16[4,8,48,256]{3,2,1,0:T(8,128)(2,1)} custom-call(s32[1,128]{1,0:T(1,128)} %bitcast.25, s32[1,128]{1,0:T(1,128)} %bitcast.27, bf16[128,1024]{1,0:T(8,128)(2,1)} %grad_ref.1, bf16[128,1024]{1,0:T(8,128)(2,1)} %gate_ref.1, bf16[128,1024]{1,0:T(8,128)(2,1)} %up_ref.1), custom_call_target="tpu_custom_call" | custom-call | tf_op jit(solution)/shard_map/pack_grads/pallas_call | solution.py:200
  9.8 8.8 %all-to-all-start = ((bf16[32,48,256]{2,1,0:T(8,128)(2,1)}), bf16[32,48,256]{2,1,0:T(8,128)(2,1)}, u32[]{:S(2)}, u32[]{:S(2)}) async-start(bf16[32,48,256]{2,1,0:T(8,128)(2,1)} %bitcast.21), calls=%async_computation | async-start | bytes 1572864 | tf_op jit(solution)/shard_map/all_to_all | solution.py:209
  18.6 0.0 all-gather.2.cloned.1.call-start
  18.6 0.0 copy-done.1
  18.7 4.7 %collective-permute-start = (bf16[32,2048]{1,0:T(8,128)(2,1)S(1)}, bf16[32,2048]{1,0:T(8,128)(2,1)}, u32[]{:S(2)}, u32[]{:S(2)}) collective-permute-start(bf16[32,2048]{1,0:T(8,128)(2,1)S(1)} %convert_element_type.12), channel_id=1, source_target_pairs={{0,32},{32,0},{1,33},{33,1},{2,34},{34,2},{3,35},{35,3},{4,36},{36... | collective-permute-start | bytes 393224 | tf_op jit(solution)/shard_map/ppermute | solution.py:213
  23.4 3.1 %pack_rows.1 = (bf16[4,8,48,512]{3,2,1,0:T(8,128)(2,1)}, bf16[192,128]{1,0:T(8,128)(2,1)}) custom-call(s32[1,128]{1,0:T(1,128)} %bitcast.26, s32[1,128]{1,0:T(1,128)} %bitcast.28, bf16[128,4096]{1,0:T(8,128)(2,1)} %x_ref), custom_call_target="tpu_custom_call" | custom-call | tf_op jit(solution)/shard_map/pack_rows/pallas_call | solution.py:219
  26.5 4.5 %collective-permute-done = bf16[32,2048]{1,0:T(8,128)(2,1)} collective-permute-done((bf16[32,2048]{1,0:T(8,128)(2,1)S(1)}, bf16[32,2048]{1,0:T(8,128)(2,1)}, u32[]{:S(2)}, u32[]{:S(2)}) %collective-permute-start) | collective-permute-done | bytes 131104 | tf_op jit(solution)/shard_map/ppermute | solution.py:213
  31.0 1.0 maximum_select_fusion.rest_0_
  32.1 0.0 copy-start
  32.1 9.9 %all-to-all-done = bf16[32,48,256]{2,1,0:T(8,128)(2,1)} async-done(((bf16[32,48,256]{2,1,0:T(8,128)(2,1)}), bf16[32,48,256]{2,1,0:T(8,128)(2,1)}, u32[]{:S(2)}, u32[]{:S(2)}) %all-to-all-start) | async-done | bytes 786464 | tf_op jit(solution)/shard_map/all_to_all | solution.py:209
  42.0 0.0 all-gather.2.cloned.1.call-update
  42.0 4.0 %all-to-all-start.1 = ((bf16[32,48,512]{2,1,0:T(8,128)(2,1)}), bf16[32,48,512]{2,1,0:T(8,128)(2,1)S(1)}, u32[]{:S(2)}, u32[]{:S(2)}) async-start(bf16[32,48,512]{2,1,0:T(8,128)(2,1)} %bitcast.22), calls=%async_computation.1 | async-start | bytes 3145728 | tf_op jit(solution)/shard_map/all_to_all | solution.py:239
  46.0 0.0 reduce-scatter.2.cloned.1.call-start
  46.1 7.9 %collective-permute-start.3 = (bf16[64,2048]{1,0:T(8,128)(2,1)S(1)}, bf16[64,2048]{1,0:T(8,128)(2,1)S(1)}, u32[]{:S(2)}, u32[]{:S(2)}) collective-permute-start(bf16[64,2048]{1,0:T(8,128)(2,1)S(1)} %maximum_select_fusion.rest_0_), channel_id=1, source_target_pairs={{0,192},{64,256},{128,320},{192,384},{256,448},{320,0},{384,64},{4... | collective-permute-start | bytes 786440 | tf_op jit(solution)/shard_map/ppermute | solution.py:246
  54.0 8.2 %collective-permute-start.4 = (bf16[64,2048]{1,0:T(8,128)(2,1)S(1)}, bf16[64,2048]{1,0:T(8,128)(2,1)S(1)}, u32[]{:S(2)}, u32[]{:S(2)}) collective-permute-start(bf16[64,2048]{1,0:T(8,128)(2,1)S(1)} %maximum_select_fusion.rest_0_), channel_id=1, source_target_pairs={{0,256},{64,320},{128,384},{192,448},{256,0},{320,64},{384,128},{4... | collective-permute-start | bytes 786440 | tf_op jit(solution)/shard_map/ppermute | solution.py:246
  62.2 1.9 %collective-permute-start.1 = (bf16[64,2048]{1,0:T(8,128)(2,1)S(1)}, bf16[64,2048]{1,0:T(8,128)(2,1)}, u32[]{:S(2)}, u32[]{:S(2)}) collective-permute-start(bf16[64,2048]{1,0:T(8,128)(2,1)S(1)} %maximum_select_fusion.rest_0_), channel_id=1, source_target_pairs={{0,64},{64,128},{128,192},{192,256},{256,320},{320,384},{384,448},... | collective-permute-start | bytes 786440 | tf_op jit(solution)/shard_map/ppermute | solution.py:246
  64.1 2.5 %collective-permute-start.2 = (bf16[64,2048]{1,0:T(8,128)(2,1)S(1)}, bf16[64,2048]{1,0:T(8,128)(2,1)}, u32[]{:S(2)}, u32[]{:S(2)}) collective-permute-start(bf16[64,2048]{1,0:T(8,128)(2,1)S(1)} %maximum_select_fusion.rest_0_), channel_id=1, source_target_pairs={{0,128},{64,192},{128,256},{192,320},{256,384},{320,448},{384,0},{... | collective-permute-start | bytes 786440 | tf_op jit(solution)/shard_map/ppermute | solution.py:246
  66.6 6.9 %collective-permute-start.5 = (bf16[64,2048]{1,0:T(8,128)(2,1)S(1)}, bf16[64,2048]{1,0:T(8,128)(2,1)}, u32[]{:S(2)}, u32[]{:S(2)}) collective-permute-start(bf16[64,2048]{1,0:T(8,128)(2,1)S(1)} %maximum_select_fusion.rest_0_), channel_id=1, source_target_pairs={{0,320},{64,384},{128,448},{192,0},{256,64},{320,128},{384,192},{4... | collective-permute-start | bytes 786440 | tf_op jit(solution)/shard_map/ppermute | solution.py:246
  73.6 0.5 collective-permute-done.3.rest_3_
  74.0 0.0 copy-start.3
  74.0 19.3 %collective-permute-start.6 = (bf16[64,2048]{1,0:T(8,128)(2,1)S(1)}, bf16[64,2048]{1,0:T(8,128)(2,1)}, u32[]{:S(2)}, u32[]{:S(2)}) collective-permute-start(bf16[64,2048]{1,0:T(8,128)(2,1)S(1)} %maximum_select_fusion.rest_0_), channel_id=1, source_target_pairs={{0,384},{64,448},{128,0},{192,64},{256,128},{320,192},{384,256},{4... | collective-permute-start | bytes 786440 | tf_op jit(solution)/shard_map/ppermute | solution.py:246
  93.4 0.0 collective-permute-done.4.rest_4_
  93.4 0.0 copy-done
  93.4 0.0 copy-start.4
  93.4 1.9 %collective-permute-start.7 = (bf16[64,2048]{1,0:T(8,128)(2,1)S(1)}, bf16[64,2048]{1,0:T(8,128)(2,1)}, u32[]{:S(2)}, u32[]{:S(2)}) collective-permute-start(bf16[64,2048]{1,0:T(8,128)(2,1)S(1)} %maximum_select_fusion.rest_0_), channel_id=1, source_target_pairs={{0,448},{64,0},{128,64},{192,128},{256,192},{320,256},{384,320},{4... | collective-permute-start | bytes 786440 | tf_op jit(solution)/shard_map/ppermute | solution.py:246
  95.4 1.7 all-to-all-done.1
  97.0 0.0 copy-done.3
  97.0 0.0 copy-done.4
  97.0 0.5 turn.1.xt_ref
  97.5 0.0 collective-permute-done.1.rest_1_
  97.5 4.3 %collective-permute-done.2.rest_2_ = bf16[64,2048]{1,0:T(8,128)(2,1)} collective-permute-done((bf16[64,2048]{1,0:T(8,128)(2,1)S(1)}, bf16[64,2048]{1,0:T(8,128)(2,1)}, u32[]{:S(2)}, u32[]{:S(2)}) %collective-permute-start.2) | collective-permute-done | bytes 262176 | tf_op jit(solution)/shard_map/ppermute | solution.py:246
  101.8 0.0 collective-permute-done.5.rest_5_
  101.8 0.7 collective-permute-done.6.rest_6_
  102.5 5.3 %collective-permute-done.7.rest_7_ = bf16[64,2048]{1,0:T(8,128)(2,1)} collective-permute-done((bf16[64,2048]{1,0:T(8,128)(2,1)S(1)}, bf16[64,2048]{1,0:T(8,128)(2,1)}, u32[]{:S(2)}, u32[]{:S(2)}) %collective-permute-start.7) | collective-permute-done | bytes 262176 | tf_op jit(solution)/shard_map/ppermute | solution.py:246
  107.8 1.4 all-gather.2.cloned.1.call-done.g_ref
  109.2 6.3 %weight_grad.1 = bf16[512,2048]{1,0:T(8,128)(2,1)} custom-call(bf16[512,1536]{1,0:T(8,128)(2,1)S(1)} %turn.1.xt_ref, bf16[8,1536,256]{2,1,0:T(8,128)(2,1)} %all-gather.2.cloned.1.call-done.g_ref), custom_call_target="tpu_custom_call" | custom-call | tf_op jit(solution)/shard_map/weight_grad/pallas_call | solution.py:257
  115.6 0.0 reduce-scatter.2.cloned.1.call-update
  115.6 6.8 %input_grad.1 = bf16[1536,512]{1,0:T(8,128)(2,1)} custom-call(s32[1]{0:T(128)} %bitcast.2.z_ref, bf16[8,1536,256]{2,1,0:T(8,128)(2,1)} %all-gather.2.cloned.1.call-done.g_ref, bf16[64,2048]{1,0:T(8,128)(2,1)} %copy-done, bf16[64,2048]{1,0:T(8,128)(2,1)} %collective-permute-done.1.rest_1_, bf16[64,2048]{1,0:T(8,128)(2,1)} %collective-permute-done.2.rest_2_, ...), custom_call_target="tpu_custom_call" | custom-call | tf_op jit(solution)/shard_map/input_grad/pallas_call | solution.py:274
  122.4 7.6 %all-to-all-start.2 = ((bf16[32,48,512]{2,1,0:T(8,128)(2,1)}), bf16[32,48,512]{2,1,0:T(8,128)(2,1)S(1)}, u32[]{:S(2)}, u32[]{:S(2)}) async-start(bf16[32,48,512]{2,1,0:T(8,128)(2,1)} %bitcast.20), calls=%async_computation.2 | async-start | bytes 3145728 | tf_op jit(solution)/shard_map/all_to_all | solution.py:290
  129.9 0.0 copy-start.2
  130.0 0.0 copy-start.5
  130.0 0.0 copy-start.6
  130.0 34.8 %reduce-scatter.2.cloned.1.call-done = bf16[64,2048]{1,0:T(8,128)(2,1)} async-done(((bf16[512,2048]{1,0:T(8,128)(2,1)}), bf16[64,2048]{1,0:T(8,128)(2,1)}) %reduce-scatter.2.cloned.1.call-update) | async-done | bytes 262160 | tf_op jit(solution)/shard_map/reduce_scatter | solution.py:271
  164.7 0.0 copy-start.7
  164.7 1.0 dynamic-slice_bitcast_fusion
  165.7 3.2 %collective-permute-start.8 = (bf16[32,2048]{1,0:T(8,128)(2,1)S(1)}, bf16[32,2048]{1,0:T(8,128)(2,1)S(1)}, u32[]{:S(2)}, u32[]{:S(2)}) collective-permute-start(bf16[32,2048]{1,0:T(8,128)(2,1)S(1)} %dynamic-slice_bitcast_fusion), channel_id=1, source_target_pairs={{0,32},{32,0},{1,33},{33,1},{2,34},{34,2},{3,35},{35,3},{4,36},{36... | collective-permute-start | bytes 393224 | tf_op jit(solution)/shard_map/ppermute | solution.py:315
  169.0 0.2 all-to-all-done.2
  169.1 2.0 %combine.1 = bf16[128,4096]{1,0:T(8,128)(2,1)} custom-call(bf16[192,128]{1,0:T(8,128)(2,1)} %get-tuple-element.31.routing_ref, bf16[4,8,48,512]{3,2,1,0:T(8,128)(2,1)S(1)} %bitcast.19), custom_call_target="tpu_custom_call" | custom-call | tf_op jit(solution)/shard_map/combine/pallas_call | solution.py:293
  171.2 2.9 %collective-permute-done.8 = bf16[32,2048]{1,0:T(8,128)(2,1)S(1)} collective-permute-done((bf16[32,2048]{1,0:T(8,128)(2,1)S(1)}, bf16[32,2048]{1,0:T(8,128)(2,1)S(1)}, u32[]{:S(2)}, u32[]{:S(2)}) %collective-permute-start.8) | collective-permute-done | bytes 131104 | tf_op jit(solution)/shard_map/ppermute | solution.py:315
  174.1 0.0 copy-done.2
  174.1 0.0 copy-done.5
  174.1 0.0 copy-done.6
  174.1 0.0 copy-done.7
  174.1 1.0 multiply_subtract_fusion
  (1 shorter events, 0.0 us)
Async XLA Ops:
  7.2 11.5 %copy-start.1 = (f32[32,2048]{1,0:T(8,128)S(1)}, f32[32,2048]{1,0:T(8,128)}, u32[]{:S(2)}) copy-start(f32[32,2048]{1,0:T(8,128)} %param.15) | copy-start | bytes 786436
  9.8 32.2 %all-to-all-start = ((bf16[32,48,256]{2,1,0:T(8,128)(2,1)}), bf16[32,48,256]{2,1,0:T(8,128)(2,1)}, u32[]{:S(2)}, u32[]{:S(2)}) async-start(bf16[32,48,256]{2,1,0:T(8,128)(2,1)} %bitcast.21), calls=%async_computation | async-start | bytes 1572864 | tf_op jit(solution)/shard_map/all_to_all | solution.py:209
  18.6 90.7 %all-gather.2.cloned.1.call-start = ((), (), s32[]{:S(2)}) async-start(), calls=%async_computation.4 | async-start | bytes 7077888 | tf_op jit(solution)/shard_map/all_gather | solution.py:232
  18.7 12.4 %collective-permute-start = (bf16[32,2048]{1,0:T(8,128)(2,1)S(1)}, bf16[32,2048]{1,0:T(8,128)(2,1)}, u32[]{:S(2)}, u32[]{:S(2)}) collective-permute-start(bf16[32,2048]{1,0:T(8,128)(2,1)S(1)} %convert_element_type.12), channel_id=1, source_target_pairs={{0,32},{32,0},{1,33},{33,1},{2,34},{34,2},{3,35},{35,3},{4,36},{36... | collective-permute-start | bytes 393224 | tf_op jit(solution)/shard_map/ppermute | solution.py:213
  32.1 61.3 %copy-start = (bf16[64,2048]{1,0:T(8,128)(2,1)}, bf16[64,2048]{1,0:T(8,128)(2,1)S(1)}, u32[]{:S(2)}) copy-start(bf16[64,2048]{1,0:T(8,128)(2,1)S(1)} %maximum_select_fusion.rest_0_) | copy-start | bytes 786436
  42.0 55.0 %all-to-all-start.1 = ((bf16[32,48,512]{2,1,0:T(8,128)(2,1)}), bf16[32,48,512]{2,1,0:T(8,128)(2,1)S(1)}, u32[]{:S(2)}, u32[]{:S(2)}) async-start(bf16[32,48,512]{2,1,0:T(8,128)(2,1)} %bitcast.22), calls=%async_computation.1 | async-start | bytes 3145728 | tf_op jit(solution)/shard_map/all_to_all | solution.py:239
  46.0 118.7 %reduce-scatter.2.cloned.1.call-start = ((), (), s32[]{:S(2)}) async-start(), calls=%async_computation.5 | async-start | bytes 2359296 | tf_op jit(solution)/shard_map/reduce_scatter | solution.py:271
  46.1 28.0 %collective-permute-start.3 = (bf16[64,2048]{1,0:T(8,128)(2,1)S(1)}, bf16[64,2048]{1,0:T(8,128)(2,1)S(1)}, u32[]{:S(2)}, u32[]{:S(2)}) collective-permute-start(bf16[64,2048]{1,0:T(8,128)(2,1)S(1)} %maximum_select_fusion.rest_0_), channel_id=1, source_target_pairs={{0,192},{64,256},{128,320},{192,384},{256,448},{320,0},{384,64},{4... | collective-permute-start | bytes 786440 | tf_op jit(solution)/shard_map/ppermute | solution.py:246
  54.0 39.4 %collective-permute-start.4 = (bf16[64,2048]{1,0:T(8,128)(2,1)S(1)}, bf16[64,2048]{1,0:T(8,128)(2,1)S(1)}, u32[]{:S(2)}, u32[]{:S(2)}) collective-permute-start(bf16[64,2048]{1,0:T(8,128)(2,1)S(1)} %maximum_select_fusion.rest_0_), channel_id=1, source_target_pairs={{0,256},{64,320},{128,384},{192,448},{256,0},{320,64},{384,128},{4... | collective-permute-start | bytes 786440 | tf_op jit(solution)/shard_map/ppermute | solution.py:246
  62.2 35.3 %collective-permute-start.1 = (bf16[64,2048]{1,0:T(8,128)(2,1)S(1)}, bf16[64,2048]{1,0:T(8,128)(2,1)}, u32[]{:S(2)}, u32[]{:S(2)}) collective-permute-start(bf16[64,2048]{1,0:T(8,128)(2,1)S(1)} %maximum_select_fusion.rest_0_), channel_id=1, source_target_pairs={{0,64},{64,128},{128,192},{192,256},{256,320},{320,384},{384,448},... | collective-permute-start | bytes 786440 | tf_op jit(solution)/shard_map/ppermute | solution.py:246
  64.1 37.6 %collective-permute-start.2 = (bf16[64,2048]{1,0:T(8,128)(2,1)S(1)}, bf16[64,2048]{1,0:T(8,128)(2,1)}, u32[]{:S(2)}, u32[]{:S(2)}) collective-permute-start(bf16[64,2048]{1,0:T(8,128)(2,1)S(1)} %maximum_select_fusion.rest_0_), channel_id=1, source_target_pairs={{0,128},{64,192},{128,256},{192,320},{256,384},{320,448},{384,0},{... | collective-permute-start | bytes 786440 | tf_op jit(solution)/shard_map/ppermute | solution.py:246
  66.6 35.2 %collective-permute-start.5 = (bf16[64,2048]{1,0:T(8,128)(2,1)S(1)}, bf16[64,2048]{1,0:T(8,128)(2,1)}, u32[]{:S(2)}, u32[]{:S(2)}) collective-permute-start(bf16[64,2048]{1,0:T(8,128)(2,1)S(1)} %maximum_select_fusion.rest_0_), channel_id=1, source_target_pairs={{0,320},{64,384},{128,448},{192,0},{256,64},{320,128},{384,192},{4... | collective-permute-start | bytes 786440 | tf_op jit(solution)/shard_map/ppermute | solution.py:246
  74.0 23.0 %copy-start.3 = (bf16[64,2048]{1,0:T(8,128)(2,1)}, bf16[64,2048]{1,0:T(8,128)(2,1)S(1)}, u32[]{:S(2)}) copy-start(bf16[64,2048]{1,0:T(8,128)(2,1)S(1)} %collective-permute-done.3.rest_3_) | copy-start | bytes 786436
  74.0 28.5 %collective-permute-start.6 = (bf16[64,2048]{1,0:T(8,128)(2,1)S(1)}, bf16[64,2048]{1,0:T(8,128)(2,1)}, u32[]{:S(2)}, u32[]{:S(2)}) collective-permute-start(bf16[64,2048]{1,0:T(8,128)(2,1)S(1)} %maximum_select_fusion.rest_0_), channel_id=1, source_target_pairs={{0,384},{64,448},{128,0},{192,64},{256,128},{320,192},{384,256},{4... | collective-permute-start | bytes 786440 | tf_op jit(solution)/shard_map/ppermute | solution.py:246
  93.4 3.6 %copy-start.4 = (bf16[64,2048]{1,0:T(8,128)(2,1)}, bf16[64,2048]{1,0:T(8,128)(2,1)S(1)}, u32[]{:S(2)}) copy-start(bf16[64,2048]{1,0:T(8,128)(2,1)S(1)} %collective-permute-done.4.rest_4_) | copy-start | bytes 786436
  93.4 14.4 %collective-permute-start.7 = (bf16[64,2048]{1,0:T(8,128)(2,1)S(1)}, bf16[64,2048]{1,0:T(8,128)(2,1)}, u32[]{:S(2)}, u32[]{:S(2)}) collective-permute-start(bf16[64,2048]{1,0:T(8,128)(2,1)S(1)} %maximum_select_fusion.rest_0_), channel_id=1, source_target_pairs={{0,448},{64,0},{128,64},{192,128},{256,192},{320,256},{384,320},{4... | collective-permute-start | bytes 786440 | tf_op jit(solution)/shard_map/ppermute | solution.py:246
  122.4 46.8 %all-to-all-start.2 = ((bf16[32,48,512]{2,1,0:T(8,128)(2,1)}), bf16[32,48,512]{2,1,0:T(8,128)(2,1)S(1)}, u32[]{:S(2)}, u32[]{:S(2)}) async-start(bf16[32,48,512]{2,1,0:T(8,128)(2,1)} %bitcast.20), calls=%async_computation.2 | async-start | bytes 3145728 | tf_op jit(solution)/shard_map/all_to_all | solution.py:290
  129.9 44.2 %copy-start.2 = (f32[32,2048]{1,0:T(8,128)S(1)}, f32[32,2048]{1,0:T(8,128)}, u32[]{:S(2)}) copy-start(f32[32,2048]{1,0:T(8,128)} %param.15) | copy-start | bytes 786436
  130.0 44.2 %copy-start.5 = (f32[32,2048]{1,0:T(8,128)S(1)}, f32[32,2048]{1,0:T(8,128)}, u32[]{:S(2)}) copy-start(f32[32,2048]{1,0:T(8,128)} %param.17) | copy-start | bytes 786436
  130.0 44.1 %copy-start.6 = (f32[32,2048]{1,0:T(8,128)S(1)}, f32[32,2048]{1,0:T(8,128)}, u32[]{:S(2)}) copy-start(f32[32,2048]{1,0:T(8,128)} %param.16) | copy-start | bytes 786436
  164.7 9.4 %copy-start.7 = (bf16[64,2048]{1,0:T(8,128)(2,1)S(1)}, bf16[64,2048]{1,0:T(8,128)(2,1)}, u32[]{:S(2)}) copy-start(bf16[64,2048]{1,0:T(8,128)(2,1)} %reduce-scatter.2.cloned.1.call-done) | copy-start | bytes 786436
  165.7 8.4 %collective-permute-start.8 = (bf16[32,2048]{1,0:T(8,128)(2,1)S(1)}, bf16[32,2048]{1,0:T(8,128)(2,1)S(1)}, u32[]{:S(2)}, u32[]{:S(2)}) collective-permute-start(bf16[32,2048]{1,0:T(8,128)(2,1)S(1)} %dynamic-slice_bitcast_fusion), channel_id=1, source_target_pairs={{0,32},{32,0},{1,33},{33,1},{2,34},{34,2},{3,35},{35,3},{4,36},{36... | collective-permute-start | bytes 393224 | tf_op jit(solution)/shard_map/ppermute | solution.py:315
Sparse Core Ops, SparseCore 0:
  42.1 67.0 all-gather.1
  115.7 49.0 reduce-scatter.1
